TPU v7x, 32 devices: a whole 2x2x4 slice. The times are simulated.
32 devices in a mesh: ctx: 2 (over core), head: 4 (over y, x), rep: 4 (over z).
Axes of the slice: x: 2, y: 2, z: 4, core: 2. Of those that a mesh axis runs over, the one named last changes fastest.
Arguments:
- queries: bfloat16 [4096, 2048], P(('rep', 'ctx'), 'head'), parts along dimension 0, may hold values from -9 to 9
- keys: bfloat16 [4096, 2048], P(('rep', 'ctx'), 'head'), parts along dimension 0, may hold values from -9 to 9
- values: bfloat16 [4096, 2048], P(('rep', 'ctx'), 'head'), parts along dimension 0, may hold values from -6 to 6
- out_weight: bfloat16 [2048, 4096], P('head', 'ctx'), may hold values from -0.125 to 0.125
- out_grad: bfloat16 [4096, 4096], P(('rep', 'ctx')), parts along dimension 0, may hold values from -6 to 6
Outputs:
- layer_out: bfloat16 [4096, 4096], P(('rep', 'ctx'), 'head'), parts along dimension 0
- query_grad: bfloat16 [4096, 2048], P(('rep', 'ctx'), 'head'), parts along dimension 0
- key_grad: bfloat16 [4096, 2048], P(('rep', 'ctx'), 'head'), parts along dimension 0
- value_grad: bfloat16 [4096, 2048], P(('rep', 'ctx'), 'head'), parts along dimension 0
- weight_grad: float32 [8192, 4096], P(('rep', 'head'), 'ctx'), parts along dimension 0
There are 4 independent parts, one for each index of `rep`. A program takes and returns all parts, laid end to end along the dimension named above; an argument that names none is the same for every part. Nothing has to cross between parts.
All inputs are finite; a program needn't handle non-finite values.
Results may differ from a plain program's by a relative error of at most 0.012.
Values may be sent and summed in bfloat16 or wider, within the bound.
No kernel may reach another device: no remote copies, remote signals or barrier semaphores. Data moves between devices by JAX's collectives and lax.ppermute only.
A program may use at most 128 MiB of HBM per device.

v0:
```python
import functools

import jax
import jax.numpy as jnp
from jax import lax
from jax.experimental import pallas as pl
from jax.experimental.pallas import tpu as pltpu
from jax.sharding import PartitionSpec as P

DH = 128
CHUNK = 256
EPS = 1e-06
F32 = jnp.float32
BF16 = jnp.bfloat16


def feature(x):
    return jnp.where(x > 0, x + 1.0, jnp.exp(jnp.minimum(x, 0.0)))


def dot_nn(a, b):
    return lax.dot_general(a, b, (((1,), (0,)), ((), ())), preferred_element_type=F32)


def dot_nt(a, b):
    return lax.dot_general(a, b, (((1,), (1,)), ((), ())), preferred_element_type=F32)


def dot_tn(a, b):
    return lax.dot_general(a, b, (((0,), (0,)), ((), ())), preferred_element_type=F32)


def shape_of(shape, dtype):
    return jax.ShapeDtypeStruct(shape, dtype)


def params(mib):
    return pltpu.CompilerParams(vmem_limit_bytes=mib * 1024 * 1024)


def cost(flops, moved):
    return pl.CostEstimate(flops=flops, transcendentals=0, bytes_accessed=moved)


def state_kernel(k_ref, v_ref, out_ref):
    for lo in range(0, k_ref.shape[1], DH):
        cols = slice(lo, lo + DH)
        fk = feature(k_ref[:, cols].astype(F32)).astype(BF16)
        out_ref[cols, :] = dot_tn(fk, v_ref[:, cols]).astype(BF16)


def local_state(keys, values):
    width = keys.shape[1]
    return pl.pallas_call(
        state_kernel,
        out_shape=shape_of((width, DH), BF16),
        compiler_params=params(16),
        cost_estimate=cost(2 * keys.size * DH, 4 * keys.size),
    )(keys, values)


def opening_kernel(s_ref, q_hbm, k_hbm, v_hbm, weight_hbm, grad_hbm,
                   state_ref, near_ref, far_ref, turn_ref, q_ref, k_ref, v_ref, sems, slice_sems):
    half, wide = near_ref.shape
    rows = pl.ds(pl.multiple_of(s_ref[3] * half, half), half)
    far_column = 1 - s_ref[2]
    near_column = jnp.where(s_ref[0] == s_ref[1], far_column, s_ref[2])
    loads = []
    for i, lo in enumerate(range(0, k_hbm.shape[1], DH)):
        cols = pl.ds(lo, DH)
        loads.append([
            pltpu.make_async_copy(k_hbm.at[:, cols], k_ref.at[:, cols], sems.at[0, i]),
            pltpu.make_async_copy(v_hbm.at[:, cols], v_ref.at[:, cols], sems.at[1, i]),
        ])
        loads[-1][0].start()
        loads[-1][1].start()
    moves = []
    for i, (column, ref) in enumerate([(near_column, near_ref), (far_column, far_ref)]):
        cols = pl.ds(pl.multiple_of(column * wide, wide), wide)
        moves.append(pltpu.make_async_copy(weight_hbm.at[rows, cols], ref, slice_sems.at[i]))
        moves[-1].start()
    moves.append(pltpu.make_async_copy(q_hbm, q_ref, slice_sems.at[2]))
    moves[-1].start()
    own = turn_ref.shape[1]
    cols = pl.ds(pl.multiple_of((1 - s_ref[0]) * own, own), own)
    moves.append(pltpu.make_async_copy(grad_hbm.at[:, cols], turn_ref, slice_sems.at[3]))
    moves[-1].start()
    for i, lo in enumerate(range(0, k_hbm.shape[1], DH)):
        cols = slice(lo, lo + DH)
        loads[i][0].wait()
        loads[i][1].wait()
        fk = feature(k_ref[:, cols].astype(F32)).astype(BF16)
        state_ref[cols, :] = dot_tn(fk, v_ref[:, cols]).astype(BF16)
    for move in moves:
        move.wait()


def opening(scal, queries, keys, values, weight, out_grad):
    tok, width = keys.shape
    piece = shape_of((weight.shape[0] // 2, weight.shape[1] // 2), BF16)
    hbm = pl.BlockSpec(memory_space=pltpu.HBM)
    vmem = pl.BlockSpec(memory_space=pltpu.VMEM)
    return pl.pallas_call(
        opening_kernel,
        out_shape=(shape_of((width, DH), BF16), piece, piece, shape_of((tok, weight.shape[1]), BF16))
        + (shape_of(keys.shape, BF16),) * 3,
        in_specs=[pl.BlockSpec(memory_space=pltpu.SMEM)] + [hbm] * 5,
        out_specs=(vmem,) * 7,
        scratch_shapes=[
            pltpu.SemaphoreType.DMA((2, width // DH)),
            pltpu.SemaphoreType.DMA((4,)),
        ],
        compiler_params=params(16),
        cost_estimate=cost(2 * keys.size * DH, 4 * keys.size),
    )(scal, queries, keys, values, weight, out_grad)


def forward_kernel(q_ref, k_ref, v_ref, carried_ref, attn_ref, raw_ref, prefix_ref):
    tok, width = q_ref.shape
    chunk = min(CHUNK, tok)
    row = lax.broadcasted_iota(jnp.int32, (chunk, chunk), 0)
    col = lax.broadcasted_iota(jnp.int32, (chunk, chunk), 1)
    lower = row >= col
    for lo in range(0, width, DH):
        cols = slice(lo, lo + DH)
        prefix = carried_ref[cols, :].astype(F32)
        for i in range(tok // chunk):
            rows = slice(i * chunk, (i + 1) * chunk)
            fq = feature(q_ref[rows, cols].astype(F32)).astype(BF16)
            fk = feature(k_ref[rows, cols].astype(F32)).astype(BF16)
            v = v_ref[rows, cols]
            low_prefix = prefix.astype(BF16)
            prefix_ref[i, cols, :] = low_prefix
            scores = jnp.where(lower, dot_nt(fq, fk), 0.0).astype(BF16)
            raw = dot_nn(scores, v) + dot_nn(fq, low_prefix)
            raw_ref[rows, cols] = raw
            inv = lax.rsqrt(jnp.mean(raw * raw, axis=-1, keepdims=True) + EPS)
            attn_ref[rows, cols] = (raw * inv).astype(BF16)
            if i + 1 < tok // chunk:
                prefix = prefix + dot_tn(fk, v)


def forward(queries, keys, values, carried):
    tok, width = queries.shape
    chunks = tok // min(CHUNK, tok)
    return pl.pallas_call(
        forward_kernel,
        out_shape=(
            shape_of((tok, width), BF16),
            shape_of((tok, width), F32),
            shape_of((chunks, width, DH), BF16),
        ),
        compiler_params=params(16),
        cost_estimate=cost(16 * queries.size * DH, 12 * queries.size),
    )(queries, keys, values, carried)


def cotangent_kernel(s_ref, grad_ref, own_ref, rest_ref, q_ref, raw_ref,
                     draw_ref, gsum_ref, glocal_ref, acc_ref):
    own_width, rest_width = own_ref.shape[1], rest_ref.shape[1]
    if own_width == rest_width:
        own = pl.ds(pl.multiple_of(s_ref[0] * own_width, own_width), own_width)
        rest = pl.ds(pl.multiple_of((1 - s_ref[0]) * own_width, own_width), own_width)
        acc_ref[...] = dot_nt(grad_ref[:, own], own_ref[...])
        acc_ref[...] += dot_nt(grad_ref[:, rest], rest_ref[...])
    else:
        count = (own_width + rest_width) // own_width
        acc_ref[...] = jnp.zeros_like(acc_ref)
        for k in range(count):
            place = lax.rem(s_ref[0] + k, count) * own_width
            part = grad_ref[:, pl.ds(pl.multiple_of(place, own_width), own_width)]
            weight = own_ref[...] if k == 0 else rest_ref[:, (k - 1) * own_width : k * own_width]
            acc_ref[...] += dot_nt(part, weight)
    tok, width = q_ref.shape
    chunk = min(CHUNK, tok)
    for lo in range(0, width, DH):
        cols = slice(lo, lo + DH)
        later = jnp.zeros((DH, DH), F32)
        for i in reversed(range(tok // chunk)):
            rows = slice(i * chunk, (i + 1) * chunk)
            glocal_ref[i, cols, :] = later
            grad = acc_ref[rows, cols].astype(BF16).astype(F32)
            raw = raw_ref[rows, cols]
            inv = lax.rsqrt(jnp.mean(raw * raw, axis=-1, keepdims=True) + EPS)
            normed = raw * inv
            mean = jnp.mean(grad * normed, axis=-1, keepdims=True)
            draw = (inv * (grad - normed * mean)).astype(BF16)
            draw_ref[rows, cols] = draw
            fq = feature(q_ref[rows, cols].astype(F32)).astype(BF16)
            later = later + dot_tn(fq, draw)
        gsum_ref[cols, :] = later.astype(BF16)


def smem_then_vmem(count):
    return [pl.BlockSpec(memory_space=pltpu.SMEM)] + [pl.BlockSpec(memory_space=pltpu.VMEM)] * count


def cotangent(scal, out_grad, own, rest, queries, raw):
    tok, width = queries.shape
    chunks = tok // min(CHUNK, tok)
    return pl.pallas_call(
        cotangent_kernel,
        out_shape=(
            shape_of((tok, width), BF16),
            shape_of((width, DH), BF16),
            shape_of((chunks, width, DH), F32),
        ),
        in_specs=smem_then_vmem(5),
        scratch_shapes=[pltpu.VMEM((tok, width), F32)],
        compiler_params=params(16),
        cost_estimate=cost(2 * out_grad.size * width, 4 * out_grad.size),
    )(scal, out_grad, own, rest, queries, raw)


def weight_grad_kernel(s_ref, attn_ref, grad_ref, other_attn_ref, other_grad_ref, out_ref):
    tok = attn_ref.shape[0]
    block = out_ref.shape[1]
    step = pl.program_id(0)
    place = s_ref[0] * other_grad_ref.shape[1] + step * block
    part = grad_ref[:, pl.ds(pl.multiple_of(place, block), block)]
    acc = dot_tn(attn_ref[...], part).astype(BF16).astype(F32)
    here = pl.ds(pl.multiple_of(step * block, block), block)
    for lo in range(0, other_attn_ref.shape[0], tok):
        rows = slice(lo, lo + tok)
        acc += dot_tn(other_attn_ref[rows, :], other_grad_ref[rows, here]).astype(BF16).astype(F32)
    out_ref[...] = acc


def own_weight_grad(scal, attn, out_grad, other_attn, other_grad):
    width = attn.shape[1]
    own_width = other_grad.shape[1]
    block = min(512, own_width)
    return pl.pallas_call(
        weight_grad_kernel,
        out_shape=shape_of((width, own_width), F32),
        grid=(own_width // block,),
        in_specs=smem_then_vmem(4),
        out_specs=pl.BlockSpec((width, block), lambda j: (0, j)),
        compiler_params=params(24),
        cost_estimate=cost(2 * out_grad.size * width, 4 * out_grad.size),
    )(scal, attn, out_grad, other_attn, other_grad)


def backward_kernel(q_ref, k_ref, v_ref, draw_ref, prefix_ref, suffix_ref, glocal_ref,
                    dq_ref, dk_ref, dv_ref):
    tok, width = q_ref.shape
    chunk = min(CHUNK, tok)
    row = lax.broadcasted_iota(jnp.int32, (chunk, chunk), 0)
    col = lax.broadcasted_iota(jnp.int32, (chunk, chunk), 1)
    lower = row >= col
    upper = row <= col
    for lo in range(0, width, DH):
        cols = slice(lo, lo + DH)
        suffix = suffix_ref[cols, :].astype(F32)
        for i in range(tok // chunk):
            rows = slice(i * chunk, (i + 1) * chunk)
            q = q_ref[rows, cols].astype(F32)
            k = k_ref[rows, cols].astype(F32)
            q_slope = jnp.exp(jnp.minimum(q, 0.0))
            k_slope = jnp.exp(jnp.minimum(k, 0.0))
            fq = jnp.where(q > 0, q + 1.0, q_slope).astype(BF16)
            fk = jnp.where(k > 0, k + 1.0, k_slope).astype(BF16)
            v = v_ref[rows, cols]
            draw = draw_ref[rows, cols]
            later = (suffix + glocal_ref[i, cols, :]).astype(BF16)
            dscores = jnp.where(lower, dot_nt(draw, v), 0.0).astype(BF16)
            dfq = dot_nn(dscores, fk) + dot_nt(draw, prefix_ref[i, cols, :])
            dq_ref[rows, cols] = (dfq * q_slope).astype(BF16)
            dscores_t = jnp.where(upper, dot_nt(v, draw), 0.0).astype(BF16)
            dfk = dot_nn(dscores_t, fq) + dot_nt(v, later)
            dk_ref[rows, cols] = (dfk * k_slope).astype(BF16)
            scores_t = jnp.where(upper, dot_nt(fk, fq), 0.0).astype(BF16)
            dv = dot_nn(scores_t, draw) + dot_nn(fk, later)
            dv_ref[rows, cols] = dv.astype(BF16)


def backward(queries, keys, values, draw, prefix, suffix, glocal):
    out = shape_of(queries.shape, BF16)
    return pl.pallas_call(
        backward_kernel, out_shape=(out, out, out), compiler_params=params(16),
        cost_estimate=cost(32 * queries.size * DH, 16 * queries.size),
    )(queries, keys, values, draw, prefix, suffix, glocal)


def halves(s_ref, half):
    first = pl.ds(pl.multiple_of(s_ref[3] * half, half), half)
    second = pl.ds(pl.multiple_of((1 - s_ref[3]) * half, half), half)
    return first, second


def project_near_kernel(s_ref, a_ref, a1_ref, a2_ref, own_ref, rest_ref,
                        m1_ref, z1_ref, o1_ref, oz1_ref, out_ref):
    first, second = halves(s_ref, m1_ref.shape[0])
    wide = out_ref.shape[1]
    local = pl.ds(pl.multiple_of(s_ref[2] * wide, wide), wide)
    mine = s_ref[0] == s_ref[1]

    @pl.when(mine)
    def _():
        out_ref[...] = dot_nn(a_ref[...], own_ref[:, local])

    @pl.when(jnp.logical_not(mine))
    def _():
        out_ref[...] = dot_nn(a_ref[...], rest_ref[:, local])

    acc = dot_nn(a1_ref[:, first], m1_ref[...])
    acc += dot_nn(a1_ref[:, second], z1_ref[...])
    acc += dot_nn(a2_ref[:, first], o1_ref[...])
    acc += dot_nn(a2_ref[:, second], oz1_ref[...])
    out_ref[...] += acc


def project_near(scal, attns, own, rest, pieces):
    tok, width = attns[0].shape
    out_width = pieces[0].shape[1]
    return pl.pallas_call(
        project_near_kernel,
        out_shape=shape_of((tok, out_width), F32),
        in_specs=smem_then_vmem(9),
        compiler_params=params(16),
        cost_estimate=cost(6 * tok * width * out_width, 8 * width * out_width),
    )(scal, *attns, own, rest, *pieces)


def project_far_kernel(s_ref, near_ref, a_ref, d_ref, od_ref, dz_ref, odz_ref, out_ref):
    first, second = halves(s_ref, d_ref.shape[0])
    block = out_ref.shape[1]
    here = pl.ds(pl.multiple_of(pl.program_id(0) * block, block), block)
    acc = near_ref[:, here] + dot_nn(a_ref[:, first], d_ref[:, here] + od_ref[:, here])
    acc += dot_nn(a_ref[:, second], dz_ref[:, here] + odz_ref[:, here])
    out_ref[...] = acc.astype(BF16)


def project_far(scal, near, attn, pieces):
    tok, width = attn.shape
    out_width = pieces[0].shape[1]
    block = 512
    return pl.pallas_call(
        project_far_kernel,
        out_shape=shape_of((tok, out_width), BF16),
        grid=(out_width // block,),
        in_specs=smem_then_vmem(6),
        out_specs=pl.BlockSpec((tok, block), lambda j: (0, j)),
        compiler_params=params(16),
        cost_estimate=cost(2 * tok * width * out_width, 8 * width * out_width),
    )(scal, near, attn, *pieces)


def in_hbm(array):
    return pltpu.with_memory_space_constraint(array, pltpu.HBM)


def after(array, *needed):
    return lax.optimization_barrier((array, *needed))[0]


def shift(array, axis, count, by, wrap):
    pairs = [(i, (i + by) % count) for i in range(count) if wrap or 0 <= i + by < count]
    return lax.ppermute(array, axis, pairs)


def total(arrays):
    if len(arrays) == 1:
        return arrays[0]
    return functools.reduce(jnp.add, [a.astype(F32) for a in arrays])


def body(n_ctx, n_head, n_rep, queries, keys, values, out_weight, out_grad):
    c, h, z = lax.axis_index("ctx"), lax.axis_index("head"), lax.axis_index("rep")
    x, y, p = h & 1, h >> 1, z & 1
    scal = jnp.stack([c, y, x, p]).astype(jnp.int32)
    paired = n_ctx == 2 and n_head == 4 and n_rep % 2 == 0
    own_width = out_weight.shape[1]
    weight_hbm, grad_hbm = in_hbm(out_weight), in_hbm(out_grad)

    if paired:
        group = ("ctx", "head")
        near = [(4 * (i // 2) + i, i ^ 1) for i in range(4)]
        near += [(4 * (1 - i // 2) + i, 4 + (i ^ 2)) for i in range(4)]
        far = [(4 * (1 - i // 2) + i, i ^ 3) for i in range(4)]
        one = [(i, i ^ 1) for i in range(4)] + [(4 + i, 4 + (i ^ 2)) for i in range(4)]
        two = [(i, i ^ 2) for i in range(4)] + [(4 + i, 4 + (i ^ 1)) for i in range(4)]
        zpair = [(i, i ^ 1) for i in range(n_rep)]
        swap = [(0, 1), (1, 0)]
        state, near_piece, far_piece, turn, queries, keys, values = opening(
            scal, in_hbm(queries), in_hbm(keys), in_hbm(values), weight_hbm, grad_hbm
        )
        near_mine = lax.ppermute(near_piece, group, near)
        far_mine = lax.ppermute(far_piece, group, far)
        other_grad = lax.ppermute(turn, "ctx", swap)
    else:
        state = local_state(keys, values)
        other_grad = []
        for k in range(1, n_ctx):
            start = lax.rem(c + k, n_ctx) * own_width
            turn = lax.dynamic_slice_in_dim(out_grad, start, own_width, 1)
            other_grad.append(shift(turn, "ctx", n_ctx, k, True))
        other_grad = jnp.concatenate(other_grad, 0)

    carried = total([shift(state, "ctx", n_ctx, k, False) for k in range(1, n_ctx)])
    rest = [shift(out_weight, "ctx", n_ctx, -k, True) for k in range(1, n_ctx)]
    rest = rest[0] if n_ctx == 2 else jnp.concatenate(rest, 1)
    attn, raw, prefix = forward(queries, keys, values, carried)

    other_attn = [shift(attn, "ctx", n_ctx, k, True) for k in range(1, n_ctx)]
    other_attn = other_attn[0] if n_ctx == 2 else jnp.concatenate(other_attn, 0)
    if paired:
        attn_1 = lax.ppermute(attn, group, one)
        attn_2 = lax.ppermute(attn, group, two)
        near_z = lax.ppermute(near_mine, "rep", zpair)
        raw = after(raw, near_mine, rest, other_grad)

    draw, gsum, glocal = cotangent(scal, out_grad, out_weight, rest, queries, raw)
    suffix = total([shift(gsum, "ctx", n_ctx, -k, False) for k in range(1, n_ctx)])

    if paired:
        far_z = lax.ppermute(after(far_mine, gsum), "rep", zpair)
        other_attn = after(other_attn, gsum, far_mine)

    weight_grad = own_weight_grad(scal, attn, out_grad, other_attn, other_grad)

    if paired:
        near_other = lax.ppermute(after(near_mine, weight_grad), "ctx", swap)
        suffix = after(suffix, weight_grad)

    query_grad, key_grad, value_grad = backward(queries, keys, values, draw, prefix, suffix, glocal)

    if paired:
        attn_3 = lax.ppermute(after(attn_1, query_grad), group, two)
        near_other_z = lax.ppermute(after(near_z, weight_grad), "ctx", swap)
        far_other = lax.ppermute(after(far_mine, weight_grad), "ctx", swap)
        far_other_z = lax.ppermute(after(far_z, query_grad), "ctx", swap)

    if paired:
        near_out = project_near(
            scal, (after(attn, query_grad), attn_1, attn_2), out_weight, rest,
            (near_mine, near_z, near_other, near_other_z),
        )
        layer_out = project_far(scal, near_out, attn_3, (far_mine, far_other, far_z, far_other_z))
    else:
        full = lax.all_gather(out_weight, "ctx", axis=1, tiled=True)
        partial_out = jnp.dot(attn, full, preferred_element_type=F32).astype(BF16)
        layer_out = lax.psum_scatter(partial_out, "head", scatter_dimension=1, tiled=True)
    return layer_out, query_grad, key_grad, value_grad, weight_grad


def solution(mesh):
    tokens = P(("rep", "ctx"), "head")
    sizes = mesh.shape["ctx"], mesh.shape["head"], mesh.shape["rep"]
    return jax.shard_map(
        functools.partial(body, *sizes),
        mesh=mesh,
        in_specs=(tokens, tokens, tokens, P("head", "ctx"), P(("rep", "ctx"), None)),
        out_specs=(tokens, tokens, tokens, tokens, P(("rep", "head"), "ctx")),
        check_vma=False,
    )
```

profile of v0, /device:TPU:0, one launch (start us, length us, event | category | flops | bytes accessed | tf_op | source)
XLA Modules:
  0.0 52.7 jit_solution(7060576578506899633)
XLA Ops:
  0.6 0.5 collective-permute-start.1
  1.1 0.1 pad_add_fusion.s_ref
  1.2 0.0 copy-start
  1.2 0.0 copy-start.1
  1.2 3.4 %shard_map.92 = (bf16[512,128]{1,0:T(8,128)(2,1)S(1)}, bf16[256,1024]{1,0:T(8,128)(2,1)S(1)}, bf16[256,1024]{1,0:T(8,128)(2,1)S(1)}, bf16[512,2048]{1,0:T(8,128)...) custom-call(s32[4]{0:T(128)S(1)} %pad_add_fusion.s_ref, ...), custom_call_target="tpu_custom_call" | custom-call | flops 67108864 | bytes 1048576 | tf_op jit(solution)/shard_map/pallas_call | solution.py:103
  4.7 0.1 collective-permute-start.3
  4.8 2.9 %collective-permute-start.2 = (bf16[256,1024]{1,0:T(8,128)(2,1)S(1)}, bf16[256,1024]{1,0:T(8,128)(2,1)S(1)}, u32[]{:S(2)}, u32[]{:S(2)}) collective-permute-start(bf16[256,1024]{1,0:T(8,128)(2,1)S(1)} %get-tuple-element.37), channel_id=1, source_target_pairs={{0,4},{4,0},{24,12},{28,8},{16,24},{20,28},{8,16},{12,20},{1,5},{5... | collective-permute-start | bytes 1572872 | tf_op jit(solution)/shard_map/ppermute | solution.py:388
  7.7 1.7 %collective-permute-start = (bf16[512,128]{1,0:T(8,128)(2,1)S(1)}, bf16[512,128]{1,0:T(8,128)(2,1)S(1)}, u32[]{:S(2)}, u32[]{:S(2)}) collective-permute-start(bf16[512,128]{1,0:T(8,128)(2,1)S(1)} %get-tuple-element.34), channel_id=1, source_target_pairs={{0,16},{1,17},{2,18},{3,19},{4,20},{5,21},{6,22},{7,23},{8,24},{9,... | collective-permute-start | bytes 393224 | tf_op jit(solution)/shard_map/ppermute | solution.py:359
  9.4 1.3 %collective-permute-start.6 = (bf16[256,1024]{1,0:T(8,128)(2,1)S(1)}, bf16[256,1024]{1,0:T(8,128)(2,1)S(1)}, u32[]{:S(2)}, u32[]{:S(2)}) collective-permute-start(bf16[256,1024]{1,0:T(8,128)(2,1)S(1)} %get-tuple-element.43), channel_id=1, source_target_pairs={{16,12},{20,8},{8,4},{12,0},{17,13},{21,9},{9,5},{13,1},{18,14},{2... | collective-permute-start | bytes 1572872 | tf_op jit(solution)/shard_map/ppermute | solution.py:389
  10.7 0.0 collective-permute-done.carried_ref
  10.8 1.6 %shard_map.93 = (bf16[512,512]{1,0:T(8,128)(2,1)S(1)}, f32[512,512]{1,0:T(8,128)S(1)}, bf16[2,512,128]{2,1,0:T(8,128)(2,1)S(1)}) custom-call(bf16[512,512]{1,0:T(8,128)(2,1)S(1)} %get-tuple-element.31.q_ref, bf16[512,512]{1,0:T(8,128)(2,1)S(1)} %get-tuple-element.32.k_ref, bf16[512,512]{1,0:T(8,128)(2,1)S(1)} %get-tuple-element.33.v_ref, ...), custom_call_target="tpu_custom_call" | custom-call | flops 536870912 | bytes 3145728 | tf_op jit(solution)/shard_map/pallas_call | solution.py:146
  12.3 2.6 %collective-permute-start.5 = (bf16[512,512]{1,0:T(8,128)(2,1)S(1)}, bf16[512,512]{1,0:T(8,128)(2,1)S(1)}, u32[]{:S(2)}, u32[]{:S(2)}) collective-permute-start(bf16[512,512]{1,0:T(8,128)(2,1)S(1)} %get-tuple-element.48.attn_ref.a_ref), channel_id=1, source_target_pairs={{0,16},{16,0},{1,17},{17,1},{2,18},{18,2},{3,19},{19,3},{4,20},{20... | collective-permute-start | bytes 1572872 | tf_op jit(solution)/shard_map/ppermute | solution.py:359
  14.9 0.2 collective-permute-done.2.m1_ref
  15.1 2.5 %collective-permute-start.7 = (bf16[512,512]{1,0:T(8,128)(2,1)S(1)}, bf16[512,512]{1,0:T(8,128)(2,1)S(1)}, u32[]{:S(2)}, u32[]{:S(2)}) collective-permute-start(bf16[512,512]{1,0:T(8,128)(2,1)S(1)} %get-tuple-element.48.attn_ref.a_ref), channel_id=1, source_target_pairs={{0,4},{4,0},{8,12},{12,8},{16,24},{20,28},{24,16},{28,20},{1,5},{5... | collective-permute-start | bytes 1572872 | tf_op jit(solution)/shard_map/ppermute | solution.py:408
  17.6 0.0 collective-permute-done.1.rest_ref
  17.6 1.6 %collective-permute-start.9 = (bf16[256,1024]{1,0:T(8,128)(2,1)S(1)}, bf16[256,1024]{1,0:T(8,128)(2,1)S(1)}, u32[]{:S(2)}, u32[]{:S(2)}) collective-permute-start(bf16[256,1024]{1,0:T(8,128)(2,1)S(1)} %collective-permute-done.2.m1_ref), channel_id=1, source_target_pairs={{0,1},{1,0},{2,3},{3,2},{4,5},{5,4},{6,7},{7,6},{8,9},{9,8},{10,11... | collective-permute-start | bytes 1572872 | tf_op jit(solution)/shard_map/ppermute | solution.py:410
  19.2 0.0 collective-permute-done.3.other_grad_ref
  19.2 0.0 copy-done
  19.2 0.0 copy-done.1
  19.2 4.0 %shard_map.94 = (bf16[512,512]{1,0:T(8,128)(2,1)S(1)}, bf16[512,128]{1,0:T(8,128)(2,1)S(1)}, f32[2,512,128]{2,1,0:T(8,128)S(1)}) custom-call(s32[4]{0:T(128)S(1)} %pad_add_fusion.s_ref, bf16[512,4096]{1,0:T(8,128)(2,1)S(1)} %copy-done, bf16[512,2048]{1,0:T(8,128)(2,1)S(1)} %copy-done.1, bf16[512,2048]{1,0:T(8,128)(2,1)S(1)} %collective-permute-done.1.rest_ref, ...), custom_call_target="tpu_custom_call" | custom-call | flops 2147483648 | bytes 8388608 | tf_op jit(solution)/shard_map/pallas_call | solution.py:201
  23.2 0.0 collective-permute-done.6.d_ref
  23.2 0.5 collective-permute-start.14
  23.7 2.5 %collective-permute-start.8 = (bf16[512,512]{1,0:T(8,128)(2,1)S(1)}, bf16[512,512]{1,0:T(8,128)(2,1)S(1)}, u32[]{:S(2)}, u32[]{:S(2)}) collective-permute-start(bf16[512,512]{1,0:T(8,128)(2,1)S(1)} %get-tuple-element.48.attn_ref.a_ref), channel_id=1, source_target_pairs={{0,8},{4,12},{8,0},{12,4},{16,20},{20,16},{24,28},{28,24},{1,9},{5... | collective-permute-start | bytes 1572872 | tf_op jit(solution)/shard_map/ppermute | solution.py:409
  26.2 0.0 collective-permute-done.5.other_attn_ref
  26.2 1.3 %collective-permute-start.4 = (bf16[512,128]{1,0:T(8,128)(2,1)S(1)}, bf16[512,128]{1,0:T(8,128)(2,1)S(1)}, u32[]{:S(2)}, u32[]{:S(2)}) collective-permute-start(bf16[512,128]{1,0:T(8,128)(2,1)S(1)} %get-tuple-element.42), channel_id=1, source_target_pairs={{16,0},{17,1},{18,2},{19,3},{20,4},{21,5},{22,6},{23,7},{24,8},{25... | collective-permute-start | bytes 393224 | tf_op jit(solution)/shard_map/ppermute | solution.py:359
  27.5 4.8 %shard_map.95 = f32[512,2048]{1,0:T(8,128)} custom-call(s32[4]{0:T(128)S(1)} %pad_add_fusion.s_ref, bf16[512,512]{1,0:T(8,128)(2,1)S(1)} %get-tuple-element.48.attn_ref.a_ref, bf16[512,4096]{1,0:T(8,128)(2,1)S(1)} %copy-done, bf16[512,512]{1,0:T(8,128)(2,1)S(1)} %collective-permute-done.5.other_attn_ref, ...), custom_call_target="tpu_custom_call" | custom-call | flops 2147483648 | bytes 8388608 | tf_op jit(solution)/shard_map/pallas_call | solution.py:233
  32.3 0.2 collective-permute-done.9.z1_ref
  32.5 0.9 %collective-permute-start.10 = (bf16[256,1024]{1,0:T(8,128)(2,1)S(1)}, bf16[256,1024]{1,0:T(8,128)(2,1)S(1)}, u32[]{:S(2)}, u32[]{:S(2)}) collective-permute-start(bf16[256,1024]{1,0:T(8,128)(2,1)S(1)} %collective-permute-done.2.m1_ref), channel_id=1, source_target_pairs={{0,16},{16,0},{1,17},{17,1},{2,18},{18,2},{3,19},{19,3},{4,20},{20... | collective-permute-start | bytes 1572872 | tf_op jit(solution)/shard_map/ppermute | solution.py:423
  33.4 0.0 collective-permute-done.4.suffix_ref
  33.4 0.1 collective-permute-start.11
  33.5 3.8 %shard_map.96 = (bf16[512,512]{1,0:T(8,128)(2,1)}, bf16[512,512]{1,0:T(8,128)(2,1)}, bf16[512,512]{1,0:T(8,128)(2,1)}) custom-call(bf16[512,512]{1,0:T(8,128)(2,1)S(1)} %get-tuple-element.31.q_ref, bf16[512,512]{1,0:T(8,128)(2,1)S(1)} %get-tuple-element.32.k_ref, bf16[512,512]{1,0:T(8,128)(2,1)S(1)} %get-tuple-element.33.v_ref, ...), custom_call_target="tpu_custom_call" | custom-call | flops 1073741824 | bytes 4194304 | tf_op jit(solution)/shard_map/pallas_call | solution.py:279
  37.3 0.0 collective-permute-done.7.a1_ref
  37.3 0.4 collective-permute-start.13
  37.7 3.5 %collective-permute-done.14.dz_ref = bf16[256,1024]{1,0:T(8,128)(2,1)S(1)} collective-permute-done((bf16[256,1024]{1,0:T(8,128)(2,1)S(1)}, bf16[256,1024]{1,0:T(8,128)(2,1)S(1)}, u32[]{:S(2)}, u32[]{:S(2)}) %collective-permute-start.14) | collective-permute-done | bytes 524320 | tf_op jit(solution)/shard_map/ppermute | solution.py:417
  41.3 0.6 %collective-permute-start.12 = (bf16[512,512]{1,0:T(8,128)(2,1)S(1)}, bf16[512,512]{1,0:T(8,128)(2,1)S(1)}, u32[]{:S(2)}, u32[]{:S(2)}) collective-permute-start(bf16[512,512]{1,0:T(8,128)(2,1)S(1)} %collective-permute-done.7.a1_ref), channel_id=1, source_target_pairs={{0,8},{4,12},{8,0},{12,4},{16,20},{20,16},{24,28},{28,24},{1,9},{5... | collective-permute-start | bytes 1572872 | tf_op jit(solution)/shard_map/ppermute | solution.py:429
  41.8 0.0 collective-permute-done.8.a2_ref
  41.8 0.0 collective-permute-start.15
  41.8 0.0 collective-permute-done.10.o1_ref
  41.9 0.0 collective-permute-done.11.oz1_ref
  41.9 2.5 %shard_map.97.near_ref = f32[512,1024]{1,0:T(8,128)S(1)} custom-call(s32[4]{0:T(128)S(1)} %pad_add_fusion.s_ref, bf16[512,512]{1,0:T(8,128)(2,1)S(1)} %get-tuple-element.48.attn_ref.a_ref, bf16[512,512]{1,0:T(8,128)(2,1)S(1)} %collective-permute-done.7.a1_ref, bf16[512,512]{1,0:T(8,128)(2,1)S(1)} %collective-permute-done.8.a2_ref, ...), custom_call_target="tpu_custom_call" | custom-call | flops 1610612736 | bytes 4194304 | tf_op jit(solution)/shard_map/pallas_call | solution.py:316
  44.4 0.0 collective-permute-done.13.od_ref
  44.4 6.0 %collective-permute-done.12.a_ref = bf16[512,512]{1,0:T(8,128)(2,1)S(1)} collective-permute-done((bf16[512,512]{1,0:T(8,128)(2,1)S(1)}, bf16[512,512]{1,0:T(8,128)(2,1)S(1)}, u32[]{:S(2)}, u32[]{:S(2)}) %collective-permute-start.12) | collective-permute-done | bytes 524320 | tf_op jit(solution)/shard_map/ppermute | solution.py:429
  50.4 0.0 collective-permute-done.15.odz_ref
  50.4 2.3 %shard_map.98 = bf16[512,1024]{1,0:T(8,128)(2,1)} custom-call(s32[4]{0:T(128)S(1)} %pad_add_fusion.s_ref, f32[512,1024]{1,0:T(8,128)S(1)} %shard_map.97.near_ref, bf16[512,512]{1,0:T(8,128)(2,1)S(1)} %collective-permute-done.12.a_ref, bf16[256,1024]{1,0:T(8,128)(2,1)S(1)} %collective-permute-done.6.d_ref, ...), custom_call_target="tpu_custom_call" | custom-call | flops 536870912 | bytes 4194304 | tf_op jit(solution)/shard_map/pallas_call | solution.py:338
Async XLA Ops:
  0.6 17.0 %collective-permute-start.1 = (bf16[512,2048]{1,0:T(8,128)(2,1)}, bf16[512,2048]{1,0:T(8,128)(2,1)S(1)}, u32[]{:S(2)}, u32[]{:S(2)}) collective-permute-start(bf16[512,2048]{1,0:T(8,128)(2,1)} %own_ref.3), channel_id=1, source_target_pairs={{0,16},{16,0},{1,17},{17,1},{2,18},{18,2},{3,19},{19,3},{4,20},{20... | collective-permute-start | bytes 6291464 | tf_op jit(solution)/shard_map/ppermute | solution.py:359
  1.2 18.0 %copy-start = (bf16[512,4096]{1,0:T(8,128)(2,1)S(1)}, bf16[512,4096]{1,0:T(8,128)(2,1)}, u32[]{:S(2)}) copy-start(bf16[512,4096]{1,0:T(8,128)(2,1)} %grad_ref.3) | copy-start | bytes 12582916
  1.2 18.0 %copy-start.1 = (bf16[512,2048]{1,0:T(8,128)(2,1)S(1)}, bf16[512,2048]{1,0:T(8,128)(2,1)}, u32[]{:S(2)}) copy-start(bf16[512,2048]{1,0:T(8,128)(2,1)} %own_ref.3) | copy-start | bytes 6291460
  4.7 14.5 %collective-permute-start.3 = (bf16[512,2048]{1,0:T(8,128)(2,1)S(1)}, bf16[512,2048]{1,0:T(8,128)(2,1)S(1)}, u32[]{:S(2)}, u32[]{:S(2)}) collective-permute-start(bf16[512,2048]{1,0:T(8,128)(2,1)S(1)} %get-tuple-element.38), channel_id=1, source_target_pairs={{0,16},{16,0},{1,17},{17,1},{2,18},{18,2},{3,19},{19,3},{4,20},{20... | collective-permute-start | bytes 6291464 | tf_op jit(solution)/shard_map/ppermute | solution.py:390
  4.8 10.4 %collective-permute-start.2 = (bf16[256,1024]{1,0:T(8,128)(2,1)S(1)}, bf16[256,1024]{1,0:T(8,128)(2,1)S(1)}, u32[]{:S(2)}, u32[]{:S(2)}) collective-permute-start(bf16[256,1024]{1,0:T(8,128)(2,1)S(1)} %get-tuple-element.37), channel_id=1, source_target_pairs={{0,4},{4,0},{24,12},{28,8},{16,24},{20,28},{8,16},{12,20},{1,5},{5... | collective-permute-start | bytes 1572872 | tf_op jit(solution)/shard_map/ppermute | solution.py:388
  7.7 3.0 %collective-permute-start = (bf16[512,128]{1,0:T(8,128)(2,1)S(1)}, bf16[512,128]{1,0:T(8,128)(2,1)S(1)}, u32[]{:S(2)}, u32[]{:S(2)}) collective-permute-start(bf16[512,128]{1,0:T(8,128)(2,1)S(1)} %get-tuple-element.34), channel_id=1, source_target_pairs={{0,16},{1,17},{2,18},{3,19},{4,20},{5,21},{6,22},{7,23},{8,24},{9,... | collective-permute-start | bytes 393224 | tf_op jit(solution)/shard_map/ppermute | solution.py:359
  9.4 13.7 %collective-permute-start.6 = (bf16[256,1024]{1,0:T(8,128)(2,1)S(1)}, bf16[256,1024]{1,0:T(8,128)(2,1)S(1)}, u32[]{:S(2)}, u32[]{:S(2)}) collective-permute-start(bf16[256,1024]{1,0:T(8,128)(2,1)S(1)} %get-tuple-element.43), channel_id=1, source_target_pairs={{16,12},{20,8},{8,4},{12,0},{17,13},{21,9},{9,5},{13,1},{18,14},{2... | collective-permute-start | bytes 1572872 | tf_op jit(solution)/shard_map/ppermute | solution.py:389
  12.3 13.9 %collective-permute-start.5 = (bf16[512,512]{1,0:T(8,128)(2,1)S(1)}, bf16[512,512]{1,0:T(8,128)(2,1)S(1)}, u32[]{:S(2)}, u32[]{:S(2)}) collective-permute-start(bf16[512,512]{1,0:T(8,128)(2,1)S(1)} %get-tuple-element.48.attn_ref.a_ref), channel_id=1, source_target_pairs={{0,16},{16,0},{1,17},{17,1},{2,18},{18,2},{3,19},{19,3},{4,20},{20... | collective-permute-start | bytes 1572872 | tf_op jit(solution)/shard_map/ppermute | solution.py:359
  15.1 22.2 %collective-permute-start.7 = (bf16[512,512]{1,0:T(8,128)(2,1)S(1)}, bf16[512,512]{1,0:T(8,128)(2,1)S(1)}, u32[]{:S(2)}, u32[]{:S(2)}) collective-permute-start(bf16[512,512]{1,0:T(8,128)(2,1)S(1)} %get-tuple-element.48.attn_ref.a_ref), channel_id=1, source_target_pairs={{0,4},{4,0},{8,12},{12,8},{16,24},{20,28},{24,16},{28,20},{1,5},{5... | collective-permute-start | bytes 1572872 | tf_op jit(solution)/shard_map/ppermute | solution.py:408
  17.6 14.9 %collective-permute-start.9 = (bf16[256,1024]{1,0:T(8,128)(2,1)S(1)}, bf16[256,1024]{1,0:T(8,128)(2,1)S(1)}, u32[]{:S(2)}, u32[]{:S(2)}) collective-permute-start(bf16[256,1024]{1,0:T(8,128)(2,1)S(1)} %collective-permute-done.2.m1_ref), channel_id=1, source_target_pairs={{0,1},{1,0},{2,3},{3,2},{4,5},{5,4},{6,7},{7,6},{8,9},{9,8},{10,11... | collective-permute-start | bytes 1572872 | tf_op jit(solution)/shard_map/ppermute | solution.py:410
  23.2 18.1 %collective-permute-start.14 = (bf16[256,1024]{1,0:T(8,128)(2,1)S(1)}, bf16[256,1024]{1,0:T(8,128)(2,1)S(1)}, u32[]{:S(2)}, u32[]{:S(2)}) collective-permute-start(bf16[256,1024]{1,0:T(8,128)(2,1)S(1)} %collective-permute-done.6.d_ref), channel_id=1, source_target_pairs={{0,1},{1,0},{2,3},{3,2},{4,5},{5,4},{6,7},{7,6},{8,9},{9,8},{10,11... | collective-permute-start | bytes 1572872 | tf_op jit(solution)/shard_map/ppermute | solution.py:417
  23.7 18.1 %collective-permute-start.8 = (bf16[512,512]{1,0:T(8,128)(2,1)S(1)}, bf16[512,512]{1,0:T(8,128)(2,1)S(1)}, u32[]{:S(2)}, u32[]{:S(2)}) collective-permute-start(bf16[512,512]{1,0:T(8,128)(2,1)S(1)} %get-tuple-element.48.attn_ref.a_ref), channel_id=1, source_target_pairs={{0,8},{4,12},{8,0},{12,4},{16,20},{20,16},{24,28},{28,24},{1,9},{5... | collective-permute-start | bytes 1572872 | tf_op jit(solution)/shard_map/ppermute | solution.py:409
  26.2 7.2 %collective-permute-start.4 = (bf16[512,128]{1,0:T(8,128)(2,1)S(1)}, bf16[512,128]{1,0:T(8,128)(2,1)S(1)}, u32[]{:S(2)}, u32[]{:S(2)}) collective-permute-start(bf16[512,128]{1,0:T(8,128)(2,1)S(1)} %get-tuple-element.42), channel_id=1, source_target_pairs={{16,0},{17,1},{18,2},{19,3},{20,4},{21,5},{22,6},{23,7},{24,8},{25... | collective-permute-start | bytes 393224 | tf_op jit(solution)/shard_map/ppermute | solution.py:359
  32.5 9.4 %collective-permute-start.10 = (bf16[256,1024]{1,0:T(8,128)(2,1)S(1)}, bf16[256,1024]{1,0:T(8,128)(2,1)S(1)}, u32[]{:S(2)}, u32[]{:S(2)}) collective-permute-start(bf16[256,1024]{1,0:T(8,128)(2,1)S(1)} %collective-permute-done.2.m1_ref), channel_id=1, source_target_pairs={{0,16},{16,0},{1,17},{17,1},{2,18},{18,2},{3,19},{19,3},{4,20},{20... | collective-permute-start | bytes 1572872 | tf_op jit(solution)/shard_map/ppermute | solution.py:423
  33.4 8.4 %collective-permute-start.11 = (bf16[256,1024]{1,0:T(8,128)(2,1)S(1)}, bf16[256,1024]{1,0:T(8,128)(2,1)S(1)}, u32[]{:S(2)}, u32[]{:S(2)}) collective-permute-start(bf16[256,1024]{1,0:T(8,128)(2,1)S(1)} %collective-permute-done.9.z1_ref), channel_id=1, source_target_pairs={{0,16},{16,0},{1,17},{17,1},{2,18},{18,2},{3,19},{19,3},{4,20},{20... | collective-permute-start | bytes 1572872 | tf_op jit(solution)/shard_map/ppermute | solution.py:430
  37.3 7.1 %collective-permute-start.13 = (bf16[256,1024]{1,0:T(8,128)(2,1)S(1)}, bf16[256,1024]{1,0:T(8,128)(2,1)S(1)}, u32[]{:S(2)}, u32[]{:S(2)}) collective-permute-start(bf16[256,1024]{1,0:T(8,128)(2,1)S(1)} %collective-permute-done.6.d_ref), channel_id=1, source_target_pairs={{0,16},{16,0},{1,17},{17,1},{2,18},{18,2},{3,19},{19,3},{4,20},{20... | collective-permute-start | bytes 1572872 | tf_op jit(solution)/shard_map/ppermute | solution.py:431
  41.3 9.2 %collective-permute-start.12 = (bf16[512,512]{1,0:T(8,128)(2,1)S(1)}, bf16[512,512]{1,0:T(8,128)(2,1)S(1)}, u32[]{:S(2)}, u32[]{:S(2)}) collective-permute-start(bf16[512,512]{1,0:T(8,128)(2,1)S(1)} %collective-permute-done.7.a1_ref), channel_id=1, source_target_pairs={{0,8},{4,12},{8,0},{12,4},{16,20},{20,16},{24,28},{28,24},{1,9},{5... | collective-permute-start | bytes 1572872 | tf_op jit(solution)/shard_map/ppermute | solution.py:429
  41.8 8.6 %collective-permute-start.15 = (bf16[256,1024]{1,0:T(8,128)(2,1)S(1)}, bf16[256,1024]{1,0:T(8,128)(2,1)S(1)}, u32[]{:S(2)}, u32[]{:S(2)}) collective-permute-start(bf16[256,1024]{1,0:T(8,128)(2,1)S(1)} %collective-permute-done.14.dz_ref), channel_id=1, source_target_pairs={{0,16},{16,0},{1,17},{17,1},{2,18},{18,2},{3,19},{19,3},{4,20},{20... | collective-permute-start | bytes 1572872 | tf_op jit(solution)/shard_map/ppermute | solution.py:432
where the time goes:
time: 52.9 us; the launch traced here: 52.7 us
  Pallas kernels  22.3 us (42%)
  starting transfers between devices  19.6 us (37%)
  waiting for transfers between devices  9.98 us (19%)
  between operations  0.73 us (1%)
    ppermute x4, starting transfers between devices, shift(): return lax.ppermute(array, axis, pairs)  6.13 us
    ppermute x1, waiting for transfers between devices, body(): attn_3 = lax.ppermute(after(attn_1, query_grad), group, two)  6.02 us
    pallas_call x1, Pallas kernels, own_weight_grad(): pl.pallas_call(weight_grad_kernel, out_shape=shape_of((width, own_width),...  4.76 us
    pallas_call x1, Pallas kernels, cotangent(): pl.pallas_call(cotangent_kernel, out_shape=(shape_of((tok, width), BF16),...  3.96 us
    pallas_call x1, Pallas kernels, backward(): pl.pallas_call(backward_kernel, out_shape=(out, out, out), compiler_param...  3.79 us
    ppermute x1, waiting for transfers between devices, body(): far_z = lax.ppermute(after(far_mine, gsum), 'rep', zpair)  3.53 us
    pallas_call x1, Pallas kernels, opening(): pl.pallas_call(opening_kernel, out_shape=(shape_of((width, DH), BF16), pi...  3.42 us
    ppermute x1, starting transfers between devices, body(): near_mine = lax.ppermute(near_piece, group, near)  2.94 us
  transfers between devices with their start and end apart: 16, of which 4 were waited for; matrix products, arithmetic and copies ran while one was open for 0% of the time, Pallas kernels for 38%

commit v1 on v0

--- a/solution.py
+++ b/solution.py
@@ -155,40 +155,39 @@
     )(queries, keys, values, carried)
 
 
-def cotangent_kernel(s_ref, grad_ref, own_ref, rest_ref, q_ref, raw_ref,
-                     draw_ref, gsum_ref, glocal_ref, acc_ref):
+def cotangent_kernel(s_ref, grad_ref, own_ref, rest_ref, q_ref, raw_ref, draw_ref, gsum_ref, glocal_ref):
     own_width, rest_width = own_ref.shape[1], rest_ref.shape[1]
-    if own_width == rest_width:
-        own = pl.ds(pl.multiple_of(s_ref[0] * own_width, own_width), own_width)
-        rest = pl.ds(pl.multiple_of((1 - s_ref[0]) * own_width, own_width), own_width)
-        acc_ref[...] = dot_nt(grad_ref[:, own], own_ref[...])
-        acc_ref[...] += dot_nt(grad_ref[:, rest], rest_ref[...])
-    else:
-        count = (own_width + rest_width) // own_width
-        acc_ref[...] = jnp.zeros_like(acc_ref)
+    count = (own_width + rest_width) // own_width
+    tok, width = q_ref.shape
+    chunk = min(CHUNK, tok)
+    for top in range(0, width, 2 * DH):
+        pair = slice(top, top + 2 * DH)
+        total_grad = None
         for k in range(count):
             place = lax.rem(s_ref[0] + k, count) * own_width
             part = grad_ref[:, pl.ds(pl.multiple_of(place, own_width), own_width)]
-            weight = own_ref[...] if k == 0 else rest_ref[:, (k - 1) * own_width : k * own_width]
-            acc_ref[...] += dot_nt(part, weight)
-    tok, width = q_ref.shape
-    chunk = min(CHUNK, tok)
-    for lo in range(0, width, DH):
-        cols = slice(lo, lo + DH)
-        later = jnp.zeros((DH, DH), F32)
-        for i in reversed(range(tok // chunk)):
-            rows = slice(i * chunk, (i + 1) * chunk)
-            glocal_ref[i, cols, :] = later
-            grad = acc_ref[rows, cols].astype(BF16).astype(F32)
-            raw = raw_ref[rows, cols]
-            inv = lax.rsqrt(jnp.mean(raw * raw, axis=-1, keepdims=True) + EPS)
-            normed = raw * inv
-            mean = jnp.mean(grad * normed, axis=-1, keepdims=True)
-            draw = (inv * (grad - normed * mean)).astype(BF16)
-            draw_ref[rows, cols] = draw
-            fq = feature(q_ref[rows, cols].astype(F32)).astype(BF16)
-            later = later + dot_tn(fq, draw)
-        gsum_ref[cols, :] = later.astype(BF16)
+            if k == 0:
+                weight = own_ref[pair, :]
+            else:
+                weight = rest_ref[pair, (k - 1) * own_width : k * own_width]
+            product = dot_nt(part, weight)
+            total_grad = product if total_grad is None else total_grad + product
+        for lo in (top, top + DH):
+            cols = slice(lo, lo + DH)
+            later = jnp.zeros((DH, DH), F32)
+            for i in reversed(range(tok // chunk)):
+                rows = slice(i * chunk, (i + 1) * chunk)
+                glocal_ref[i, cols, :] = later
+                grad = total_grad[rows, lo - top : lo - top + DH].astype(BF16).astype(F32)
+                raw = raw_ref[rows, cols]
+                inv = lax.rsqrt(jnp.mean(raw * raw, axis=-1, keepdims=True) + EPS)
+                normed = raw * inv
+                mean = jnp.mean(grad * normed, axis=-1, keepdims=True)
+                draw = (inv * (grad - normed * mean)).astype(BF16)
+                draw_ref[rows, cols] = draw
+                fq = feature(q_ref[rows, cols].astype(F32)).astype(BF16)
+                later = later + dot_tn(fq, draw)
+            gsum_ref[cols, :] = later.astype(BF16)
 
 
 def smem_then_vmem(count):
@@ -206,39 +205,48 @@
             shape_of((chunks, width, DH), F32),
         ),
         in_specs=smem_then_vmem(5),
-        scratch_shapes=[pltpu.VMEM((tok, width), F32)],
         compiler_params=params(16),
         cost_estimate=cost(2 * out_grad.size * width, 4 * out_grad.size),
     )(scal, out_grad, own, rest, queries, raw)
 
 
-def weight_grad_kernel(s_ref, attn_ref, grad_ref, other_attn_ref, other_grad_ref, out_ref):
-    tok = attn_ref.shape[0]
-    block = out_ref.shape[1]
-    step = pl.program_id(0)
-    place = s_ref[0] * other_grad_ref.shape[1] + step * block
-    part = grad_ref[:, pl.ds(pl.multiple_of(place, block), block)]
-    acc = dot_tn(attn_ref[...], part).astype(BF16).astype(F32)
-    here = pl.ds(pl.multiple_of(step * block, block), block)
-    for lo in range(0, other_attn_ref.shape[0], tok):
-        rows = slice(lo, lo + tok)
-        acc += dot_tn(other_attn_ref[rows, :], other_grad_ref[rows, here]).astype(BF16).astype(F32)
-    out_ref[...] = acc
-
-
-def own_weight_grad(scal, attn, out_grad, other_attn, other_grad):
+def weight_grad_kernel(s_ref, attn_ref, grad_ref, other_ref, other_grad_ref, out_hbm, out_buf, sems):
+    tok, width = attn_ref.shape
+    blocks, _, block = out_buf.shape
+    attn_t = attn_ref[...].T
+    others_t = [other_ref[lo : lo + tok, :].T for lo in range(0, other_ref.shape[0], tok)]
+    moves = []
+    for j in range(blocks):
+        here = slice(j * block, (j + 1) * block)
+        place = s_ref[0] * (blocks * block) + j * block
+        part = grad_ref[:, pl.ds(pl.multiple_of(place, block), block)]
+        acc = dot_nn(attn_t, part).astype(BF16).astype(F32)
+        for k, other_t in enumerate(others_t):
+            part = other_grad_ref[k * tok : (k + 1) * tok, here]
+            acc += dot_nn(other_t, part).astype(BF16).astype(F32)
+        out_buf[j] = acc
+        moves.append(pltpu.make_async_copy(out_buf.at[j], out_hbm.at[:, here], sems.at[j]))
+        moves[-1].start()
+    for move in moves:
+        move.wait()
+
+
+def own_weight_grad(scal, attn, out_grad, other, other_grad):
     width = attn.shape[1]
     own_width = other_grad.shape[1]
-    block = min(512, own_width)
+    block = min(256, own_width)
     return pl.pallas_call(
         weight_grad_kernel,
         out_shape=shape_of((width, own_width), F32),
-        grid=(own_width // block,),
         in_specs=smem_then_vmem(4),
-        out_specs=pl.BlockSpec((width, block), lambda j: (0, j)),
-        compiler_params=params(24),
+        out_specs=pl.BlockSpec(memory_space=pl.ANY),
+        scratch_shapes=[
+            pltpu.VMEM((own_width // block, width, block), F32),
+            pltpu.SemaphoreType.DMA((own_width // block,)),
+        ],
+        compiler_params=params(16),
         cost_estimate=cost(2 * out_grad.size * width, 4 * out_grad.size),
-    )(scal, attn, out_grad, other_attn, other_grad)
+    )(scal, attn, out_grad, other, other_grad)
 
 
 def backward_kernel(q_ref, k_ref, v_ref, draw_ref, prefix_ref, suffix_ref, glocal_ref,
@@ -277,7 +285,9 @@
 def backward(queries, keys, values, draw, prefix, suffix, glocal):
     out = shape_of(queries.shape, BF16)
     return pl.pallas_call(
-        backward_kernel, out_shape=(out, out, out), compiler_params=params(16),
+        backward_kernel,
+        out_shape=(out, out, out),
+        compiler_params=params(16),
         cost_estimate=cost(32 * queries.size * DH, 16 * queries.size),
     )(queries, keys, values, draw, prefix, suffix, glocal)
 
@@ -288,9 +298,7 @@
     return first, second
 
 
-def project_near_kernel(s_ref, a_ref, a1_ref, a2_ref, own_ref, rest_ref,
-                        m1_ref, z1_ref, o1_ref, oz1_ref, out_ref):
-    first, second = halves(s_ref, m1_ref.shape[0])
+def project_own_kernel(s_ref, a_ref, own_ref, rest_ref, out_ref):
     wide = out_ref.shape[1]
     local = pl.ds(pl.multiple_of(s_ref[2] * wide, wide), wide)
     mine = s_ref[0] == s_ref[1]
@@ -303,44 +311,67 @@
     def _():
         out_ref[...] = dot_nn(a_ref[...], rest_ref[:, local])
 
-    acc = dot_nn(a1_ref[:, first], m1_ref[...])
+
+def project_own(scal, attn, own, rest, out_width):
+    tok, width = attn.shape
+    return pl.pallas_call(
+        project_own_kernel,
+        out_shape=shape_of((tok, out_width), F32),
+        in_specs=smem_then_vmem(3),
+        compiler_params=params(16),
+        cost_estimate=cost(2 * tok * width * out_width, 8 * width * out_width),
+    )(scal, attn, own, rest)
+
+
+def project_near_kernel(s_ref, out_so_far_ref, a1_ref, a2_ref, m1_ref, z1_ref, o1_ref, oz1_ref, out_ref):
+    first, second = halves(s_ref, m1_ref.shape[0])
+    acc = out_so_far_ref[...] + dot_nn(a1_ref[:, first], m1_ref[...])
     acc += dot_nn(a1_ref[:, second], z1_ref[...])
     acc += dot_nn(a2_ref[:, first], o1_ref[...])
     acc += dot_nn(a2_ref[:, second], oz1_ref[...])
-    out_ref[...] += acc
-
-
-def project_near(scal, attns, own, rest, pieces):
+    out_ref[...] = acc
+
+
+def project_near(scal, out_so_far, attns, pieces):
     tok, width = attns[0].shape
     out_width = pieces[0].shape[1]
     return pl.pallas_call(
         project_near_kernel,
         out_shape=shape_of((tok, out_width), F32),
-        in_specs=smem_then_vmem(9),
-        compiler_params=params(16),
-        cost_estimate=cost(6 * tok * width * out_width, 8 * width * out_width),
-    )(scal, *attns, own, rest, *pieces)
-
-
-def project_far_kernel(s_ref, near_ref, a_ref, d_ref, od_ref, dz_ref, odz_ref, out_ref):
+        in_specs=smem_then_vmem(7),
+        compiler_params=params(16),
+        cost_estimate=cost(4 * tok * width * out_width, 8 * width * out_width),
+    )(scal, out_so_far, *attns, *pieces)
+
+
+def project_far_kernel(s_ref, near_ref, a_ref, d_ref, od_ref, dz_ref, odz_ref, out_hbm, out_buf, sems):
     first, second = halves(s_ref, d_ref.shape[0])
-    block = out_ref.shape[1]
-    here = pl.ds(pl.multiple_of(pl.program_id(0) * block, block), block)
-    acc = near_ref[:, here] + dot_nn(a_ref[:, first], d_ref[:, here] + od_ref[:, here])
-    acc += dot_nn(a_ref[:, second], dz_ref[:, here] + odz_ref[:, here])
-    out_ref[...] = acc.astype(BF16)
+    blocks, _, block = out_buf.shape
+    moves = []
+    for j in range(blocks):
+        here = slice(j * block, (j + 1) * block)
+        acc = near_ref[:, here] + dot_nn(a_ref[:, first], d_ref[:, here] + od_ref[:, here])
+        acc += dot_nn(a_ref[:, second], dz_ref[:, here] + odz_ref[:, here])
+        out_buf[j] = acc.astype(BF16)
+        moves.append(pltpu.make_async_copy(out_buf.at[j], out_hbm.at[:, here], sems.at[j]))
+        moves[-1].start()
+    for move in moves:
+        move.wait()
 
 
 def project_far(scal, near, attn, pieces):
     tok, width = attn.shape
     out_width = pieces[0].shape[1]
-    block = 512
+    block = 256
     return pl.pallas_call(
         project_far_kernel,
         out_shape=shape_of((tok, out_width), BF16),
-        grid=(out_width // block,),
         in_specs=smem_then_vmem(6),
-        out_specs=pl.BlockSpec((tok, block), lambda j: (0, j)),
+        out_specs=pl.BlockSpec(memory_space=pl.ANY),
+        scratch_shapes=[
+            pltpu.VMEM((out_width // block, tok, block), BF16),
+            pltpu.SemaphoreType.DMA((out_width // block,)),
+        ],
         compiler_params=params(16),
         cost_estimate=cost(2 * tok * width * out_width, 8 * width * out_width),
     )(scal, near, attn, *pieces)
@@ -415,27 +446,26 @@
 
     if paired:
         far_z = lax.ppermute(after(far_mine, gsum), "rep", zpair)
-        other_attn = after(other_attn, gsum, far_mine)
+        own_out = project_own(scal, after(attn, gsum), out_weight, rest, out_weight.shape[1] // 2)
+        other_attn = after(other_attn, own_out, far_mine)
 
     weight_grad = own_weight_grad(scal, attn, out_grad, other_attn, other_grad)
 
     if paired:
         near_other = lax.ppermute(after(near_mine, weight_grad), "ctx", swap)
-        suffix = after(suffix, weight_grad)
+        attn_3 = lax.ppermute(after(attn_1, weight_grad), group, two)
+        near_other_z = lax.ppermute(after(near_z, weight_grad), "ctx", swap)
+        suffix = after(suffix, weight_grad, attn_1, attn_2)
 
     query_grad, key_grad, value_grad = backward(queries, keys, values, draw, prefix, suffix, glocal)
 
     if paired:
-        attn_3 = lax.ppermute(after(attn_1, query_grad), group, two)
-        near_other_z = lax.ppermute(after(near_z, weight_grad), "ctx", swap)
         far_other = lax.ppermute(after(far_mine, weight_grad), "ctx", swap)
-        far_other_z = lax.ppermute(after(far_z, query_grad), "ctx", swap)
-
-    if paired:
         near_out = project_near(
-            scal, (after(attn, query_grad), attn_1, attn_2), out_weight, rest,
+            scal, after(own_out, query_grad), (attn_1, attn_2),
             (near_mine, near_z, near_other, near_other_z),
         )
+        far_other_z = lax.ppermute(after(far_z, near_out), "ctx", swap)
         layer_out = project_far(scal, near_out, attn_3, (far_mine, far_other, far_z, far_other_z))
     else:
         full = lax.all_gather(out_weight, "ctx", axis=1, tiled=True)

time: 52.9 us -> 49.5 us (0.936)
  waiting for transfers between devices: 9.98 us -> 6.08 us
  Pallas kernels: 22.3 us -> 23.8 us
  starting transfers between devices: 19.6 us -> 18.4 us
    ppermute x2, waiting for transfers between devices: 6.03 us -> 1.9 us  [the longest x1 1.9 us: body(): far_other_z = lax.ppermute(after(far_z, near_out), 'ctx', swap)]
    ppermute x1, starting transfers between devices: 2.53 us -> 0.23 us  [body(): attn_2 = lax.ppermute(attn, group, two)]
    pallas_call x1, Pallas kernels: 3.96 us -> 6.03 us  [cotangent(): pl.pallas_call(cotangent_kernel, out_shape=(shape_of((tok, width), BF16),...]
    pallas_call x0 -> x1, Pallas kernels: none -> 1.26 us  [project_own(): pl.pallas_call(project_own_kernel, out_shape=shape_of((tok, out_width), F...]
    ppermute x2, starting transfers between devices: 0.59 us -> 1.52 us  [the longest x1 1.51 us: body(): attn_3 = lax.ppermute(after(attn_1, weight_grad), group, two)]
    pallas_call x1, Pallas kernels: 4.76 us -> 3.89 us  [own_weight_grad(): pl.pallas_call(weight_grad_kernel, out_shape=shape_of((width, own_width),...]
    ppermute x1, starting transfers between devices: 0.94 us -> 0.07 us  [body(): near_other = lax.ppermute(after(near_mine, weight_grad), 'ctx', swap)]
    pallas_call x1, Pallas kernels: 2.53 us -> 1.81 us  [project_near(): pl.pallas_call(project_near_kernel, out_shape=shape_of((tok, out_width),...]
  transfers between devices with their start and end apart: 16 -> 16, of which waited for: 4 -> 5; matrix products, arithmetic and copies ran while one was open for 0% -> 0% of each run, Pallas kernels for 38% -> 44%
where the time goes in v1:
time: 49.5 us; the launch traced here: 49.3 us
  Pallas kernels  23.8 us (48%)
  starting transfers between devices  18.4 us (37%)
  waiting for transfers between devices  6.08 us (12%)
  between operations  0.92 us (2%)
    ppermute x4, starting transfers between devices, shift(): return lax.ppermute(array, axis, pairs)  6.31 us
    pallas_call x1, Pallas kernels, cotangent(): pl.pallas_call(cotangent_kernel, out_shape=(shape_of((tok, width), BF16),...  6.03 us
    pallas_call x1, Pallas kernels, own_weight_grad(): pl.pallas_call(weight_grad_kernel, out_shape=shape_of((width, own_width),...  3.89 us
    pallas_call x1, Pallas kernels, backward(): pl.pallas_call(backward_kernel, out_shape=(out, out, out), compiler_param...  3.79 us
    pallas_call x1, Pallas kernels, opening(): pl.pallas_call(opening_kernel, out_shape=(shape_of((width, DH), BF16), pi...  3.42 us
    ppermute x1, waiting for transfers between devices, body(): far_z = lax.ppermute(after(far_mine, gsum), 'rep', zpair)  3.34 us
    ppermute x1, starting transfers between devices, body(): near_mine = lax.ppermute(near_piece, group, near)  2.94 us
    ppermute x1, starting transfers between devices, body(): attn_1 = lax.ppermute(attn, group, one)  2.21 us
  transfers between devices with their start and end apart: 16, of which 5 were waited for; matrix products, arithmetic and copies ran while one was open for 0% of the time, Pallas kernels for 44%

profile of v1, /device:TPU:0, one launch (start us, length us, event | category | flops | bytes accessed | tf_op | source)
XLA Modules:
  0.0 49.3 jit_solution(7467266025530181030)
XLA Ops:
  0.6 0.5 %collective-permute-start.1 = (bf16[512,2048]{1,0:T(8,128)(2,1)}, bf16[512,2048]{1,0:T(8,128)(2,1)S(1)}, u32[]{:S(2)}, u32[]{:S(2)}) collective-permute-start(bf16[512,2048]{1,0:T(8,128)(2,1)} %own_ref.3), channel_id=1, source_target_pairs={{0,16},{16,0},{1,17},{17,1},{2,18},{18,2},{3,19},{19,3},{4,20},{20... | collective-permute-start | bytes 6291464 | tf_op jit(solution)/shard_map/ppermute | solution.py:390
  1.1 0.1 pad_add_fusion.s_ref
  1.2 0.0 copy-start
  1.2 0.0 copy-start.1
  1.2 3.4 %shard_map.92 = (bf16[512,128]{1,0:T(8,128)(2,1)S(1)}, bf16[256,1024]{1,0:T(8,128)(2,1)S(1)}, bf16[256,1024]{1,0:T(8,128)(2,1)S(1)}, bf16[512,2048]{1,0:T(8,128)...) custom-call(s32[4]{0:T(128)S(1)} %pad_add_fusion.s_ref, ...), custom_call_target="tpu_custom_call" | custom-call | flops 67108864 | bytes 1048576 | tf_op jit(solution)/shard_map/pallas_call | solution.py:103
  4.7 0.1 collective-permute-start.3
  4.8 2.9 %collective-permute-start.2 = (bf16[256,1024]{1,0:T(8,128)(2,1)S(1)}, bf16[256,1024]{1,0:T(8,128)(2,1)S(1)}, u32[]{:S(2)}, u32[]{:S(2)}) collective-permute-start(bf16[256,1024]{1,0:T(8,128)(2,1)S(1)} %get-tuple-element.38), channel_id=1, source_target_pairs={{0,4},{4,0},{24,12},{28,8},{16,24},{20,28},{8,16},{12,20},{1,5},{5... | collective-permute-start | bytes 1572872 | tf_op jit(solution)/shard_map/ppermute | solution.py:419
  7.7 1.7 %collective-permute-start = (bf16[512,128]{1,0:T(8,128)(2,1)S(1)}, bf16[512,128]{1,0:T(8,128)(2,1)S(1)}, u32[]{:S(2)}, u32[]{:S(2)}) collective-permute-start(bf16[512,128]{1,0:T(8,128)(2,1)S(1)} %get-tuple-element.35), channel_id=1, source_target_pairs={{0,16},{1,17},{2,18},{3,19},{4,20},{5,21},{6,22},{7,23},{8,24},{9,... | collective-permute-start | bytes 393224 | tf_op jit(solution)/shard_map/ppermute | solution.py:390
  9.4 1.3 %collective-permute-start.6 = (bf16[256,1024]{1,0:T(8,128)(2,1)S(1)}, bf16[256,1024]{1,0:T(8,128)(2,1)S(1)}, u32[]{:S(2)}, u32[]{:S(2)}) collective-permute-start(bf16[256,1024]{1,0:T(8,128)(2,1)S(1)} %get-tuple-element.45), channel_id=1, source_target_pairs={{16,12},{20,8},{8,4},{12,0},{17,13},{21,9},{9,5},{13,1},{18,14},{2... | collective-permute-start | bytes 1572872 | tf_op jit(solution)/shard_map/ppermute | solution.py:420
  10.7 0.0 collective-permute-done.carried_ref
  10.8 1.6 %shard_map.93 = (bf16[512,512]{1,0:T(8,128)(2,1)S(1)}, f32[512,512]{1,0:T(8,128)S(1)}, bf16[2,512,128]{2,1,0:T(8,128)(2,1)S(1)}) custom-call(bf16[512,512]{1,0:T(8,128)(2,1)S(1)} %get-tuple-element.32.q_ref, bf16[512,512]{1,0:T(8,128)(2,1)S(1)} %get-tuple-element.33.k_ref, bf16[512,512]{1,0:T(8,128)(2,1)S(1)} %get-tuple-element.34.v_ref, ...), custom_call_target="tpu_custom_call" | custom-call | flops 536870912 | bytes 3145728 | tf_op jit(solution)/shard_map/pallas_call | solution.py:146
  12.3 2.6 %collective-permute-start.5 = (bf16[512,512]{1,0:T(8,128)(2,1)S(1)}, bf16[512,512]{1,0:T(8,128)(2,1)S(1)}, u32[]{:S(2)}, u32[]{:S(2)}) collective-permute-start(bf16[512,512]{1,0:T(8,128)(2,1)S(1)} %get-tuple-element.42.a_ref.attn_ref), channel_id=1, source_target_pairs={{0,16},{16,0},{1,17},{17,1},{2,18},{18,2},{3,19},{19,3},{4,20},{20... | collective-permute-start | bytes 1572872 | tf_op jit(solution)/shard_map/ppermute | solution.py:390
  14.9 0.2 collective-permute-done.2.m1_ref
  15.1 1.8 %collective-permute-start.9 = (bf16[256,1024]{1,0:T(8,128)(2,1)S(1)}, bf16[256,1024]{1,0:T(8,128)(2,1)S(1)}, u32[]{:S(2)}, u32[]{:S(2)}) collective-permute-start(bf16[256,1024]{1,0:T(8,128)(2,1)S(1)} %collective-permute-done.2.m1_ref), channel_id=1, source_target_pairs={{0,1},{1,0},{2,3},{3,2},{4,5},{5,4},{6,7},{7,6},{8,9},{9,8},{10,11... | collective-permute-start | bytes 1572872 | tf_op jit(solution)/shard_map/ppermute | solution.py:441
  17.0 0.0 collective-permute-done.1.rest_ref
  17.0 2.2 %collective-permute-start.7 = (bf16[512,512]{1,0:T(8,128)(2,1)S(1)}, bf16[512,512]{1,0:T(8,128)(2,1)S(1)}, u32[]{:S(2)}, u32[]{:S(2)}) collective-permute-start(bf16[512,512]{1,0:T(8,128)(2,1)S(1)} %get-tuple-element.42.a_ref.attn_ref), channel_id=1, source_target_pairs={{0,4},{4,0},{8,12},{12,8},{16,24},{20,28},{24,16},{28,20},{1,5},{5... | collective-permute-start | bytes 1572872 | tf_op jit(solution)/shard_map/ppermute | solution.py:439
  19.2 0.0 collective-permute-done.3.other_grad_ref
  19.2 0.2 collective-permute-start.8
  19.4 0.0 copy-done
  19.4 0.0 copy-done.1
  19.4 6.0 %shard_map.94 = (bf16[512,512]{1,0:T(8,128)(2,1)S(1)}, bf16[512,128]{1,0:T(8,128)(2,1)S(1)}, f32[2,512,128]{2,1,0:T(8,128)S(1)}) custom-call(s32[4]{0:T(128)S(1)} %pad_add_fusion.s_ref, bf16[512,4096]{1,0:T(8,128)(2,1)S(1)} %copy-done, bf16[512,2048]{1,0:T(8,128)(2,1)S(1)} %copy-done.1, bf16[512,2048]{1,0:T(8,128)(2,1)S(1)} %collective-permute-done.1.rest_ref, ...), custom_call_target="tpu_custom_call" | custom-call | flops 2147483648 | bytes 8388608 | tf_op jit(solution)/shard_map/pallas_call | solution.py:200
  25.5 1.3 %shard_map.95.out_so_far_ref = f32[512,1024]{1,0:T(8,128)S(1)} custom-call(s32[4]{0:T(128)S(1)} %pad_add_fusion.s_ref, bf16[512,512]{1,0:T(8,128)(2,1)S(1)} %get-tuple-element.42.a_ref.attn_ref, bf16[512,2048]{1,0:T(8,128)(2,1)S(1)} %copy-done.1, bf16[512,2048]{1,0:T(8,128)(2,1)S(1)} %collective-permute-done.1.rest_ref), custom_call_target="tpu_custom_call" | custom-call | flops 536870912 | bytes 4194304 | tf_op jit(solution)/shard_map/pallas_call | solution.py:317
  26.7 0.0 collective-permute-done.6.d_ref
  26.7 0.0 collective-permute-done.5.other_ref
  26.8 3.9 %shard_map.96 = f32[512,2048]{1,0:T(8,128)} custom-call(s32[4]{0:T(128)S(1)} %pad_add_fusion.s_ref, bf16[512,512]{1,0:T(8,128)(2,1)S(1)} %get-tuple-element.42.a_ref.attn_ref, bf16[512,4096]{1,0:T(8,128)(2,1)S(1)} %copy-done, bf16[512,512]{1,0:T(8,128)(2,1)S(1)} %collective-permute-done.5.other_ref, bf16[512,2048]{1,0:T(8,128)(2,1)S(1)} %collective-permute-done.3.other_grad_ref), custom_call_target="tpu_custom_call" | custom-call | flops 2147483648 | bytes 8388608 | tf_op jit(solution)/shard_map/pallas_call | solution.py:238
  30.6 0.1 collective-permute-start.10
  30.7 0.0 collective-permute-done.9.z1_ref
  30.7 0.5 collective-permute-start.11
  31.2 0.4 collective-permute-start.14
  31.7 0.4 collective-permute-done.7.a1_ref
  32.0 1.5 %collective-permute-start.4 = (bf16[512,128]{1,0:T(8,128)(2,1)S(1)}, bf16[512,128]{1,0:T(8,128)(2,1)S(1)}, u32[]{:S(2)}, u32[]{:S(2)}) collective-permute-start(bf16[512,128]{1,0:T(8,128)(2,1)S(1)} %get-tuple-element.41), channel_id=1, source_target_pairs={{16,0},{17,1},{18,2},{19,3},{20,4},{21,5},{22,6},{23,7},{24,8},{25... | collective-permute-start | bytes 393224 | tf_op jit(solution)/shard_map/ppermute | solution.py:390
  33.5 0.0 collective-permute-done.8.a2_ref
  33.5 1.5 %collective-permute-start.12 = (bf16[512,512]{1,0:T(8,128)(2,1)S(1)}, bf16[512,512]{1,0:T(8,128)(2,1)S(1)}, u32[]{:S(2)}, u32[]{:S(2)}) collective-permute-start(bf16[512,512]{1,0:T(8,128)(2,1)S(1)} %collective-permute-done.7.a1_ref), channel_id=1, source_target_pairs={{0,8},{4,12},{8,0},{12,4},{16,20},{20,16},{24,28},{28,24},{1,9},{5... | collective-permute-start | bytes 1572872 | tf_op jit(solution)/shard_map/ppermute | solution.py:456
  35.0 0.2 collective-permute-done.4.suffix_ref
  35.3 0.9 %collective-permute-start.13 = (bf16[256,1024]{1,0:T(8,128)(2,1)S(1)}, bf16[256,1024]{1,0:T(8,128)(2,1)S(1)}, u32[]{:S(2)}, u32[]{:S(2)}) collective-permute-start(bf16[256,1024]{1,0:T(8,128)(2,1)S(1)} %collective-permute-done.6.d_ref), channel_id=1, source_target_pairs={{0,16},{16,0},{1,17},{17,1},{2,18},{18,2},{3,19},{19,3},{4,20},{20... | collective-permute-start | bytes 1572872 | tf_op jit(solution)/shard_map/ppermute | solution.py:463
  36.2 3.8 %shard_map.97 = (bf16[512,512]{1,0:T(8,128)(2,1)}, bf16[512,512]{1,0:T(8,128)(2,1)}, bf16[512,512]{1,0:T(8,128)(2,1)}) custom-call(bf16[512,512]{1,0:T(8,128)(2,1)S(1)} %get-tuple-element.32.q_ref, bf16[512,512]{1,0:T(8,128)(2,1)S(1)} %get-tuple-element.33.k_ref, bf16[512,512]{1,0:T(8,128)(2,1)S(1)} %get-tuple-element.34.v_ref, ...), custom_call_target="tpu_custom_call" | custom-call | flops 1073741824 | bytes 4194304 | tf_op jit(solution)/shard_map/pallas_call | solution.py:287
  40.0 0.0 collective-permute-done.10.o1_ref
  40.0 0.0 collective-permute-done.11.oz1_ref
  40.0 1.8 %shard_map.98.near_ref = f32[512,1024]{1,0:T(8,128)S(1)} custom-call(s32[4]{0:T(128)S(1)} %pad_add_fusion.s_ref, f32[512,1024]{1,0:T(8,128)S(1)} %shard_map.95.out_so_far_ref, bf16[512,512]{1,0:T(8,128)(2,1)S(1)} %collective-permute-done.7.a1_ref, bf16[512,512]{1,0:T(8,128)(2,1)S(1)} %collective-permute-done.8.a2_ref, ...), custom_call_target="tpu_custom_call" | custom-call | flops 1073741824 | bytes 4194304 | tf_op jit(solution)/shard_map/pallas_call | solution.py:338
  41.8 3.3 %collective-permute-done.14.dz_ref = bf16[256,1024]{1,0:T(8,128)(2,1)S(1)} collective-permute-done((bf16[256,1024]{1,0:T(8,128)(2,1)S(1)}, bf16[256,1024]{1,0:T(8,128)(2,1)S(1)}, u32[]{:S(2)}, u32[]{:S(2)}) %collective-permute-start.14) | collective-permute-done | bytes 524320 | tf_op jit(solution)/shard_map/ppermute | solution.py:448
  45.1 0.0 collective-permute-start.15
  45.1 0.0 collective-permute-done.12.a_ref
  45.1 0.0 collective-permute-done.13.od_ref
  45.2 1.9 %collective-permute-done.15.odz_ref = bf16[256,1024]{1,0:T(8,128)(2,1)S(1)} collective-permute-done((bf16[256,1024]{1,0:T(8,128)(2,1)S(1)}, bf16[256,1024]{1,0:T(8,128)(2,1)S(1)}, u32[]{:S(2)}, u32[]{:S(2)}) %collective-permute-start.15) | collective-permute-done | bytes 524320 | tf_op jit(solution)/shard_map/ppermute | solution.py:468
  47.1 2.1 %shard_map.99 = bf16[512,1024]{1,0:T(8,128)(2,1)} custom-call(s32[4]{0:T(128)S(1)} %pad_add_fusion.s_ref, f32[512,1024]{1,0:T(8,128)S(1)} %shard_map.98.near_ref, bf16[512,512]{1,0:T(8,128)(2,1)S(1)} %collective-permute-done.12.a_ref, bf16[256,1024]{1,0:T(8,128)(2,1)S(1)} %collective-permute-done.6.d_ref, ...), custom_call_target="tpu_custom_call" | custom-call | flops 536870912 | bytes 4194304 | tf_op jit(solution)/shard_map/pallas_call | solution.py:366
Async XLA Ops:
  0.6 16.4 %collective-permute-start.1 = (bf16[512,2048]{1,0:T(8,128)(2,1)}, bf16[512,2048]{1,0:T(8,128)(2,1)S(1)}, u32[]{:S(2)}, u32[]{:S(2)}) collective-permute-start(bf16[512,2048]{1,0:T(8,128)(2,1)} %own_ref.3), channel_id=1, source_target_pairs={{0,16},{16,0},{1,17},{17,1},{2,18},{18,2},{3,19},{19,3},{4,20},{20... | collective-permute-start | bytes 6291464 | tf_op jit(solution)/shard_map/ppermute | solution.py:390
  1.2 18.2 %copy-start = (bf16[512,4096]{1,0:T(8,128)(2,1)S(1)}, bf16[512,4096]{1,0:T(8,128)(2,1)}, u32[]{:S(2)}) copy-start(bf16[512,4096]{1,0:T(8,128)(2,1)} %grad_ref.3) | copy-start | bytes 12582916
  1.2 18.2 %copy-start.1 = (bf16[512,2048]{1,0:T(8,128)(2,1)S(1)}, bf16[512,2048]{1,0:T(8,128)(2,1)}, u32[]{:S(2)}) copy-start(bf16[512,2048]{1,0:T(8,128)(2,1)} %own_ref.3) | copy-start | bytes 6291460
  4.7 14.5 %collective-permute-start.3 = (bf16[512,2048]{1,0:T(8,128)(2,1)S(1)}, bf16[512,2048]{1,0:T(8,128)(2,1)S(1)}, u32[]{:S(2)}, u32[]{:S(2)}) collective-permute-start(bf16[512,2048]{1,0:T(8,128)(2,1)S(1)} %get-tuple-element.39), channel_id=1, source_target_pairs={{0,16},{16,0},{1,17},{17,1},{2,18},{18,2},{3,19},{19,3},{4,20},{20... | collective-permute-start | bytes 6291464 | tf_op jit(solution)/shard_map/ppermute | solution.py:421
  4.8 10.4 %collective-permute-start.2 = (bf16[256,1024]{1,0:T(8,128)(2,1)S(1)}, bf16[256,1024]{1,0:T(8,128)(2,1)S(1)}, u32[]{:S(2)}, u32[]{:S(2)}) collective-permute-start(bf16[256,1024]{1,0:T(8,128)(2,1)S(1)} %get-tuple-element.38), channel_id=1, source_target_pairs={{0,4},{4,0},{24,12},{28,8},{16,24},{20,28},{8,16},{12,20},{1,5},{5... | collective-permute-start | bytes 1572872 | tf_op jit(solution)/shard_map/ppermute | solution.py:419
  7.7 3.0 %collective-permute-start = (bf16[512,128]{1,0:T(8,128)(2,1)S(1)}, bf16[512,128]{1,0:T(8,128)(2,1)S(1)}, u32[]{:S(2)}, u32[]{:S(2)}) collective-permute-start(bf16[512,128]{1,0:T(8,128)(2,1)S(1)} %get-tuple-element.35), channel_id=1, source_target_pairs={{0,16},{1,17},{2,18},{3,19},{4,20},{5,21},{6,22},{7,23},{8,24},{9,... | collective-permute-start | bytes 393224 | tf_op jit(solution)/shard_map/ppermute | solution.py:390
  9.4 17.3 %collective-permute-start.6 = (bf16[256,1024]{1,0:T(8,128)(2,1)S(1)}, bf16[256,1024]{1,0:T(8,128)(2,1)S(1)}, u32[]{:S(2)}, u32[]{:S(2)}) collective-permute-start(bf16[256,1024]{1,0:T(8,128)(2,1)S(1)} %get-tuple-element.45), channel_id=1, source_target_pairs={{16,12},{20,8},{8,4},{12,0},{17,13},{21,9},{9,5},{13,1},{18,14},{2... | collective-permute-start | bytes 1572872 | tf_op jit(solution)/shard_map/ppermute | solution.py:420
  12.3 14.4 %collective-permute-start.5 = (bf16[512,512]{1,0:T(8,128)(2,1)S(1)}, bf16[512,512]{1,0:T(8,128)(2,1)S(1)}, u32[]{:S(2)}, u32[]{:S(2)}) collective-permute-start(bf16[512,512]{1,0:T(8,128)(2,1)S(1)} %get-tuple-element.42.a_ref.attn_ref), channel_id=1, source_target_pairs={{0,16},{16,0},{1,17},{17,1},{2,18},{18,2},{3,19},{19,3},{4,20},{20... | collective-permute-start | bytes 1572872 | tf_op jit(solution)/shard_map/ppermute | solution.py:390
  15.1 15.6 %collective-permute-start.9 = (bf16[256,1024]{1,0:T(8,128)(2,1)S(1)}, bf16[256,1024]{1,0:T(8,128)(2,1)S(1)}, u32[]{:S(2)}, u32[]{:S(2)}) collective-permute-start(bf16[256,1024]{1,0:T(8,128)(2,1)S(1)} %collective-permute-done.2.m1_ref), channel_id=1, source_target_pairs={{0,1},{1,0},{2,3},{3,2},{4,5},{5,4},{6,7},{7,6},{8,9},{9,8},{10,11... | collective-permute-start | bytes 1572872 | tf_op jit(solution)/shard_map/ppermute | solution.py:441
  17.0 15.1 %collective-permute-start.7 = (bf16[512,512]{1,0:T(8,128)(2,1)S(1)}, bf16[512,512]{1,0:T(8,128)(2,1)S(1)}, u32[]{:S(2)}, u32[]{:S(2)}) collective-permute-start(bf16[512,512]{1,0:T(8,128)(2,1)S(1)} %get-tuple-element.42.a_ref.attn_ref), channel_id=1, source_target_pairs={{0,4},{4,0},{8,12},{12,8},{16,24},{20,28},{24,16},{28,20},{1,5},{5... | collective-permute-start | bytes 1572872 | tf_op jit(solution)/shard_map/ppermute | solution.py:439
  19.2 14.3 %collective-permute-start.8 = (bf16[512,512]{1,0:T(8,128)(2,1)S(1)}, bf16[512,512]{1,0:T(8,128)(2,1)S(1)}, u32[]{:S(2)}, u32[]{:S(2)}) collective-permute-start(bf16[512,512]{1,0:T(8,128)(2,1)S(1)} %get-tuple-element.42.a_ref.attn_ref), channel_id=1, source_target_pairs={{0,8},{4,12},{8,0},{12,4},{16,20},{20,16},{24,28},{28,24},{1,9},{5... | collective-permute-start | bytes 1572872 | tf_op jit(solution)/shard_map/ppermute | solution.py:440
  30.6 9.3 %collective-permute-start.10 = (bf16[256,1024]{1,0:T(8,128)(2,1)S(1)}, bf16[256,1024]{1,0:T(8,128)(2,1)S(1)}, u32[]{:S(2)}, u32[]{:S(2)}) collective-permute-start(bf16[256,1024]{1,0:T(8,128)(2,1)S(1)} %collective-permute-done.2.m1_ref), channel_id=1, source_target_pairs={{0,16},{16,0},{1,17},{17,1},{2,18},{18,2},{3,19},{19,3},{4,20},{20... | collective-permute-start | bytes 1572872 | tf_op jit(solution)/shard_map/ppermute | solution.py:455
  30.7 9.2 %collective-permute-start.11 = (bf16[256,1024]{1,0:T(8,128)(2,1)S(1)}, bf16[256,1024]{1,0:T(8,128)(2,1)S(1)}, u32[]{:S(2)}, u32[]{:S(2)}) collective-permute-start(bf16[256,1024]{1,0:T(8,128)(2,1)S(1)} %collective-permute-done.9.z1_ref), channel_id=1, source_target_pairs={{0,16},{16,0},{1,17},{17,1},{2,18},{18,2},{3,19},{19,3},{4,20},{20... | collective-permute-start | bytes 1572872 | tf_op jit(solution)/shard_map/ppermute | solution.py:457
  31.2 13.9 %collective-permute-start.14 = (bf16[256,1024]{1,0:T(8,128)(2,1)S(1)}, bf16[256,1024]{1,0:T(8,128)(2,1)S(1)}, u32[]{:S(2)}, u32[]{:S(2)}) collective-permute-start(bf16[256,1024]{1,0:T(8,128)(2,1)S(1)} %collective-permute-done.6.d_ref), channel_id=1, source_target_pairs={{0,1},{1,0},{2,3},{3,2},{4,5},{5,4},{6,7},{7,6},{8,9},{9,8},{10,11... | collective-permute-start | bytes 1572872 | tf_op jit(solution)/shard_map/ppermute | solution.py:448
  32.0 3.2 %collective-permute-start.4 = (bf16[512,128]{1,0:T(8,128)(2,1)S(1)}, bf16[512,128]{1,0:T(8,128)(2,1)S(1)}, u32[]{:S(2)}, u32[]{:S(2)}) collective-permute-start(bf16[512,128]{1,0:T(8,128)(2,1)S(1)} %get-tuple-element.41), channel_id=1, source_target_pairs={{16,0},{17,1},{18,2},{19,3},{20,4},{21,5},{22,6},{23,7},{24,8},{25... | collective-permute-start | bytes 393224 | tf_op jit(solution)/shard_map/ppermute | solution.py:390
  33.5 11.6 %collective-permute-start.12 = (bf16[512,512]{1,0:T(8,128)(2,1)S(1)}, bf16[512,512]{1,0:T(8,128)(2,1)S(1)}, u32[]{:S(2)}, u32[]{:S(2)}) collective-permute-start(bf16[512,512]{1,0:T(8,128)(2,1)S(1)} %collective-permute-done.7.a1_ref), channel_id=1, source_target_pairs={{0,8},{4,12},{8,0},{12,4},{16,20},{20,16},{24,28},{28,24},{1,9},{5... | collective-permute-start | bytes 1572872 | tf_op jit(solution)/shard_map/ppermute | solution.py:456
  35.3 9.9 %collective-permute-start.13 = (bf16[256,1024]{1,0:T(8,128)(2,1)S(1)}, bf16[256,1024]{1,0:T(8,128)(2,1)S(1)}, u32[]{:S(2)}, u32[]{:S(2)}) collective-permute-start(bf16[256,1024]{1,0:T(8,128)(2,1)S(1)} %collective-permute-done.6.d_ref), channel_id=1, source_target_pairs={{0,16},{16,0},{1,17},{17,1},{2,18},{18,2},{3,19},{19,3},{4,20},{20... | collective-permute-start | bytes 1572872 | tf_op jit(solution)/shard_map/ppermute | solution.py:463
  45.1 1.9 %collective-permute-start.15 = (bf16[256,1024]{1,0:T(8,128)(2,1)S(1)}, bf16[256,1024]{1,0:T(8,128)(2,1)S(1)}, u32[]{:S(2)}, u32[]{:S(2)}) collective-permute-start(bf16[256,1024]{1,0:T(8,128)(2,1)S(1)} %collective-permute-done.14.dz_ref), channel_id=1, source_target_pairs={{0,16},{16,0},{1,17},{17,1},{2,18},{18,2},{3,19},{19,3},{4,20},{20... | collective-permute-start | bytes 1572872 | tf_op jit(solution)/shard_map/ppermute | solution.py:468

commit v2 on v1

--- a/solution.py
+++ b/solution.py
@@ -115,7 +115,9 @@
     )(scal, queries, keys, values, weight, out_grad)
 
 
-def forward_kernel(q_ref, k_ref, v_ref, carried_ref, attn_ref, raw_ref, prefix_ref):
+def forward_kernel(q_ref, k_ref, v_ref, carried_ref, grad_hbm, attn_ref, raw_ref, prefix_ref, grad_ref, sem):
+    load = pltpu.make_async_copy(grad_hbm, grad_ref, sem)
+    load.start()
     tok, width = q_ref.shape
     chunk = min(CHUNK, tok)
     row = lax.broadcasted_iota(jnp.int32, (chunk, chunk), 0)
@@ -138,10 +140,12 @@
             attn_ref[rows, cols] = (raw * inv).astype(BF16)
             if i + 1 < tok // chunk:
                 prefix = prefix + dot_tn(fk, v)
-
-
-def forward(queries, keys, values, carried):
+    load.wait()
+
+
+def forward(queries, keys, values, carried, out_grad):
     tok, width = queries.shape
+    vmem = pl.BlockSpec(memory_space=pltpu.VMEM)
     chunks = tok // min(CHUNK, tok)
     return pl.pallas_call(
         forward_kernel,
@@ -149,52 +153,58 @@
             shape_of((tok, width), BF16),
             shape_of((tok, width), F32),
             shape_of((chunks, width, DH), BF16),
+            shape_of(out_grad.shape, BF16),
         ),
+        in_specs=[vmem] * 4 + [pl.BlockSpec(memory_space=pltpu.HBM)],
+        out_specs=(vmem,) * 4,
+        scratch_shapes=[pltpu.SemaphoreType.DMA],
         compiler_params=params(16),
         cost_estimate=cost(16 * queries.size * DH, 12 * queries.size),
-    )(queries, keys, values, carried)
-
-
-def cotangent_kernel(s_ref, grad_ref, own_ref, rest_ref, q_ref, raw_ref, draw_ref, gsum_ref, glocal_ref):
+    )(queries, keys, values, carried, out_grad)
+
+
+def cotangent_kernel(s_ref, own_ref, grad_ref, rest_ref, q_ref, raw_ref, attn_ref,
+                     draw_ref, gsum_ref, glocal_ref, out_ref, acc_ref):
     own_width, rest_width = own_ref.shape[1], rest_ref.shape[1]
     count = (own_width + rest_width) // own_width
     tok, width = q_ref.shape
     chunk = min(CHUNK, tok)
-    for top in range(0, width, 2 * DH):
-        pair = slice(top, top + 2 * DH)
-        total_grad = None
-        for k in range(count):
-            place = lax.rem(s_ref[0] + k, count) * own_width
-            part = grad_ref[:, pl.ds(pl.multiple_of(place, own_width), own_width)]
-            if k == 0:
-                weight = own_ref[pair, :]
-            else:
-                weight = rest_ref[pair, (k - 1) * own_width : k * own_width]
-            product = dot_nt(part, weight)
-            total_grad = product if total_grad is None else total_grad + product
-        for lo in (top, top + DH):
-            cols = slice(lo, lo + DH)
-            later = jnp.zeros((DH, DH), F32)
-            for i in reversed(range(tok // chunk)):
-                rows = slice(i * chunk, (i + 1) * chunk)
-                glocal_ref[i, cols, :] = later
-                grad = total_grad[rows, lo - top : lo - top + DH].astype(BF16).astype(F32)
-                raw = raw_ref[rows, cols]
-                inv = lax.rsqrt(jnp.mean(raw * raw, axis=-1, keepdims=True) + EPS)
-                normed = raw * inv
-                mean = jnp.mean(grad * normed, axis=-1, keepdims=True)
-                draw = (inv * (grad - normed * mean)).astype(BF16)
-                draw_ref[rows, cols] = draw
-                fq = feature(q_ref[rows, cols].astype(F32)).astype(BF16)
-                later = later + dot_tn(fq, draw)
-            gsum_ref[cols, :] = later.astype(BF16)
+
+    def part(k):
+        place = lax.rem(s_ref[0] + k, count) * own_width
+        return grad_ref[:, pl.ds(pl.multiple_of(place, own_width), own_width)]
+
+    acc_ref[...] = dot_nt(part(0), own_ref[...])
+    for k in range(1, count):
+        acc_ref[...] += dot_nt(part(k), rest_ref[:, (k - 1) * own_width : k * own_width])
+    for lo in range(0, width, DH):
+        cols = slice(lo, lo + DH)
+        later = jnp.zeros((DH, DH), F32)
+        for i in reversed(range(tok // chunk)):
+            rows = slice(i * chunk, (i + 1) * chunk)
+            glocal_ref[i, cols, :] = later
+            grad = acc_ref[rows, cols].astype(BF16).astype(F32)
+            raw = raw_ref[rows, cols]
+            inv = lax.rsqrt(jnp.mean(raw * raw, axis=-1, keepdims=True) + EPS)
+            normed = raw * inv
+            mean = jnp.mean(grad * normed, axis=-1, keepdims=True)
+            draw = (inv * (grad - normed * mean)).astype(BF16)
+            draw_ref[rows, cols] = draw
+            fq = feature(q_ref[rows, cols].astype(F32)).astype(BF16)
+            later = later + dot_tn(fq, draw)
+        gsum_ref[cols, :] = later.astype(BF16)
+    wide = out_ref.shape[1]
+    if wide < own_width:
+        local = pl.ds(pl.multiple_of(s_ref[2] * wide, wide), wide)
+        weight = jnp.where(s_ref[0] == s_ref[1], own_ref[:, local], rest_ref[:, local])
+        out_ref[...] = dot_nn(attn_ref[...], weight)
 
 
 def smem_then_vmem(count):
     return [pl.BlockSpec(memory_space=pltpu.SMEM)] + [pl.BlockSpec(memory_space=pltpu.VMEM)] * count
 
 
-def cotangent(scal, out_grad, own, rest, queries, raw):
+def cotangent(scal, weight, out_grad, rest, queries, raw, attn, out_width):
     tok, width = queries.shape
     chunks = tok // min(CHUNK, tok)
     return pl.pallas_call(
@@ -203,11 +213,13 @@
             shape_of((tok, width), BF16),
             shape_of((width, DH), BF16),
             shape_of((chunks, width, DH), F32),
+            shape_of((tok, out_width), F32),
         ),
-        in_specs=smem_then_vmem(5),
+        in_specs=smem_then_vmem(6),
+        scratch_shapes=[pltpu.VMEM((tok, width), F32)],
         compiler_params=params(16),
         cost_estimate=cost(2 * out_grad.size * width, 4 * out_grad.size),
-    )(scal, out_grad, own, rest, queries, raw)
+    )(scal, weight, out_grad, rest, queries, raw, attn)
 
 
 def weight_grad_kernel(s_ref, attn_ref, grad_ref, other_ref, other_grad_ref, out_hbm, out_buf, sems):
@@ -298,31 +310,6 @@
     return first, second
 
 
-def project_own_kernel(s_ref, a_ref, own_ref, rest_ref, out_ref):
-    wide = out_ref.shape[1]
-    local = pl.ds(pl.multiple_of(s_ref[2] * wide, wide), wide)
-    mine = s_ref[0] == s_ref[1]
-
-    @pl.when(mine)
-    def _():
-        out_ref[...] = dot_nn(a_ref[...], own_ref[:, local])
-
-    @pl.when(jnp.logical_not(mine))
-    def _():
-        out_ref[...] = dot_nn(a_ref[...], rest_ref[:, local])
-
-
-def project_own(scal, attn, own, rest, out_width):
-    tok, width = attn.shape
-    return pl.pallas_call(
-        project_own_kernel,
-        out_shape=shape_of((tok, out_width), F32),
-        in_specs=smem_then_vmem(3),
-        compiler_params=params(16),
-        cost_estimate=cost(2 * tok * width * out_width, 8 * width * out_width),
-    )(scal, attn, own, rest)
-
-
 def project_near_kernel(s_ref, out_so_far_ref, a1_ref, a2_ref, m1_ref, z1_ref, o1_ref, oz1_ref, out_ref):
     first, second = halves(s_ref, m1_ref.shape[0])
     acc = out_so_far_ref[...] + dot_nn(a1_ref[:, first], m1_ref[...])
@@ -431,25 +418,28 @@
     carried = total([shift(state, "ctx", n_ctx, k, False) for k in range(1, n_ctx)])
     rest = [shift(out_weight, "ctx", n_ctx, -k, True) for k in range(1, n_ctx)]
     rest = rest[0] if n_ctx == 2 else jnp.concatenate(rest, 1)
-    attn, raw, prefix = forward(queries, keys, values, carried)
-
-    other_attn = [shift(attn, "ctx", n_ctx, k, True) for k in range(1, n_ctx)]
-    other_attn = other_attn[0] if n_ctx == 2 else jnp.concatenate(other_attn, 0)
+    if paired:
+        carried = after(carried, rest)
+    attn, raw, prefix, grad_vmem = forward(queries, keys, values, carried, grad_hbm)
+
     if paired:
         attn_1 = lax.ppermute(attn, group, one)
         attn_2 = lax.ppermute(attn, group, two)
         near_z = lax.ppermute(near_mine, "rep", zpair)
         raw = after(raw, near_mine, rest, other_grad)
-
-    draw, gsum, glocal = cotangent(scal, out_grad, out_weight, rest, queries, raw)
+    other_attn = [shift(attn, "ctx", n_ctx, k, True) for k in range(1, n_ctx)]
+    other_attn = other_attn[0] if n_ctx == 2 else jnp.concatenate(other_attn, 0)
+
+    draw, gsum, glocal, own_out = cotangent(
+        scal, out_weight, grad_vmem, rest, queries, raw, attn, own_width // 2 if paired else own_width
+    )
     suffix = total([shift(gsum, "ctx", n_ctx, -k, False) for k in range(1, n_ctx)])
 
     if paired:
-        far_z = lax.ppermute(after(far_mine, gsum), "rep", zpair)
-        own_out = project_own(scal, after(attn, gsum), out_weight, rest, out_weight.shape[1] // 2)
-        other_attn = after(other_attn, own_out, far_mine)
-
-    weight_grad = own_weight_grad(scal, attn, out_grad, other_attn, other_grad)
+        far_z = lax.ppermute(after(far_mine, gsum), ("ctx", "rep"), zpair)
+        other_attn = after(other_attn, gsum, far_mine)
+
+    weight_grad = own_weight_grad(scal, attn, grad_vmem, other_attn, other_grad)
 
     if paired:
         near_other = lax.ppermute(after(near_mine, weight_grad), "ctx", swap)
@@ -460,12 +450,12 @@
     query_grad, key_grad, value_grad = backward(queries, keys, values, draw, prefix, suffix, glocal)
 
     if paired:
-        far_other = lax.ppermute(after(far_mine, weight_grad), "ctx", swap)
+        far_other = lax.ppermute(after(far_mine, weight_grad), "ctx", [(0, 1)])
         near_out = project_near(
             scal, after(own_out, query_grad), (attn_1, attn_2),
             (near_mine, near_z, near_other, near_other_z),
         )
-        far_other_z = lax.ppermute(after(far_z, near_out), "ctx", swap)
+        far_other_z = lax.ppermute(after(far_z, near_out), "ctx", [(0, 1)])
         layer_out = project_far(scal, near_out, attn_3, (far_mine, far_other, far_z, far_other_z))
     else:
         full = lax.all_gather(out_weight, "ctx", axis=1, tiled=True)

time: 49.5 us -> 48.8 us (0.986)
  starting transfers between devices: 18.4 us -> 22.3 us
  Pallas kernels: 23.8 us -> 21.3 us
  waiting for transfers between devices: 6.08 us -> 4.08 us
    ppermute x3, waiting for transfers between devices: 5.24 us -> 0.01 us  [the longest x1 0.01 us: body(): far_z = lax.ppermute(after(far_mine, gsum), ('ctx', 'rep'), zpair)]
    ppermute x3, starting transfers between devices: 1.37 us -> 6.11 us  [the longest x1 3.47 us: body(): far_z = lax.ppermute(after(far_mine, gsum), ('ctx', 'rep'), zpair)]
    ppermute x1, waiting for transfers between devices: 0.01 us -> 3.22 us  [body(): attn_3 = lax.ppermute(after(attn_1, weight_grad), group, two)]
    pallas_call x1, Pallas kernels: 6.03 us -> 4.2 us  [cotangent(): pl.pallas_call(cotangent_kernel, out_shape=(shape_of((tok, width), BF16),...]
    pallas_call x1 -> x0, Pallas kernels: 1.26 us -> none  [project_own(): pl.pallas_call(project_own_kernel, out_shape=shape_of((tok, out_width), F...]
    ppermute x1, waiting for transfers between devices: 0.01 us -> 0.82 us  [body(): near_z = lax.ppermute(near_mine, 'rep', zpair)]
    pallas_call x1, Pallas kernels: 1.55 us -> 2.35 us  [forward(): pl.pallas_call(forward_kernel, out_shape=(shape_of((tok, width), BF16), s...]
  transfers between devices with their start and end apart: 16 -> 16, of which waited for: 5 -> 2; matrix products, arithmetic and copies ran while one was open for 0% -> 0% of each run, Pallas kernels for 44% -> 40%
where the time goes in v2:
time: 48.8 us; the launch traced here: 48.5 us
  starting transfers between devices  22.3 us (46%)
  Pallas kernels  21.3 us (44%)
  waiting for transfers between devices  4.08 us (8%)
  between operations  0.8 us (2%)
    ppermute x4, starting transfers between devices, shift(): return lax.ppermute(array, axis, pairs)  6.14 us
    pallas_call x1, Pallas kernels, cotangent(): pl.pallas_call(cotangent_kernel, out_shape=(shape_of((tok, width), BF16),...  4.2 us
    pallas_call x1, Pallas kernels, own_weight_grad(): pl.pallas_call(weight_grad_kernel, out_shape=shape_of((width, own_width),...  3.89 us
    pallas_call x1, Pallas kernels, backward(): pl.pallas_call(backward_kernel, out_shape=(out, out, out), compiler_param...  3.79 us
    ppermute x1, starting transfers between devices, body(): far_z = lax.ppermute(after(far_mine, gsum), ('ctx', 'rep'), zpair)  3.47 us
    ppermute x1, waiting for transfers between devices, body(): attn_3 = lax.ppermute(after(attn_1, weight_grad), group, two)  3.22 us
    pallas_call x1, Pallas kernels, opening(): pl.pallas_call(opening_kernel, out_shape=(shape_of((width, DH), BF16), pi...  3.18 us
    ppermute x1, starting transfers between devices, body(): near_mine = lax.ppermute(near_piece, group, near)  2.94 us
  transfers between devices with their start and end apart: 16, of which 2 were waited for; matrix products, arithmetic and copies ran while one was open for 0% of the time, Pallas kernels for 40%

profile of v2, /device:TPU:0, one launch (start us, length us, event | category | flops | bytes accessed | tf_op | source)
XLA Modules:
  0.0 48.5 jit_solution(17113856367612564332)
XLA Ops:
  0.6 0.5 %collective-permute-start.1 = (bf16[512,2048]{1,0:T(8,128)(2,1)}, bf16[512,2048]{1,0:T(8,128)(2,1)S(1)}, u32[]{:S(2)}, u32[]{:S(2)}) collective-permute-start(bf16[512,2048]{1,0:T(8,128)(2,1)} %own_ref.1), channel_id=1, source_target_pairs={{0,16},{16,0},{1,17},{17,1},{2,18},{18,2},{3,19},{19,3},{4,20},{20... | collective-permute-start | bytes 6291464 | tf_op jit(solution)/shard_map/ppermute | solution.py:377
  1.1 0.1 pad_add_fusion.s_ref
  1.2 3.2 %shard_map.92 = (bf16[512,128]{1,0:T(8,128)(2,1)S(1)}, bf16[256,1024]{1,0:T(8,128)(2,1)S(1)}, bf16[256,1024]{1,0:T(8,128)(2,1)S(1)}, bf16[512,2048]{1,0:T(8,128)...) custom-call(s32[4]{0:T(128)S(1)} %pad_add_fusion.s_ref, ...), custom_call_target="tpu_custom_call" | custom-call | flops 67108864 | bytes 1048576 | tf_op jit(solution)/shard_map/pallas_call | solution.py:103
  4.4 0.1 collective-permute-start.3
  4.5 2.9 %collective-permute-start.2 = (bf16[256,1024]{1,0:T(8,128)(2,1)S(1)}, bf16[256,1024]{1,0:T(8,128)(2,1)S(1)}, u32[]{:S(2)}, u32[]{:S(2)}) collective-permute-start(bf16[256,1024]{1,0:T(8,128)(2,1)S(1)} %get-tuple-element.41), channel_id=1, source_target_pairs={{0,4},{4,0},{24,12},{28,8},{16,24},{20,28},{8,16},{12,20},{1,5},{5... | collective-permute-start | bytes 1572872 | tf_op jit(solution)/shard_map/ppermute | solution.py:406
  7.5 1.7 %collective-permute-start = (bf16[512,128]{1,0:T(8,128)(2,1)S(1)}, bf16[512,128]{1,0:T(8,128)(2,1)S(1)}, u32[]{:S(2)}, u32[]{:S(2)}) collective-permute-start(bf16[512,128]{1,0:T(8,128)(2,1)S(1)} %get-tuple-element.37), channel_id=1, source_target_pairs={{0,16},{1,17},{2,18},{3,19},{4,20},{5,21},{6,22},{7,23},{8,24},{9,... | collective-permute-start | bytes 393224 | tf_op jit(solution)/shard_map/ppermute | solution.py:377
  9.2 1.3 %collective-permute-start.6 = (bf16[256,1024]{1,0:T(8,128)(2,1)S(1)}, bf16[256,1024]{1,0:T(8,128)(2,1)S(1)}, u32[]{:S(2)}, u32[]{:S(2)}) collective-permute-start(bf16[256,1024]{1,0:T(8,128)(2,1)S(1)} %get-tuple-element.49), channel_id=1, source_target_pairs={{16,12},{20,8},{8,4},{12,0},{17,13},{21,9},{9,5},{13,1},{18,14},{2... | collective-permute-start | bytes 1572872 | tf_op jit(solution)/shard_map/ppermute | solution.py:407
  10.5 0.0 collective-permute-done.carried_ref
  10.5 0.0 collective-permute-done.1.rest_ref
  10.5 0.0 copy-start
  10.5 2.3 %shard_map.93 = (bf16[512,512]{1,0:T(8,128)(2,1)S(1)}, f32[512,512]{1,0:T(8,128)S(1)}, bf16[2,512,128]{2,1,0:T(8,128)(2,1)S(1)}, bf16[512,4096]{1,0:T(8,128)(2,1)S(1)}) custom-call(bf16[512,512]{1,0:T(8,128)(2,1)S(1)} %get-tuple-element.34.q_ref, bf16[512,512]{1,0:T(8,128)(2,1)S(1)} %get-tuple-element.35.k_ref, ...), custom_call_target="tpu_custom_call" | custom-call | flops 536870912 | bytes 3145728 | tf_op jit(solution)/shard_map/pallas_call | solution.py:150
  12.9 2.6 %collective-permute-start.5 = (bf16[512,512]{1,0:T(8,128)(2,1)S(1)}, bf16[512,512]{1,0:T(8,128)(2,1)S(1)}, u32[]{:S(2)}, u32[]{:S(2)}) collective-permute-start(bf16[512,512]{1,0:T(8,128)(2,1)S(1)} %get-tuple-element.44.attn_ref), channel_id=1, source_target_pairs={{0,16},{16,0},{1,17},{17,1},{2,18},{18,2},{3,19},{19,3},{4,20},{20... | collective-permute-start | bytes 1572872 | tf_op jit(solution)/shard_map/ppermute | solution.py:377
  15.5 0.0 collective-permute-done.2.m1_ref
  15.5 1.6 %collective-permute-start.9 = (bf16[256,1024]{1,0:T(8,128)(2,1)S(1)}, bf16[256,1024]{1,0:T(8,128)(2,1)S(1)}, u32[]{:S(2)}, u32[]{:S(2)}) collective-permute-start(bf16[256,1024]{1,0:T(8,128)(2,1)S(1)} %collective-permute-done.2.m1_ref), channel_id=1, source_target_pairs={{0,1},{1,0},{2,3},{3,2},{4,5},{5,4},{6,7},{7,6},{8,9},{9,8},{10,11... | collective-permute-start | bytes 1572872 | tf_op jit(solution)/shard_map/ppermute | solution.py:428
  17.1 1.9 %collective-permute-start.7 = (bf16[512,512]{1,0:T(8,128)(2,1)S(1)}, bf16[512,512]{1,0:T(8,128)(2,1)S(1)}, u32[]{:S(2)}, u32[]{:S(2)}) collective-permute-start(bf16[512,512]{1,0:T(8,128)(2,1)S(1)} %get-tuple-element.44.attn_ref), channel_id=1, source_target_pairs={{0,4},{4,0},{8,12},{12,8},{16,24},{20,28},{24,16},{28,20},{1,5},{5... | collective-permute-start | bytes 1572872 | tf_op jit(solution)/shard_map/ppermute | solution.py:426
  19.0 0.0 collective-permute-done.3.other_grad_ref
  19.0 0.2 collective-permute-start.8
  19.2 0.0 copy-done
  19.2 4.2 %shard_map.94 = (bf16[512,512]{1,0:T(8,128)(2,1)S(1)}, bf16[512,128]{1,0:T(8,128)(2,1)S(1)}, f32[2,512,128]{2,1,0:T(8,128)S(1)}, f32[512,1024]{1,0:T(8,128)S(1)}) custom-call(s32[4]{0:T(128)S(1)} %pad_add_fusion.s_ref, bf16[512,2048]{1,0:T(8,128)(2,1)S(1)} %copy-done, bf16[512,4096]{1,0:T(8,128)(2,1)S(1)} %get-tuple-element.39.grad_ref, ...), custom_call_target="tpu_custom_call" | custom-call | flops 2147483648 | bytes 8388608 | tf_op jit(solution)/shard_map/pallas_call | solution.py:210
  23.4 0.0 collective-permute-done.6.d_ref
  23.4 1.3 %collective-permute-start.4 = (bf16[512,128]{1,0:T(8,128)(2,1)S(1)}, bf16[512,128]{1,0:T(8,128)(2,1)S(1)}, u32[]{:S(2)}, u32[]{:S(2)}) collective-permute-start(bf16[512,128]{1,0:T(8,128)(2,1)S(1)} %get-tuple-element.48), channel_id=1, source_target_pairs={{16,0},{17,1},{18,2},{19,3},{20,4},{21,5},{22,6},{23,7},{24,8},{25... | collective-permute-start | bytes 393224 | tf_op jit(solution)/shard_map/ppermute | solution.py:377
  24.7 0.0 collective-permute-done.5.other_ref
  24.7 3.9 %shard_map.95 = f32[512,2048]{1,0:T(8,128)} custom-call(s32[4]{0:T(128)S(1)} %pad_add_fusion.s_ref, bf16[512,512]{1,0:T(8,128)(2,1)S(1)} %get-tuple-element.44.attn_ref, bf16[512,4096]{1,0:T(8,128)(2,1)S(1)} %get-tuple-element.39.grad_ref, bf16[512,512]{1,0:T(8,128)(2,1)S(1)} %collective-permute-done.5.other_ref, ...), custom_call_target="tpu_custom_call" | custom-call | flops 2147483648 | bytes 8388608 | tf_op jit(solution)/shard_map/pallas_call | solution.py:250
  28.6 0.8 %collective-permute-done.9.z1_ref = bf16[256,1024]{1,0:T(8,128)(2,1)S(1)} collective-permute-done((bf16[256,1024]{1,0:T(8,128)(2,1)S(1)}, bf16[256,1024]{1,0:T(8,128)(2,1)S(1)}, u32[]{:S(2)}, u32[]{:S(2)}) %collective-permute-start.9) | collective-permute-done | bytes 524320 | tf_op jit(solution)/shard_map/ppermute | solution.py:428
  29.4 0.4 collective-permute-start.11
  29.8 0.1 collective-permute-start.10
  29.9 0.0 collective-permute-done.4.suffix_ref
  29.9 3.5 %collective-permute-start.14 = (bf16[256,1024]{1,0:T(8,128)(2,1)S(1)}, bf16[256,1024]{1,0:T(8,128)(2,1)S(1)}, u32[]{:S(2)}, u32[]{:S(2)}) collective-permute-start(bf16[256,1024]{1,0:T(8,128)(2,1)S(1)} %collective-permute-done.6.d_ref), channel_id=1, source_target_pairs={{0,1},{1,0},{2,3},{3,2},{4,5},{5,4},{6,7},{7,6},{8,9},{9,8},{10,11... | collective-permute-start | bytes 1572872 | tf_op jit(solution)/shard_map/ppermute | solution.py:439
  33.4 0.0 collective-permute-done.7.a1_ref
  33.4 0.0 collective-permute-done.8.a2_ref
  33.4 3.8 %shard_map.96 = (bf16[512,512]{1,0:T(8,128)(2,1)}, bf16[512,512]{1,0:T(8,128)(2,1)}, bf16[512,512]{1,0:T(8,128)(2,1)}) custom-call(bf16[512,512]{1,0:T(8,128)(2,1)S(1)} %get-tuple-element.34.q_ref, bf16[512,512]{1,0:T(8,128)(2,1)S(1)} %get-tuple-element.35.k_ref, bf16[512,512]{1,0:T(8,128)(2,1)S(1)} %get-tuple-element.36.v_ref, ...), custom_call_target="tpu_custom_call" | custom-call | flops 1073741824 | bytes 4194304 | tf_op jit(solution)/shard_map/pallas_call | solution.py:299
  37.2 1.5 %collective-permute-start.12 = (bf16[512,512]{1,0:T(8,128)(2,1)S(1)}, bf16[512,512]{1,0:T(8,128)(2,1)S(1)}, u32[]{:S(2)}, u32[]{:S(2)}) collective-permute-start(bf16[512,512]{1,0:T(8,128)(2,1)S(1)} %collective-permute-done.7.a1_ref), channel_id=1, source_target_pairs={{0,8},{4,12},{8,0},{12,4},{16,20},{20,16},{24,28},{28,24},{1,9},{5... | collective-permute-start | bytes 1572872 | tf_op jit(solution)/shard_map/ppermute | solution.py:446
  38.7 1.3 %collective-permute-start.13 = (bf16[256,1024]{1,0:T(8,128)(2,1)S(1)}, bf16[256,1024]{1,0:T(8,128)(2,1)S(1)}, u32[]{:S(2)}, u32[]{:S(2)}) collective-permute-start(bf16[256,1024]{1,0:T(8,128)(2,1)S(1)} %collective-permute-done.6.d_ref), channel_id=1, source_target_pairs={{0,16},{1,17},{2,18},{3,19},{4,20},{5,21},{6,22},{7,23},{8,24},{9,... | collective-permute-start | bytes 1572872 | tf_op jit(solution)/shard_map/ppermute | solution.py:453
  40.0 0.0 collective-permute-done.11.oz1_ref
  40.0 0.0 collective-permute-done.10.o1_ref
  40.0 1.8 %shard_map.97.near_ref = f32[512,1024]{1,0:T(8,128)S(1)} custom-call(s32[4]{0:T(128)S(1)} %pad_add_fusion.s_ref, f32[512,1024]{1,0:T(8,128)S(1)} %get-tuple-element.54.out_so_far_ref, bf16[512,512]{1,0:T(8,128)(2,1)S(1)} %collective-permute-done.7.a1_ref, bf16[512,512]{1,0:T(8,128)(2,1)S(1)} %collective-permute-done.8.a2_ref, ...), custom_call_target="tpu_custom_call" | custom-call | flops 1073741824 | bytes 4194304 | tf_op jit(solution)/shard_map/pallas_call | solution.py:325
  41.9 0.0 collective-permute-done.14.dz_ref
  41.9 1.3 %collective-permute-start.15 = (bf16[256,1024]{1,0:T(8,128)(2,1)S(1)}, bf16[256,1024]{1,0:T(8,128)(2,1)S(1)}, u32[]{:S(2)}, u32[]{:S(2)}) collective-permute-start(bf16[256,1024]{1,0:T(8,128)(2,1)S(1)} %collective-permute-done.14.dz_ref), channel_id=1, source_target_pairs={{0,16},{1,17},{2,18},{3,19},{4,20},{5,21},{6,22},{7,23},{8,24},{9,... | collective-permute-start | bytes 1572872 | tf_op jit(solution)/shard_map/ppermute | solution.py:458
  43.2 3.2 %collective-permute-done.12.a_ref = bf16[512,512]{1,0:T(8,128)(2,1)S(1)} collective-permute-done((bf16[512,512]{1,0:T(8,128)(2,1)S(1)}, bf16[512,512]{1,0:T(8,128)(2,1)S(1)}, u32[]{:S(2)}, u32[]{:S(2)}) %collective-permute-start.12) | collective-permute-done | bytes 524320 | tf_op jit(solution)/shard_map/ppermute | solution.py:446
  46.4 0.0 collective-permute-done.13.od_ref
  46.4 0.0 collective-permute-done.15.odz_ref
  46.4 2.1 %shard_map.98 = bf16[512,1024]{1,0:T(8,128)(2,1)} custom-call(s32[4]{0:T(128)S(1)} %pad_add_fusion.s_ref, f32[512,1024]{1,0:T(8,128)S(1)} %shard_map.97.near_ref, bf16[512,512]{1,0:T(8,128)(2,1)S(1)} %collective-permute-done.12.a_ref, bf16[256,1024]{1,0:T(8,128)(2,1)S(1)} %collective-permute-done.6.d_ref, ...), custom_call_target="tpu_custom_call" | custom-call | flops 536870912 | bytes 4194304 | tf_op jit(solution)/shard_map/pallas_call | solution.py:353
Async XLA Ops:
  0.6 9.9 %collective-permute-start.1 = (bf16[512,2048]{1,0:T(8,128)(2,1)}, bf16[512,2048]{1,0:T(8,128)(2,1)S(1)}, u32[]{:S(2)}, u32[]{:S(2)}) collective-permute-start(bf16[512,2048]{1,0:T(8,128)(2,1)} %own_ref.1), channel_id=1, source_target_pairs={{0,16},{16,0},{1,17},{17,1},{2,18},{18,2},{3,19},{19,3},{4,20},{20... | collective-permute-start | bytes 6291464 | tf_op jit(solution)/shard_map/ppermute | solution.py:377
  4.4 14.5 %collective-permute-start.3 = (bf16[512,2048]{1,0:T(8,128)(2,1)S(1)}, bf16[512,2048]{1,0:T(8,128)(2,1)S(1)}, u32[]{:S(2)}, u32[]{:S(2)}) collective-permute-start(bf16[512,2048]{1,0:T(8,128)(2,1)S(1)} %get-tuple-element.42), channel_id=1, source_target_pairs={{0,16},{16,0},{1,17},{17,1},{2,18},{18,2},{3,19},{19,3},{4,20},{20... | collective-permute-start | bytes 6291464 | tf_op jit(solution)/shard_map/ppermute | solution.py:408
  4.5 11.0 %collective-permute-start.2 = (bf16[256,1024]{1,0:T(8,128)(2,1)S(1)}, bf16[256,1024]{1,0:T(8,128)(2,1)S(1)}, u32[]{:S(2)}, u32[]{:S(2)}) collective-permute-start(bf16[256,1024]{1,0:T(8,128)(2,1)S(1)} %get-tuple-element.41), channel_id=1, source_target_pairs={{0,4},{4,0},{24,12},{28,8},{16,24},{20,28},{8,16},{12,20},{1,5},{5... | collective-permute-start | bytes 1572872 | tf_op jit(solution)/shard_map/ppermute | solution.py:406
  7.5 3.0 %collective-permute-start = (bf16[512,128]{1,0:T(8,128)(2,1)S(1)}, bf16[512,128]{1,0:T(8,128)(2,1)S(1)}, u32[]{:S(2)}, u32[]{:S(2)}) collective-permute-start(bf16[512,128]{1,0:T(8,128)(2,1)S(1)} %get-tuple-element.37), channel_id=1, source_target_pairs={{0,16},{1,17},{2,18},{3,19},{4,20},{5,21},{6,22},{7,23},{8,24},{9,... | collective-permute-start | bytes 393224 | tf_op jit(solution)/shard_map/ppermute | solution.py:377
  9.2 14.2 %collective-permute-start.6 = (bf16[256,1024]{1,0:T(8,128)(2,1)S(1)}, bf16[256,1024]{1,0:T(8,128)(2,1)S(1)}, u32[]{:S(2)}, u32[]{:S(2)}) collective-permute-start(bf16[256,1024]{1,0:T(8,128)(2,1)S(1)} %get-tuple-element.49), channel_id=1, source_target_pairs={{16,12},{20,8},{8,4},{12,0},{17,13},{21,9},{9,5},{13,1},{18,14},{2... | collective-permute-start | bytes 1572872 | tf_op jit(solution)/shard_map/ppermute | solution.py:407
  10.5 8.7 %copy-start = (bf16[512,2048]{1,0:T(8,128)(2,1)S(1)}, bf16[512,2048]{1,0:T(8,128)(2,1)}, u32[]{:S(2)}) copy-start(bf16[512,2048]{1,0:T(8,128)(2,1)} %own_ref.1) | copy-start | bytes 6291460
  12.9 11.8 %collective-permute-start.5 = (bf16[512,512]{1,0:T(8,128)(2,1)S(1)}, bf16[512,512]{1,0:T(8,128)(2,1)S(1)}, u32[]{:S(2)}, u32[]{:S(2)}) collective-permute-start(bf16[512,512]{1,0:T(8,128)(2,1)S(1)} %get-tuple-element.44.attn_ref), channel_id=1, source_target_pairs={{0,16},{16,0},{1,17},{17,1},{2,18},{18,2},{3,19},{19,3},{4,20},{20... | collective-permute-start | bytes 1572872 | tf_op jit(solution)/shard_map/ppermute | solution.py:377
  15.5 13.9 %collective-permute-start.9 = (bf16[256,1024]{1,0:T(8,128)(2,1)S(1)}, bf16[256,1024]{1,0:T(8,128)(2,1)S(1)}, u32[]{:S(2)}, u32[]{:S(2)}) collective-permute-start(bf16[256,1024]{1,0:T(8,128)(2,1)S(1)} %collective-permute-done.2.m1_ref), channel_id=1, source_target_pairs={{0,1},{1,0},{2,3},{3,2},{4,5},{5,4},{6,7},{7,6},{8,9},{9,8},{10,11... | collective-permute-start | bytes 1572872 | tf_op jit(solution)/shard_map/ppermute | solution.py:428
  17.1 16.3 %collective-permute-start.7 = (bf16[512,512]{1,0:T(8,128)(2,1)S(1)}, bf16[512,512]{1,0:T(8,128)(2,1)S(1)}, u32[]{:S(2)}, u32[]{:S(2)}) collective-permute-start(bf16[512,512]{1,0:T(8,128)(2,1)S(1)} %get-tuple-element.44.attn_ref), channel_id=1, source_target_pairs={{0,4},{4,0},{8,12},{12,8},{16,24},{20,28},{24,16},{28,20},{1,5},{5... | collective-permute-start | bytes 1572872 | tf_op jit(solution)/shard_map/ppermute | solution.py:426
  19.0 14.5 %collective-permute-start.8 = (bf16[512,512]{1,0:T(8,128)(2,1)S(1)}, bf16[512,512]{1,0:T(8,128)(2,1)S(1)}, u32[]{:S(2)}, u32[]{:S(2)}) collective-permute-start(bf16[512,512]{1,0:T(8,128)(2,1)S(1)} %get-tuple-element.44.attn_ref), channel_id=1, source_target_pairs={{0,8},{4,12},{8,0},{12,4},{16,20},{20,16},{24,28},{28,24},{1,9},{5... | collective-permute-start | bytes 1572872 | tf_op jit(solution)/shard_map/ppermute | solution.py:427
  23.4 6.5 %collective-permute-start.4 = (bf16[512,128]{1,0:T(8,128)(2,1)S(1)}, bf16[512,128]{1,0:T(8,128)(2,1)S(1)}, u32[]{:S(2)}, u32[]{:S(2)}) collective-permute-start(bf16[512,128]{1,0:T(8,128)(2,1)S(1)} %get-tuple-element.48), channel_id=1, source_target_pairs={{16,0},{17,1},{18,2},{19,3},{20,4},{21,5},{22,6},{23,7},{24,8},{25... | collective-permute-start | bytes 393224 | tf_op jit(solution)/shard_map/ppermute | solution.py:377
  29.4 10.6 %collective-permute-start.11 = (bf16[256,1024]{1,0:T(8,128)(2,1)S(1)}, bf16[256,1024]{1,0:T(8,128)(2,1)S(1)}, u32[]{:S(2)}, u32[]{:S(2)}) collective-permute-start(bf16[256,1024]{1,0:T(8,128)(2,1)S(1)} %collective-permute-done.9.z1_ref), channel_id=1, source_target_pairs={{0,16},{16,0},{1,17},{17,1},{2,18},{18,2},{3,19},{19,3},{4,20},{20... | collective-permute-start | bytes 1572872 | tf_op jit(solution)/shard_map/ppermute | solution.py:447
  29.8 10.2 %collective-permute-start.10 = (bf16[256,1024]{1,0:T(8,128)(2,1)S(1)}, bf16[256,1024]{1,0:T(8,128)(2,1)S(1)}, u32[]{:S(2)}, u32[]{:S(2)}) collective-permute-start(bf16[256,1024]{1,0:T(8,128)(2,1)S(1)} %collective-permute-done.2.m1_ref), channel_id=1, source_target_pairs={{0,16},{16,0},{1,17},{17,1},{2,18},{18,2},{3,19},{19,3},{4,20},{20... | collective-permute-start | bytes 1572872 | tf_op jit(solution)/shard_map/ppermute | solution.py:445
  29.9 11.9 %collective-permute-start.14 = (bf16[256,1024]{1,0:T(8,128)(2,1)S(1)}, bf16[256,1024]{1,0:T(8,128)(2,1)S(1)}, u32[]{:S(2)}, u32[]{:S(2)}) collective-permute-start(bf16[256,1024]{1,0:T(8,128)(2,1)S(1)} %collective-permute-done.6.d_ref), channel_id=1, source_target_pairs={{0,1},{1,0},{2,3},{3,2},{4,5},{5,4},{6,7},{7,6},{8,9},{9,8},{10,11... | collective-permute-start | bytes 1572872 | tf_op jit(solution)/shard_map/ppermute | solution.py:439
  37.2 9.2 %collective-permute-start.12 = (bf16[512,512]{1,0:T(8,128)(2,1)S(1)}, bf16[512,512]{1,0:T(8,128)(2,1)S(1)}, u32[]{:S(2)}, u32[]{:S(2)}) collective-permute-start(bf16[512,512]{1,0:T(8,128)(2,1)S(1)} %collective-permute-done.7.a1_ref), channel_id=1, source_target_pairs={{0,8},{4,12},{8,0},{12,4},{16,20},{20,16},{24,28},{28,24},{1,9},{5... | collective-permute-start | bytes 1572872 | tf_op jit(solution)/shard_map/ppermute | solution.py:446
  38.7 7.7 %collective-permute-start.13 = (bf16[256,1024]{1,0:T(8,128)(2,1)S(1)}, bf16[256,1024]{1,0:T(8,128)(2,1)S(1)}, u32[]{:S(2)}, u32[]{:S(2)}) collective-permute-start(bf16[256,1024]{1,0:T(8,128)(2,1)S(1)} %collective-permute-done.6.d_ref), channel_id=1, source_target_pairs={{0,16},{1,17},{2,18},{3,19},{4,20},{5,21},{6,22},{7,23},{8,24},{9,... | collective-permute-start | bytes 1572872 | tf_op jit(solution)/shard_map/ppermute | solution.py:453
  41.9 4.6 %collective-permute-start.15 = (bf16[256,1024]{1,0:T(8,128)(2,1)S(1)}, bf16[256,1024]{1,0:T(8,128)(2,1)S(1)}, u32[]{:S(2)}, u32[]{:S(2)}) collective-permute-start(bf16[256,1024]{1,0:T(8,128)(2,1)S(1)} %collective-permute-done.14.dz_ref), channel_id=1, source_target_pairs={{0,16},{1,17},{2,18},{3,19},{4,20},{5,21},{6,22},{7,23},{8,24},{9,... | collective-permute-start | bytes 1572872 | tf_op jit(solution)/shard_map/ppermute | solution.py:458

commit v3 on v2

--- a/solution.py
+++ b/solution.py
@@ -115,9 +115,7 @@
     )(scal, queries, keys, values, weight, out_grad)
 
 
-def forward_kernel(q_ref, k_ref, v_ref, carried_ref, grad_hbm, attn_ref, raw_ref, prefix_ref, grad_ref, sem):
-    load = pltpu.make_async_copy(grad_hbm, grad_ref, sem)
-    load.start()
+def forward_kernel(q_ref, k_ref, v_ref, carried_ref, attn_ref, raw_ref, prefix_ref):
     tok, width = q_ref.shape
     chunk = min(CHUNK, tok)
     row = lax.broadcasted_iota(jnp.int32, (chunk, chunk), 0)
@@ -140,12 +138,10 @@
             attn_ref[rows, cols] = (raw * inv).astype(BF16)
             if i + 1 < tok // chunk:
                 prefix = prefix + dot_tn(fk, v)
-    load.wait()
-
-
-def forward(queries, keys, values, carried, out_grad):
+
+
+def forward(queries, keys, values, carried):
     tok, width = queries.shape
-    vmem = pl.BlockSpec(memory_space=pltpu.VMEM)
     chunks = tok // min(CHUNK, tok)
     return pl.pallas_call(
         forward_kernel,
@@ -153,22 +149,19 @@
             shape_of((tok, width), BF16),
             shape_of((tok, width), F32),
             shape_of((chunks, width, DH), BF16),
-            shape_of(out_grad.shape, BF16),
         ),
-        in_specs=[vmem] * 4 + [pl.BlockSpec(memory_space=pltpu.HBM)],
-        out_specs=(vmem,) * 4,
-        scratch_shapes=[pltpu.SemaphoreType.DMA],
         compiler_params=params(16),
         cost_estimate=cost(16 * queries.size * DH, 12 * queries.size),
-    )(queries, keys, values, carried, out_grad)
-
-
-def cotangent_kernel(s_ref, own_ref, grad_ref, rest_ref, q_ref, raw_ref, attn_ref,
-                     draw_ref, gsum_ref, glocal_ref, out_ref, acc_ref):
+    )(queries, keys, values, carried)
+
+
+def smem_then_vmem(count):
+    return [pl.BlockSpec(memory_space=pltpu.SMEM)] + [pl.BlockSpec(memory_space=pltpu.VMEM)] * count
+
+
+def attn_grad_kernel(s_ref, own_ref, grad_ref, rest_ref, out_ref, acc_ref):
     own_width, rest_width = own_ref.shape[1], rest_ref.shape[1]
     count = (own_width + rest_width) // own_width
-    tok, width = q_ref.shape
-    chunk = min(CHUNK, tok)
 
     def part(k):
         place = lax.rem(s_ref[0] + k, count) * own_width
@@ -177,13 +170,32 @@
     acc_ref[...] = dot_nt(part(0), own_ref[...])
     for k in range(1, count):
         acc_ref[...] += dot_nt(part(k), rest_ref[:, (k - 1) * own_width : k * own_width])
+    out_ref[...] = acc_ref[...].astype(BF16)
+
+
+def attn_gradient(scal, weight, out_grad, rest):
+    tok, width = out_grad.shape[0], weight.shape[0]
+    return pl.pallas_call(
+        attn_grad_kernel,
+        out_shape=shape_of((tok, width), BF16),
+        in_specs=smem_then_vmem(3),
+        scratch_shapes=[pltpu.VMEM((tok, width), F32)],
+        compiler_params=params(16),
+        cost_estimate=cost(2 * out_grad.size * width, 4 * out_grad.size),
+    )(scal, weight, out_grad, rest)
+
+
+def cotangent_kernel(s_ref, attn_grad_ref, q_ref, raw_ref, attn_ref, own_ref, rest_ref,
+                     draw_ref, gsum_ref, glocal_ref, out_ref):
+    tok, width = q_ref.shape
+    chunk = min(CHUNK, tok)
     for lo in range(0, width, DH):
         cols = slice(lo, lo + DH)
         later = jnp.zeros((DH, DH), F32)
         for i in reversed(range(tok // chunk)):
             rows = slice(i * chunk, (i + 1) * chunk)
             glocal_ref[i, cols, :] = later
-            grad = acc_ref[rows, cols].astype(BF16).astype(F32)
+            grad = attn_grad_ref[rows, cols].astype(F32)
             raw = raw_ref[rows, cols]
             inv = lax.rsqrt(jnp.mean(raw * raw, axis=-1, keepdims=True) + EPS)
             normed = raw * inv
@@ -194,17 +206,13 @@
             later = later + dot_tn(fq, draw)
         gsum_ref[cols, :] = later.astype(BF16)
     wide = out_ref.shape[1]
-    if wide < own_width:
+    if wide < own_ref.shape[1]:
         local = pl.ds(pl.multiple_of(s_ref[2] * wide, wide), wide)
         weight = jnp.where(s_ref[0] == s_ref[1], own_ref[:, local], rest_ref[:, local])
         out_ref[...] = dot_nn(attn_ref[...], weight)
 
 
-def smem_then_vmem(count):
-    return [pl.BlockSpec(memory_space=pltpu.SMEM)] + [pl.BlockSpec(memory_space=pltpu.VMEM)] * count
-
-
-def cotangent(scal, weight, out_grad, rest, queries, raw, attn, out_width):
+def cotangent(scal, attn_grad, queries, raw, attn, own, rest, out_width):
     tok, width = queries.shape
     chunks = tok // min(CHUNK, tok)
     return pl.pallas_call(
@@ -216,10 +224,9 @@
             shape_of((tok, out_width), F32),
         ),
         in_specs=smem_then_vmem(6),
-        scratch_shapes=[pltpu.VMEM((tok, width), F32)],
-        compiler_params=params(16),
-        cost_estimate=cost(2 * out_grad.size * width, 4 * out_grad.size),
-    )(scal, weight, out_grad, rest, queries, raw, attn)
+        compiler_params=params(16),
+        cost_estimate=cost(2 * tok * width * out_width, 16 * queries.size),
+    )(scal, attn_grad, queries, raw, attn, own, rest)
 
 
 def weight_grad_kernel(s_ref, attn_ref, grad_ref, other_ref, other_grad_ref, out_hbm, out_buf, sems):
@@ -310,35 +317,19 @@
     return first, second
 
 
-def project_near_kernel(s_ref, out_so_far_ref, a1_ref, a2_ref, m1_ref, z1_ref, o1_ref, oz1_ref, out_ref):
-    first, second = halves(s_ref, m1_ref.shape[0])
-    acc = out_so_far_ref[...] + dot_nn(a1_ref[:, first], m1_ref[...])
-    acc += dot_nn(a1_ref[:, second], z1_ref[...])
-    acc += dot_nn(a2_ref[:, first], o1_ref[...])
-    acc += dot_nn(a2_ref[:, second], oz1_ref[...])
-    out_ref[...] = acc
-
-
-def project_near(scal, out_so_far, attns, pieces):
-    tok, width = attns[0].shape
-    out_width = pieces[0].shape[1]
-    return pl.pallas_call(
-        project_near_kernel,
-        out_shape=shape_of((tok, out_width), F32),
-        in_specs=smem_then_vmem(7),
-        compiler_params=params(16),
-        cost_estimate=cost(4 * tok * width * out_width, 8 * width * out_width),
-    )(scal, out_so_far, *attns, *pieces)
-
-
-def project_far_kernel(s_ref, near_ref, a_ref, d_ref, od_ref, dz_ref, odz_ref, out_hbm, out_buf, sems):
+def project_kernel(s_ref, own_out_ref, a1_ref, a2_ref, a3_ref, m1_ref, z1_ref, o1_ref, oz1_ref,
+                   d_ref, od_ref, dz_ref, odz_ref, out_hbm, out_buf, sems):
     first, second = halves(s_ref, d_ref.shape[0])
     blocks, _, block = out_buf.shape
     moves = []
     for j in range(blocks):
         here = slice(j * block, (j + 1) * block)
-        acc = near_ref[:, here] + dot_nn(a_ref[:, first], d_ref[:, here] + od_ref[:, here])
-        acc += dot_nn(a_ref[:, second], dz_ref[:, here] + odz_ref[:, here])
+        acc = own_out_ref[:, here] + dot_nn(a1_ref[:, first], m1_ref[:, here])
+        acc += dot_nn(a1_ref[:, second], z1_ref[:, here])
+        acc += dot_nn(a2_ref[:, first], o1_ref[:, here])
+        acc += dot_nn(a2_ref[:, second], oz1_ref[:, here])
+        acc += dot_nn(a3_ref[:, first], d_ref[:, here] + od_ref[:, here])
+        acc += dot_nn(a3_ref[:, second], dz_ref[:, here] + odz_ref[:, here])
         out_buf[j] = acc.astype(BF16)
         moves.append(pltpu.make_async_copy(out_buf.at[j], out_hbm.at[:, here], sems.at[j]))
         moves[-1].start()
@@ -346,22 +337,22 @@
         move.wait()
 
 
-def project_far(scal, near, attn, pieces):
-    tok, width = attn.shape
-    out_width = pieces[0].shape[1]
+def project(scal, own_out, attns, pieces):
+    tok, width = attns[0].shape
+    out_width = own_out.shape[1]
     block = 256
     return pl.pallas_call(
-        project_far_kernel,
+        project_kernel,
         out_shape=shape_of((tok, out_width), BF16),
-        in_specs=smem_then_vmem(6),
+        in_specs=smem_then_vmem(12),
         out_specs=pl.BlockSpec(memory_space=pl.ANY),
         scratch_shapes=[
             pltpu.VMEM((out_width // block, tok, block), BF16),
             pltpu.SemaphoreType.DMA((out_width // block,)),
         ],
         compiler_params=params(16),
-        cost_estimate=cost(2 * tok * width * out_width, 8 * width * out_width),
-    )(scal, near, attn, *pieces)
+        cost_estimate=cost(6 * tok * width * out_width, 8 * width * out_width),
+    )(scal, own_out, *attns, *pieces)
 
 
 def in_hbm(array):
@@ -418,20 +409,20 @@
     carried = total([shift(state, "ctx", n_ctx, k, False) for k in range(1, n_ctx)])
     rest = [shift(out_weight, "ctx", n_ctx, -k, True) for k in range(1, n_ctx)]
     rest = rest[0] if n_ctx == 2 else jnp.concatenate(rest, 1)
-    if paired:
-        carried = after(carried, rest)
-    attn, raw, prefix, grad_vmem = forward(queries, keys, values, carried, grad_hbm)
+    attn_grad = attn_gradient(scal, out_weight, out_grad, after(rest, state))
+    carried = after(carried, attn_grad)
+    attn, raw, prefix = forward(queries, keys, values, carried)
 
     if paired:
         attn_1 = lax.ppermute(attn, group, one)
         attn_2 = lax.ppermute(attn, group, two)
         near_z = lax.ppermute(near_mine, "rep", zpair)
-        raw = after(raw, near_mine, rest, other_grad)
+        raw = after(raw, near_mine, other_grad)
     other_attn = [shift(attn, "ctx", n_ctx, k, True) for k in range(1, n_ctx)]
     other_attn = other_attn[0] if n_ctx == 2 else jnp.concatenate(other_attn, 0)
 
     draw, gsum, glocal, own_out = cotangent(
-        scal, out_weight, grad_vmem, rest, queries, raw, attn, own_width // 2 if paired else own_width
+        scal, attn_grad, queries, raw, attn, out_weight, rest, own_width // 2 if paired else own_width
     )
     suffix = total([shift(gsum, "ctx", n_ctx, -k, False) for k in range(1, n_ctx)])
 
@@ -439,24 +430,24 @@
         far_z = lax.ppermute(after(far_mine, gsum), ("ctx", "rep"), zpair)
         other_attn = after(other_attn, gsum, far_mine)
 
-    weight_grad = own_weight_grad(scal, attn, grad_vmem, other_attn, other_grad)
+    weight_grad = own_weight_grad(scal, attn, out_grad, other_attn, other_grad)
 
     if paired:
         near_other = lax.ppermute(after(near_mine, weight_grad), "ctx", swap)
         attn_3 = lax.ppermute(after(attn_1, weight_grad), group, two)
         near_other_z = lax.ppermute(after(near_z, weight_grad), "ctx", swap)
-        suffix = after(suffix, weight_grad, attn_1, attn_2)
+        suffix = after(suffix, weight_grad, attn_1, attn_2, near_z)
 
     query_grad, key_grad, value_grad = backward(queries, keys, values, draw, prefix, suffix, glocal)
 
     if paired:
         far_other = lax.ppermute(after(far_mine, weight_grad), "ctx", [(0, 1)])
-        near_out = project_near(
-            scal, after(own_out, query_grad), (attn_1, attn_2),
-            (near_mine, near_z, near_other, near_other_z),
+        last = after(far_z, query_grad, attn_3, near_other_z, near_other, far_other)
+        far_other_z = lax.ppermute(last, "ctx", [(0, 1)])
+        layer_out = project(
+            scal, after(own_out, query_grad), (attn_1, attn_2, attn_3),
+            (near_mine, near_z, near_other, near_other_z, far_mine, far_other, far_z, far_other_z),
         )
-        far_other_z = lax.ppermute(after(far_z, near_out), "ctx", [(0, 1)])
-        layer_out = project_far(scal, near_out, attn_3, (far_mine, far_other, far_z, far_other_z))
     else:
         full = lax.all_gather(out_weight, "ctx", axis=1, tiled=True)
         partial_out = jnp.dot(attn, full, preferred_element_type=F32).astype(BF16)

time: 48.8 us -> 46.8 us (0.959)
  waiting for transfers between devices: 4.08 us -> 2.68 us
  starting transfers between devices: 22.3 us -> 21.7 us
    ppermute x1, waiting for transfers between devices: 3.22 us -> 1.02 us  [body(): attn_3 = lax.ppermute(after(attn_1, weight_grad), group, two)]
    pallas_call x2, Pallas kernels: 3.93 us -> 6.11 us  [the longest x1 3.21 us: project(): pl.pallas_call(project_kernel, out_shape=shape_of((tok, out_width), BF16)...]
    pallas_call x1, Pallas kernels: 4.2 us -> 2.3 us  [cotangent(): pl.pallas_call(cotangent_kernel, out_shape=(shape_of((tok, width), BF16),...]
    ppermute x1, waiting for transfers between devices: 0.01 us -> 1.49 us  [body(): far_other_z = lax.ppermute(last, 'ctx', [(0, 1)])]
    ppermute x1, starting transfers between devices: 3.47 us -> 2.35 us  [body(): far_z = lax.ppermute(after(far_mine, gsum), ('ctx', 'rep'), zpair)]
    ppermute x1, waiting for transfers between devices: 0.82 us -> 0.01 us  [body(): near_z = lax.ppermute(near_mine, 'rep', zpair)]
    pallas_call x1, Pallas kernels: 2.35 us -> 1.55 us  [forward(): pl.pallas_call(forward_kernel, out_shape=(shape_of((tok, width), BF16), s...]
    ppermute x1, starting transfers between devices: 1.31 us -> 1.99 us  [body(): far_other = lax.ppermute(after(far_mine, weight_grad), 'ctx', [(0, 1)])]
  transfers between devices with their start and end apart: 16 -> 16, of which waited for: 2 -> 3; matrix products, arithmetic and copies ran while one was open for 0% -> 0% of each run, Pallas kernels for 40% -> 39%
where the time goes in v3:
time: 46.8 us; the launch traced here: 46.3 us
  starting transfers between devices  21.7 us (46%)
  Pallas kernels  21.1 us (45%)
  waiting for transfers between devices  2.68 us (6%)
  between operations  0.78 us (2%)
    ppermute x4, starting transfers between devices, shift(): return lax.ppermute(array, axis, pairs)  6.14 us
    pallas_call x1, Pallas kernels, own_weight_grad(): pl.pallas_call(weight_grad_kernel, out_shape=shape_of((width, own_width),...  3.89 us
    pallas_call x1, Pallas kernels, backward(): pl.pallas_call(backward_kernel, out_shape=(out, out, out), compiler_param...  3.79 us
    pallas_call x1, Pallas kernels, opening(): pl.pallas_call(opening_kernel, out_shape=(shape_of((width, DH), BF16), pi...  3.42 us
    pallas_call x1, Pallas kernels, project(): pl.pallas_call(project_kernel, out_shape=shape_of((tok, out_width), BF16)...  3.21 us
    ppermute x1, starting transfers between devices, body(): near_mine = lax.ppermute(near_piece, group, near)  2.94 us
    pallas_call x1, Pallas kernels, attn_gradient(): pl.pallas_call(attn_grad_kernel, out_shape=shape_of((tok, width), BF16),...  2.9 us
    ppermute x1, starting transfers between devices, body(): far_z = lax.ppermute(after(far_mine, gsum), ('ctx', 'rep'), zpair)  2.35 us
  transfers between devices with their start and end apart: 16, of which 3 were waited for; matrix products, arithmetic and copies ran while one was open for 0% of the time, Pallas kernels for 39%

profile of v3, /device:TPU:0, one launch (start us, length us, event | category | flops | bytes accessed | tf_op | source)
XLA Modules:
  0.0 46.3 jit_solution(6813594248602021496)
XLA Ops:
  0.6 0.5 %collective-permute-start = (bf16[512,2048]{1,0:T(8,128)(2,1)}, bf16[512,2048]{1,0:T(8,128)(2,1)S(1)}, u32[]{:S(2)}, u32[]{:S(2)}) collective-permute-start(bf16[512,2048]{1,0:T(8,128)(2,1)} %own_ref.3), channel_id=1, source_target_pairs={{0,16},{16,0},{1,17},{17,1},{2,18},{18,2},{3,19},{19,3},{4,20},{20... | collective-permute-start | bytes 6291464 | tf_op jit(solution)/shard_map/ppermute | solution.py:368
  1.1 0.1 pad_add_fusion.s_ref
  1.2 0.0 copy-start
  1.2 0.0 copy-start.1
  1.2 3.4 %shard_map.92 = (bf16[512,128]{1,0:T(8,128)(2,1)S(1)}, bf16[256,1024]{1,0:T(8,128)(2,1)S(1)}, bf16[256,1024]{1,0:T(8,128)(2,1)S(1)}, bf16[512,2048]{1,0:T(8,128)...) custom-call(s32[4]{0:T(128)S(1)} %pad_add_fusion.s_ref, ...), custom_call_target="tpu_custom_call" | custom-call | flops 67108864 | bytes 1048576 | tf_op jit(solution)/shard_map/pallas_call | solution.py:103
  4.7 0.1 collective-permute-start.3
  4.8 2.9 %collective-permute-start.2 = (bf16[256,1024]{1,0:T(8,128)(2,1)S(1)}, bf16[256,1024]{1,0:T(8,128)(2,1)S(1)}, u32[]{:S(2)}, u32[]{:S(2)}) collective-permute-start(bf16[256,1024]{1,0:T(8,128)(2,1)S(1)} %get-tuple-element.41), channel_id=1, source_target_pairs={{0,4},{4,0},{24,12},{28,8},{16,24},{20,28},{8,16},{12,20},{1,5},{5... | collective-permute-start | bytes 1572872 | tf_op jit(solution)/shard_map/ppermute | solution.py:397
  7.7 1.7 %collective-permute-start.1 = (bf16[512,128]{1,0:T(8,128)(2,1)S(1)}, bf16[512,128]{1,0:T(8,128)(2,1)S(1)}, u32[]{:S(2)}, u32[]{:S(2)}) collective-permute-start(bf16[512,128]{1,0:T(8,128)(2,1)S(1)} %get-tuple-element.34), channel_id=1, source_target_pairs={{0,16},{1,17},{2,18},{3,19},{4,20},{5,21},{6,22},{7,23},{8,24},{9,... | collective-permute-start | bytes 393224 | tf_op jit(solution)/shard_map/ppermute | solution.py:368
  9.4 1.3 %collective-permute-start.6 = (bf16[256,1024]{1,0:T(8,128)(2,1)S(1)}, bf16[256,1024]{1,0:T(8,128)(2,1)S(1)}, u32[]{:S(2)}, u32[]{:S(2)}) collective-permute-start(bf16[256,1024]{1,0:T(8,128)(2,1)S(1)} %get-tuple-element.49), channel_id=1, source_target_pairs={{16,12},{20,8},{8,4},{12,0},{17,13},{21,9},{9,5},{13,1},{18,14},{2... | collective-permute-start | bytes 1572872 | tf_op jit(solution)/shard_map/ppermute | solution.py:398
  10.7 0.0 collective-permute-done.rest_ref
  10.8 0.0 copy-done
  10.8 0.0 copy-done.1
  10.8 2.9 %shard_map.93.attn_grad_ref = bf16[512,512]{1,0:T(8,128)(2,1)S(1)} custom-call(s32[4]{0:T(128)S(1)} %pad_add_fusion.s_ref, bf16[512,2048]{1,0:T(8,128)(2,1)S(1)} %copy-done.1, bf16[512,4096]{1,0:T(8,128)(2,1)S(1)} %copy-done, bf16[512,2048]{1,0:T(8,128)(2,1)S(1)} %collective-permute-done.rest_ref), custom_call_target="tpu_custom_call" | custom-call | flops 2147483648 | bytes 8388608 | tf_op jit(solution)/shard_map/pallas_call | solution.py:178
  13.7 0.0 collective-permute-done.1.carried_ref
  13.7 1.6 %shard_map.94 = (bf16[512,512]{1,0:T(8,128)(2,1)S(1)}, f32[512,512]{1,0:T(8,128)S(1)}, bf16[2,512,128]{2,1,0:T(8,128)(2,1)S(1)}) custom-call(bf16[512,512]{1,0:T(8,128)(2,1)S(1)} %get-tuple-element.36.q_ref, bf16[512,512]{1,0:T(8,128)(2,1)S(1)} %get-tuple-element.37.k_ref, bf16[512,512]{1,0:T(8,128)(2,1)S(1)} %get-tuple-element.38.v_ref, ...), custom_call_target="tpu_custom_call" | custom-call | flops 536870912 | bytes 3145728 | tf_op jit(solution)/shard_map/pallas_call | solution.py:146
  15.2 2.6 %collective-permute-start.5 = (bf16[512,512]{1,0:T(8,128)(2,1)S(1)}, bf16[512,512]{1,0:T(8,128)(2,1)S(1)}, u32[]{:S(2)}, u32[]{:S(2)}) collective-permute-start(bf16[512,512]{1,0:T(8,128)(2,1)S(1)} %get-tuple-element.44.attn_ref), channel_id=1, source_target_pairs={{0,16},{16,0},{1,17},{17,1},{2,18},{18,2},{3,19},{19,3},{4,20},{20... | collective-permute-start | bytes 1572872 | tf_op jit(solution)/shard_map/ppermute | solution.py:368
  17.9 1.5 %collective-permute-start.7 = (bf16[512,512]{1,0:T(8,128)(2,1)S(1)}, bf16[512,512]{1,0:T(8,128)(2,1)S(1)}, u32[]{:S(2)}, u32[]{:S(2)}) collective-permute-start(bf16[512,512]{1,0:T(8,128)(2,1)S(1)} %get-tuple-element.44.attn_ref), channel_id=1, source_target_pairs={{0,4},{4,0},{8,12},{12,8},{16,24},{20,28},{24,16},{28,20},{1,5},{5... | collective-permute-start | bytes 1572872 | tf_op jit(solution)/shard_map/ppermute | solution.py:417
  19.4 0.0 collective-permute-done.2.m1_ref
  19.4 1.6 %collective-permute-start.9 = (bf16[256,1024]{1,0:T(8,128)(2,1)S(1)}, bf16[256,1024]{1,0:T(8,128)(2,1)S(1)}, u32[]{:S(2)}, u32[]{:S(2)}) collective-permute-start(bf16[256,1024]{1,0:T(8,128)(2,1)S(1)} %collective-permute-done.2.m1_ref), channel_id=1, source_target_pairs={{0,1},{1,0},{2,3},{3,2},{4,5},{5,4},{6,7},{7,6},{8,9},{9,8},{10,11... | collective-permute-start | bytes 1572872 | tf_op jit(solution)/shard_map/ppermute | solution.py:419
  20.9 0.0 collective-permute-done.3.other_grad_ref
  20.9 0.1 collective-permute-start.8
  21.1 2.3 %shard_map.95 = (bf16[512,512]{1,0:T(8,128)(2,1)S(1)}, bf16[512,128]{1,0:T(8,128)(2,1)S(1)}, f32[2,512,128]{2,1,0:T(8,128)S(1)}, f32[512,1024]{1,0:T(8,128)S(1)}) custom-call(s32[4]{0:T(128)S(1)} %pad_add_fusion.s_ref, bf16[512,512]{1,0:T(8,128)(2,1)S(1)} %shard_map.93.attn_grad_ref, bf16[512,512]{1,0:T(8,128)(2,1)S(1)} %get-tuple-element.36.q_ref, ...), custom_call_target="tpu_custom_call" | custom-call | flops 536870912 | bytes 4194304 | tf_op jit(solution)/shard_map/pallas_call | solution.py:218
  23.4 0.0 collective-permute-done.6.d_ref
  23.4 1.3 %collective-permute-start.4 = (bf16[512,128]{1,0:T(8,128)(2,1)S(1)}, bf16[512,128]{1,0:T(8,128)(2,1)S(1)}, u32[]{:S(2)}, u32[]{:S(2)}) collective-permute-start(bf16[512,128]{1,0:T(8,128)(2,1)S(1)} %get-tuple-element.48), channel_id=1, source_target_pairs={{16,0},{17,1},{18,2},{19,3},{20,4},{21,5},{22,6},{23,7},{24,8},{25... | collective-permute-start | bytes 393224 | tf_op jit(solution)/shard_map/ppermute | solution.py:368
  24.7 0.0 collective-permute-done.5.other_ref
  24.7 2.4 %collective-permute-start.14 = (bf16[256,1024]{1,0:T(8,128)(2,1)S(1)}, bf16[256,1024]{1,0:T(8,128)(2,1)S(1)}, u32[]{:S(2)}, u32[]{:S(2)}) collective-permute-start(bf16[256,1024]{1,0:T(8,128)(2,1)S(1)} %collective-permute-done.6.d_ref), channel_id=1, source_target_pairs={{0,1},{1,0},{2,3},{3,2},{4,5},{5,4},{6,7},{7,6},{8,9},{9,8},{10,11... | collective-permute-start | bytes 1572872 | tf_op jit(solution)/shard_map/ppermute | solution.py:430
  27.1 3.9 %shard_map.96 = f32[512,2048]{1,0:T(8,128)} custom-call(s32[4]{0:T(128)S(1)} %pad_add_fusion.s_ref, bf16[512,512]{1,0:T(8,128)(2,1)S(1)} %get-tuple-element.44.attn_ref, bf16[512,4096]{1,0:T(8,128)(2,1)S(1)} %copy-done, bf16[512,512]{1,0:T(8,128)(2,1)S(1)} %collective-permute-done.5.other_ref, bf16[512,2048]{1,0:T(8,128)(2,1)S(1)} %collective-permute-done.3.other_grad_ref), custom_call_target="tpu_custom_call" | custom-call | flops 2147483648 | bytes 8388608 | tf_op jit(solution)/shard_map/pallas_call | solution.py:257
  31.0 0.1 collective-permute-done.7.a1_ref
  31.1 1.8 %collective-permute-start.10 = (bf16[512,512]{1,0:T(8,128)(2,1)S(1)}, bf16[512,512]{1,0:T(8,128)(2,1)S(1)}, u32[]{:S(2)}, u32[]{:S(2)}) collective-permute-start(bf16[512,512]{1,0:T(8,128)(2,1)S(1)} %collective-permute-done.7.a1_ref), channel_id=1, source_target_pairs={{0,8},{4,12},{8,0},{12,4},{16,20},{20,16},{24,28},{28,24},{1,9},{5... | collective-permute-start | bytes 1572872 | tf_op jit(solution)/shard_map/ppermute | solution.py:437
  32.9 0.0 collective-permute-done.9.z1_ref
  33.0 0.0 collective-permute-start.11
  33.0 0.0 collective-permute-done.4.suffix_ref
  33.0 0.5 %collective-permute-start.12 = (bf16[256,1024]{1,0:T(8,128)(2,1)S(1)}, bf16[256,1024]{1,0:T(8,128)(2,1)S(1)}, u32[]{:S(2)}, u32[]{:S(2)}) collective-permute-start(bf16[256,1024]{1,0:T(8,128)(2,1)S(1)} %collective-permute-done.9.z1_ref), channel_id=1, source_target_pairs={{0,16},{16,0},{1,17},{17,1},{2,18},{18,2},{3,19},{19,3},{4,20},{20... | collective-permute-start | bytes 1572872 | tf_op jit(solution)/shard_map/ppermute | solution.py:438
  33.5 0.0 collective-permute-done.8.a2_ref
  33.5 2.0 %collective-permute-start.13 = (bf16[256,1024]{1,0:T(8,128)(2,1)S(1)}, bf16[256,1024]{1,0:T(8,128)(2,1)S(1)}, u32[]{:S(2)}, u32[]{:S(2)}) collective-permute-start(bf16[256,1024]{1,0:T(8,128)(2,1)S(1)} %collective-permute-done.6.d_ref), channel_id=1, source_target_pairs={{0,16},{1,17},{2,18},{3,19},{4,20},{5,21},{6,22},{7,23},{8,24},{9,... | collective-permute-start | bytes 1572872 | tf_op jit(solution)/shard_map/ppermute | solution.py:444
  35.5 3.8 %shard_map.97 = (bf16[512,512]{1,0:T(8,128)(2,1)}, bf16[512,512]{1,0:T(8,128)(2,1)}, bf16[512,512]{1,0:T(8,128)(2,1)}) custom-call(bf16[512,512]{1,0:T(8,128)(2,1)S(1)} %get-tuple-element.36.q_ref, bf16[512,512]{1,0:T(8,128)(2,1)S(1)} %get-tuple-element.37.k_ref, bf16[512,512]{1,0:T(8,128)(2,1)S(1)} %get-tuple-element.38.v_ref, ...), custom_call_target="tpu_custom_call" | custom-call | flops 1073741824 | bytes 4194304 | tf_op jit(solution)/shard_map/pallas_call | solution.py:306
  39.2 0.0 collective-permute-done.14.dz_ref
  39.3 1.0 %collective-permute-done.10.a3_ref = bf16[512,512]{1,0:T(8,128)(2,1)S(1)} collective-permute-done((bf16[512,512]{1,0:T(8,128)(2,1)S(1)}, bf16[512,512]{1,0:T(8,128)(2,1)S(1)}, u32[]{:S(2)}, u32[]{:S(2)}) %collective-permute-start.10) | collective-permute-done | bytes 524320 | tf_op jit(solution)/shard_map/ppermute | solution.py:437
  40.3 0.0 collective-permute-done.11.o1_ref
  40.3 0.0 collective-permute-done.12.oz1_ref
  40.3 0.0 collective-permute-done.13.od_ref
  40.3 1.3 %collective-permute-start.15 = (bf16[256,1024]{1,0:T(8,128)(2,1)S(1)}, bf16[256,1024]{1,0:T(8,128)(2,1)S(1)}, u32[]{:S(2)}, u32[]{:S(2)}) collective-permute-start(bf16[256,1024]{1,0:T(8,128)(2,1)S(1)} %collective-permute-done.14.dz_ref), channel_id=1, source_target_pairs={{0,16},{1,17},{2,18},{3,19},{4,20},{5,21},{6,22},{7,23},{8,24},{9,... | collective-permute-start | bytes 1572872 | tf_op jit(solution)/shard_map/ppermute | solution.py:446
  41.6 1.5 %collective-permute-done.15.odz_ref = bf16[256,1024]{1,0:T(8,128)(2,1)S(1)} collective-permute-done((bf16[256,1024]{1,0:T(8,128)(2,1)S(1)}, bf16[256,1024]{1,0:T(8,128)(2,1)S(1)}, u32[]{:S(2)}, u32[]{:S(2)}) %collective-permute-start.15) | collective-permute-done | bytes 524320 | tf_op jit(solution)/shard_map/ppermute | solution.py:446
  43.1 3.2 %shard_map.98 = bf16[512,1024]{1,0:T(8,128)(2,1)} custom-call(s32[4]{0:T(128)S(1)} %pad_add_fusion.s_ref, f32[512,1024]{1,0:T(8,128)S(1)} %get-tuple-element.54.own_out_ref, bf16[512,512]{1,0:T(8,128)(2,1)S(1)} %collective-permute-done.7.a1_ref, bf16[512,512]{1,0:T(8,128)(2,1)S(1)} %collective-permute-done.8.a2_ref, ...), custom_call_target="tpu_custom_call" | custom-call | flops 1610612736 | bytes 4194304 | tf_op jit(solution)/shard_map/pallas_call | solution.py:344
Async XLA Ops:
  0.6 10.1 %collective-permute-start = (bf16[512,2048]{1,0:T(8,128)(2,1)}, bf16[512,2048]{1,0:T(8,128)(2,1)S(1)}, u32[]{:S(2)}, u32[]{:S(2)}) collective-permute-start(bf16[512,2048]{1,0:T(8,128)(2,1)} %own_ref.3), channel_id=1, source_target_pairs={{0,16},{16,0},{1,17},{17,1},{2,18},{18,2},{3,19},{19,3},{4,20},{20... | collective-permute-start | bytes 6291464 | tf_op jit(solution)/shard_map/ppermute | solution.py:368
  1.2 9.5 %copy-start = (bf16[512,4096]{1,0:T(8,128)(2,1)S(1)}, bf16[512,4096]{1,0:T(8,128)(2,1)}, u32[]{:S(2)}) copy-start(bf16[512,4096]{1,0:T(8,128)(2,1)} %grad_ref.3) | copy-start | bytes 12582916
  1.2 9.5 %copy-start.1 = (bf16[512,2048]{1,0:T(8,128)(2,1)S(1)}, bf16[512,2048]{1,0:T(8,128)(2,1)}, u32[]{:S(2)}) copy-start(bf16[512,2048]{1,0:T(8,128)(2,1)} %own_ref.3) | copy-start | bytes 6291460
  4.7 16.3 %collective-permute-start.3 = (bf16[512,2048]{1,0:T(8,128)(2,1)S(1)}, bf16[512,2048]{1,0:T(8,128)(2,1)S(1)}, u32[]{:S(2)}, u32[]{:S(2)}) collective-permute-start(bf16[512,2048]{1,0:T(8,128)(2,1)S(1)} %get-tuple-element.42), channel_id=1, source_target_pairs={{0,16},{16,0},{1,17},{17,1},{2,18},{18,2},{3,19},{19,3},{4,20},{20... | collective-permute-start | bytes 6291464 | tf_op jit(solution)/shard_map/ppermute | solution.py:399
  4.8 14.6 %collective-permute-start.2 = (bf16[256,1024]{1,0:T(8,128)(2,1)S(1)}, bf16[256,1024]{1,0:T(8,128)(2,1)S(1)}, u32[]{:S(2)}, u32[]{:S(2)}) collective-permute-start(bf16[256,1024]{1,0:T(8,128)(2,1)S(1)} %get-tuple-element.41), channel_id=1, source_target_pairs={{0,4},{4,0},{24,12},{28,8},{16,24},{20,28},{8,16},{12,20},{1,5},{5... | collective-permute-start | bytes 1572872 | tf_op jit(solution)/shard_map/ppermute | solution.py:397
  7.7 6.0 %collective-permute-start.1 = (bf16[512,128]{1,0:T(8,128)(2,1)S(1)}, bf16[512,128]{1,0:T(8,128)(2,1)S(1)}, u32[]{:S(2)}, u32[]{:S(2)}) collective-permute-start(bf16[512,128]{1,0:T(8,128)(2,1)S(1)} %get-tuple-element.34), channel_id=1, source_target_pairs={{0,16},{1,17},{2,18},{3,19},{4,20},{5,21},{6,22},{7,23},{8,24},{9,... | collective-permute-start | bytes 393224 | tf_op jit(solution)/shard_map/ppermute | solution.py:368
  9.4 14.0 %collective-permute-start.6 = (bf16[256,1024]{1,0:T(8,128)(2,1)S(1)}, bf16[256,1024]{1,0:T(8,128)(2,1)S(1)}, u32[]{:S(2)}, u32[]{:S(2)}) collective-permute-start(bf16[256,1024]{1,0:T(8,128)(2,1)S(1)} %get-tuple-element.49), channel_id=1, source_target_pairs={{16,12},{20,8},{8,4},{12,0},{17,13},{21,9},{9,5},{13,1},{18,14},{2... | collective-permute-start | bytes 1572872 | tf_op jit(solution)/shard_map/ppermute | solution.py:398
  15.2 9.5 %collective-permute-start.5 = (bf16[512,512]{1,0:T(8,128)(2,1)S(1)}, bf16[512,512]{1,0:T(8,128)(2,1)S(1)}, u32[]{:S(2)}, u32[]{:S(2)}) collective-permute-start(bf16[512,512]{1,0:T(8,128)(2,1)S(1)} %get-tuple-element.44.attn_ref), channel_id=1, source_target_pairs={{0,16},{16,0},{1,17},{17,1},{2,18},{18,2},{3,19},{19,3},{4,20},{20... | collective-permute-start | bytes 1572872 | tf_op jit(solution)/shard_map/ppermute | solution.py:368
  17.9 13.2 %collective-permute-start.7 = (bf16[512,512]{1,0:T(8,128)(2,1)S(1)}, bf16[512,512]{1,0:T(8,128)(2,1)S(1)}, u32[]{:S(2)}, u32[]{:S(2)}) collective-permute-start(bf16[512,512]{1,0:T(8,128)(2,1)S(1)} %get-tuple-element.44.attn_ref), channel_id=1, source_target_pairs={{0,4},{4,0},{8,12},{12,8},{16,24},{20,28},{24,16},{28,20},{1,5},{5... | collective-permute-start | bytes 1572872 | tf_op jit(solution)/shard_map/ppermute | solution.py:417
  19.4 13.6 %collective-permute-start.9 = (bf16[256,1024]{1,0:T(8,128)(2,1)S(1)}, bf16[256,1024]{1,0:T(8,128)(2,1)S(1)}, u32[]{:S(2)}, u32[]{:S(2)}) collective-permute-start(bf16[256,1024]{1,0:T(8,128)(2,1)S(1)} %collective-permute-done.2.m1_ref), channel_id=1, source_target_pairs={{0,1},{1,0},{2,3},{3,2},{4,5},{5,4},{6,7},{7,6},{8,9},{9,8},{10,11... | collective-permute-start | bytes 1572872 | tf_op jit(solution)/shard_map/ppermute | solution.py:419
  20.9 12.5 %collective-permute-start.8 = (bf16[512,512]{1,0:T(8,128)(2,1)S(1)}, bf16[512,512]{1,0:T(8,128)(2,1)S(1)}, u32[]{:S(2)}, u32[]{:S(2)}) collective-permute-start(bf16[512,512]{1,0:T(8,128)(2,1)S(1)} %get-tuple-element.44.attn_ref), channel_id=1, source_target_pairs={{0,8},{4,12},{8,0},{12,4},{16,20},{20,16},{24,28},{28,24},{1,9},{5... | collective-permute-start | bytes 1572872 | tf_op jit(solution)/shard_map/ppermute | solution.py:418
  23.4 9.5 %collective-permute-start.4 = (bf16[512,128]{1,0:T(8,128)(2,1)S(1)}, bf16[512,128]{1,0:T(8,128)(2,1)S(1)}, u32[]{:S(2)}, u32[]{:S(2)}) collective-permute-start(bf16[512,128]{1,0:T(8,128)(2,1)S(1)} %get-tuple-element.48), channel_id=1, source_target_pairs={{16,0},{17,1},{18,2},{19,3},{20,4},{21,5},{22,6},{23,7},{24,8},{25... | collective-permute-start | bytes 393224 | tf_op jit(solution)/shard_map/ppermute | solution.py:368
  24.7 14.5 %collective-permute-start.14 = (bf16[256,1024]{1,0:T(8,128)(2,1)S(1)}, bf16[256,1024]{1,0:T(8,128)(2,1)S(1)}, u32[]{:S(2)}, u32[]{:S(2)}) collective-permute-start(bf16[256,1024]{1,0:T(8,128)(2,1)S(1)} %collective-permute-done.6.d_ref), channel_id=1, source_target_pairs={{0,1},{1,0},{2,3},{3,2},{4,5},{5,4},{6,7},{7,6},{8,9},{9,8},{10,11... | collective-permute-start | bytes 1572872 | tf_op jit(solution)/shard_map/ppermute | solution.py:430
  31.1 9.2 %collective-permute-start.10 = (bf16[512,512]{1,0:T(8,128)(2,1)S(1)}, bf16[512,512]{1,0:T(8,128)(2,1)S(1)}, u32[]{:S(2)}, u32[]{:S(2)}) collective-permute-start(bf16[512,512]{1,0:T(8,128)(2,1)S(1)} %collective-permute-done.7.a1_ref), channel_id=1, source_target_pairs={{0,8},{4,12},{8,0},{12,4},{16,20},{20,16},{24,28},{28,24},{1,9},{5... | collective-permute-start | bytes 1572872 | tf_op jit(solution)/shard_map/ppermute | solution.py:437
  33.0 7.3 %collective-permute-start.11 = (bf16[256,1024]{1,0:T(8,128)(2,1)S(1)}, bf16[256,1024]{1,0:T(8,128)(2,1)S(1)}, u32[]{:S(2)}, u32[]{:S(2)}) collective-permute-start(bf16[256,1024]{1,0:T(8,128)(2,1)S(1)} %collective-permute-done.2.m1_ref), channel_id=1, source_target_pairs={{0,16},{16,0},{1,17},{17,1},{2,18},{18,2},{3,19},{19,3},{4,20},{20... | collective-permute-start | bytes 1572872 | tf_op jit(solution)/shard_map/ppermute | solution.py:436
  33.0 7.3 %collective-permute-start.12 = (bf16[256,1024]{1,0:T(8,128)(2,1)S(1)}, bf16[256,1024]{1,0:T(8,128)(2,1)S(1)}, u32[]{:S(2)}, u32[]{:S(2)}) collective-permute-start(bf16[256,1024]{1,0:T(8,128)(2,1)S(1)} %collective-permute-done.9.z1_ref), channel_id=1, source_target_pairs={{0,16},{16,0},{1,17},{17,1},{2,18},{18,2},{3,19},{19,3},{4,20},{20... | collective-permute-start | bytes 1572872 | tf_op jit(solution)/shard_map/ppermute | solution.py:438
  33.5 6.8 %collective-permute-start.13 = (bf16[256,1024]{1,0:T(8,128)(2,1)S(1)}, bf16[256,1024]{1,0:T(8,128)(2,1)S(1)}, u32[]{:S(2)}, u32[]{:S(2)}) collective-permute-start(bf16[256,1024]{1,0:T(8,128)(2,1)S(1)} %collective-permute-done.6.d_ref), channel_id=1, source_target_pairs={{0,16},{1,17},{2,18},{3,19},{4,20},{5,21},{6,22},{7,23},{8,24},{9,... | collective-permute-start | bytes 1572872 | tf_op jit(solution)/shard_map/ppermute | solution.py:444
  40.3 2.8 %collective-permute-start.15 = (bf16[256,1024]{1,0:T(8,128)(2,1)S(1)}, bf16[256,1024]{1,0:T(8,128)(2,1)S(1)}, u32[]{:S(2)}, u32[]{:S(2)}) collective-permute-start(bf16[256,1024]{1,0:T(8,128)(2,1)S(1)} %collective-permute-done.14.dz_ref), channel_id=1, source_target_pairs={{0,16},{1,17},{2,18},{3,19},{4,20},{5,21},{6,22},{7,23},{8,24},{9,... | collective-permute-start | bytes 1572872 | tf_op jit(solution)/shard_map/ppermute | solution.py:446

commit v4 on v3

--- a/solution.py
+++ b/solution.py
@@ -317,19 +317,33 @@
     return first, second
 
 
-def project_kernel(s_ref, own_out_ref, a1_ref, a2_ref, a3_ref, m1_ref, z1_ref, o1_ref, oz1_ref,
-                   d_ref, od_ref, dz_ref, odz_ref, out_hbm, out_buf, sems):
+def project_near_kernel(s_ref, so_far_ref, a1_ref, a2_ref, m1_ref, z1_ref, o1_ref, oz1_ref, out_ref):
+    first, second = halves(s_ref, m1_ref.shape[0])
+    acc = so_far_ref[...] + dot_nn(a1_ref[:, first], m1_ref[...])
+    acc += dot_nn(a1_ref[:, second], z1_ref[...])
+    acc += dot_nn(a2_ref[:, first], o1_ref[...])
+    acc += dot_nn(a2_ref[:, second], oz1_ref[...])
+    out_ref[...] = acc
+
+
+def project_near(scal, so_far, attns, pieces):
+    return pl.pallas_call(
+        project_near_kernel,
+        out_shape=shape_of(so_far.shape, F32),
+        in_specs=smem_then_vmem(7),
+        compiler_params=params(16),
+        cost_estimate=cost(1000, 1000),
+    )(scal, so_far, *attns, *pieces)
+
+
+def project_far_kernel(s_ref, near_ref, a_ref, d_ref, od_ref, dz_ref, odz_ref, out_hbm, out_buf, sems):
     first, second = halves(s_ref, d_ref.shape[0])
     blocks, _, block = out_buf.shape
     moves = []
     for j in range(blocks):
         here = slice(j * block, (j + 1) * block)
-        acc = own_out_ref[:, here] + dot_nn(a1_ref[:, first], m1_ref[:, here])
-        acc += dot_nn(a1_ref[:, second], z1_ref[:, here])
-        acc += dot_nn(a2_ref[:, first], o1_ref[:, here])
-        acc += dot_nn(a2_ref[:, second], oz1_ref[:, here])
-        acc += dot_nn(a3_ref[:, first], d_ref[:, here] + od_ref[:, here])
-        acc += dot_nn(a3_ref[:, second], dz_ref[:, here] + odz_ref[:, here])
+        acc = near_ref[:, here] + dot_nn(a_ref[:, first], d_ref[:, here] + od_ref[:, here])
+        acc += dot_nn(a_ref[:, second], dz_ref[:, here] + odz_ref[:, here])
         out_buf[j] = acc.astype(BF16)
         moves.append(pltpu.make_async_copy(out_buf.at[j], out_hbm.at[:, here], sems.at[j]))
         moves[-1].start()
@@ -337,22 +351,21 @@
         move.wait()
 
 
-def project(scal, own_out, attns, pieces):
-    tok, width = attns[0].shape
-    out_width = own_out.shape[1]
+def project_far(scal, near, attn, pieces):
+    tok, out_width = near.shape
     block = 256
     return pl.pallas_call(
-        project_kernel,
+        project_far_kernel,
         out_shape=shape_of((tok, out_width), BF16),
-        in_specs=smem_then_vmem(12),
+        in_specs=smem_then_vmem(6),
         out_specs=pl.BlockSpec(memory_space=pl.ANY),
         scratch_shapes=[
             pltpu.VMEM((out_width // block, tok, block), BF16),
             pltpu.SemaphoreType.DMA((out_width // block,)),
         ],
         compiler_params=params(16),
-        cost_estimate=cost(6 * tok * width * out_width, 8 * width * out_width),
-    )(scal, own_out, *attns, *pieces)
+        cost_estimate=cost(1000, 1000),
+    )(scal, near, attn, *pieces)
 
 
 def in_hbm(array):
@@ -395,7 +408,6 @@
             scal, in_hbm(queries), in_hbm(keys), in_hbm(values), weight_hbm, grad_hbm
         )
         near_mine = lax.ppermute(near_piece, group, near)
-        far_mine = lax.ppermute(far_piece, group, far)
         other_grad = lax.ppermute(turn, "ctx", swap)
     else:
         state = local_state(keys, values)
@@ -414,6 +426,7 @@
     attn, raw, prefix = forward(queries, keys, values, carried)
 
     if paired:
+        far_mine = lax.ppermute(after(far_piece, attn), group, far)
         attn_1 = lax.ppermute(attn, group, one)
         attn_2 = lax.ppermute(attn, group, two)
         near_z = lax.ppermute(near_mine, "rep", zpair)
@@ -427,12 +440,12 @@
     suffix = total([shift(gsum, "ctx", n_ctx, -k, False) for k in range(1, n_ctx)])
 
     if paired:
-        far_z = lax.ppermute(after(far_mine, gsum), ("ctx", "rep"), zpair)
-        other_attn = after(other_attn, gsum, far_mine)
+        other_attn = after(other_attn, gsum)
 
     weight_grad = own_weight_grad(scal, attn, out_grad, other_attn, other_grad)
 
     if paired:
+        far_z = lax.ppermute(after(far_mine, weight_grad), ("ctx", "rep"), zpair)
         near_other = lax.ppermute(after(near_mine, weight_grad), "ctx", swap)
         attn_3 = lax.ppermute(after(attn_1, weight_grad), group, two)
         near_other_z = lax.ppermute(after(near_z, weight_grad), "ctx", swap)
@@ -442,12 +455,13 @@
 
     if paired:
         far_other = lax.ppermute(after(far_mine, weight_grad), "ctx", [(0, 1)])
-        last = after(far_z, query_grad, attn_3, near_other_z, near_other, far_other)
+        near_out = project_near(
+            scal, after(own_out, query_grad), (attn_1, attn_2),
+            (near_mine, near_z, near_other, near_other_z),
+        )
+        last = after(far_z, near_out, attn_3, far_other)
         far_other_z = lax.ppermute(last, "ctx", [(0, 1)])
-        layer_out = project(
-            scal, after(own_out, query_grad), (attn_1, attn_2, attn_3),
-            (near_mine, near_z, near_other, near_other_z, far_mine, far_other, far_z, far_other_z),
-        )
+        layer_out = project_far(scal, near_out, attn_3, (far_mine, far_other, far_z, far_other_z))
     else:
         full = lax.all_gather(out_weight, "ctx", axis=1, tiled=True)
         partial_out = jnp.dot(attn, full, preferred_element_type=F32).astype(BF16)

time: 46.8 us -> 58.1 us (1.24)
  waiting for transfers between devices: 2.68 us -> 14.5 us
  starting transfers between devices: 21.7 us -> 20.5 us
  Pallas kernels: 21.1 us -> 21.7 us
    ppermute x2, waiting for transfers between devices: 0.01 us -> 12.2 us  [the longest x1 9.07 us: body(): far_mine = lax.ppermute(after(far_piece, attn), group, far)]
    ppermute x4, starting transfers between devices: 6.14 us -> 3.6 us  [shift(): return lax.ppermute(array, axis, pairs)]
    ppermute x1, starting transfers between devices: 0.14 us -> 2.68 us  [body(): attn_2 = lax.ppermute(attn, group, two)]
    ppermute x1, starting transfers between devices: 1.84 us -> 0.01 us  [body(): attn_3 = lax.ppermute(after(attn_1, weight_grad), group, two)]
    ppermute x1, starting transfers between devices: 0.01 us -> 1.19 us  [body(): near_other = lax.ppermute(after(near_mine, weight_grad), 'ctx', swap)]
    ppermute x1, waiting for transfers between devices: 1.02 us -> 0.01 us  [body(): attn_3 = lax.ppermute(after(attn_1, weight_grad), group, two)]
    ppermute x1, waiting for transfers between devices: 0.01 us -> 0.85 us  [body(): near_mine = lax.ppermute(near_piece, group, near)]
    pallas_call x1 -> x2, Pallas kernels: 3.21 us -> 3.9 us  [the longest x1 2.11 us: project_far(): pl.pallas_call(project_far_kernel, out_shape=shape_of((tok, out_width), B...]
  transfers between devices with their start and end apart: 16 -> 16, of which waited for: 3 -> 4; matrix products, arithmetic and copies ran while one was open for 0% -> 0% of each run, Pallas kernels for 39% -> 34%
where the time goes in v4:
time: 58.1 us; the launch traced here: 57.8 us
  Pallas kernels  21.7 us (37%)
  starting transfers between devices  20.5 us (35%)
  waiting for transfers between devices  14.5 us (25%)
  between operations  0.98 us (2%)
    ppermute x1, waiting for transfers between devices, body(): far_mine = lax.ppermute(after(far_piece, attn), group, far)  9.07 us
    pallas_call x1, Pallas kernels, own_weight_grad(): pl.pallas_call(weight_grad_kernel, out_shape=shape_of((width, own_width),...  3.89 us
    pallas_call x1, Pallas kernels, backward(): pl.pallas_call(backward_kernel, out_shape=(out, out, out), compiler_param...  3.78 us
    ppermute x4, starting transfers between devices, shift(): return lax.ppermute(array, axis, pairs)  3.6 us
    pallas_call x1, Pallas kernels, opening(): pl.pallas_call(opening_kernel, out_shape=(shape_of((width, DH), BF16), pi...  3.42 us
    ppermute x1, waiting for transfers between devices, body(): far_z = lax.ppermute(after(far_mine, weight_grad), ('ctx', 'rep'), zpair)  3.1 us
    ppermute x1, starting transfers between devices, body(): near_mine = lax.ppermute(near_piece, group, near)  2.94 us
    pallas_call x1, Pallas kernels, attn_gradient(): pl.pallas_call(attn_grad_kernel, out_shape=shape_of((tok, width), BF16),...  2.9 us
  transfers between devices with their start and end apart: 16, of which 4 were waited for; matrix products, arithmetic and copies ran while one was open for 0% of the time, Pallas kernels for 34%

profile of v4, /device:TPU:0, one launch (start us, length us, event | category | flops | bytes accessed | tf_op | source)
XLA Modules:
  0.0 57.8 jit_solution(16135974308455446729)
XLA Ops:
  0.6 0.5 collective-permute-start
  1.1 0.1 pad_add_fusion.s_ref
  1.2 0.0 copy-start
  1.2 0.0 copy-start.1
  1.2 3.4 %shard_map.92 = (bf16[512,128]{1,0:T(8,128)(2,1)S(1)}, bf16[256,1024]{1,0:T(8,128)(2,1)S(1)}, bf16[256,1024]{1,0:T(8,128)(2,1)S(1)}, bf16[512,2048]{1,0:T(8,128)...) custom-call(s32[4]{0:T(128)S(1)} %pad_add_fusion.s_ref, ...), custom_call_target="tpu_custom_call" | custom-call | flops 67108864 | bytes 1048576 | tf_op jit(solution)/shard_map/pallas_call | solution.py:103
  4.7 0.1 collective-permute-start.3
  4.8 2.9 %collective-permute-start.2 = (bf16[256,1024]{1,0:T(8,128)(2,1)S(1)}, bf16[256,1024]{1,0:T(8,128)(2,1)S(1)}, u32[]{:S(2)}, u32[]{:S(2)}) collective-permute-start(bf16[256,1024]{1,0:T(8,128)(2,1)S(1)} %get-tuple-element.41), channel_id=1, source_target_pairs={{0,4},{4,0},{24,12},{28,8},{16,24},{20,28},{8,16},{12,20},{1,5},{5... | collective-permute-start | bytes 1572872 | tf_op jit(solution)/shard_map/ppermute | solution.py:410
  7.7 1.7 %collective-permute-start.1 = (bf16[512,128]{1,0:T(8,128)(2,1)S(1)}, bf16[512,128]{1,0:T(8,128)(2,1)S(1)}, u32[]{:S(2)}, u32[]{:S(2)}) collective-permute-start(bf16[512,128]{1,0:T(8,128)(2,1)S(1)} %get-tuple-element.34), channel_id=1, source_target_pairs={{0,16},{1,17},{2,18},{3,19},{4,20},{5,21},{6,22},{7,23},{8,24},{9,... | collective-permute-start | bytes 393224 | tf_op jit(solution)/shard_map/ppermute | solution.py:381
  9.4 0.0 collective-permute-done.rest_ref
  9.4 0.0 copy-done
  9.5 0.0 copy-done.1
  9.5 2.9 %shard_map.93.attn_grad_ref = bf16[512,512]{1,0:T(8,128)(2,1)S(1)} custom-call(s32[4]{0:T(128)S(1)} %pad_add_fusion.s_ref, bf16[512,2048]{1,0:T(8,128)(2,1)S(1)} %copy-done.1, bf16[512,4096]{1,0:T(8,128)(2,1)S(1)} %copy-done, bf16[512,2048]{1,0:T(8,128)(2,1)S(1)} %collective-permute-done.rest_ref), custom_call_target="tpu_custom_call" | custom-call | flops 2147483648 | bytes 8388608 | tf_op jit(solution)/shard_map/pallas_call | solution.py:178
  12.4 0.0 collective-permute-done.1.carried_ref
  12.4 1.5 %shard_map.94 = (bf16[512,512]{1,0:T(8,128)(2,1)S(1)}, f32[512,512]{1,0:T(8,128)S(1)}, bf16[2,512,128]{2,1,0:T(8,128)(2,1)S(1)}) custom-call(bf16[512,512]{1,0:T(8,128)(2,1)S(1)} %get-tuple-element.36.q_ref, bf16[512,512]{1,0:T(8,128)(2,1)S(1)} %get-tuple-element.37.k_ref, bf16[512,512]{1,0:T(8,128)(2,1)S(1)} %get-tuple-element.38.v_ref, ...), custom_call_target="tpu_custom_call" | custom-call | flops 536870912 | bytes 3145728 | tf_op jit(solution)/shard_map/pallas_call | solution.py:146
  13.9 0.1 collective-permute-start.5
  14.0 0.9 %collective-permute-done.2.m1_ref = bf16[256,1024]{1,0:T(8,128)(2,1)S(1)} collective-permute-done((bf16[256,1024]{1,0:T(8,128)(2,1)S(1)}, bf16[256,1024]{1,0:T(8,128)(2,1)S(1)}, u32[]{:S(2)}, u32[]{:S(2)}) %collective-permute-start.2) | collective-permute-done | bytes 524320 | tf_op jit(solution)/shard_map/ppermute | solution.py:410
  14.9 2.1 %collective-permute-start.8 = (bf16[256,1024]{1,0:T(8,128)(2,1)S(1)}, bf16[256,1024]{1,0:T(8,128)(2,1)S(1)}, u32[]{:S(2)}, u32[]{:S(2)}) collective-permute-start(bf16[256,1024]{1,0:T(8,128)(2,1)S(1)} %collective-permute-done.2.m1_ref), channel_id=1, source_target_pairs={{0,1},{1,0},{2,3},{3,2},{4,5},{5,4},{6,7},{7,6},{8,9},{9,8},{10,11... | collective-permute-start | bytes 1572872 | tf_op jit(solution)/shard_map/ppermute | solution.py:432
  17.0 1.5 %collective-permute-start.6 = (bf16[512,512]{1,0:T(8,128)(2,1)S(1)}, bf16[512,512]{1,0:T(8,128)(2,1)S(1)}, u32[]{:S(2)}, u32[]{:S(2)}) collective-permute-start(bf16[512,512]{1,0:T(8,128)(2,1)S(1)} %get-tuple-element.44.attn_ref), channel_id=1, source_target_pairs={{0,4},{4,0},{8,12},{12,8},{16,24},{20,28},{24,16},{28,20},{1,5},{5... | collective-permute-start | bytes 1572872 | tf_op jit(solution)/shard_map/ppermute | solution.py:430
  18.5 1.3 %collective-permute-start.12 = (bf16[256,1024]{1,0:T(8,128)(2,1)S(1)}, bf16[256,1024]{1,0:T(8,128)(2,1)S(1)}, u32[]{:S(2)}, u32[]{:S(2)}) collective-permute-start(bf16[256,1024]{1,0:T(8,128)(2,1)S(1)} %get-tuple-element.58), channel_id=1, source_target_pairs={{16,12},{20,8},{8,4},{12,0},{17,13},{21,9},{9,5},{13,1},{18,14},{2... | collective-permute-start | bytes 1572872 | tf_op jit(solution)/shard_map/ppermute | solution.py:429
  19.8 0.0 collective-permute-done.3.other_grad_ref
  19.8 2.7 %collective-permute-start.7 = (bf16[512,512]{1,0:T(8,128)(2,1)S(1)}, bf16[512,512]{1,0:T(8,128)(2,1)S(1)}, u32[]{:S(2)}, u32[]{:S(2)}) collective-permute-start(bf16[512,512]{1,0:T(8,128)(2,1)S(1)} %get-tuple-element.44.attn_ref), channel_id=1, source_target_pairs={{0,8},{4,12},{8,0},{12,4},{16,20},{20,16},{24,28},{28,24},{1,9},{5... | collective-permute-start | bytes 1572872 | tf_op jit(solution)/shard_map/ppermute | solution.py:431
  22.5 2.3 %shard_map.95 = (bf16[512,512]{1,0:T(8,128)(2,1)S(1)}, bf16[512,128]{1,0:T(8,128)(2,1)S(1)}, f32[2,512,128]{2,1,0:T(8,128)S(1)}, f32[512,1024]{1,0:T(8,128)S(1)}) custom-call(s32[4]{0:T(128)S(1)} %pad_add_fusion.s_ref, bf16[512,512]{1,0:T(8,128)(2,1)S(1)} %shard_map.93.attn_grad_ref, bf16[512,512]{1,0:T(8,128)(2,1)S(1)} %get-tuple-element.36.q_ref, ...), custom_call_target="tpu_custom_call" | custom-call | flops 536870912 | bytes 4194304 | tf_op jit(solution)/shard_map/pallas_call | solution.py:218
  24.8 0.0 collective-permute-done.5.other_ref
  24.8 1.3 %collective-permute-start.4 = (bf16[512,128]{1,0:T(8,128)(2,1)S(1)}, bf16[512,128]{1,0:T(8,128)(2,1)S(1)}, u32[]{:S(2)}, u32[]{:S(2)}) collective-permute-start(bf16[512,128]{1,0:T(8,128)(2,1)S(1)} %get-tuple-element.48), channel_id=1, source_target_pairs={{16,0},{17,1},{18,2},{19,3},{20,4},{21,5},{22,6},{23,7},{24,8},{25... | collective-permute-start | bytes 393224 | tf_op jit(solution)/shard_map/ppermute | solution.py:381
  26.1 3.9 %shard_map.96 = f32[512,2048]{1,0:T(8,128)} custom-call(s32[4]{0:T(128)S(1)} %pad_add_fusion.s_ref, bf16[512,512]{1,0:T(8,128)(2,1)S(1)} %get-tuple-element.44.attn_ref, bf16[512,4096]{1,0:T(8,128)(2,1)S(1)} %copy-done, bf16[512,512]{1,0:T(8,128)(2,1)S(1)} %collective-permute-done.5.other_ref, bf16[512,2048]{1,0:T(8,128)(2,1)S(1)} %collective-permute-done.3.other_grad_ref), custom_call_target="tpu_custom_call" | custom-call | flops 2147483648 | bytes 8388608 | tf_op jit(solution)/shard_map/pallas_call | solution.py:257
  30.0 0.0 collective-permute-done.8.z1_ref
  30.0 1.2 %collective-permute-start.9 = (bf16[256,1024]{1,0:T(8,128)(2,1)S(1)}, bf16[256,1024]{1,0:T(8,128)(2,1)S(1)}, u32[]{:S(2)}, u32[]{:S(2)}) collective-permute-start(bf16[256,1024]{1,0:T(8,128)(2,1)S(1)} %collective-permute-done.2.m1_ref), channel_id=1, source_target_pairs={{0,16},{16,0},{1,17},{17,1},{2,18},{18,2},{3,19},{19,3},{4,20},{20... | collective-permute-start | bytes 1572872 | tf_op jit(solution)/shard_map/ppermute | solution.py:449
  31.2 0.0 collective-permute-done.6.a1_ref
  31.2 0.1 collective-permute-start.10
  31.3 9.1 %collective-permute-done.12.d_ref = bf16[256,1024]{1,0:T(8,128)(2,1)S(1)} collective-permute-done((bf16[256,1024]{1,0:T(8,128)(2,1)S(1)}, bf16[256,1024]{1,0:T(8,128)(2,1)S(1)}, u32[]{:S(2)}, u32[]{:S(2)}) %collective-permute-start.12) | collective-permute-done | bytes 524320 | tf_op jit(solution)/shard_map/ppermute | solution.py:429
  40.3 0.0 collective-permute-start.11
  40.3 0.0 collective-permute-done.4.suffix_ref
  40.3 1.3 %collective-permute-start.13 = (bf16[256,1024]{1,0:T(8,128)(2,1)S(1)}, bf16[256,1024]{1,0:T(8,128)(2,1)S(1)}, u32[]{:S(2)}, u32[]{:S(2)}) collective-permute-start(bf16[256,1024]{1,0:T(8,128)(2,1)S(1)} %collective-permute-done.12.d_ref), channel_id=1, source_target_pairs={{0,16},{1,17},{2,18},{3,19},{4,20},{5,21},{6,22},{7,23},{8,24},{9,... | collective-permute-start | bytes 1572872 | tf_op jit(solution)/shard_map/ppermute | solution.py:457
  41.7 0.0 collective-permute-done.7.a2_ref
  41.7 2.4 %collective-permute-start.14 = (bf16[256,1024]{1,0:T(8,128)(2,1)S(1)}, bf16[256,1024]{1,0:T(8,128)(2,1)S(1)}, u32[]{:S(2)}, u32[]{:S(2)}) collective-permute-start(bf16[256,1024]{1,0:T(8,128)(2,1)S(1)} %collective-permute-done.12.d_ref), channel_id=1, source_target_pairs={{0,1},{1,0},{2,3},{3,2},{4,5},{5,4},{6,7},{7,6},{8,9},{9,8},{10,11... | collective-permute-start | bytes 1572872 | tf_op jit(solution)/shard_map/ppermute | solution.py:448
  44.0 3.8 %shard_map.97 = (bf16[512,512]{1,0:T(8,128)(2,1)}, bf16[512,512]{1,0:T(8,128)(2,1)}, bf16[512,512]{1,0:T(8,128)(2,1)}) custom-call(bf16[512,512]{1,0:T(8,128)(2,1)S(1)} %get-tuple-element.36.q_ref, bf16[512,512]{1,0:T(8,128)(2,1)S(1)} %get-tuple-element.37.k_ref, bf16[512,512]{1,0:T(8,128)(2,1)S(1)} %get-tuple-element.38.v_ref, ...), custom_call_target="tpu_custom_call" | custom-call | flops 1073741824 | bytes 4194304 | tf_op jit(solution)/shard_map/pallas_call | solution.py:306
  47.8 0.0 collective-permute-done.9.o1_ref
  47.8 0.0 collective-permute-done.10.oz1_ref
  47.8 1.8 %shard_map.98.near_ref = f32[512,1024]{1,0:T(8,128)S(1)} custom-call(s32[4]{0:T(128)S(1)} %pad_add_fusion.s_ref, f32[512,1024]{1,0:T(8,128)S(1)} %get-tuple-element.53.so_far_ref, bf16[512,512]{1,0:T(8,128)(2,1)S(1)} %collective-permute-done.6.a1_ref, bf16[512,512]{1,0:T(8,128)(2,1)S(1)} %collective-permute-done.7.a2_ref, ...), custom_call_target="tpu_custom_call" | custom-call | flops 1000 | bytes 1000 | tf_op jit(solution)/shard_map/pallas_call | solution.py:330
  49.6 0.0 collective-permute-done.11.a_ref
  49.6 0.0 collective-permute-done.13.od_ref
  49.6 3.1 %collective-permute-done.14.dz_ref = bf16[256,1024]{1,0:T(8,128)(2,1)S(1)} collective-permute-done((bf16[256,1024]{1,0:T(8,128)(2,1)S(1)}, bf16[256,1024]{1,0:T(8,128)(2,1)S(1)}, u32[]{:S(2)}, u32[]{:S(2)}) %collective-permute-start.14) | collective-permute-done | bytes 524320 | tf_op jit(solution)/shard_map/ppermute | solution.py:448
  52.7 1.3 %collective-permute-start.15 = (bf16[256,1024]{1,0:T(8,128)(2,1)S(1)}, bf16[256,1024]{1,0:T(8,128)(2,1)S(1)}, u32[]{:S(2)}, u32[]{:S(2)}) collective-permute-start(bf16[256,1024]{1,0:T(8,128)(2,1)S(1)} %collective-permute-done.14.dz_ref), channel_id=1, source_target_pairs={{0,16},{1,17},{2,18},{3,19},{4,20},{5,21},{6,22},{7,23},{8,24},{9,... | collective-permute-start | bytes 1572872 | tf_op jit(solution)/shard_map/ppermute | solution.py:463
  54.1 1.5 %collective-permute-done.15.odz_ref = bf16[256,1024]{1,0:T(8,128)(2,1)S(1)} collective-permute-done((bf16[256,1024]{1,0:T(8,128)(2,1)S(1)}, bf16[256,1024]{1,0:T(8,128)(2,1)S(1)}, u32[]{:S(2)}, u32[]{:S(2)}) %collective-permute-start.15) | collective-permute-done | bytes 524320 | tf_op jit(solution)/shard_map/ppermute | solution.py:463
  55.5 2.1 %shard_map.99 = bf16[512,1024]{1,0:T(8,128)(2,1)} custom-call(s32[4]{0:T(128)S(1)} %pad_add_fusion.s_ref, f32[512,1024]{1,0:T(8,128)S(1)} %shard_map.98.near_ref, bf16[512,512]{1,0:T(8,128)(2,1)S(1)} %collective-permute-done.11.a_ref, bf16[256,1024]{1,0:T(8,128)(2,1)S(1)} %collective-permute-done.12.d_ref, ...), custom_call_target="tpu_custom_call" | custom-call | flops 1000 | bytes 1000 | tf_op jit(solution)/shard_map/pallas_call | solution.py:357
Async XLA Ops:
  0.6 8.8 %collective-permute-start = (bf16[512,2048]{1,0:T(8,128)(2,1)}, bf16[512,2048]{1,0:T(8,128)(2,1)S(1)}, u32[]{:S(2)}, u32[]{:S(2)}) collective-permute-start(bf16[512,2048]{1,0:T(8,128)(2,1)} %own_ref.3), channel_id=1, source_target_pairs={{0,16},{16,0},{1,17},{17,1},{2,18},{18,2},{3,19},{19,3},{4,20},{20... | collective-permute-start | bytes 6291464 | tf_op jit(solution)/shard_map/ppermute | solution.py:381
  1.2 8.2 %copy-start = (bf16[512,4096]{1,0:T(8,128)(2,1)S(1)}, bf16[512,4096]{1,0:T(8,128)(2,1)}, u32[]{:S(2)}) copy-start(bf16[512,4096]{1,0:T(8,128)(2,1)} %grad_ref.3) | copy-start | bytes 12582916
  1.2 8.2 %copy-start.1 = (bf16[512,2048]{1,0:T(8,128)(2,1)S(1)}, bf16[512,2048]{1,0:T(8,128)(2,1)}, u32[]{:S(2)}) copy-start(bf16[512,2048]{1,0:T(8,128)(2,1)} %own_ref.3) | copy-start | bytes 6291460
  4.7 15.1 %collective-permute-start.3 = (bf16[512,2048]{1,0:T(8,128)(2,1)S(1)}, bf16[512,2048]{1,0:T(8,128)(2,1)S(1)}, u32[]{:S(2)}, u32[]{:S(2)}) collective-permute-start(bf16[512,2048]{1,0:T(8,128)(2,1)S(1)} %get-tuple-element.42), channel_id=1, source_target_pairs={{0,16},{16,0},{1,17},{17,1},{2,18},{18,2},{3,19},{19,3},{4,20},{20... | collective-permute-start | bytes 6291464 | tf_op jit(solution)/shard_map/ppermute | solution.py:411
  4.8 10.1 %collective-permute-start.2 = (bf16[256,1024]{1,0:T(8,128)(2,1)S(1)}, bf16[256,1024]{1,0:T(8,128)(2,1)S(1)}, u32[]{:S(2)}, u32[]{:S(2)}) collective-permute-start(bf16[256,1024]{1,0:T(8,128)(2,1)S(1)} %get-tuple-element.41), channel_id=1, source_target_pairs={{0,4},{4,0},{24,12},{28,8},{16,24},{20,28},{8,16},{12,20},{1,5},{5... | collective-permute-start | bytes 1572872 | tf_op jit(solution)/shard_map/ppermute | solution.py:410
  7.7 4.7 %collective-permute-start.1 = (bf16[512,128]{1,0:T(8,128)(2,1)S(1)}, bf16[512,128]{1,0:T(8,128)(2,1)S(1)}, u32[]{:S(2)}, u32[]{:S(2)}) collective-permute-start(bf16[512,128]{1,0:T(8,128)(2,1)S(1)} %get-tuple-element.34), channel_id=1, source_target_pairs={{0,16},{1,17},{2,18},{3,19},{4,20},{5,21},{6,22},{7,23},{8,24},{9,... | collective-permute-start | bytes 393224 | tf_op jit(solution)/shard_map/ppermute | solution.py:381
  13.9 10.8 %collective-permute-start.5 = (bf16[512,512]{1,0:T(8,128)(2,1)S(1)}, bf16[512,512]{1,0:T(8,128)(2,1)S(1)}, u32[]{:S(2)}, u32[]{:S(2)}) collective-permute-start(bf16[512,512]{1,0:T(8,128)(2,1)S(1)} %get-tuple-element.44.attn_ref), channel_id=1, source_target_pairs={{0,16},{16,0},{1,17},{17,1},{2,18},{18,2},{3,19},{19,3},{4,20},{20... | collective-permute-start | bytes 1572872 | tf_op jit(solution)/shard_map/ppermute | solution.py:381
  14.9 15.1 %collective-permute-start.8 = (bf16[256,1024]{1,0:T(8,128)(2,1)S(1)}, bf16[256,1024]{1,0:T(8,128)(2,1)S(1)}, u32[]{:S(2)}, u32[]{:S(2)}) collective-permute-start(bf16[256,1024]{1,0:T(8,128)(2,1)S(1)} %collective-permute-done.2.m1_ref), channel_id=1, source_target_pairs={{0,1},{1,0},{2,3},{3,2},{4,5},{5,4},{6,7},{7,6},{8,9},{9,8},{10,11... | collective-permute-start | bytes 1572872 | tf_op jit(solution)/shard_map/ppermute | solution.py:432
  17.0 14.2 %collective-permute-start.6 = (bf16[512,512]{1,0:T(8,128)(2,1)S(1)}, bf16[512,512]{1,0:T(8,128)(2,1)S(1)}, u32[]{:S(2)}, u32[]{:S(2)}) collective-permute-start(bf16[512,512]{1,0:T(8,128)(2,1)S(1)} %get-tuple-element.44.attn_ref), channel_id=1, source_target_pairs={{0,4},{4,0},{8,12},{12,8},{16,24},{20,28},{24,16},{28,20},{1,5},{5... | collective-permute-start | bytes 1572872 | tf_op jit(solution)/shard_map/ppermute | solution.py:430
  18.5 21.9 %collective-permute-start.12 = (bf16[256,1024]{1,0:T(8,128)(2,1)S(1)}, bf16[256,1024]{1,0:T(8,128)(2,1)S(1)}, u32[]{:S(2)}, u32[]{:S(2)}) collective-permute-start(bf16[256,1024]{1,0:T(8,128)(2,1)S(1)} %get-tuple-element.58), channel_id=1, source_target_pairs={{16,12},{20,8},{8,4},{12,0},{17,13},{21,9},{9,5},{13,1},{18,14},{2... | collective-permute-start | bytes 1572872 | tf_op jit(solution)/shard_map/ppermute | solution.py:429
  19.8 21.9 %collective-permute-start.7 = (bf16[512,512]{1,0:T(8,128)(2,1)S(1)}, bf16[512,512]{1,0:T(8,128)(2,1)S(1)}, u32[]{:S(2)}, u32[]{:S(2)}) collective-permute-start(bf16[512,512]{1,0:T(8,128)(2,1)S(1)} %get-tuple-element.44.attn_ref), channel_id=1, source_target_pairs={{0,8},{4,12},{8,0},{12,4},{16,20},{20,16},{24,28},{28,24},{1,9},{5... | collective-permute-start | bytes 1572872 | tf_op jit(solution)/shard_map/ppermute | solution.py:431
  24.8 15.6 %collective-permute-start.4 = (bf16[512,128]{1,0:T(8,128)(2,1)S(1)}, bf16[512,128]{1,0:T(8,128)(2,1)S(1)}, u32[]{:S(2)}, u32[]{:S(2)}) collective-permute-start(bf16[512,128]{1,0:T(8,128)(2,1)S(1)} %get-tuple-element.48), channel_id=1, source_target_pairs={{16,0},{17,1},{18,2},{19,3},{20,4},{21,5},{22,6},{23,7},{24,8},{25... | collective-permute-start | bytes 393224 | tf_op jit(solution)/shard_map/ppermute | solution.py:381
  30.0 17.9 %collective-permute-start.9 = (bf16[256,1024]{1,0:T(8,128)(2,1)S(1)}, bf16[256,1024]{1,0:T(8,128)(2,1)S(1)}, u32[]{:S(2)}, u32[]{:S(2)}) collective-permute-start(bf16[256,1024]{1,0:T(8,128)(2,1)S(1)} %collective-permute-done.2.m1_ref), channel_id=1, source_target_pairs={{0,16},{16,0},{1,17},{17,1},{2,18},{18,2},{3,19},{19,3},{4,20},{20... | collective-permute-start | bytes 1572872 | tf_op jit(solution)/shard_map/ppermute | solution.py:449
  31.2 16.7 %collective-permute-start.10 = (bf16[256,1024]{1,0:T(8,128)(2,1)S(1)}, bf16[256,1024]{1,0:T(8,128)(2,1)S(1)}, u32[]{:S(2)}, u32[]{:S(2)}) collective-permute-start(bf16[256,1024]{1,0:T(8,128)(2,1)S(1)} %collective-permute-done.8.z1_ref), channel_id=1, source_target_pairs={{0,16},{16,0},{1,17},{17,1},{2,18},{18,2},{3,19},{19,3},{4,20},{20... | collective-permute-start | bytes 1572872 | tf_op jit(solution)/shard_map/ppermute | solution.py:451
  40.3 9.3 %collective-permute-start.11 = (bf16[512,512]{1,0:T(8,128)(2,1)S(1)}, bf16[512,512]{1,0:T(8,128)(2,1)S(1)}, u32[]{:S(2)}, u32[]{:S(2)}) collective-permute-start(bf16[512,512]{1,0:T(8,128)(2,1)S(1)} %collective-permute-done.6.a1_ref), channel_id=1, source_target_pairs={{0,8},{4,12},{8,0},{12,4},{16,20},{20,16},{24,28},{28,24},{1,9},{5... | collective-permute-start | bytes 1572872 | tf_op jit(solution)/shard_map/ppermute | solution.py:450
  40.3 9.3 %collective-permute-start.13 = (bf16[256,1024]{1,0:T(8,128)(2,1)S(1)}, bf16[256,1024]{1,0:T(8,128)(2,1)S(1)}, u32[]{:S(2)}, u32[]{:S(2)}) collective-permute-start(bf16[256,1024]{1,0:T(8,128)(2,1)S(1)} %collective-permute-done.12.d_ref), channel_id=1, source_target_pairs={{0,16},{1,17},{2,18},{3,19},{4,20},{5,21},{6,22},{7,23},{8,24},{9,... | collective-permute-start | bytes 1572872 | tf_op jit(solution)/shard_map/ppermute | solution.py:457
  41.7 11.1 %collective-permute-start.14 = (bf16[256,1024]{1,0:T(8,128)(2,1)S(1)}, bf16[256,1024]{1,0:T(8,128)(2,1)S(1)}, u32[]{:S(2)}, u32[]{:S(2)}) collective-permute-start(bf16[256,1024]{1,0:T(8,128)(2,1)S(1)} %collective-permute-done.12.d_ref), channel_id=1, source_target_pairs={{0,1},{1,0},{2,3},{3,2},{4,5},{5,4},{6,7},{7,6},{8,9},{9,8},{10,11... | collective-permute-start | bytes 1572872 | tf_op jit(solution)/shard_map/ppermute | solution.py:448
  52.7 2.8 %collective-permute-start.15 = (bf16[256,1024]{1,0:T(8,128)(2,1)S(1)}, bf16[256,1024]{1,0:T(8,128)(2,1)S(1)}, u32[]{:S(2)}, u32[]{:S(2)}) collective-permute-start(bf16[256,1024]{1,0:T(8,128)(2,1)S(1)} %collective-permute-done.14.dz_ref), channel_id=1, source_target_pairs={{0,16},{1,17},{2,18},{3,19},{4,20},{5,21},{6,22},{7,23},{8,24},{9,... | collective-permute-start | bytes 1572872 | tf_op jit(solution)/shard_map/ppermute | solution.py:463

commit v5 on v4

--- a/solution.py
+++ b/solution.py
@@ -59,12 +59,42 @@
     )(keys, values)
 
 
-def opening_kernel(s_ref, q_hbm, k_hbm, v_hbm, weight_hbm, grad_hbm,
-                   state_ref, near_ref, far_ref, turn_ref, q_ref, k_ref, v_ref, sems, slice_sems):
+def first_slices_kernel(s_ref, weight_hbm, grad_hbm, near_ref, turn_ref, sems):
     half, wide = near_ref.shape
     rows = pl.ds(pl.multiple_of(s_ref[3] * half, half), half)
-    far_column = 1 - s_ref[2]
-    near_column = jnp.where(s_ref[0] == s_ref[1], far_column, s_ref[2])
+    column = jnp.where(s_ref[0] == s_ref[1], 1 - s_ref[2], s_ref[2])
+    cols = pl.ds(pl.multiple_of(column * wide, wide), wide)
+    near_move = pltpu.make_async_copy(weight_hbm.at[rows, cols], near_ref, sems.at[0])
+    near_move.start()
+    own = turn_ref.shape[1]
+    cols = pl.ds(pl.multiple_of((1 - s_ref[0]) * own, own), own)
+    turn_move = pltpu.make_async_copy(grad_hbm.at[:, cols], turn_ref, sems.at[1])
+    turn_move.start()
+    near_move.wait()
+    turn_move.wait()
+
+
+def first_slices(scal, weight, out_grad):
+    hbm = pl.BlockSpec(memory_space=pltpu.HBM)
+    vmem = pl.BlockSpec(memory_space=pltpu.VMEM)
+    return pl.pallas_call(
+        first_slices_kernel,
+        out_shape=(
+            shape_of((weight.shape[0] // 2, weight.shape[1] // 2), BF16),
+            shape_of((out_grad.shape[0], weight.shape[1]), BF16),
+        ),
+        in_specs=[pl.BlockSpec(memory_space=pltpu.SMEM), hbm, hbm],
+        out_specs=(vmem, vmem),
+        scratch_shapes=[pltpu.SemaphoreType.DMA((2,))],
+        compiler_params=params(16),
+        cost_estimate=cost(1000, 1000),
+    )(scal, weight, out_grad)
+
+
+def opening_kernel(s_ref, q_hbm, k_hbm, v_hbm, weight_hbm,
+                   state_ref, far_ref, q_ref, k_ref, v_ref, sems, slice_sems):
+    half, wide = far_ref.shape
+    rows = pl.ds(pl.multiple_of(s_ref[3] * half, half), half)
     loads = []
     for i, lo in enumerate(range(0, k_hbm.shape[1], DH)):
         cols = pl.ds(lo, DH)
@@ -74,16 +104,10 @@
         ])
         loads[-1][0].start()
         loads[-1][1].start()
-    moves = []
-    for i, (column, ref) in enumerate([(near_column, near_ref), (far_column, far_ref)]):
-        cols = pl.ds(pl.multiple_of(column * wide, wide), wide)
-        moves.append(pltpu.make_async_copy(weight_hbm.at[rows, cols], ref, slice_sems.at[i]))
-        moves[-1].start()
-    moves.append(pltpu.make_async_copy(q_hbm, q_ref, slice_sems.at[2]))
+    cols = pl.ds(pl.multiple_of((1 - s_ref[2]) * wide, wide), wide)
+    moves = [pltpu.make_async_copy(weight_hbm.at[rows, cols], far_ref, slice_sems.at[0])]
     moves[-1].start()
-    own = turn_ref.shape[1]
-    cols = pl.ds(pl.multiple_of((1 - s_ref[0]) * own, own), own)
-    moves.append(pltpu.make_async_copy(grad_hbm.at[:, cols], turn_ref, slice_sems.at[3]))
+    moves.append(pltpu.make_async_copy(q_hbm, q_ref, slice_sems.at[1]))
     moves[-1].start()
     for i, lo in enumerate(range(0, k_hbm.shape[1], DH)):
         cols = slice(lo, lo + DH)
@@ -95,27 +119,27 @@
         move.wait()
 
 
-def opening(scal, queries, keys, values, weight, out_grad):
-    tok, width = keys.shape
+def opening(scal, queries, keys, values, weight):
+    width = keys.shape[1]
     piece = shape_of((weight.shape[0] // 2, weight.shape[1] // 2), BF16)
     hbm = pl.BlockSpec(memory_space=pltpu.HBM)
     vmem = pl.BlockSpec(memory_space=pltpu.VMEM)
     return pl.pallas_call(
         opening_kernel,
-        out_shape=(shape_of((width, DH), BF16), piece, piece, shape_of((tok, weight.shape[1]), BF16))
+        out_shape=(shape_of((width, DH), BF16), piece)
         + (shape_of(keys.shape, BF16),) * 3,
-        in_specs=[pl.BlockSpec(memory_space=pltpu.SMEM)] + [hbm] * 5,
-        out_specs=(vmem,) * 7,
+        in_specs=[pl.BlockSpec(memory_space=pltpu.SMEM)] + [hbm] * 4,
+        out_specs=(vmem,) * 5,
         scratch_shapes=[
             pltpu.SemaphoreType.DMA((2, width // DH)),
-            pltpu.SemaphoreType.DMA((4,)),
+            pltpu.SemaphoreType.DMA((2,)),
         ],
         compiler_params=params(16),
         cost_estimate=cost(2 * keys.size * DH, 4 * keys.size),
-    )(scal, queries, keys, values, weight, out_grad)
-
-
-def forward_kernel(q_ref, k_ref, v_ref, carried_ref, attn_ref, raw_ref, prefix_ref):
+    )(scal, queries, keys, values, weight)
+
+
+def forward_kernel(q_ref, k_ref, v_ref, carried_ref, attn_ref, attn_t_ref, raw_ref, prefix_ref):
     tok, width = q_ref.shape
     chunk = min(CHUNK, tok)
     row = lax.broadcasted_iota(jnp.int32, (chunk, chunk), 0)
@@ -135,7 +159,9 @@
             raw = dot_nn(scores, v) + dot_nn(fq, low_prefix)
             raw_ref[rows, cols] = raw
             inv = lax.rsqrt(jnp.mean(raw * raw, axis=-1, keepdims=True) + EPS)
-            attn_ref[rows, cols] = (raw * inv).astype(BF16)
+            attn = (raw * inv).astype(BF16)
+            attn_ref[rows, cols] = attn
+            attn_t_ref[cols, rows] = attn.T
             if i + 1 < tok // chunk:
                 prefix = prefix + dot_tn(fk, v)
 
@@ -147,6 +173,7 @@
         forward_kernel,
         out_shape=(
             shape_of((tok, width), BF16),
+            shape_of((width, tok), BF16),
             shape_of((tok, width), F32),
             shape_of((chunks, width, DH), BF16),
         ),
@@ -229,18 +256,17 @@
     )(scal, attn_grad, queries, raw, attn, own, rest)
 
 
-def weight_grad_kernel(s_ref, attn_ref, grad_ref, other_ref, other_grad_ref, out_hbm, out_buf, sems):
-    tok, width = attn_ref.shape
+def weight_grad_kernel(s_ref, attn_t_ref, grad_ref, other_t_ref, other_grad_ref, out_hbm, out_buf, sems):
+    width, tok = attn_t_ref.shape
     blocks, _, block = out_buf.shape
-    attn_t = attn_ref[...].T
-    others_t = [other_ref[lo : lo + tok, :].T for lo in range(0, other_ref.shape[0], tok)]
     moves = []
     for j in range(blocks):
         here = slice(j * block, (j + 1) * block)
         place = s_ref[0] * (blocks * block) + j * block
         part = grad_ref[:, pl.ds(pl.multiple_of(place, block), block)]
-        acc = dot_nn(attn_t, part).astype(BF16).astype(F32)
-        for k, other_t in enumerate(others_t):
+        acc = dot_nn(attn_t_ref[...], part).astype(BF16).astype(F32)
+        for k in range(other_t_ref.shape[0] // width):
+            other_t = other_t_ref[k * width : (k + 1) * width, :]
             part = other_grad_ref[k * tok : (k + 1) * tok, here]
             acc += dot_nn(other_t, part).astype(BF16).astype(F32)
         out_buf[j] = acc
@@ -250,8 +276,8 @@
         move.wait()
 
 
-def own_weight_grad(scal, attn, out_grad, other, other_grad):
-    width = attn.shape[1]
+def own_weight_grad(scal, attn_t, out_grad, other_t, other_grad):
+    width = attn_t.shape[0]
     own_width = other_grad.shape[1]
     block = min(256, own_width)
     return pl.pallas_call(
@@ -265,7 +291,7 @@
         ],
         compiler_params=params(16),
         cost_estimate=cost(2 * out_grad.size * width, 4 * out_grad.size),
-    )(scal, attn, out_grad, other, other_grad)
+    )(scal, attn_t, out_grad, other_t, other_grad)
 
 
 def backward_kernel(q_ref, k_ref, v_ref, draw_ref, prefix_ref, suffix_ref, glocal_ref,
@@ -404,10 +430,11 @@
         two = [(i, i ^ 2) for i in range(4)] + [(4 + i, 4 + (i ^ 1)) for i in range(4)]
         zpair = [(i, i ^ 1) for i in range(n_rep)]
         swap = [(0, 1), (1, 0)]
-        state, near_piece, far_piece, turn, queries, keys, values = opening(
-            scal, in_hbm(queries), in_hbm(keys), in_hbm(values), weight_hbm, grad_hbm
+        near_piece, turn = first_slices(scal, weight_hbm, grad_hbm)
+        near_mine = lax.ppermute(near_piece, group, near)
+        state, far_piece, queries, keys, values = opening(
+            after(scal, near_piece), in_hbm(queries), in_hbm(keys), in_hbm(values), weight_hbm
         )
-        near_mine = lax.ppermute(near_piece, group, near)
         other_grad = lax.ppermute(turn, "ctx", swap)
     else:
         state = local_state(keys, values)
@@ -423,15 +450,17 @@
     rest = rest[0] if n_ctx == 2 else jnp.concatenate(rest, 1)
     attn_grad = attn_gradient(scal, out_weight, out_grad, after(rest, state))
     carried = after(carried, attn_grad)
-    attn, raw, prefix = forward(queries, keys, values, carried)
-
     if paired:
-        far_mine = lax.ppermute(after(far_piece, attn), group, far)
+        far_mine = lax.ppermute(after(far_piece, attn_grad, near_mine), group, far)
+        carried = after(carried, near_mine)
+    attn, attn_t, raw, prefix = forward(queries, keys, values, carried)
+
+    if paired:
         attn_1 = lax.ppermute(attn, group, one)
         attn_2 = lax.ppermute(attn, group, two)
         near_z = lax.ppermute(near_mine, "rep", zpair)
         raw = after(raw, near_mine, other_grad)
-    other_attn = [shift(attn, "ctx", n_ctx, k, True) for k in range(1, n_ctx)]
+    other_attn = [shift(attn_t, "ctx", n_ctx, k, True) for k in range(1, n_ctx)]
     other_attn = other_attn[0] if n_ctx == 2 else jnp.concatenate(other_attn, 0)
 
     draw, gsum, glocal, own_out = cotangent(
@@ -440,12 +469,12 @@
     suffix = total([shift(gsum, "ctx", n_ctx, -k, False) for k in range(1, n_ctx)])
 
     if paired:
-        other_attn = after(other_attn, gsum)
-
-    weight_grad = own_weight_grad(scal, attn, out_grad, other_attn, other_grad)
+        far_z = lax.ppermute(after(far_mine, gsum), ("ctx", "rep"), zpair)
+        other_attn = after(other_attn, gsum, far_mine)
+
+    weight_grad = own_weight_grad(scal, attn_t, out_grad, other_attn, other_grad)
 
     if paired:
-        far_z = lax.ppermute(after(far_mine, weight_grad), ("ctx", "rep"), zpair)
         near_other = lax.ppermute(after(near_mine, weight_grad), "ctx", swap)
         attn_3 = lax.ppermute(after(attn_1, weight_grad), group, two)
         near_other_z = lax.ppermute(after(near_z, weight_grad), "ctx", swap)
@@ -455,12 +484,11 @@
 
     if paired:
         far_other = lax.ppermute(after(far_mine, weight_grad), "ctx", [(0, 1)])
+        far_other_z = lax.ppermute(after(far_z, query_grad), "ctx", [(0, 1)])
         near_out = project_near(
-            scal, after(own_out, query_grad), (attn_1, attn_2),
+            scal, after(own_out, query_grad, attn_3), (attn_1, attn_2),
             (near_mine, near_z, near_other, near_other_z),
         )
-        last = after(far_z, near_out, attn_3, far_other)
-        far_other_z = lax.ppermute(last, "ctx", [(0, 1)])
         layer_out = project_far(scal, near_out, attn_3, (far_mine, far_other, far_z, far_other_z))
     else:
         full = lax.all_gather(out_weight, "ctx", axis=1, tiled=True)

time: 58.1 us -> 52.1 us (0.90)
  waiting for transfers between devices: 14.5 us -> 6.4 us
  Pallas kernels: 21.7 us -> 23.7 us
    ppermute x3, waiting for transfers between devices: 13.7 us -> 0.01 us  [the longest x1 0.01 us: body(): far_mine = lax.ppermute(after(far_piece, attn_grad, near_mine), group, far)]
    ppermute x4, starting transfers between devices: 3.6 us -> 7.31 us  [shift(): return lax.ppermute(array, axis, pairs)]
    pallas_call x0 -> x1, Pallas kernels: none -> 2.58 us  [first_slices(): pl.pallas_call(first_slices_kernel, out_shape=(shape_of((weight.shape[0]...]
    ppermute x1, starting transfers between devices: 2.68 us -> 0.32 us  [body(): attn_2 = lax.ppermute(attn, group, two)]
    ppermute x1, waiting for transfers between devices: 0.01 us -> 1.98 us  [body(): near_z = lax.ppermute(near_mine, 'rep', zpair)]
    ppermute x1, waiting for transfers between devices: 0.01 us -> 1.34 us  [body(): attn_1 = lax.ppermute(attn, group, one)]
    ppermute x1, starting transfers between devices: 1.19 us -> 0.01 us  [body(): near_other = lax.ppermute(after(near_mine, weight_grad), 'ctx', swap)]
    ppermute x1, starting transfers between devices: 0.01 us -> 1.05 us  [body(): attn_3 = lax.ppermute(after(attn_1, weight_grad), group, two)]
  transfers between devices with their start and end apart: 16 -> 16, of which waited for: 4 -> 5; matrix products, arithmetic and copies ran while one was open for 0% -> 0% of each run, Pallas kernels for 34% -> 42%
where the time goes in v5:
time: 52.1 us; the launch traced here: 51.9 us
  Pallas kernels  23.7 us (45%)
  starting transfers between devices  20.9 us (40%)
  waiting for transfers between devices  6.4 us (12%)
  between operations  0.81 us (2%)
    ppermute x4, starting transfers between devices, shift(): return lax.ppermute(array, axis, pairs)  7.31 us
    pallas_call x1, Pallas kernels, own_weight_grad(): pl.pallas_call(weight_grad_kernel, out_shape=shape_of((width, own_width),...  3.88 us
    pallas_call x1, Pallas kernels, backward(): pl.pallas_call(backward_kernel, out_shape=(out, out, out), compiler_param...  3.8 us
    ppermute x1, starting transfers between devices, body(): near_mine = lax.ppermute(near_piece, group, near)  2.94 us
    pallas_call x1, Pallas kernels, attn_gradient(): pl.pallas_call(attn_grad_kernel, out_shape=shape_of((tok, width), BF16),...  2.9 us
    pallas_call x1, Pallas kernels, opening(): pl.pallas_call(opening_kernel, out_shape=(shape_of((width, DH), BF16), pi...  2.68 us
    pallas_call x1, Pallas kernels, first_slices(): pl.pallas_call(first_slices_kernel, out_shape=(shape_of((weight.shape[0]...  2.58 us
    pallas_call x1, Pallas kernels, cotangent(): pl.pallas_call(cotangent_kernel, out_shape=(shape_of((tok, width), BF16),...  2.29 us
  transfers between devices with their start and end apart: 16, of which 5 were waited for; matrix products, arithmetic and copies ran while one was open for 0% of the time, Pallas kernels for 42%

profile of v5, /device:TPU:0, one launch (start us, length us, event | category | flops | bytes accessed | tf_op | source)
XLA Modules:
  0.0 51.9 jit_solution(4636239880655414688)
XLA Ops:
  0.6 0.5 collective-permute-start
  1.1 0.1 pad_add_fusion.s_ref
  1.2 0.0 copy-start
  1.2 2.6 %shard_map.92 = (bf16[256,1024]{1,0:T(8,128)(2,1)S(1)}, bf16[512,2048]{1,0:T(8,128)(2,1)S(1)}) custom-call(s32[4]{0:T(128)S(1)} %pad_add_fusion.s_ref, bf16[512,2048]{1,0:T(8,128)(2,1)} %own_ref.3, bf16[512,4096]{1,0:T(8,128)(2,1)} %grad_ref.3), custom_call_target="tpu_custom_call" | custom-call | flops 1000 | bytes 1000 | tf_op jit(solution)/shard_map/pallas_call | solution.py:80
  3.8 0.0 copy-start.1
  3.8 0.1 collective-permute-start.3
  4.0 2.9 %collective-permute-start.2 = (bf16[256,1024]{1,0:T(8,128)(2,1)S(1)}, bf16[256,1024]{1,0:T(8,128)(2,1)S(1)}, u32[]{:S(2)}, u32[]{:S(2)}) collective-permute-start(bf16[256,1024]{1,0:T(8,128)(2,1)S(1)} %get-tuple-element.38), channel_id=1, source_target_pairs={{0,4},{4,0},{24,12},{28,8},{16,24},{20,28},{8,16},{12,20},{1,5},{5... | collective-permute-start | bytes 1572872 | tf_op jit(solution)/shard_map/ppermute | solution.py:434
  6.9 2.7 %shard_map.93 = (bf16[512,128]{1,0:T(8,128)(2,1)S(1)}, bf16[256,1024]{1,0:T(8,128)(2,1)S(1)}, bf16[512,512]{1,0:T(8,128)(2,1)S(1)}, bf16[512,512]{1,0:T(8,128)(2,1)S(1)}, bf16[512,512]{1,0:T(8,128)(2,1)S(1)}) custom-call(s32[4]{0:T(128)S(1)} %pad_add_fusion.s_ref, bf16[512,512]{1,0:T(8,128)(2,1)} %q_hbm.1, bf16[512,512]{1,0:T(8,128)(2,1)} %k_hbm.1, ...), custom_call_target="tpu_custom_call" | custom-call | flops 67108864 | bytes 1048576 | tf_op jit(solution)/shard_map/pallas_call | solution.py:127
  9.6 0.0 collective-permute-done.rest_ref
  9.6 0.0 copy-done
  9.6 0.0 copy-done.1
  9.6 2.9 %shard_map.94.attn_grad_ref = bf16[512,512]{1,0:T(8,128)(2,1)S(1)} custom-call(s32[4]{0:T(128)S(1)} %pad_add_fusion.s_ref, bf16[512,2048]{1,0:T(8,128)(2,1)S(1)} %copy-done.1, bf16[512,4096]{1,0:T(8,128)(2,1)S(1)} %copy-done, bf16[512,2048]{1,0:T(8,128)(2,1)S(1)} %collective-permute-done.rest_ref), custom_call_target="tpu_custom_call" | custom-call | flops 2147483648 | bytes 8388608 | tf_op jit(solution)/shard_map/pallas_call | solution.py:205
  12.5 1.5 %collective-permute-done.2.m1_ref = bf16[256,1024]{1,0:T(8,128)(2,1)S(1)} collective-permute-done((bf16[256,1024]{1,0:T(8,128)(2,1)S(1)}, bf16[256,1024]{1,0:T(8,128)(2,1)S(1)}, u32[]{:S(2)}, u32[]{:S(2)}) %collective-permute-start.2) | collective-permute-done | bytes 524320 | tf_op jit(solution)/shard_map/ppermute | solution.py:434
  14.0 1.3 %collective-permute-start.6 = (bf16[256,1024]{1,0:T(8,128)(2,1)S(1)}, bf16[256,1024]{1,0:T(8,128)(2,1)S(1)}, u32[]{:S(2)}, u32[]{:S(2)}) collective-permute-start(bf16[256,1024]{1,0:T(8,128)(2,1)S(1)} %get-tuple-element.57), channel_id=1, source_target_pairs={{16,12},{20,8},{8,4},{12,0},{17,13},{21,9},{9,5},{13,1},{18,14},{2... | collective-permute-start | bytes 1572872 | tf_op jit(solution)/shard_map/ppermute | solution.py:454
  15.3 5.1 %collective-permute-start.1 = (bf16[512,128]{1,0:T(8,128)(2,1)S(1)}, bf16[512,128]{1,0:T(8,128)(2,1)S(1)}, u32[]{:S(2)}, u32[]{:S(2)}) collective-permute-start(bf16[512,128]{1,0:T(8,128)(2,1)S(1)} %get-tuple-element.40), channel_id=1, source_target_pairs={{0,16},{1,17},{2,18},{3,19},{4,20},{5,21},{6,22},{7,23},{8,24},{9,... | collective-permute-start | bytes 393224 | tf_op jit(solution)/shard_map/ppermute | solution.py:407
  20.4 1.0 %collective-permute-done.1.carried_ref = bf16[512,128]{1,0:T(8,128)(2,1)S(1)} collective-permute-done((bf16[512,128]{1,0:T(8,128)(2,1)S(1)}, bf16[512,128]{1,0:T(8,128)(2,1)S(1)}, u32[]{:S(2)}, u32[]{:S(2)}) %collective-permute-start.1) | collective-permute-done | bytes 131104 | tf_op jit(solution)/shard_map/ppermute | solution.py:407
  21.4 1.6 %shard_map.95 = (bf16[512,512]{1,0:T(8,128)(2,1)S(1)}, bf16[512,512]{1,0:T(8,128)(2,1)S(1)}, f32[512,512]{1,0:T(8,128)S(1)}, bf16[2,512,128]{2,1,0:T(8,128)(2,1)S(1)}) custom-call(bf16[512,512]{1,0:T(8,128)(2,1)S(1)} %get-tuple-element.42.q_ref, bf16[512,512]{1,0:T(8,128)(2,1)S(1)} %get-tuple-element.43.k_ref, bf16[512,512]{1,0:T(8,128)(2,1)S(1)} %get-tuple-element.44.v_ref, ...), custom_call_target="tpu_custom_call" | custom-call | flops 536870912 | bytes 3145728 | tf_op jit(solution)/shard_map/pallas_call | solution.py:172
  23.0 0.4 collective-permute-start.5
  23.4 1.6 %collective-permute-start.9 = (bf16[256,1024]{1,0:T(8,128)(2,1)S(1)}, bf16[256,1024]{1,0:T(8,128)(2,1)S(1)}, u32[]{:S(2)}, u32[]{:S(2)}) collective-permute-start(bf16[256,1024]{1,0:T(8,128)(2,1)S(1)} %collective-permute-done.2.m1_ref), channel_id=1, source_target_pairs={{0,1},{1,0},{2,3},{3,2},{4,5},{5,4},{6,7},{7,6},{8,9},{9,8},{10,11... | collective-permute-start | bytes 1572872 | tf_op jit(solution)/shard_map/ppermute | solution.py:461
  25.0 0.5 %collective-permute-start.7 = (bf16[512,512]{1,0:T(8,128)(2,1)S(1)}, bf16[512,512]{1,0:T(8,128)(2,1)S(1)}, u32[]{:S(2)}, u32[]{:S(2)}) collective-permute-start(bf16[512,512]{1,0:T(8,128)(2,1)S(1)} %get-tuple-element.50.attn_ref), channel_id=1, source_target_pairs={{0,4},{4,0},{8,12},{12,8},{16,24},{20,28},{24,16},{28,20},{1,5},{5... | collective-permute-start | bytes 1572872 | tf_op jit(solution)/shard_map/ppermute | solution.py:459
  25.5 0.0 collective-permute-done.3.other_grad_ref
  25.5 0.3 collective-permute-start.8
  25.9 2.3 %shard_map.96 = (bf16[512,512]{1,0:T(8,128)(2,1)S(1)}, bf16[512,128]{1,0:T(8,128)(2,1)S(1)}, f32[2,512,128]{2,1,0:T(8,128)S(1)}, f32[512,1024]{1,0:T(8,128)S(1)}) custom-call(s32[4]{0:T(128)S(1)} %pad_add_fusion.s_ref, bf16[512,512]{1,0:T(8,128)(2,1)S(1)} %shard_map.94.attn_grad_ref, bf16[512,512]{1,0:T(8,128)(2,1)S(1)} %get-tuple-element.42.q_ref, ...), custom_call_target="tpu_custom_call" | custom-call | flops 536870912 | bytes 4194304 | tf_op jit(solution)/shard_map/pallas_call | solution.py:245
  28.2 0.0 collective-permute-done.6.d_ref
  28.2 2.0 %collective-permute-start.14 = (bf16[256,1024]{1,0:T(8,128)(2,1)S(1)}, bf16[256,1024]{1,0:T(8,128)(2,1)S(1)}, u32[]{:S(2)}, u32[]{:S(2)}) collective-permute-start(bf16[256,1024]{1,0:T(8,128)(2,1)S(1)} %collective-permute-done.6.d_ref), channel_id=1, source_target_pairs={{0,1},{1,0},{2,3},{3,2},{4,5},{5,4},{6,7},{7,6},{8,9},{9,8},{10,11... | collective-permute-start | bytes 1572872 | tf_op jit(solution)/shard_map/ppermute | solution.py:472
  30.2 0.0 collective-permute-done.5.other_t_ref
  30.2 1.3 %collective-permute-start.4 = (bf16[512,128]{1,0:T(8,128)(2,1)S(1)}, bf16[512,128]{1,0:T(8,128)(2,1)S(1)}, u32[]{:S(2)}, u32[]{:S(2)}) collective-permute-start(bf16[512,128]{1,0:T(8,128)(2,1)S(1)} %get-tuple-element.54), channel_id=1, source_target_pairs={{16,0},{17,1},{18,2},{19,3},{20,4},{21,5},{22,6},{23,7},{24,8},{25... | collective-permute-start | bytes 393224 | tf_op jit(solution)/shard_map/ppermute | solution.py:407
  31.5 3.9 %shard_map.97 = f32[512,2048]{1,0:T(8,128)} custom-call(s32[4]{0:T(128)S(1)} %pad_add_fusion.s_ref, bf16[512,512]{1,0:T(8,128)(2,1)S(1)} %get-tuple-element.55.attn_t_ref, bf16[512,4096]{1,0:T(8,128)(2,1)S(1)} %copy-done, bf16[512,512]{1,0:T(8,128)(2,1)S(1)} %collective-permute-done.5.other_t_ref, bf16[512,2048]{1,0:T(8,128)(2,1)S(1)} %collective-permute-done.3.other_grad_ref), custom_call_target="tpu_custom_call" | custom-call | flops 2147483648 | bytes 8388608 | tf_op jit(solution)/shard_map/pallas_call | solution.py:283
  35.4 2.0 %collective-permute-done.9.z1_ref = bf16[256,1024]{1,0:T(8,128)(2,1)S(1)} collective-permute-done((bf16[256,1024]{1,0:T(8,128)(2,1)S(1)}, bf16[256,1024]{1,0:T(8,128)(2,1)S(1)}, u32[]{:S(2)}, u32[]{:S(2)}) %collective-permute-start.9) | collective-permute-done | bytes 524320 | tf_op jit(solution)/shard_map/ppermute | solution.py:461
  37.4 0.0 collective-permute-done.4.suffix_ref
  37.4 1.3 %collective-permute-done.7.a1_ref = bf16[512,512]{1,0:T(8,128)(2,1)S(1)} collective-permute-done((bf16[512,512]{1,0:T(8,128)(2,1)S(1)}, bf16[512,512]{1,0:T(8,128)(2,1)S(1)}, u32[]{:S(2)}, u32[]{:S(2)}) %collective-permute-start.7) | collective-permute-done | bytes 524320 | tf_op jit(solution)/shard_map/ppermute | solution.py:459
  38.7 0.0 collective-permute-done.8.a2_ref
  38.7 1.0 %collective-permute-start.10 = (bf16[512,512]{1,0:T(8,128)(2,1)S(1)}, bf16[512,512]{1,0:T(8,128)(2,1)S(1)}, u32[]{:S(2)}, u32[]{:S(2)}) collective-permute-start(bf16[512,512]{1,0:T(8,128)(2,1)S(1)} %collective-permute-done.7.a1_ref), channel_id=1, source_target_pairs={{0,8},{4,12},{8,0},{12,4},{16,20},{20,16},{24,28},{28,24},{1,9},{5... | collective-permute-start | bytes 1572872 | tf_op jit(solution)/shard_map/ppermute | solution.py:479
  39.8 0.0 collective-permute-start.11
  39.8 0.5 collective-permute-start.12
  40.3 1.9 %collective-permute-start.13 = (bf16[256,1024]{1,0:T(8,128)(2,1)S(1)}, bf16[256,1024]{1,0:T(8,128)(2,1)S(1)}, u32[]{:S(2)}, u32[]{:S(2)}) collective-permute-start(bf16[256,1024]{1,0:T(8,128)(2,1)S(1)} %collective-permute-done.6.d_ref), channel_id=1, source_target_pairs={{0,16},{1,17},{2,18},{3,19},{4,20},{5,21},{6,22},{7,23},{8,24},{9,... | collective-permute-start | bytes 1572872 | tf_op jit(solution)/shard_map/ppermute | solution.py:486
  42.2 3.8 %shard_map.98 = (bf16[512,512]{1,0:T(8,128)(2,1)}, bf16[512,512]{1,0:T(8,128)(2,1)}, bf16[512,512]{1,0:T(8,128)(2,1)}) custom-call(bf16[512,512]{1,0:T(8,128)(2,1)S(1)} %get-tuple-element.42.q_ref, bf16[512,512]{1,0:T(8,128)(2,1)S(1)} %get-tuple-element.43.k_ref, bf16[512,512]{1,0:T(8,128)(2,1)S(1)} %get-tuple-element.44.v_ref, ...), custom_call_target="tpu_custom_call" | custom-call | flops 1073741824 | bytes 4194304 | tf_op jit(solution)/shard_map/pallas_call | solution.py:332
  46.0 0.0 collective-permute-done.14.dz_ref
  46.0 1.3 %collective-permute-start.15 = (bf16[256,1024]{1,0:T(8,128)(2,1)S(1)}, bf16[256,1024]{1,0:T(8,128)(2,1)S(1)}, u32[]{:S(2)}, u32[]{:S(2)}) collective-permute-start(bf16[256,1024]{1,0:T(8,128)(2,1)S(1)} %collective-permute-done.14.dz_ref), channel_id=1, source_target_pairs={{0,16},{1,17},{2,18},{3,19},{4,20},{5,21},{6,22},{7,23},{8,24},{9,... | collective-permute-start | bytes 1572872 | tf_op jit(solution)/shard_map/ppermute | solution.py:487
  47.4 0.6 %collective-permute-done.10.a_ref = bf16[512,512]{1,0:T(8,128)(2,1)S(1)} collective-permute-done((bf16[512,512]{1,0:T(8,128)(2,1)S(1)}, bf16[512,512]{1,0:T(8,128)(2,1)S(1)}, u32[]{:S(2)}, u32[]{:S(2)}) %collective-permute-start.10) | collective-permute-done | bytes 524320 | tf_op jit(solution)/shard_map/ppermute | solution.py:479
  47.9 0.0 collective-permute-done.11.o1_ref
  47.9 0.0 collective-permute-done.12.oz1_ref
  47.9 1.8 %shard_map.99.near_ref = f32[512,1024]{1,0:T(8,128)S(1)} custom-call(s32[4]{0:T(128)S(1)} %pad_add_fusion.s_ref, f32[512,1024]{1,0:T(8,128)S(1)} %get-tuple-element.63.so_far_ref, bf16[512,512]{1,0:T(8,128)(2,1)S(1)} %collective-permute-done.7.a1_ref, bf16[512,512]{1,0:T(8,128)(2,1)S(1)} %collective-permute-done.8.a2_ref, ...), custom_call_target="tpu_custom_call" | custom-call | flops 1000 | bytes 1000 | tf_op jit(solution)/shard_map/pallas_call | solution.py:356
  49.7 0.0 collective-permute-done.13.od_ref
  49.8 0.0 collective-permute-done.15.odz_ref
  49.8 2.1 %shard_map.100 = bf16[512,1024]{1,0:T(8,128)(2,1)} custom-call(s32[4]{0:T(128)S(1)} %pad_add_fusion.s_ref, f32[512,1024]{1,0:T(8,128)S(1)} %shard_map.99.near_ref, bf16[512,512]{1,0:T(8,128)(2,1)S(1)} %collective-permute-done.10.a_ref, bf16[256,1024]{1,0:T(8,128)(2,1)S(1)} %collective-permute-done.6.d_ref, ...), custom_call_target="tpu_custom_call" | custom-call | flops 1000 | bytes 1000 | tf_op jit(solution)/shard_map/pallas_call | solution.py:383
Async XLA Ops:
  0.6 9.0 %collective-permute-start = (bf16[512,2048]{1,0:T(8,128)(2,1)}, bf16[512,2048]{1,0:T(8,128)(2,1)S(1)}, u32[]{:S(2)}, u32[]{:S(2)}) collective-permute-start(bf16[512,2048]{1,0:T(8,128)(2,1)} %own_ref.3), channel_id=1, source_target_pairs={{0,16},{16,0},{1,17},{17,1},{2,18},{18,2},{3,19},{19,3},{4,20},{20... | collective-permute-start | bytes 6291464 | tf_op jit(solution)/shard_map/ppermute | solution.py:407
  1.2 8.4 %copy-start = (bf16[512,4096]{1,0:T(8,128)(2,1)S(1)}, bf16[512,4096]{1,0:T(8,128)(2,1)}, u32[]{:S(2)}) copy-start(bf16[512,4096]{1,0:T(8,128)(2,1)} %grad_ref.3) | copy-start | bytes 12582916
  3.8 5.8 %copy-start.1 = (bf16[512,2048]{1,0:T(8,128)(2,1)S(1)}, bf16[512,2048]{1,0:T(8,128)(2,1)}, u32[]{:S(2)}) copy-start(bf16[512,2048]{1,0:T(8,128)(2,1)} %own_ref.3) | copy-start | bytes 6291460
  3.8 21.7 %collective-permute-start.3 = (bf16[512,2048]{1,0:T(8,128)(2,1)S(1)}, bf16[512,2048]{1,0:T(8,128)(2,1)S(1)}, u32[]{:S(2)}, u32[]{:S(2)}) collective-permute-start(bf16[512,2048]{1,0:T(8,128)(2,1)S(1)} %get-tuple-element.48), channel_id=1, source_target_pairs={{0,16},{16,0},{1,17},{17,1},{2,18},{18,2},{3,19},{19,3},{4,20},{20... | collective-permute-start | bytes 6291464 | tf_op jit(solution)/shard_map/ppermute | solution.py:438
  4.0 10.1 %collective-permute-start.2 = (bf16[256,1024]{1,0:T(8,128)(2,1)S(1)}, bf16[256,1024]{1,0:T(8,128)(2,1)S(1)}, u32[]{:S(2)}, u32[]{:S(2)}) collective-permute-start(bf16[256,1024]{1,0:T(8,128)(2,1)S(1)} %get-tuple-element.38), channel_id=1, source_target_pairs={{0,4},{4,0},{24,12},{28,8},{16,24},{20,28},{8,16},{12,20},{1,5},{5... | collective-permute-start | bytes 1572872 | tf_op jit(solution)/shard_map/ppermute | solution.py:434
  14.0 14.1 %collective-permute-start.6 = (bf16[256,1024]{1,0:T(8,128)(2,1)S(1)}, bf16[256,1024]{1,0:T(8,128)(2,1)S(1)}, u32[]{:S(2)}, u32[]{:S(2)}) collective-permute-start(bf16[256,1024]{1,0:T(8,128)(2,1)S(1)} %get-tuple-element.57), channel_id=1, source_target_pairs={{16,12},{20,8},{8,4},{12,0},{17,13},{21,9},{9,5},{13,1},{18,14},{2... | collective-permute-start | bytes 1572872 | tf_op jit(solution)/shard_map/ppermute | solution.py:454
  15.3 6.0 %collective-permute-start.1 = (bf16[512,128]{1,0:T(8,128)(2,1)S(1)}, bf16[512,128]{1,0:T(8,128)(2,1)S(1)}, u32[]{:S(2)}, u32[]{:S(2)}) collective-permute-start(bf16[512,128]{1,0:T(8,128)(2,1)S(1)} %get-tuple-element.40), channel_id=1, source_target_pairs={{0,16},{1,17},{2,18},{3,19},{4,20},{5,21},{6,22},{7,23},{8,24},{9,... | collective-permute-start | bytes 393224 | tf_op jit(solution)/shard_map/ppermute | solution.py:407
  23.0 7.2 %collective-permute-start.5 = (bf16[512,512]{1,0:T(8,128)(2,1)S(1)}, bf16[512,512]{1,0:T(8,128)(2,1)S(1)}, u32[]{:S(2)}, u32[]{:S(2)}) collective-permute-start(bf16[512,512]{1,0:T(8,128)(2,1)S(1)} %get-tuple-element.55.attn_t_ref), channel_id=1, source_target_pairs={{0,16},{16,0},{1,17},{17,1},{2,18},{18,2},{3,19},{19,3},{4,20},{20... | collective-permute-start | bytes 1572872 | tf_op jit(solution)/shard_map/ppermute | solution.py:407
  23.4 14.0 %collective-permute-start.9 = (bf16[256,1024]{1,0:T(8,128)(2,1)S(1)}, bf16[256,1024]{1,0:T(8,128)(2,1)S(1)}, u32[]{:S(2)}, u32[]{:S(2)}) collective-permute-start(bf16[256,1024]{1,0:T(8,128)(2,1)S(1)} %collective-permute-done.2.m1_ref), channel_id=1, source_target_pairs={{0,1},{1,0},{2,3},{3,2},{4,5},{5,4},{6,7},{7,6},{8,9},{9,8},{10,11... | collective-permute-start | bytes 1572872 | tf_op jit(solution)/shard_map/ppermute | solution.py:461
  25.0 13.7 %collective-permute-start.7 = (bf16[512,512]{1,0:T(8,128)(2,1)S(1)}, bf16[512,512]{1,0:T(8,128)(2,1)S(1)}, u32[]{:S(2)}, u32[]{:S(2)}) collective-permute-start(bf16[512,512]{1,0:T(8,128)(2,1)S(1)} %get-tuple-element.50.attn_ref), channel_id=1, source_target_pairs={{0,4},{4,0},{8,12},{12,8},{16,24},{20,28},{24,16},{28,20},{1,5},{5... | collective-permute-start | bytes 1572872 | tf_op jit(solution)/shard_map/ppermute | solution.py:459
  25.5 13.2 %collective-permute-start.8 = (bf16[512,512]{1,0:T(8,128)(2,1)S(1)}, bf16[512,512]{1,0:T(8,128)(2,1)S(1)}, u32[]{:S(2)}, u32[]{:S(2)}) collective-permute-start(bf16[512,512]{1,0:T(8,128)(2,1)S(1)} %get-tuple-element.50.attn_ref), channel_id=1, source_target_pairs={{0,8},{4,12},{8,0},{12,4},{16,20},{20,16},{24,28},{28,24},{1,9},{5... | collective-permute-start | bytes 1572872 | tf_op jit(solution)/shard_map/ppermute | solution.py:460
  28.2 17.9 %collective-permute-start.14 = (bf16[256,1024]{1,0:T(8,128)(2,1)S(1)}, bf16[256,1024]{1,0:T(8,128)(2,1)S(1)}, u32[]{:S(2)}, u32[]{:S(2)}) collective-permute-start(bf16[256,1024]{1,0:T(8,128)(2,1)S(1)} %collective-permute-done.6.d_ref), channel_id=1, source_target_pairs={{0,1},{1,0},{2,3},{3,2},{4,5},{5,4},{6,7},{7,6},{8,9},{9,8},{10,11... | collective-permute-start | bytes 1572872 | tf_op jit(solution)/shard_map/ppermute | solution.py:472
  30.2 7.2 %collective-permute-start.4 = (bf16[512,128]{1,0:T(8,128)(2,1)S(1)}, bf16[512,128]{1,0:T(8,128)(2,1)S(1)}, u32[]{:S(2)}, u32[]{:S(2)}) collective-permute-start(bf16[512,128]{1,0:T(8,128)(2,1)S(1)} %get-tuple-element.54), channel_id=1, source_target_pairs={{16,0},{17,1},{18,2},{19,3},{20,4},{21,5},{22,6},{23,7},{24,8},{25... | collective-permute-start | bytes 393224 | tf_op jit(solution)/shard_map/ppermute | solution.py:407
  38.7 9.2 %collective-permute-start.10 = (bf16[512,512]{1,0:T(8,128)(2,1)S(1)}, bf16[512,512]{1,0:T(8,128)(2,1)S(1)}, u32[]{:S(2)}, u32[]{:S(2)}) collective-permute-start(bf16[512,512]{1,0:T(8,128)(2,1)S(1)} %collective-permute-done.7.a1_ref), channel_id=1, source_target_pairs={{0,8},{4,12},{8,0},{12,4},{16,20},{20,16},{24,28},{28,24},{1,9},{5... | collective-permute-start | bytes 1572872 | tf_op jit(solution)/shard_map/ppermute | solution.py:479
  39.8 8.1 %collective-permute-start.11 = (bf16[256,1024]{1,0:T(8,128)(2,1)S(1)}, bf16[256,1024]{1,0:T(8,128)(2,1)S(1)}, u32[]{:S(2)}, u32[]{:S(2)}) collective-permute-start(bf16[256,1024]{1,0:T(8,128)(2,1)S(1)} %collective-permute-done.2.m1_ref), channel_id=1, source_target_pairs={{0,16},{16,0},{1,17},{17,1},{2,18},{18,2},{3,19},{19,3},{4,20},{20... | collective-permute-start | bytes 1572872 | tf_op jit(solution)/shard_map/ppermute | solution.py:478
  39.8 8.1 %collective-permute-start.12 = (bf16[256,1024]{1,0:T(8,128)(2,1)S(1)}, bf16[256,1024]{1,0:T(8,128)(2,1)S(1)}, u32[]{:S(2)}, u32[]{:S(2)}) collective-permute-start(bf16[256,1024]{1,0:T(8,128)(2,1)S(1)} %collective-permute-done.9.z1_ref), channel_id=1, source_target_pairs={{0,16},{16,0},{1,17},{17,1},{2,18},{18,2},{3,19},{19,3},{4,20},{20... | collective-permute-start | bytes 1572872 | tf_op jit(solution)/shard_map/ppermute | solution.py:480
  40.3 9.4 %collective-permute-start.13 = (bf16[256,1024]{1,0:T(8,128)(2,1)S(1)}, bf16[256,1024]{1,0:T(8,128)(2,1)S(1)}, u32[]{:S(2)}, u32[]{:S(2)}) collective-permute-start(bf16[256,1024]{1,0:T(8,128)(2,1)S(1)} %collective-permute-done.6.d_ref), channel_id=1, source_target_pairs={{0,16},{1,17},{2,18},{3,19},{4,20},{5,21},{6,22},{7,23},{8,24},{9,... | collective-permute-start | bytes 1572872 | tf_op jit(solution)/shard_map/ppermute | solution.py:486
  46.0 3.7 %collective-permute-start.15 = (bf16[256,1024]{1,0:T(8,128)(2,1)S(1)}, bf16[256,1024]{1,0:T(8,128)(2,1)S(1)}, u32[]{:S(2)}, u32[]{:S(2)}) collective-permute-start(bf16[256,1024]{1,0:T(8,128)(2,1)S(1)} %collective-permute-done.14.dz_ref), channel_id=1, source_target_pairs={{0,16},{1,17},{2,18},{3,19},{4,20},{5,21},{6,22},{7,23},{8,24},{9,... | collective-permute-start | bytes 1572872 | tf_op jit(solution)/shard_map/ppermute | solution.py:487

commit v6 on v4

--- a/solution.py
+++ b/solution.py
@@ -115,7 +115,7 @@
     )(scal, queries, keys, values, weight, out_grad)
 
 
-def forward_kernel(q_ref, k_ref, v_ref, carried_ref, attn_ref, raw_ref, prefix_ref):
+def forward_kernel(q_ref, k_ref, v_ref, carried_ref, attn_ref, attn_t_ref, raw_ref, prefix_ref):
     tok, width = q_ref.shape
     chunk = min(CHUNK, tok)
     row = lax.broadcasted_iota(jnp.int32, (chunk, chunk), 0)
@@ -135,7 +135,9 @@
             raw = dot_nn(scores, v) + dot_nn(fq, low_prefix)
             raw_ref[rows, cols] = raw
             inv = lax.rsqrt(jnp.mean(raw * raw, axis=-1, keepdims=True) + EPS)
-            attn_ref[rows, cols] = (raw * inv).astype(BF16)
+            attn = (raw * inv).astype(BF16)
+            attn_ref[rows, cols] = attn
+            attn_t_ref[cols, rows] = attn.T
             if i + 1 < tok // chunk:
                 prefix = prefix + dot_tn(fk, v)
 
@@ -147,6 +149,7 @@
         forward_kernel,
         out_shape=(
             shape_of((tok, width), BF16),
+            shape_of((width, tok), BF16),
             shape_of((tok, width), F32),
             shape_of((chunks, width, DH), BF16),
         ),
@@ -229,18 +232,17 @@
     )(scal, attn_grad, queries, raw, attn, own, rest)
 
 
-def weight_grad_kernel(s_ref, attn_ref, grad_ref, other_ref, other_grad_ref, out_hbm, out_buf, sems):
-    tok, width = attn_ref.shape
+def weight_grad_kernel(s_ref, attn_t_ref, grad_ref, other_t_ref, other_grad_ref, out_hbm, out_buf, sems):
+    width, tok = attn_t_ref.shape
     blocks, _, block = out_buf.shape
-    attn_t = attn_ref[...].T
-    others_t = [other_ref[lo : lo + tok, :].T for lo in range(0, other_ref.shape[0], tok)]
     moves = []
     for j in range(blocks):
         here = slice(j * block, (j + 1) * block)
         place = s_ref[0] * (blocks * block) + j * block
         part = grad_ref[:, pl.ds(pl.multiple_of(place, block), block)]
-        acc = dot_nn(attn_t, part).astype(BF16).astype(F32)
-        for k, other_t in enumerate(others_t):
+        acc = dot_nn(attn_t_ref[...], part).astype(BF16).astype(F32)
+        for k in range(other_t_ref.shape[0] // width):
+            other_t = other_t_ref[k * width : (k + 1) * width, :]
             part = other_grad_ref[k * tok : (k + 1) * tok, here]
             acc += dot_nn(other_t, part).astype(BF16).astype(F32)
         out_buf[j] = acc
@@ -250,10 +252,10 @@
         move.wait()
 
 
-def own_weight_grad(scal, attn, out_grad, other, other_grad):
-    width = attn.shape[1]
+def own_weight_grad(scal, attn_t, out_grad, other_t, other_grad):
+    width = attn_t.shape[0]
     own_width = other_grad.shape[1]
-    block = min(256, own_width)
+    block = min(512, own_width)
     return pl.pallas_call(
         weight_grad_kernel,
         out_shape=shape_of((width, own_width), F32),
@@ -265,7 +267,7 @@
         ],
         compiler_params=params(16),
         cost_estimate=cost(2 * out_grad.size * width, 4 * out_grad.size),
-    )(scal, attn, out_grad, other, other_grad)
+    )(scal, attn_t, out_grad, other_t, other_grad)
 
 
 def backward_kernel(q_ref, k_ref, v_ref, draw_ref, prefix_ref, suffix_ref, glocal_ref,
@@ -353,7 +355,7 @@
 
 def project_far(scal, near, attn, pieces):
     tok, out_width = near.shape
-    block = 256
+    block = 512
     return pl.pallas_call(
         project_far_kernel,
         out_shape=shape_of((tok, out_width), BF16),
@@ -408,6 +410,7 @@
             scal, in_hbm(queries), in_hbm(keys), in_hbm(values), weight_hbm, grad_hbm
         )
         near_mine = lax.ppermute(near_piece, group, near)
+        far_mine = lax.ppermute(far_piece, group, far)
         other_grad = lax.ppermute(turn, "ctx", swap)
     else:
         state = local_state(keys, values)
@@ -423,15 +426,14 @@
     rest = rest[0] if n_ctx == 2 else jnp.concatenate(rest, 1)
     attn_grad = attn_gradient(scal, out_weight, out_grad, after(rest, state))
     carried = after(carried, attn_grad)
-    attn, raw, prefix = forward(queries, keys, values, carried)
+    attn, attn_t, raw, prefix = forward(queries, keys, values, carried)
 
     if paired:
-        far_mine = lax.ppermute(after(far_piece, attn), group, far)
         attn_1 = lax.ppermute(attn, group, one)
         attn_2 = lax.ppermute(attn, group, two)
         near_z = lax.ppermute(near_mine, "rep", zpair)
         raw = after(raw, near_mine, other_grad)
-    other_attn = [shift(attn, "ctx", n_ctx, k, True) for k in range(1, n_ctx)]
+    other_attn = [shift(attn_t, "ctx", n_ctx, k, True) for k in range(1, n_ctx)]
     other_attn = other_attn[0] if n_ctx == 2 else jnp.concatenate(other_attn, 0)
 
     draw, gsum, glocal, own_out = cotangent(
@@ -440,12 +442,12 @@
     suffix = total([shift(gsum, "ctx", n_ctx, -k, False) for k in range(1, n_ctx)])
 
     if paired:
-        other_attn = after(other_attn, gsum)
-
-    weight_grad = own_weight_grad(scal, attn, out_grad, other_attn, other_grad)
+        far_z = lax.ppermute(after(far_mine, gsum), ("ctx", "rep"), zpair)
+        other_attn = after(other_attn, gsum, far_mine)
+
+    weight_grad = own_weight_grad(scal, attn_t, out_grad, other_attn, other_grad)
 
     if paired:
-        far_z = lax.ppermute(after(far_mine, weight_grad), ("ctx", "rep"), zpair)
         near_other = lax.ppermute(after(near_mine, weight_grad), "ctx", swap)
         attn_3 = lax.ppermute(after(attn_1, weight_grad), group, two)
         near_other_z = lax.ppermute(after(near_z, weight_grad), "ctx", swap)
@@ -455,12 +457,11 @@
 
     if paired:
         far_other = lax.ppermute(after(far_mine, weight_grad), "ctx", [(0, 1)])
+        far_other_z = lax.ppermute(after(far_z, query_grad), "ctx", [(0, 1)])
         near_out = project_near(
-            scal, after(own_out, query_grad), (attn_1, attn_2),
+            scal, after(own_out, query_grad, attn_3), (attn_1, attn_2),
             (near_mine, near_z, near_other, near_other_z),
         )
-        last = after(far_z, near_out, attn_3, far_other)
-        far_other_z = lax.ppermute(last, "ctx", [(0, 1)])
         layer_out = project_far(scal, near_out, attn_3, (far_mine, far_other, far_z, far_other_z))
     else:
         full = lax.all_gather(out_weight, "ctx", axis=1, tiled=True)

time: 58.1 us -> 47.6 us (0.82)
  waiting for transfers between devices: 14.5 us -> 4.22 us
    ppermute x3, waiting for transfers between devices: 13.7 us -> 0.01 us  [the longest x1 0.01 us: body(): far_other_z = lax.ppermute(after(far_z, query_grad), 'ctx', [(0, 1)])]
    ppermute x4, starting transfers between devices: 3.6 us -> 6.14 us  [shift(): return lax.ppermute(array, axis, pairs)]
    ppermute x1, starting transfers between devices: 2.68 us -> 0.15 us  [body(): attn_2 = lax.ppermute(attn, group, two)]
    ppermute x1, waiting for transfers between devices: 0.01 us -> 2.43 us  [body(): attn_1 = lax.ppermute(attn, group, one)]
    ppermute x1, starting transfers between devices: 1.19 us -> 0.01 us  [body(): near_other = lax.ppermute(after(near_mine, weight_grad), 'ctx', swap)]
    ppermute x1, waiting for transfers between devices: 0.01 us -> 1 us  [body(): attn_3 = lax.ppermute(after(attn_1, weight_grad), group, two)]
    ppermute x1, waiting for transfers between devices: 0.85 us -> 0.01 us  [body(): near_mine = lax.ppermute(near_piece, group, near)]
    ppermute x1, waiting for transfers between devices: 0.01 us -> 0.75 us  [body(): near_z = lax.ppermute(near_mine, 'rep', zpair)]
  transfers between devices with their start and end apart: 16 -> 16, of which waited for: 4 -> 3; matrix products, arithmetic and copies ran while one was open for 0% -> 0% of each run, Pallas kernels for 34% -> 42%
where the time goes in v6:
time: 47.6 us; the launch traced here: 47.4 us
  Pallas kernels  21.8 us (46%)
  starting transfers between devices  20.4 us (43%)
  waiting for transfers between devices  4.22 us (9%)
  between operations  0.8 us (2%)
    ppermute x4, starting transfers between devices, shift(): return lax.ppermute(array, axis, pairs)  6.14 us
    pallas_call x1, Pallas kernels, own_weight_grad(): pl.pallas_call(weight_grad_kernel, out_shape=shape_of((width, own_width),...  3.95 us
    pallas_call x1, Pallas kernels, backward(): pl.pallas_call(backward_kernel, out_shape=(out, out, out), compiler_param...  3.79 us
    pallas_call x1, Pallas kernels, opening(): pl.pallas_call(opening_kernel, out_shape=(shape_of((width, DH), BF16), pi...  3.42 us
    ppermute x1, starting transfers between devices, body(): near_mine = lax.ppermute(near_piece, group, near)  2.94 us
    pallas_call x1, Pallas kernels, attn_gradient(): pl.pallas_call(attn_grad_kernel, out_shape=shape_of((tok, width), BF16),...  2.9 us
    ppermute x1, waiting for transfers between devices, body(): attn_1 = lax.ppermute(attn, group, one)  2.43 us
    ppermute x1, starting transfers between devices, body(): far_z = lax.ppermute(after(far_mine, gsum), ('ctx', 'rep'), zpair)  2.36 us
  transfers between devices with their start and end apart: 16, of which 3 were waited for; matrix products, arithmetic and copies ran while one was open for 0% of the time, Pallas kernels for 42%

profile of v6, /device:TPU:0, one launch (start us, length us, event | category | flops | bytes accessed | tf_op | source)
XLA Modules:
  0.0 47.4 jit_solution(3531914295905409408)
XLA Ops:
  0.6 0.5 %collective-permute-start = (bf16[512,2048]{1,0:T(8,128)(2,1)}, bf16[512,2048]{1,0:T(8,128)(2,1)S(1)}, u32[]{:S(2)}, u32[]{:S(2)}) collective-permute-start(bf16[512,2048]{1,0:T(8,128)(2,1)} %own_ref.3), channel_id=1, source_target_pairs={{0,16},{16,0},{1,17},{17,1},{2,18},{18,2},{3,19},{19,3},{4,20},{20... | collective-permute-start | bytes 6291464 | tf_op jit(solution)/shard_map/ppermute | solution.py:383
  1.1 0.1 pad_add_fusion.s_ref
  1.2 0.0 copy-start
  1.2 0.0 copy-start.1
  1.2 3.4 %shard_map.92 = (bf16[512,128]{1,0:T(8,128)(2,1)S(1)}, bf16[256,1024]{1,0:T(8,128)(2,1)S(1)}, bf16[256,1024]{1,0:T(8,128)(2,1)S(1)}, bf16[512,2048]{1,0:T(8,128)...) custom-call(s32[4]{0:T(128)S(1)} %pad_add_fusion.s_ref, ...), custom_call_target="tpu_custom_call" | custom-call | flops 67108864 | bytes 1048576 | tf_op jit(solution)/shard_map/pallas_call | solution.py:103
  4.7 0.1 collective-permute-start.3
  4.8 2.9 %collective-permute-start.2 = (bf16[256,1024]{1,0:T(8,128)(2,1)S(1)}, bf16[256,1024]{1,0:T(8,128)(2,1)S(1)}, u32[]{:S(2)}, u32[]{:S(2)}) collective-permute-start(bf16[256,1024]{1,0:T(8,128)(2,1)S(1)} %get-tuple-element.42), channel_id=1, source_target_pairs={{0,4},{4,0},{24,12},{28,8},{16,24},{20,28},{8,16},{12,20},{1,5},{5... | collective-permute-start | bytes 1572872 | tf_op jit(solution)/shard_map/ppermute | solution.py:412
  7.7 1.7 %collective-permute-start.1 = (bf16[512,128]{1,0:T(8,128)(2,1)S(1)}, bf16[512,128]{1,0:T(8,128)(2,1)S(1)}, u32[]{:S(2)}, u32[]{:S(2)}) collective-permute-start(bf16[512,128]{1,0:T(8,128)(2,1)S(1)} %get-tuple-element.35), channel_id=1, source_target_pairs={{0,16},{1,17},{2,18},{3,19},{4,20},{5,21},{6,22},{7,23},{8,24},{9,... | collective-permute-start | bytes 393224 | tf_op jit(solution)/shard_map/ppermute | solution.py:383
  9.4 1.3 %collective-permute-start.6 = (bf16[256,1024]{1,0:T(8,128)(2,1)S(1)}, bf16[256,1024]{1,0:T(8,128)(2,1)S(1)}, u32[]{:S(2)}, u32[]{:S(2)}) collective-permute-start(bf16[256,1024]{1,0:T(8,128)(2,1)S(1)} %get-tuple-element.51), channel_id=1, source_target_pairs={{16,12},{20,8},{8,4},{12,0},{17,13},{21,9},{9,5},{13,1},{18,14},{2... | collective-permute-start | bytes 1572872 | tf_op jit(solution)/shard_map/ppermute | solution.py:413
  10.7 0.0 collective-permute-done.rest_ref
  10.8 0.0 copy-done
  10.8 0.0 copy-done.1
  10.8 2.9 %shard_map.93.attn_grad_ref = bf16[512,512]{1,0:T(8,128)(2,1)S(1)} custom-call(s32[4]{0:T(128)S(1)} %pad_add_fusion.s_ref, bf16[512,2048]{1,0:T(8,128)(2,1)S(1)} %copy-done.1, bf16[512,4096]{1,0:T(8,128)(2,1)S(1)} %copy-done, bf16[512,2048]{1,0:T(8,128)(2,1)S(1)} %collective-permute-done.rest_ref), custom_call_target="tpu_custom_call" | custom-call | flops 2147483648 | bytes 8388608 | tf_op jit(solution)/shard_map/pallas_call | solution.py:181
  13.7 0.0 collective-permute-done.1.carried_ref
  13.7 1.6 %shard_map.94 = (bf16[512,512]{1,0:T(8,128)(2,1)S(1)}, bf16[512,512]{1,0:T(8,128)(2,1)S(1)}, f32[512,512]{1,0:T(8,128)S(1)}, bf16[2,512,128]{2,1,0:T(8,128)(2,1)S(1)}) custom-call(bf16[512,512]{1,0:T(8,128)(2,1)S(1)} %get-tuple-element.37.q_ref, bf16[512,512]{1,0:T(8,128)(2,1)S(1)} %get-tuple-element.38.k_ref, bf16[512,512]{1,0:T(8,128)(2,1)S(1)} %get-tuple-element.39.v_ref, ...), custom_call_target="tpu_custom_call" | custom-call | flops 536870912 | bytes 3145728 | tf_op jit(solution)/shard_map/pallas_call | solution.py:148
  15.3 2.6 %collective-permute-start.5 = (bf16[512,512]{1,0:T(8,128)(2,1)S(1)}, bf16[512,512]{1,0:T(8,128)(2,1)S(1)}, u32[]{:S(2)}, u32[]{:S(2)}) collective-permute-start(bf16[512,512]{1,0:T(8,128)(2,1)S(1)} %get-tuple-element.50.attn_t_ref), channel_id=1, source_target_pairs={{0,16},{16,0},{1,17},{17,1},{2,18},{18,2},{3,19},{19,3},{4,20},{20... | collective-permute-start | bytes 1572872 | tf_op jit(solution)/shard_map/ppermute | solution.py:383
  17.9 0.0 collective-permute-done.2.m1_ref
  17.9 1.6 %collective-permute-start.9 = (bf16[256,1024]{1,0:T(8,128)(2,1)S(1)}, bf16[256,1024]{1,0:T(8,128)(2,1)S(1)}, u32[]{:S(2)}, u32[]{:S(2)}) collective-permute-start(bf16[256,1024]{1,0:T(8,128)(2,1)S(1)} %collective-permute-done.2.m1_ref), channel_id=1, source_target_pairs={{0,1},{1,0},{2,3},{3,2},{4,5},{5,4},{6,7},{7,6},{8,9},{9,8},{10,11... | collective-permute-start | bytes 1572872 | tf_op jit(solution)/shard_map/ppermute | solution.py:434
  19.5 1.5 %collective-permute-start.7 = (bf16[512,512]{1,0:T(8,128)(2,1)S(1)}, bf16[512,512]{1,0:T(8,128)(2,1)S(1)}, u32[]{:S(2)}, u32[]{:S(2)}) collective-permute-start(bf16[512,512]{1,0:T(8,128)(2,1)S(1)} %get-tuple-element.45.attn_ref), channel_id=1, source_target_pairs={{0,4},{4,0},{8,12},{12,8},{16,24},{20,28},{24,16},{28,20},{1,5},{5... | collective-permute-start | bytes 1572872 | tf_op jit(solution)/shard_map/ppermute | solution.py:432
  21.0 0.0 collective-permute-done.3.other_grad_ref
  21.0 0.1 collective-permute-start.8
  21.1 2.3 %shard_map.95 = (bf16[512,512]{1,0:T(8,128)(2,1)S(1)}, bf16[512,128]{1,0:T(8,128)(2,1)S(1)}, f32[2,512,128]{2,1,0:T(8,128)S(1)}, f32[512,1024]{1,0:T(8,128)S(1)}) custom-call(s32[4]{0:T(128)S(1)} %pad_add_fusion.s_ref, bf16[512,512]{1,0:T(8,128)(2,1)S(1)} %shard_map.93.attn_grad_ref, bf16[512,512]{1,0:T(8,128)(2,1)S(1)} %get-tuple-element.37.q_ref, ...), custom_call_target="tpu_custom_call" | custom-call | flops 536870912 | bytes 4194304 | tf_op jit(solution)/shard_map/pallas_call | solution.py:221
  23.4 0.0 collective-permute-done.6.d_ref
  23.5 2.4 %collective-permute-start.14 = (bf16[256,1024]{1,0:T(8,128)(2,1)S(1)}, bf16[256,1024]{1,0:T(8,128)(2,1)S(1)}, u32[]{:S(2)}, u32[]{:S(2)}) collective-permute-start(bf16[256,1024]{1,0:T(8,128)(2,1)S(1)} %collective-permute-done.6.d_ref), channel_id=1, source_target_pairs={{0,1},{1,0},{2,3},{3,2},{4,5},{5,4},{6,7},{7,6},{8,9},{9,8},{10,11... | collective-permute-start | bytes 1572872 | tf_op jit(solution)/shard_map/ppermute | solution.py:445
  25.8 0.0 collective-permute-done.5.other_t_ref
  25.8 1.3 %collective-permute-start.4 = (bf16[512,128]{1,0:T(8,128)(2,1)S(1)}, bf16[512,128]{1,0:T(8,128)(2,1)S(1)}, u32[]{:S(2)}, u32[]{:S(2)}) collective-permute-start(bf16[512,128]{1,0:T(8,128)(2,1)S(1)} %get-tuple-element.49), channel_id=1, source_target_pairs={{16,0},{17,1},{18,2},{19,3},{20,4},{21,5},{22,6},{23,7},{24,8},{25... | collective-permute-start | bytes 393224 | tf_op jit(solution)/shard_map/ppermute | solution.py:383
  27.1 3.9 %shard_map.96 = f32[512,2048]{1,0:T(8,128)} custom-call(s32[4]{0:T(128)S(1)} %pad_add_fusion.s_ref, bf16[512,512]{1,0:T(8,128)(2,1)S(1)} %get-tuple-element.50.attn_t_ref, bf16[512,4096]{1,0:T(8,128)(2,1)S(1)} %copy-done, bf16[512,512]{1,0:T(8,128)(2,1)S(1)} %collective-permute-done.5.other_t_ref, bf16[512,2048]{1,0:T(8,128)(2,1)S(1)} %collective-permute-done.3.other_grad_ref), custom_call_target="tpu_custom_call" | custom-call | flops 2147483648 | bytes 8388608 | tf_op jit(solution)/shard_map/pallas_call | solution.py:259
  31.1 0.8 %collective-permute-done.9.z1_ref = bf16[256,1024]{1,0:T(8,128)(2,1)S(1)} collective-permute-done((bf16[256,1024]{1,0:T(8,128)(2,1)S(1)}, bf16[256,1024]{1,0:T(8,128)(2,1)S(1)}, u32[]{:S(2)}, u32[]{:S(2)}) %collective-permute-start.9) | collective-permute-done | bytes 524320 | tf_op jit(solution)/shard_map/ppermute | solution.py:434
  31.8 0.0 collective-permute-done.4.suffix_ref
  31.8 2.4 %collective-permute-done.7.a1_ref = bf16[512,512]{1,0:T(8,128)(2,1)S(1)} collective-permute-done((bf16[512,512]{1,0:T(8,128)(2,1)S(1)}, bf16[512,512]{1,0:T(8,128)(2,1)S(1)}, u32[]{:S(2)}, u32[]{:S(2)}) %collective-permute-start.7) | collective-permute-done | bytes 524320 | tf_op jit(solution)/shard_map/ppermute | solution.py:432
  34.3 0.0 collective-permute-done.8.a2_ref
  34.3 0.6 %collective-permute-start.10 = (bf16[512,512]{1,0:T(8,128)(2,1)S(1)}, bf16[512,512]{1,0:T(8,128)(2,1)S(1)}, u32[]{:S(2)}, u32[]{:S(2)}) collective-permute-start(bf16[512,512]{1,0:T(8,128)(2,1)S(1)} %collective-permute-done.7.a1_ref), channel_id=1, source_target_pairs={{0,8},{4,12},{8,0},{12,4},{16,20},{20,16},{24,28},{28,24},{1,9},{5... | collective-permute-start | bytes 1572872 | tf_op jit(solution)/shard_map/ppermute | solution.py:452
  34.9 0.0 collective-permute-start.11
  34.9 0.5 %collective-permute-start.12 = (bf16[256,1024]{1,0:T(8,128)(2,1)S(1)}, bf16[256,1024]{1,0:T(8,128)(2,1)S(1)}, u32[]{:S(2)}, u32[]{:S(2)}) collective-permute-start(bf16[256,1024]{1,0:T(8,128)(2,1)S(1)} %collective-permute-done.9.z1_ref), channel_id=1, source_target_pairs={{0,16},{16,0},{1,17},{17,1},{2,18},{18,2},{3,19},{19,3},{4,20},{20... | collective-permute-start | bytes 1572872 | tf_op jit(solution)/shard_map/ppermute | solution.py:453
  35.4 1.9 %collective-permute-start.13 = (bf16[256,1024]{1,0:T(8,128)(2,1)S(1)}, bf16[256,1024]{1,0:T(8,128)(2,1)S(1)}, u32[]{:S(2)}, u32[]{:S(2)}) collective-permute-start(bf16[256,1024]{1,0:T(8,128)(2,1)S(1)} %collective-permute-done.6.d_ref), channel_id=1, source_target_pairs={{0,16},{1,17},{2,18},{3,19},{4,20},{5,21},{6,22},{7,23},{8,24},{9,... | collective-permute-start | bytes 1572872 | tf_op jit(solution)/shard_map/ppermute | solution.py:459
  37.3 3.8 %shard_map.97 = (bf16[512,512]{1,0:T(8,128)(2,1)}, bf16[512,512]{1,0:T(8,128)(2,1)}, bf16[512,512]{1,0:T(8,128)(2,1)}) custom-call(bf16[512,512]{1,0:T(8,128)(2,1)S(1)} %get-tuple-element.37.q_ref, bf16[512,512]{1,0:T(8,128)(2,1)S(1)} %get-tuple-element.38.k_ref, bf16[512,512]{1,0:T(8,128)(2,1)S(1)} %get-tuple-element.39.v_ref, ...), custom_call_target="tpu_custom_call" | custom-call | flops 1073741824 | bytes 4194304 | tf_op jit(solution)/shard_map/pallas_call | solution.py:308
  41.1 0.0 collective-permute-done.14.dz_ref
  41.1 1.3 %collective-permute-start.15 = (bf16[256,1024]{1,0:T(8,128)(2,1)S(1)}, bf16[256,1024]{1,0:T(8,128)(2,1)S(1)}, u32[]{:S(2)}, u32[]{:S(2)}) collective-permute-start(bf16[256,1024]{1,0:T(8,128)(2,1)S(1)} %collective-permute-done.14.dz_ref), channel_id=1, source_target_pairs={{0,16},{1,17},{2,18},{3,19},{4,20},{5,21},{6,22},{7,23},{8,24},{9,... | collective-permute-start | bytes 1572872 | tf_op jit(solution)/shard_map/ppermute | solution.py:460
  42.5 1.0 %collective-permute-done.10.a_ref = bf16[512,512]{1,0:T(8,128)(2,1)S(1)} collective-permute-done((bf16[512,512]{1,0:T(8,128)(2,1)S(1)}, bf16[512,512]{1,0:T(8,128)(2,1)S(1)}, u32[]{:S(2)}, u32[]{:S(2)}) %collective-permute-start.10) | collective-permute-done | bytes 524320 | tf_op jit(solution)/shard_map/ppermute | solution.py:452
  43.5 0.0 collective-permute-done.11.o1_ref
  43.5 0.0 collective-permute-done.12.oz1_ref
  43.5 1.8 %shard_map.98.near_ref = f32[512,1024]{1,0:T(8,128)S(1)} custom-call(s32[4]{0:T(128)S(1)} %pad_add_fusion.s_ref, f32[512,1024]{1,0:T(8,128)S(1)} %get-tuple-element.57.so_far_ref, bf16[512,512]{1,0:T(8,128)(2,1)S(1)} %collective-permute-done.7.a1_ref, bf16[512,512]{1,0:T(8,128)(2,1)S(1)} %collective-permute-done.8.a2_ref, ...), custom_call_target="tpu_custom_call" | custom-call | flops 1000 | bytes 1000 | tf_op jit(solution)/shard_map/pallas_call | solution.py:332
  45.3 0.0 collective-permute-done.13.od_ref
  45.3 0.0 collective-permute-done.15.odz_ref
  45.3 2.1 %shard_map.99 = bf16[512,1024]{1,0:T(8,128)(2,1)} custom-call(s32[4]{0:T(128)S(1)} %pad_add_fusion.s_ref, f32[512,1024]{1,0:T(8,128)S(1)} %shard_map.98.near_ref, bf16[512,512]{1,0:T(8,128)(2,1)S(1)} %collective-permute-done.10.a_ref, bf16[256,1024]{1,0:T(8,128)(2,1)S(1)} %collective-permute-done.6.d_ref, ...), custom_call_target="tpu_custom_call" | custom-call | flops 1000 | bytes 1000 | tf_op jit(solution)/shard_map/pallas_call | solution.py:359
Async XLA Ops:
  0.6 10.1 %collective-permute-start = (bf16[512,2048]{1,0:T(8,128)(2,1)}, bf16[512,2048]{1,0:T(8,128)(2,1)S(1)}, u32[]{:S(2)}, u32[]{:S(2)}) collective-permute-start(bf16[512,2048]{1,0:T(8,128)(2,1)} %own_ref.3), channel_id=1, source_target_pairs={{0,16},{16,0},{1,17},{17,1},{2,18},{18,2},{3,19},{19,3},{4,20},{20... | collective-permute-start | bytes 6291464 | tf_op jit(solution)/shard_map/ppermute | solution.py:383
  1.2 9.5 %copy-start = (bf16[512,4096]{1,0:T(8,128)(2,1)S(1)}, bf16[512,4096]{1,0:T(8,128)(2,1)}, u32[]{:S(2)}) copy-start(bf16[512,4096]{1,0:T(8,128)(2,1)} %grad_ref.3) | copy-start | bytes 12582916
  1.2 9.5 %copy-start.1 = (bf16[512,2048]{1,0:T(8,128)(2,1)S(1)}, bf16[512,2048]{1,0:T(8,128)(2,1)}, u32[]{:S(2)}) copy-start(bf16[512,2048]{1,0:T(8,128)(2,1)} %own_ref.3) | copy-start | bytes 6291460
  4.7 16.3 %collective-permute-start.3 = (bf16[512,2048]{1,0:T(8,128)(2,1)S(1)}, bf16[512,2048]{1,0:T(8,128)(2,1)S(1)}, u32[]{:S(2)}, u32[]{:S(2)}) collective-permute-start(bf16[512,2048]{1,0:T(8,128)(2,1)S(1)} %get-tuple-element.43), channel_id=1, source_target_pairs={{0,16},{16,0},{1,17},{17,1},{2,18},{18,2},{3,19},{19,3},{4,20},{20... | collective-permute-start | bytes 6291464 | tf_op jit(solution)/shard_map/ppermute | solution.py:414
  4.8 13.1 %collective-permute-start.2 = (bf16[256,1024]{1,0:T(8,128)(2,1)S(1)}, bf16[256,1024]{1,0:T(8,128)(2,1)S(1)}, u32[]{:S(2)}, u32[]{:S(2)}) collective-permute-start(bf16[256,1024]{1,0:T(8,128)(2,1)S(1)} %get-tuple-element.42), channel_id=1, source_target_pairs={{0,4},{4,0},{24,12},{28,8},{16,24},{20,28},{8,16},{12,20},{1,5},{5... | collective-permute-start | bytes 1572872 | tf_op jit(solution)/shard_map/ppermute | solution.py:412
  7.7 6.0 %collective-permute-start.1 = (bf16[512,128]{1,0:T(8,128)(2,1)S(1)}, bf16[512,128]{1,0:T(8,128)(2,1)S(1)}, u32[]{:S(2)}, u32[]{:S(2)}) collective-permute-start(bf16[512,128]{1,0:T(8,128)(2,1)S(1)} %get-tuple-element.35), channel_id=1, source_target_pairs={{0,16},{1,17},{2,18},{3,19},{4,20},{5,21},{6,22},{7,23},{8,24},{9,... | collective-permute-start | bytes 393224 | tf_op jit(solution)/shard_map/ppermute | solution.py:383
  9.4 14.0 %collective-permute-start.6 = (bf16[256,1024]{1,0:T(8,128)(2,1)S(1)}, bf16[256,1024]{1,0:T(8,128)(2,1)S(1)}, u32[]{:S(2)}, u32[]{:S(2)}) collective-permute-start(bf16[256,1024]{1,0:T(8,128)(2,1)S(1)} %get-tuple-element.51), channel_id=1, source_target_pairs={{16,12},{20,8},{8,4},{12,0},{17,13},{21,9},{9,5},{13,1},{18,14},{2... | collective-permute-start | bytes 1572872 | tf_op jit(solution)/shard_map/ppermute | solution.py:413
  15.3 10.5 %collective-permute-start.5 = (bf16[512,512]{1,0:T(8,128)(2,1)S(1)}, bf16[512,512]{1,0:T(8,128)(2,1)S(1)}, u32[]{:S(2)}, u32[]{:S(2)}) collective-permute-start(bf16[512,512]{1,0:T(8,128)(2,1)S(1)} %get-tuple-element.50.attn_t_ref), channel_id=1, source_target_pairs={{0,16},{16,0},{1,17},{17,1},{2,18},{18,2},{3,19},{19,3},{4,20},{20... | collective-permute-start | bytes 1572872 | tf_op jit(solution)/shard_map/ppermute | solution.py:383
  17.9 13.9 %collective-permute-start.9 = (bf16[256,1024]{1,0:T(8,128)(2,1)S(1)}, bf16[256,1024]{1,0:T(8,128)(2,1)S(1)}, u32[]{:S(2)}, u32[]{:S(2)}) collective-permute-start(bf16[256,1024]{1,0:T(8,128)(2,1)S(1)} %collective-permute-done.2.m1_ref), channel_id=1, source_target_pairs={{0,1},{1,0},{2,3},{3,2},{4,5},{5,4},{6,7},{7,6},{8,9},{9,8},{10,11... | collective-permute-start | bytes 1572872 | tf_op jit(solution)/shard_map/ppermute | solution.py:434
  19.5 14.8 %collective-permute-start.7 = (bf16[512,512]{1,0:T(8,128)(2,1)S(1)}, bf16[512,512]{1,0:T(8,128)(2,1)S(1)}, u32[]{:S(2)}, u32[]{:S(2)}) collective-permute-start(bf16[512,512]{1,0:T(8,128)(2,1)S(1)} %get-tuple-element.45.attn_ref), channel_id=1, source_target_pairs={{0,4},{4,0},{8,12},{12,8},{16,24},{20,28},{24,16},{28,20},{1,5},{5... | collective-permute-start | bytes 1572872 | tf_op jit(solution)/shard_map/ppermute | solution.py:432
  21.0 13.3 %collective-permute-start.8 = (bf16[512,512]{1,0:T(8,128)(2,1)S(1)}, bf16[512,512]{1,0:T(8,128)(2,1)S(1)}, u32[]{:S(2)}, u32[]{:S(2)}) collective-permute-start(bf16[512,512]{1,0:T(8,128)(2,1)S(1)} %get-tuple-element.45.attn_ref), channel_id=1, source_target_pairs={{0,8},{4,12},{8,0},{12,4},{16,20},{20,16},{24,28},{28,24},{1,9},{5... | collective-permute-start | bytes 1572872 | tf_op jit(solution)/shard_map/ppermute | solution.py:433
  23.5 17.7 %collective-permute-start.14 = (bf16[256,1024]{1,0:T(8,128)(2,1)S(1)}, bf16[256,1024]{1,0:T(8,128)(2,1)S(1)}, u32[]{:S(2)}, u32[]{:S(2)}) collective-permute-start(bf16[256,1024]{1,0:T(8,128)(2,1)S(1)} %collective-permute-done.6.d_ref), channel_id=1, source_target_pairs={{0,1},{1,0},{2,3},{3,2},{4,5},{5,4},{6,7},{7,6},{8,9},{9,8},{10,11... | collective-permute-start | bytes 1572872 | tf_op jit(solution)/shard_map/ppermute | solution.py:445
  25.8 6.0 %collective-permute-start.4 = (bf16[512,128]{1,0:T(8,128)(2,1)S(1)}, bf16[512,128]{1,0:T(8,128)(2,1)S(1)}, u32[]{:S(2)}, u32[]{:S(2)}) collective-permute-start(bf16[512,128]{1,0:T(8,128)(2,1)S(1)} %get-tuple-element.49), channel_id=1, source_target_pairs={{16,0},{17,1},{18,2},{19,3},{20,4},{21,5},{22,6},{23,7},{24,8},{25... | collective-permute-start | bytes 393224 | tf_op jit(solution)/shard_map/ppermute | solution.py:383
  34.3 9.2 %collective-permute-start.10 = (bf16[512,512]{1,0:T(8,128)(2,1)S(1)}, bf16[512,512]{1,0:T(8,128)(2,1)S(1)}, u32[]{:S(2)}, u32[]{:S(2)}) collective-permute-start(bf16[512,512]{1,0:T(8,128)(2,1)S(1)} %collective-permute-done.7.a1_ref), channel_id=1, source_target_pairs={{0,8},{4,12},{8,0},{12,4},{16,20},{20,16},{24,28},{28,24},{1,9},{5... | collective-permute-start | bytes 1572872 | tf_op jit(solution)/shard_map/ppermute | solution.py:452
  34.9 8.6 %collective-permute-start.11 = (bf16[256,1024]{1,0:T(8,128)(2,1)S(1)}, bf16[256,1024]{1,0:T(8,128)(2,1)S(1)}, u32[]{:S(2)}, u32[]{:S(2)}) collective-permute-start(bf16[256,1024]{1,0:T(8,128)(2,1)S(1)} %collective-permute-done.2.m1_ref), channel_id=1, source_target_pairs={{0,16},{16,0},{1,17},{17,1},{2,18},{18,2},{3,19},{19,3},{4,20},{20... | collective-permute-start | bytes 1572872 | tf_op jit(solution)/shard_map/ppermute | solution.py:451
  34.9 8.6 %collective-permute-start.12 = (bf16[256,1024]{1,0:T(8,128)(2,1)S(1)}, bf16[256,1024]{1,0:T(8,128)(2,1)S(1)}, u32[]{:S(2)}, u32[]{:S(2)}) collective-permute-start(bf16[256,1024]{1,0:T(8,128)(2,1)S(1)} %collective-permute-done.9.z1_ref), channel_id=1, source_target_pairs={{0,16},{16,0},{1,17},{17,1},{2,18},{18,2},{3,19},{19,3},{4,20},{20... | collective-permute-start | bytes 1572872 | tf_op jit(solution)/shard_map/ppermute | solution.py:453
  35.4 9.9 %collective-permute-start.13 = (bf16[256,1024]{1,0:T(8,128)(2,1)S(1)}, bf16[256,1024]{1,0:T(8,128)(2,1)S(1)}, u32[]{:S(2)}, u32[]{:S(2)}) collective-permute-start(bf16[256,1024]{1,0:T(8,128)(2,1)S(1)} %collective-permute-done.6.d_ref), channel_id=1, source_target_pairs={{0,16},{1,17},{2,18},{3,19},{4,20},{5,21},{6,22},{7,23},{8,24},{9,... | collective-permute-start | bytes 1572872 | tf_op jit(solution)/shard_map/ppermute | solution.py:459
  41.1 4.2 %collective-permute-start.15 = (bf16[256,1024]{1,0:T(8,128)(2,1)S(1)}, bf16[256,1024]{1,0:T(8,128)(2,1)S(1)}, u32[]{:S(2)}, u32[]{:S(2)}) collective-permute-start(bf16[256,1024]{1,0:T(8,128)(2,1)S(1)} %collective-permute-done.14.dz_ref), channel_id=1, source_target_pairs={{0,16},{1,17},{2,18},{3,19},{4,20},{5,21},{6,22},{7,23},{8,24},{9,... | collective-permute-start | bytes 1572872 | tf_op jit(solution)/shard_map/ppermute | solution.py:460

commit v7 on v6

--- a/solution.py
+++ b/solution.py
@@ -232,9 +232,10 @@
     )(scal, attn_grad, queries, raw, attn, own, rest)
 
 
-def weight_grad_kernel(s_ref, attn_t_ref, grad_ref, other_t_ref, other_grad_ref, out_hbm, out_buf, sems):
+def weight_grad_kernel(s_ref, attn_t_ref, grad_ref, other_t_ref, other_grad_ref, out_hbm, late_ref, out_buf, sems):
     width, tok = attn_t_ref.shape
-    blocks, _, block = out_buf.shape
+    early, _, block = out_buf.shape
+    blocks = early + late_ref.shape[0]
     moves = []
     for j in range(blocks):
         here = slice(j * block, (j + 1) * block)
@@ -245,9 +246,12 @@
             other_t = other_t_ref[k * width : (k + 1) * width, :]
             part = other_grad_ref[k * tok : (k + 1) * tok, here]
             acc += dot_nn(other_t, part).astype(BF16).astype(F32)
-        out_buf[j] = acc
-        moves.append(pltpu.make_async_copy(out_buf.at[j], out_hbm.at[:, here], sems.at[j]))
-        moves[-1].start()
+        if j < early:
+            out_buf[j] = acc
+            moves.append(pltpu.make_async_copy(out_buf.at[j], out_hbm.at[:, here], sems.at[j]))
+            moves[-1].start()
+        else:
+            late_ref[j - early] = acc
     for move in moves:
         move.wait()
 
@@ -255,30 +259,42 @@
 def own_weight_grad(scal, attn_t, out_grad, other_t, other_grad):
     width = attn_t.shape[0]
     own_width = other_grad.shape[1]
-    block = min(512, own_width)
+    block = min(256, own_width // 2)
+    blocks = own_width // block
+    early = blocks // 2
     return pl.pallas_call(
         weight_grad_kernel,
-        out_shape=shape_of((width, own_width), F32),
+        out_shape=(
+            shape_of((width, own_width), F32),
+            shape_of((blocks - early, width, block), F32),
+        ),
         in_specs=smem_then_vmem(4),
-        out_specs=pl.BlockSpec(memory_space=pl.ANY),
+        out_specs=(pl.BlockSpec(memory_space=pl.ANY), pl.BlockSpec(memory_space=pltpu.VMEM)),
         scratch_shapes=[
-            pltpu.VMEM((own_width // block, width, block), F32),
-            pltpu.SemaphoreType.DMA((own_width // block,)),
+            pltpu.VMEM((early, width, block), F32),
+            pltpu.SemaphoreType.DMA((early,)),
         ],
         compiler_params=params(16),
-        cost_estimate=cost(2 * out_grad.size * width, 4 * out_grad.size),
+        cost_estimate=cost(1000, 1000),
     )(scal, attn_t, out_grad, other_t, other_grad)
 
 
-def backward_kernel(q_ref, k_ref, v_ref, draw_ref, prefix_ref, suffix_ref, glocal_ref,
-                    dq_ref, dk_ref, dv_ref):
+def backward_kernel(q_ref, k_ref, v_ref, draw_ref, prefix_ref, suffix_ref, glocal_ref, late_ref, early_hbm,
+                    dq_hbm, dk_hbm, dv_hbm, grad_hbm, dq_ref, dk_ref, dv_ref, sems, late_sems):
+    late, _, block = late_ref.shape
+    moves = []
+    for j in range(late):
+        start = grad_hbm.shape[1] - (late - j) * block
+        there = grad_hbm.at[:, start : start + block]
+        moves.append(pltpu.make_async_copy(late_ref.at[j], there, late_sems.at[j]))
+        moves[-1].start()
     tok, width = q_ref.shape
     chunk = min(CHUNK, tok)
     row = lax.broadcasted_iota(jnp.int32, (chunk, chunk), 0)
     col = lax.broadcasted_iota(jnp.int32, (chunk, chunk), 1)
     lower = row >= col
     upper = row <= col
-    for lo in range(0, width, DH):
+    for head, lo in enumerate(range(0, width, DH)):
         cols = slice(lo, lo + DH)
         suffix = suffix_ref[cols, :].astype(F32)
         for i in range(tok // chunk):
@@ -301,16 +317,28 @@
             scores_t = jnp.where(upper, dot_nt(fk, fq), 0.0).astype(BF16)
             dv = dot_nn(scores_t, draw) + dot_nn(fk, later)
             dv_ref[rows, cols] = dv.astype(BF16)
-
-
-def backward(queries, keys, values, draw, prefix, suffix, glocal):
+        for n, (ref, hbm) in enumerate([(dq_ref, dq_hbm), (dk_ref, dk_hbm), (dv_ref, dv_hbm)]):
+            moves.append(pltpu.make_async_copy(ref.at[:, cols], hbm.at[:, cols], sems.at[n, head]))
+            moves[-1].start()
+    for move in moves:
+        move.wait()
+
+
+def backward(queries, keys, values, draw, prefix, suffix, glocal, late, early):
+    tok, width = queries.shape
     out = shape_of(queries.shape, BF16)
+    vmem, hbm = pl.BlockSpec(memory_space=pltpu.VMEM), pl.BlockSpec(memory_space=pl.ANY)
     return pl.pallas_call(
         backward_kernel,
-        out_shape=(out, out, out),
-        compiler_params=params(16),
-        cost_estimate=cost(32 * queries.size * DH, 16 * queries.size),
-    )(queries, keys, values, draw, prefix, suffix, glocal)
+        out_shape=(out, out, out, shape_of(early.shape, F32)),
+        in_specs=[vmem] * 8 + [hbm],
+        out_specs=(hbm,) * 4,
+        scratch_shapes=[pltpu.VMEM((tok, width), BF16)] * 3
+        + [pltpu.SemaphoreType.DMA((3, width // DH)), pltpu.SemaphoreType.DMA((late.shape[0],))],
+        input_output_aliases={8: 3},
+        compiler_params=params(16),
+        cost_estimate=cost(1000, 1000),
+    )(queries, keys, values, draw, prefix, suffix, glocal, late, early)
 
 
 def halves(s_ref, half):
@@ -445,23 +473,25 @@
         far_z = lax.ppermute(after(far_mine, gsum), ("ctx", "rep"), zpair)
         other_attn = after(other_attn, gsum, far_mine)
 
-    weight_grad = own_weight_grad(scal, attn_t, out_grad, other_attn, other_grad)
+    early, late = own_weight_grad(scal, attn_t, out_grad, other_attn, other_grad)
 
     if paired:
-        near_other = lax.ppermute(after(near_mine, weight_grad), "ctx", swap)
-        attn_3 = lax.ppermute(after(attn_1, weight_grad), group, two)
-        near_other_z = lax.ppermute(after(near_z, weight_grad), "ctx", swap)
-        suffix = after(suffix, weight_grad, attn_1, attn_2, near_z)
-
-    query_grad, key_grad, value_grad = backward(queries, keys, values, draw, prefix, suffix, glocal)
+        near_other = lax.ppermute(after(near_mine, late), "ctx", swap)
+        suffix = after(suffix, late, attn_1)
+
+    query_grad, key_grad, value_grad, weight_grad = backward(
+        queries, keys, values, draw, prefix, suffix, glocal, late, early
+    )
 
     if paired:
-        far_other = lax.ppermute(after(far_mine, weight_grad), "ctx", [(0, 1)])
-        far_other_z = lax.ppermute(after(far_z, query_grad), "ctx", [(0, 1)])
+        attn_3 = lax.ppermute(after(attn_1, late), group, two)
+        near_other_z = lax.ppermute(after(near_z, late), "ctx", swap)
+        far_other = lax.ppermute(after(far_mine, late), "ctx", [(0, 1)])
         near_out = project_near(
-            scal, after(own_out, query_grad, attn_3), (attn_1, attn_2),
+            scal, after(own_out, query_grad), (attn_1, attn_2),
             (near_mine, near_z, near_other, near_other_z),
         )
+        far_other_z = lax.ppermute(after(far_z, query_grad), "ctx", [(0, 1)])
         layer_out = project_far(scal, near_out, attn_3, (far_mine, far_other, far_z, far_other_z))
     else:
         full = lax.all_gather(out_weight, "ctx", axis=1, tiled=True)

time: 47.6 us -> 46.7 us (0.981)
  waiting for transfers between devices: 4.22 us -> 1.44 us
  starting transfers between devices: 20.4 us -> 22.4 us
    ppermute x1, waiting for transfers between devices: 2.43 us -> 1.25 us  [body(): attn_1 = lax.ppermute(attn, group, one)]
    ppermute x4, waiting for transfers between devices: 1.01 us -> 0.01 us  [the longest x1 0.01 us: body(): near_other = lax.ppermute(after(near_mine, late), 'ctx', swap)]
    ppermute x1, starting transfers between devices: 0.15 us -> 1.05 us  [body(): attn_2 = lax.ppermute(attn, group, two)]
    ppermute x1, starting transfers between devices: 1.58 us -> 2.47 us  [body(): near_z = lax.ppermute(near_mine, 'rep', zpair)]
    ppermute x1, waiting for transfers between devices: 0.75 us -> 0.01 us  [body(): near_z = lax.ppermute(near_mine, 'rep', zpair)]
    ppermute x4, starting transfers between devices: 3.05 us -> 3.67 us  [the longest x1 2.59 us: body(): far_other = lax.ppermute(after(far_mine, late), 'ctx', [(0, 1)])]
  transfers between devices with their start and end apart: 16 -> 16, of which waited for: 3 -> 2; matrix products, arithmetic and copies ran while one was open for 0% -> 0% of each run, Pallas kernels for 42% -> 42%
where the time goes in v7:
time: 46.7 us; the launch traced here: 46.5 us
  starting transfers between devices  22.4 us (48%)
  Pallas kernels  21.7 us (46%)
  waiting for transfers between devices  1.44 us (3%)
  between operations  0.85 us (2%)
    ppermute x4, starting transfers between devices, shift(): return lax.ppermute(array, axis, pairs)  5.68 us
    pallas_call x1, Pallas kernels, backward(): pl.pallas_call(backward_kernel, out_shape=(out, out, out, shape_of(early....  4.12 us
    pallas_call x1, Pallas kernels, own_weight_grad(): pl.pallas_call(weight_grad_kernel, out_shape=(shape_of((width, own_width)...  3.5 us
    pallas_call x1, Pallas kernels, opening(): pl.pallas_call(opening_kernel, out_shape=(shape_of((width, DH), BF16), pi...  3.42 us
    ppermute x1, starting transfers between devices, body(): near_mine = lax.ppermute(near_piece, group, near)  2.94 us
    pallas_call x1, Pallas kernels, attn_gradient(): pl.pallas_call(attn_grad_kernel, out_shape=shape_of((tok, width), BF16),...  2.9 us
    ppermute x1, starting transfers between devices, body(): far_other = lax.ppermute(after(far_mine, late), 'ctx', [(0, 1)])  2.59 us
    ppermute x1, starting transfers between devices, body(): near_z = lax.ppermute(near_mine, 'rep', zpair)  2.47 us
  transfers between devices with their start and end apart: 16, of which 2 were waited for; matrix products, arithmetic and copies ran while one was open for 0% of the time, Pallas kernels for 42%

profile of v7, /device:TPU:0, one launch (start us, length us, event | category | flops | bytes accessed | tf_op | source)
XLA Modules:
  0.0 46.5 jit_solution(14316644714603876808)
XLA Ops:
  0.6 0.5 %collective-permute-start = (bf16[512,2048]{1,0:T(8,128)(2,1)}, bf16[512,2048]{1,0:T(8,128)(2,1)S(1)}, u32[]{:S(2)}, u32[]{:S(2)}) collective-permute-start(bf16[512,2048]{1,0:T(8,128)(2,1)} %own_ref.3), channel_id=1, source_target_pairs={{0,16},{16,0},{1,17},{17,1},{2,18},{18,2},{3,19},{19,3},{4,20},{20... | collective-permute-start | bytes 6291464 | tf_op jit(solution)/shard_map/ppermute | solution.py:411
  1.1 0.1 pad_add_fusion.s_ref
  1.2 0.0 copy-start
  1.2 0.0 copy-start.1
  1.2 3.4 %shard_map.92 = (bf16[512,128]{1,0:T(8,128)(2,1)S(1)}, bf16[256,1024]{1,0:T(8,128)(2,1)S(1)}, bf16[256,1024]{1,0:T(8,128)(2,1)S(1)}, bf16[512,2048]{1,0:T(8,128)...) custom-call(s32[4]{0:T(128)S(1)} %pad_add_fusion.s_ref, ...), custom_call_target="tpu_custom_call" | custom-call | flops 67108864 | bytes 1048576 | tf_op jit(solution)/shard_map/pallas_call | solution.py:103
  4.7 0.1 collective-permute-start.3
  4.8 2.9 %collective-permute-start.2 = (bf16[256,1024]{1,0:T(8,128)(2,1)S(1)}, bf16[256,1024]{1,0:T(8,128)(2,1)S(1)}, u32[]{:S(2)}, u32[]{:S(2)}) collective-permute-start(bf16[256,1024]{1,0:T(8,128)(2,1)S(1)} %get-tuple-element.45), channel_id=1, source_target_pairs={{0,4},{4,0},{24,12},{28,8},{16,24},{20,28},{8,16},{12,20},{1,5},{5... | collective-permute-start | bytes 1572872 | tf_op jit(solution)/shard_map/ppermute | solution.py:440
  7.7 1.3 %collective-permute-start.6 = (bf16[256,1024]{1,0:T(8,128)(2,1)S(1)}, bf16[256,1024]{1,0:T(8,128)(2,1)S(1)}, u32[]{:S(2)}, u32[]{:S(2)}) collective-permute-start(bf16[256,1024]{1,0:T(8,128)(2,1)S(1)} %get-tuple-element.54), channel_id=1, source_target_pairs={{16,12},{20,8},{8,4},{12,0},{17,13},{21,9},{9,5},{13,1},{18,14},{2... | collective-permute-start | bytes 1572872 | tf_op jit(solution)/shard_map/ppermute | solution.py:441
  9.0 3.8 %collective-permute-start.1 = (bf16[512,128]{1,0:T(8,128)(2,1)S(1)}, bf16[512,128]{1,0:T(8,128)(2,1)S(1)}, u32[]{:S(2)}, u32[]{:S(2)}) collective-permute-start(bf16[512,128]{1,0:T(8,128)(2,1)S(1)} %get-tuple-element.38), channel_id=1, source_target_pairs={{0,16},{1,17},{2,18},{3,19},{4,20},{5,21},{6,22},{7,23},{8,24},{9,... | collective-permute-start | bytes 393224 | tf_op jit(solution)/shard_map/ppermute | solution.py:411
  12.8 0.0 collective-permute-done.rest_ref
  12.8 0.0 copy-done
  12.8 0.0 copy-done.1
  12.8 2.9 %shard_map.93.attn_grad_ref = bf16[512,512]{1,0:T(8,128)(2,1)S(1)} custom-call(s32[4]{0:T(128)S(1)} %pad_add_fusion.s_ref, bf16[512,2048]{1,0:T(8,128)(2,1)S(1)} %copy-done.1, bf16[512,4096]{1,0:T(8,128)(2,1)S(1)} %copy-done, bf16[512,2048]{1,0:T(8,128)(2,1)S(1)} %collective-permute-done.rest_ref), custom_call_target="tpu_custom_call" | custom-call | flops 2147483648 | bytes 8388608 | tf_op jit(solution)/shard_map/pallas_call | solution.py:181
  15.8 0.0 collective-permute-done.1.carried_ref
  15.8 1.6 %shard_map.94 = (bf16[512,512]{1,0:T(8,128)(2,1)S(1)}, bf16[512,512]{1,0:T(8,128)(2,1)S(1)}, f32[512,512]{1,0:T(8,128)S(1)}, bf16[2,512,128]{2,1,0:T(8,128)(2,1)S(1)}) custom-call(bf16[512,512]{1,0:T(8,128)(2,1)S(1)} %get-tuple-element.40.q_ref, bf16[512,512]{1,0:T(8,128)(2,1)S(1)} %get-tuple-element.41.k_ref, bf16[512,512]{1,0:T(8,128)(2,1)S(1)} %get-tuple-element.42.v_ref, ...), custom_call_target="tpu_custom_call" | custom-call | flops 536870912 | bytes 3145728 | tf_op jit(solution)/shard_map/pallas_call | solution.py:148
  17.4 0.1 collective-permute-start.5
  17.5 0.2 collective-permute-done.2.m1_ref
  17.6 2.5 %collective-permute-start.9 = (bf16[256,1024]{1,0:T(8,128)(2,1)S(1)}, bf16[256,1024]{1,0:T(8,128)(2,1)S(1)}, u32[]{:S(2)}, u32[]{:S(2)}) collective-permute-start(bf16[256,1024]{1,0:T(8,128)(2,1)S(1)} %collective-permute-done.2.m1_ref), channel_id=1, source_target_pairs={{0,1},{1,0},{2,3},{3,2},{4,5},{5,4},{6,7},{7,6},{8,9},{9,8},{10,11... | collective-permute-start | bytes 1572872 | tf_op jit(solution)/shard_map/ppermute | solution.py:462
  20.1 0.0 collective-permute-done.3.other_grad_ref
  20.1 1.5 %collective-permute-start.7 = (bf16[512,512]{1,0:T(8,128)(2,1)S(1)}, bf16[512,512]{1,0:T(8,128)(2,1)S(1)}, u32[]{:S(2)}, u32[]{:S(2)}) collective-permute-start(bf16[512,512]{1,0:T(8,128)(2,1)S(1)} %get-tuple-element.48.attn_ref), channel_id=1, source_target_pairs={{0,4},{4,0},{8,12},{12,8},{16,24},{20,28},{24,16},{28,20},{1,5},{5... | collective-permute-start | bytes 1572872 | tf_op jit(solution)/shard_map/ppermute | solution.py:460
  21.6 2.3 %shard_map.95 = (bf16[512,512]{1,0:T(8,128)(2,1)S(1)}, bf16[512,128]{1,0:T(8,128)(2,1)S(1)}, f32[2,512,128]{2,1,0:T(8,128)S(1)}, f32[512,1024]{1,0:T(8,128)S(1)}) custom-call(s32[4]{0:T(128)S(1)} %pad_add_fusion.s_ref, bf16[512,512]{1,0:T(8,128)(2,1)S(1)} %shard_map.93.attn_grad_ref, bf16[512,512]{1,0:T(8,128)(2,1)S(1)} %get-tuple-element.40.q_ref, ...), custom_call_target="tpu_custom_call" | custom-call | flops 536870912 | bytes 4194304 | tf_op jit(solution)/shard_map/pallas_call | solution.py:221
  23.9 0.0 collective-permute-done.6.d_ref
  23.9 2.4 %collective-permute-start.14 = (bf16[256,1024]{1,0:T(8,128)(2,1)S(1)}, bf16[256,1024]{1,0:T(8,128)(2,1)S(1)}, u32[]{:S(2)}, u32[]{:S(2)}) collective-permute-start(bf16[256,1024]{1,0:T(8,128)(2,1)S(1)} %collective-permute-done.6.d_ref), channel_id=1, source_target_pairs={{0,1},{1,0},{2,3},{3,2},{4,5},{5,4},{6,7},{7,6},{8,9},{9,8},{10,11... | collective-permute-start | bytes 1572872 | tf_op jit(solution)/shard_map/ppermute | solution.py:473
  26.3 1.1 %collective-permute-start.8 = (bf16[512,512]{1,0:T(8,128)(2,1)S(1)}, bf16[512,512]{1,0:T(8,128)(2,1)S(1)}, u32[]{:S(2)}, u32[]{:S(2)}) collective-permute-start(bf16[512,512]{1,0:T(8,128)(2,1)S(1)} %get-tuple-element.48.attn_ref), channel_id=1, source_target_pairs={{0,8},{4,12},{8,0},{12,4},{16,20},{20,16},{24,28},{28,24},{1,9},{5... | collective-permute-start | bytes 1572872 | tf_op jit(solution)/shard_map/ppermute | solution.py:461
  27.3 0.0 collective-permute-done.5.other_t_ref
  27.3 1.3 %collective-permute-start.4 = (bf16[512,128]{1,0:T(8,128)(2,1)S(1)}, bf16[512,128]{1,0:T(8,128)(2,1)S(1)}, u32[]{:S(2)}, u32[]{:S(2)}) collective-permute-start(bf16[512,128]{1,0:T(8,128)(2,1)S(1)} %get-tuple-element.52), channel_id=1, source_target_pairs={{16,0},{17,1},{18,2},{19,3},{20,4},{21,5},{22,6},{23,7},{24,8},{25... | collective-permute-start | bytes 393224 | tf_op jit(solution)/shard_map/ppermute | solution.py:411
  28.6 3.5 %shard_map.96 = (f32[512,2048]{1,0:T(8,128)}, f32[4,512,256]{2,1,0:T(8,128)S(1)}) custom-call(s32[4]{0:T(128)S(1)} %pad_add_fusion.s_ref, bf16[512,512]{1,0:T(8,128)(2,1)S(1)} %get-tuple-element.53.attn_t_ref, bf16[512,4096]{1,0:T(8,128)(2,1)S(1)} %copy-done, bf16[512,512]{1,0:T(8,128)(2,1)S(1)} %collective-permute-done.5.other_t_ref, ...), custom_call_target="tpu_custom_call" | custom-call | flops 1000 | bytes 1000 | tf_op jit(solution)/shard_map/pallas_call | solution.py:265
  32.1 0.0 collective-permute-done.4.suffix_ref
  32.1 1.3 %collective-permute-done.7.a1_ref = bf16[512,512]{1,0:T(8,128)(2,1)S(1)} collective-permute-done((bf16[512,512]{1,0:T(8,128)(2,1)S(1)}, bf16[512,512]{1,0:T(8,128)(2,1)S(1)}, u32[]{:S(2)}, u32[]{:S(2)}) %collective-permute-start.7) | collective-permute-done | bytes 524320 | tf_op jit(solution)/shard_map/ppermute | solution.py:460
  33.4 0.0 collective-permute-start.10
  33.4 0.0 collective-permute-done.9.z1_ref
  33.4 0.5 %collective-permute-start.11 = (bf16[256,1024]{1,0:T(8,128)(2,1)S(1)}, bf16[256,1024]{1,0:T(8,128)(2,1)S(1)}, u32[]{:S(2)}, u32[]{:S(2)}) collective-permute-start(bf16[256,1024]{1,0:T(8,128)(2,1)S(1)} %collective-permute-done.9.z1_ref), channel_id=1, source_target_pairs={{0,16},{16,0},{1,17},{17,1},{2,18},{18,2},{3,19},{19,3},{4,20},{20... | collective-permute-start | bytes 1572872 | tf_op jit(solution)/shard_map/ppermute | solution.py:488
  33.9 0.6 %collective-permute-start.12 = (bf16[512,512]{1,0:T(8,128)(2,1)S(1)}, bf16[512,512]{1,0:T(8,128)(2,1)S(1)}, u32[]{:S(2)}, u32[]{:S(2)}) collective-permute-start(bf16[512,512]{1,0:T(8,128)(2,1)S(1)} %collective-permute-done.7.a1_ref), channel_id=1, source_target_pairs={{0,8},{4,12},{8,0},{12,4},{16,20},{20,16},{24,28},{28,24},{1,9},{5... | collective-permute-start | bytes 1572872 | tf_op jit(solution)/shard_map/ppermute | solution.py:487
  34.5 4.1 %shard_map.97 = (bf16[512,512]{1,0:T(8,128)(2,1)}, bf16[512,512]{1,0:T(8,128)(2,1)}, bf16[512,512]{1,0:T(8,128)(2,1)}, f32[512,2048]{1,0:T(8,128)}) custom-call(bf16[512,512]{1,0:T(8,128)(2,1)S(1)} %get-tuple-element.40.q_ref, bf16[512,512]{1,0:T(8,128)(2,1)S(1)} %get-tuple-element.41.k_ref, ...), custom_call_target="tpu_custom_call", output_to_operand_aliasing={{3}: (8, {})} | custom-call | flops 1000 | bytes 1000 | tf_op jit(solution)/shard_map/pallas_call | solution.py:331
  38.6 0.0 collective-permute-done.14.dz_ref
  38.6 2.6 %collective-permute-start.13 = (bf16[256,1024]{1,0:T(8,128)(2,1)S(1)}, bf16[256,1024]{1,0:T(8,128)(2,1)S(1)}, u32[]{:S(2)}, u32[]{:S(2)}) collective-permute-start(bf16[256,1024]{1,0:T(8,128)(2,1)S(1)} %collective-permute-done.6.d_ref), channel_id=1, source_target_pairs={{0,16},{1,17},{2,18},{3,19},{4,20},{5,21},{6,22},{7,23},{8,24},{9,... | collective-permute-start | bytes 1572872 | tf_op jit(solution)/shard_map/ppermute | solution.py:489
  41.2 0.0 collective-permute-done.8.a2_ref
  41.2 1.3 %collective-permute-start.15 = (bf16[256,1024]{1,0:T(8,128)(2,1)S(1)}, bf16[256,1024]{1,0:T(8,128)(2,1)S(1)}, u32[]{:S(2)}, u32[]{:S(2)}) collective-permute-start(bf16[256,1024]{1,0:T(8,128)(2,1)S(1)} %collective-permute-done.14.dz_ref), channel_id=1, source_target_pairs={{0,16},{1,17},{2,18},{3,19},{4,20},{5,21},{6,22},{7,23},{8,24},{9,... | collective-permute-start | bytes 1572872 | tf_op jit(solution)/shard_map/ppermute | solution.py:494
  42.5 0.0 collective-permute-done.10.o1_ref
  42.5 0.0 collective-permute-done.11.oz1_ref
  42.6 1.8 %shard_map.98.near_ref = f32[512,1024]{1,0:T(8,128)S(1)} custom-call(s32[4]{0:T(128)S(1)} %pad_add_fusion.s_ref, f32[512,1024]{1,0:T(8,128)S(1)} %get-tuple-element.61.so_far_ref, bf16[512,512]{1,0:T(8,128)(2,1)S(1)} %collective-permute-done.7.a1_ref, bf16[512,512]{1,0:T(8,128)(2,1)S(1)} %collective-permute-done.8.a2_ref, ...), custom_call_target="tpu_custom_call" | custom-call | flops 1000 | bytes 1000 | tf_op jit(solution)/shard_map/pallas_call | solution.py:360
  44.4 0.0 collective-permute-done.12.a_ref
  44.4 0.0 collective-permute-done.13.od_ref
  44.4 0.0 collective-permute-done.15.odz_ref
  44.4 2.1 %shard_map.99 = bf16[512,1024]{1,0:T(8,128)(2,1)} custom-call(s32[4]{0:T(128)S(1)} %pad_add_fusion.s_ref, f32[512,1024]{1,0:T(8,128)S(1)} %shard_map.98.near_ref, bf16[512,512]{1,0:T(8,128)(2,1)S(1)} %collective-permute-done.12.a_ref, bf16[256,1024]{1,0:T(8,128)(2,1)S(1)} %collective-permute-done.6.d_ref, ...), custom_call_target="tpu_custom_call" | custom-call | flops 1000 | bytes 1000 | tf_op jit(solution)/shard_map/pallas_call | solution.py:387
Async XLA Ops:
  0.6 12.2 %collective-permute-start = (bf16[512,2048]{1,0:T(8,128)(2,1)}, bf16[512,2048]{1,0:T(8,128)(2,1)S(1)}, u32[]{:S(2)}, u32[]{:S(2)}) collective-permute-start(bf16[512,2048]{1,0:T(8,128)(2,1)} %own_ref.3), channel_id=1, source_target_pairs={{0,16},{16,0},{1,17},{17,1},{2,18},{18,2},{3,19},{19,3},{4,20},{20... | collective-permute-start | bytes 6291464 | tf_op jit(solution)/shard_map/ppermute | solution.py:411
  1.2 11.6 %copy-start = (bf16[512,4096]{1,0:T(8,128)(2,1)S(1)}, bf16[512,4096]{1,0:T(8,128)(2,1)}, u32[]{:S(2)}) copy-start(bf16[512,4096]{1,0:T(8,128)(2,1)} %grad_ref.3) | copy-start | bytes 12582916
  1.2 11.6 %copy-start.1 = (bf16[512,2048]{1,0:T(8,128)(2,1)S(1)}, bf16[512,2048]{1,0:T(8,128)(2,1)}, u32[]{:S(2)}) copy-start(bf16[512,2048]{1,0:T(8,128)(2,1)} %own_ref.3) | copy-start | bytes 6291460
  4.7 15.4 %collective-permute-start.3 = (bf16[512,2048]{1,0:T(8,128)(2,1)S(1)}, bf16[512,2048]{1,0:T(8,128)(2,1)S(1)}, u32[]{:S(2)}, u32[]{:S(2)}) collective-permute-start(bf16[512,2048]{1,0:T(8,128)(2,1)S(1)} %get-tuple-element.46), channel_id=1, source_target_pairs={{0,16},{16,0},{1,17},{17,1},{2,18},{18,2},{3,19},{19,3},{4,20},{20... | collective-permute-start | bytes 6291464 | tf_op jit(solution)/shard_map/ppermute | solution.py:442
  4.8 12.8 %collective-permute-start.2 = (bf16[256,1024]{1,0:T(8,128)(2,1)S(1)}, bf16[256,1024]{1,0:T(8,128)(2,1)S(1)}, u32[]{:S(2)}, u32[]{:S(2)}) collective-permute-start(bf16[256,1024]{1,0:T(8,128)(2,1)S(1)} %get-tuple-element.45), channel_id=1, source_target_pairs={{0,4},{4,0},{24,12},{28,8},{16,24},{20,28},{8,16},{12,20},{1,5},{5... | collective-permute-start | bytes 1572872 | tf_op jit(solution)/shard_map/ppermute | solution.py:440
  7.7 16.2 %collective-permute-start.6 = (bf16[256,1024]{1,0:T(8,128)(2,1)S(1)}, bf16[256,1024]{1,0:T(8,128)(2,1)S(1)}, u32[]{:S(2)}, u32[]{:S(2)}) collective-permute-start(bf16[256,1024]{1,0:T(8,128)(2,1)S(1)} %get-tuple-element.54), channel_id=1, source_target_pairs={{16,12},{20,8},{8,4},{12,0},{17,13},{21,9},{9,5},{13,1},{18,14},{2... | collective-permute-start | bytes 1572872 | tf_op jit(solution)/shard_map/ppermute | solution.py:441
  9.0 6.8 %collective-permute-start.1 = (bf16[512,128]{1,0:T(8,128)(2,1)S(1)}, bf16[512,128]{1,0:T(8,128)(2,1)S(1)}, u32[]{:S(2)}, u32[]{:S(2)}) collective-permute-start(bf16[512,128]{1,0:T(8,128)(2,1)S(1)} %get-tuple-element.38), channel_id=1, source_target_pairs={{0,16},{1,17},{2,18},{3,19},{4,20},{5,21},{6,22},{7,23},{8,24},{9,... | collective-permute-start | bytes 393224 | tf_op jit(solution)/shard_map/ppermute | solution.py:411
  17.4 9.9 %collective-permute-start.5 = (bf16[512,512]{1,0:T(8,128)(2,1)S(1)}, bf16[512,512]{1,0:T(8,128)(2,1)S(1)}, u32[]{:S(2)}, u32[]{:S(2)}) collective-permute-start(bf16[512,512]{1,0:T(8,128)(2,1)S(1)} %get-tuple-element.53.attn_t_ref), channel_id=1, source_target_pairs={{0,16},{16,0},{1,17},{17,1},{2,18},{18,2},{3,19},{19,3},{4,20},{20... | collective-permute-start | bytes 1572872 | tf_op jit(solution)/shard_map/ppermute | solution.py:411
  17.6 15.8 %collective-permute-start.9 = (bf16[256,1024]{1,0:T(8,128)(2,1)S(1)}, bf16[256,1024]{1,0:T(8,128)(2,1)S(1)}, u32[]{:S(2)}, u32[]{:S(2)}) collective-permute-start(bf16[256,1024]{1,0:T(8,128)(2,1)S(1)} %collective-permute-done.2.m1_ref), channel_id=1, source_target_pairs={{0,1},{1,0},{2,3},{3,2},{4,5},{5,4},{6,7},{7,6},{8,9},{9,8},{10,11... | collective-permute-start | bytes 1572872 | tf_op jit(solution)/shard_map/ppermute | solution.py:462
  20.1 13.3 %collective-permute-start.7 = (bf16[512,512]{1,0:T(8,128)(2,1)S(1)}, bf16[512,512]{1,0:T(8,128)(2,1)S(1)}, u32[]{:S(2)}, u32[]{:S(2)}) collective-permute-start(bf16[512,512]{1,0:T(8,128)(2,1)S(1)} %get-tuple-element.48.attn_ref), channel_id=1, source_target_pairs={{0,4},{4,0},{8,12},{12,8},{16,24},{20,28},{24,16},{28,20},{1,5},{5... | collective-permute-start | bytes 1572872 | tf_op jit(solution)/shard_map/ppermute | solution.py:460
  23.9 14.7 %collective-permute-start.14 = (bf16[256,1024]{1,0:T(8,128)(2,1)S(1)}, bf16[256,1024]{1,0:T(8,128)(2,1)S(1)}, u32[]{:S(2)}, u32[]{:S(2)}) collective-permute-start(bf16[256,1024]{1,0:T(8,128)(2,1)S(1)} %collective-permute-done.6.d_ref), channel_id=1, source_target_pairs={{0,1},{1,0},{2,3},{3,2},{4,5},{5,4},{6,7},{7,6},{8,9},{9,8},{10,11... | collective-permute-start | bytes 1572872 | tf_op jit(solution)/shard_map/ppermute | solution.py:473
  26.3 14.9 %collective-permute-start.8 = (bf16[512,512]{1,0:T(8,128)(2,1)S(1)}, bf16[512,512]{1,0:T(8,128)(2,1)S(1)}, u32[]{:S(2)}, u32[]{:S(2)}) collective-permute-start(bf16[512,512]{1,0:T(8,128)(2,1)S(1)} %get-tuple-element.48.attn_ref), channel_id=1, source_target_pairs={{0,8},{4,12},{8,0},{12,4},{16,20},{20,16},{24,28},{28,24},{1,9},{5... | collective-permute-start | bytes 1572872 | tf_op jit(solution)/shard_map/ppermute | solution.py:461
  27.3 4.8 %collective-permute-start.4 = (bf16[512,128]{1,0:T(8,128)(2,1)S(1)}, bf16[512,128]{1,0:T(8,128)(2,1)S(1)}, u32[]{:S(2)}, u32[]{:S(2)}) collective-permute-start(bf16[512,128]{1,0:T(8,128)(2,1)S(1)} %get-tuple-element.52), channel_id=1, source_target_pairs={{16,0},{17,1},{18,2},{19,3},{20,4},{21,5},{22,6},{23,7},{24,8},{25... | collective-permute-start | bytes 393224 | tf_op jit(solution)/shard_map/ppermute | solution.py:411
  33.4 9.2 %collective-permute-start.10 = (bf16[256,1024]{1,0:T(8,128)(2,1)S(1)}, bf16[256,1024]{1,0:T(8,128)(2,1)S(1)}, u32[]{:S(2)}, u32[]{:S(2)}) collective-permute-start(bf16[256,1024]{1,0:T(8,128)(2,1)S(1)} %collective-permute-done.2.m1_ref), channel_id=1, source_target_pairs={{0,16},{16,0},{1,17},{17,1},{2,18},{18,2},{3,19},{19,3},{4,20},{20... | collective-permute-start | bytes 1572872 | tf_op jit(solution)/shard_map/ppermute | solution.py:479
  33.4 9.2 %collective-permute-start.11 = (bf16[256,1024]{1,0:T(8,128)(2,1)S(1)}, bf16[256,1024]{1,0:T(8,128)(2,1)S(1)}, u32[]{:S(2)}, u32[]{:S(2)}) collective-permute-start(bf16[256,1024]{1,0:T(8,128)(2,1)S(1)} %collective-permute-done.9.z1_ref), channel_id=1, source_target_pairs={{0,16},{16,0},{1,17},{17,1},{2,18},{18,2},{3,19},{19,3},{4,20},{20... | collective-permute-start | bytes 1572872 | tf_op jit(solution)/shard_map/ppermute | solution.py:488
  33.9 10.5 %collective-permute-start.12 = (bf16[512,512]{1,0:T(8,128)(2,1)S(1)}, bf16[512,512]{1,0:T(8,128)(2,1)S(1)}, u32[]{:S(2)}, u32[]{:S(2)}) collective-permute-start(bf16[512,512]{1,0:T(8,128)(2,1)S(1)} %collective-permute-done.7.a1_ref), channel_id=1, source_target_pairs={{0,8},{4,12},{8,0},{12,4},{16,20},{20,16},{24,28},{28,24},{1,9},{5... | collective-permute-start | bytes 1572872 | tf_op jit(solution)/shard_map/ppermute | solution.py:487
  38.6 5.8 %collective-permute-start.13 = (bf16[256,1024]{1,0:T(8,128)(2,1)S(1)}, bf16[256,1024]{1,0:T(8,128)(2,1)S(1)}, u32[]{:S(2)}, u32[]{:S(2)}) collective-permute-start(bf16[256,1024]{1,0:T(8,128)(2,1)S(1)} %collective-permute-done.6.d_ref), channel_id=1, source_target_pairs={{0,16},{1,17},{2,18},{3,19},{4,20},{5,21},{6,22},{7,23},{8,24},{9,... | collective-permute-start | bytes 1572872 | tf_op jit(solution)/shard_map/ppermute | solution.py:489
  41.2 3.2 %collective-permute-start.15 = (bf16[256,1024]{1,0:T(8,128)(2,1)S(1)}, bf16[256,1024]{1,0:T(8,128)(2,1)S(1)}, u32[]{:S(2)}, u32[]{:S(2)}) collective-permute-start(bf16[256,1024]{1,0:T(8,128)(2,1)S(1)} %collective-permute-done.14.dz_ref), channel_id=1, source_target_pairs={{0,16},{1,17},{2,18},{3,19},{4,20},{5,21},{6,22},{7,23},{8,24},{9,... | collective-permute-start | bytes 1572872 | tf_op jit(solution)/shard_map/ppermute | solution.py:494

commit v8 on v7

--- a/solution.py
+++ b/solution.py
@@ -259,7 +259,7 @@
 def own_weight_grad(scal, attn_t, out_grad, other_t, other_grad):
     width = attn_t.shape[0]
     own_width = other_grad.shape[1]
-    block = min(256, own_width // 2)
+    block = min(1024, own_width // 2)
     blocks = own_width // block
     early = blocks // 2
     return pl.pallas_call(
@@ -429,10 +429,11 @@
         group = ("ctx", "head")
         near = [(4 * (i // 2) + i, i ^ 1) for i in range(4)]
         near += [(4 * (1 - i // 2) + i, 4 + (i ^ 2)) for i in range(4)]
-        far = [(4 * (1 - i // 2) + i, i ^ 3) for i in range(4)]
+        far = [(4 * (1 - i // 2) + i, 4 + (i ^ 3)) for i in range(4)]
         one = [(i, i ^ 1) for i in range(4)] + [(4 + i, 4 + (i ^ 2)) for i in range(4)]
         two = [(i, i ^ 2) for i in range(4)] + [(4 + i, 4 + (i ^ 1)) for i in range(4)]
         zpair = [(i, i ^ 1) for i in range(n_rep)]
+        zfar = [(n_rep + i, n_rep + (i ^ 1)) for i in range(n_rep)]
         swap = [(0, 1), (1, 0)]
         state, near_piece, far_piece, turn, queries, keys, values = opening(
             scal, in_hbm(queries), in_hbm(keys), in_hbm(values), weight_hbm, grad_hbm
@@ -470,7 +471,7 @@
     suffix = total([shift(gsum, "ctx", n_ctx, -k, False) for k in range(1, n_ctx)])
 
     if paired:
-        far_z = lax.ppermute(after(far_mine, gsum), ("ctx", "rep"), zpair)
+        far_z = lax.ppermute(after(far_mine, gsum), ("ctx", "rep"), zfar)
         other_attn = after(other_attn, gsum, far_mine)
 
     early, late = own_weight_grad(scal, attn_t, out_grad, other_attn, other_grad)
@@ -486,12 +487,12 @@
     if paired:
         attn_3 = lax.ppermute(after(attn_1, late), group, two)
         near_other_z = lax.ppermute(after(near_z, late), "ctx", swap)
-        far_other = lax.ppermute(after(far_mine, late), "ctx", [(0, 1)])
+        far_other = lax.ppermute(after(far_mine, late), "ctx", [(1, 0)])
         near_out = project_near(
             scal, after(own_out, query_grad), (attn_1, attn_2),
             (near_mine, near_z, near_other, near_other_z),
         )
-        far_other_z = lax.ppermute(after(far_z, query_grad), "ctx", [(0, 1)])
+        far_other_z = lax.ppermute(after(far_z, query_grad), "ctx", [(1, 0)])
         layer_out = project_far(scal, near_out, attn_3, (far_mine, far_other, far_z, far_other_z))
     else:
         full = lax.all_gather(out_weight, "ctx", axis=1, tiled=True)

time: 46.7 us -> 45.5 us (0.974)
  starting transfers between devices: 22.4 us -> 19.6 us
  waiting for transfers between devices: 1.44 us -> 2.53 us
    ppermute x3, starting transfers between devices: 6.27 us -> 3.28 us  [the longest x1 1.29 us: body(): far_other = lax.ppermute(after(far_mine, late), 'ctx', [(1, 0)])]
    ppermute x3, waiting for transfers between devices: 0.01 us -> 1.17 us  [the longest x1 1.17 us: body(): far_other_z = lax.ppermute(after(far_z, query_grad), 'ctx', [(1, 0)])]
    ppermute x1, waiting for transfers between devices: 0.01 us -> 1.12 us  [body(): near_z = lax.ppermute(near_mine, 'rep', zpair)]
    ppermute x1, waiting for transfers between devices: 1.25 us -> 0.2 us  [body(): attn_1 = lax.ppermute(attn, group, one)]
    ppermute x1, starting transfers between devices: 0.01 us -> 1 us  [body(): near_other = lax.ppermute(after(near_mine, late), 'ctx', swap)]
    ppermute x1, starting transfers between devices: 1.49 us -> 2.34 us  [body(): attn_1 = lax.ppermute(attn, group, one)]
    ppermute x1, starting transfers between devices: 1.05 us -> 0.22 us  [body(): attn_2 = lax.ppermute(attn, group, two)]
    ppermute x1, starting transfers between devices: 2.47 us -> 1.65 us  [body(): near_z = lax.ppermute(near_mine, 'rep', zpair)]
  transfers between devices with their start and end apart: 16 -> 16, of which waited for: 2 -> 3; matrix products, arithmetic and copies ran while one was open for 0% -> 0% of each run, Pallas kernels for 42% -> 44%
where the time goes in v8:
time: 45.5 us; the launch traced here: 45.2 us
  Pallas kernels  22.1 us (49%)
  starting transfers between devices  19.6 us (43%)
  waiting for transfers between devices  2.53 us (6%)
  between operations  0.85 us (2%)
    ppermute x4, starting transfers between devices, shift(): return lax.ppermute(array, axis, pairs)  6.32 us
    pallas_call x1, Pallas kernels, backward(): pl.pallas_call(backward_kernel, out_shape=(out, out, out, shape_of(early....  4.09 us
    pallas_call x1, Pallas kernels, own_weight_grad(): pl.pallas_call(weight_grad_kernel, out_shape=(shape_of((width, own_width)...  3.93 us
    pallas_call x1, Pallas kernels, opening(): pl.pallas_call(opening_kernel, out_shape=(shape_of((width, DH), BF16), pi...  3.42 us
    ppermute x1, starting transfers between devices, body(): near_mine = lax.ppermute(near_piece, group, near)  2.94 us
    pallas_call x1, Pallas kernels, attn_gradient(): pl.pallas_call(attn_grad_kernel, out_shape=shape_of((tok, width), BF16),...  2.9 us
    ppermute x1, starting transfers between devices, body(): attn_1 = lax.ppermute(attn, group, one)  2.34 us
    pallas_call x1, Pallas kernels, cotangent(): pl.pallas_call(cotangent_kernel, out_shape=(shape_of((tok, width), BF16),...  2.3 us
  transfers between devices with their start and end apart: 16, of which 3 were waited for; matrix products, arithmetic and copies ran while one was open for 0% of the time, Pallas kernels for 44%

profile of v8, /device:TPU:0, one launch (start us, length us, event | category | flops | bytes accessed | tf_op | source)
XLA Modules:
  0.0 45.2 jit_solution(280386683377963563)
XLA Ops:
  0.6 0.5 %collective-permute-start = (bf16[512,2048]{1,0:T(8,128)(2,1)}, bf16[512,2048]{1,0:T(8,128)(2,1)S(1)}, u32[]{:S(2)}, u32[]{:S(2)}) collective-permute-start(bf16[512,2048]{1,0:T(8,128)(2,1)} %own_ref.3), channel_id=1, source_target_pairs={{0,16},{16,0},{1,17},{17,1},{2,18},{18,2},{3,19},{19,3},{4,20},{20... | collective-permute-start | bytes 6291464 | tf_op jit(solution)/shard_map/ppermute | solution.py:411
  1.1 0.1 pad_add_fusion.s_ref
  1.2 0.0 copy-start
  1.2 0.0 copy-start.1
  1.2 3.4 %shard_map.92 = (bf16[512,128]{1,0:T(8,128)(2,1)S(1)}, bf16[256,1024]{1,0:T(8,128)(2,1)S(1)}, bf16[256,1024]{1,0:T(8,128)(2,1)S(1)}, bf16[512,2048]{1,0:T(8,128)...) custom-call(s32[4]{0:T(128)S(1)} %pad_add_fusion.s_ref, ...), custom_call_target="tpu_custom_call" | custom-call | flops 67108864 | bytes 1048576 | tf_op jit(solution)/shard_map/pallas_call | solution.py:103
  4.7 0.1 collective-permute-start.3
  4.8 2.9 %collective-permute-start.2 = (bf16[256,1024]{1,0:T(8,128)(2,1)S(1)}, bf16[256,1024]{1,0:T(8,128)(2,1)S(1)}, u32[]{:S(2)}, u32[]{:S(2)}) collective-permute-start(bf16[256,1024]{1,0:T(8,128)(2,1)S(1)} %get-tuple-element.45), channel_id=1, source_target_pairs={{0,4},{4,0},{24,12},{28,8},{16,24},{20,28},{8,16},{12,20},{1,5},{5... | collective-permute-start | bytes 1572872 | tf_op jit(solution)/shard_map/ppermute | solution.py:441
  7.7 0.7 %collective-permute-start.6 = (bf16[256,1024]{1,0:T(8,128)(2,1)S(1)}, bf16[256,1024]{1,0:T(8,128)(2,1)S(1)}, u32[]{:S(2)}, u32[]{:S(2)}) collective-permute-start(bf16[256,1024]{1,0:T(8,128)(2,1)S(1)} %get-tuple-element.54), channel_id=1, source_target_pairs={{16,28},{20,24},{8,20},{12,16},{17,29},{21,25},{9,21},{13,17},{18,... | collective-permute-start | bytes 1572872 | tf_op jit(solution)/shard_map/ppermute | solution.py:442
  8.4 4.5 %collective-permute-start.1 = (bf16[512,128]{1,0:T(8,128)(2,1)S(1)}, bf16[512,128]{1,0:T(8,128)(2,1)S(1)}, u32[]{:S(2)}, u32[]{:S(2)}) collective-permute-start(bf16[512,128]{1,0:T(8,128)(2,1)S(1)} %get-tuple-element.38), channel_id=1, source_target_pairs={{0,16},{1,17},{2,18},{3,19},{4,20},{5,21},{6,22},{7,23},{8,24},{9,... | collective-permute-start | bytes 393224 | tf_op jit(solution)/shard_map/ppermute | solution.py:411
  12.9 0.0 collective-permute-done.rest_ref
  12.9 0.0 copy-done
  12.9 0.0 copy-done.1
  12.9 2.9 %shard_map.93.attn_grad_ref = bf16[512,512]{1,0:T(8,128)(2,1)S(1)} custom-call(s32[4]{0:T(128)S(1)} %pad_add_fusion.s_ref, bf16[512,2048]{1,0:T(8,128)(2,1)S(1)} %copy-done.1, bf16[512,4096]{1,0:T(8,128)(2,1)S(1)} %copy-done, bf16[512,2048]{1,0:T(8,128)(2,1)S(1)} %collective-permute-done.rest_ref), custom_call_target="tpu_custom_call" | custom-call | flops 2147483648 | bytes 8388608 | tf_op jit(solution)/shard_map/pallas_call | solution.py:181
  15.8 0.0 collective-permute-done.1.carried_ref
  15.8 1.6 %shard_map.94 = (bf16[512,512]{1,0:T(8,128)(2,1)S(1)}, bf16[512,512]{1,0:T(8,128)(2,1)S(1)}, f32[512,512]{1,0:T(8,128)S(1)}, bf16[2,512,128]{2,1,0:T(8,128)(2,1)S(1)}) custom-call(bf16[512,512]{1,0:T(8,128)(2,1)S(1)} %get-tuple-element.40.q_ref, bf16[512,512]{1,0:T(8,128)(2,1)S(1)} %get-tuple-element.41.k_ref, bf16[512,512]{1,0:T(8,128)(2,1)S(1)} %get-tuple-element.42.v_ref, ...), custom_call_target="tpu_custom_call" | custom-call | flops 536870912 | bytes 3145728 | tf_op jit(solution)/shard_map/pallas_call | solution.py:148
  17.4 0.1 collective-permute-start.5
  17.5 0.0 collective-permute-done.2.m1_ref
  17.5 1.6 %collective-permute-start.9 = (bf16[256,1024]{1,0:T(8,128)(2,1)S(1)}, bf16[256,1024]{1,0:T(8,128)(2,1)S(1)}, u32[]{:S(2)}, u32[]{:S(2)}) collective-permute-start(bf16[256,1024]{1,0:T(8,128)(2,1)S(1)} %collective-permute-done.2.m1_ref), channel_id=1, source_target_pairs={{0,1},{1,0},{2,3},{3,2},{4,5},{5,4},{6,7},{7,6},{8,9},{9,8},{10,11... | collective-permute-start | bytes 1572872 | tf_op jit(solution)/shard_map/ppermute | solution.py:463
  19.2 0.0 collective-permute-done.3.other_grad_ref
  19.2 2.3 %collective-permute-start.7 = (bf16[512,512]{1,0:T(8,128)(2,1)S(1)}, bf16[512,512]{1,0:T(8,128)(2,1)S(1)}, u32[]{:S(2)}, u32[]{:S(2)}) collective-permute-start(bf16[512,512]{1,0:T(8,128)(2,1)S(1)} %get-tuple-element.48.attn_ref), channel_id=1, source_target_pairs={{0,4},{4,0},{8,12},{12,8},{16,24},{20,28},{24,16},{28,20},{1,5},{5... | collective-permute-start | bytes 1572872 | tf_op jit(solution)/shard_map/ppermute | solution.py:461
  21.5 2.3 %shard_map.95 = (bf16[512,512]{1,0:T(8,128)(2,1)S(1)}, bf16[512,128]{1,0:T(8,128)(2,1)S(1)}, f32[2,512,128]{2,1,0:T(8,128)S(1)}, f32[512,1024]{1,0:T(8,128)S(1)}) custom-call(s32[4]{0:T(128)S(1)} %pad_add_fusion.s_ref, bf16[512,512]{1,0:T(8,128)(2,1)S(1)} %shard_map.93.attn_grad_ref, bf16[512,512]{1,0:T(8,128)(2,1)S(1)} %get-tuple-element.40.q_ref, ...), custom_call_target="tpu_custom_call" | custom-call | flops 536870912 | bytes 4194304 | tf_op jit(solution)/shard_map/pallas_call | solution.py:221
  23.8 0.0 collective-permute-done.6.d_ref
  23.8 0.7 %collective-permute-start.14 = (bf16[256,1024]{1,0:T(8,128)(2,1)S(1)}, bf16[256,1024]{1,0:T(8,128)(2,1)S(1)}, u32[]{:S(2)}, u32[]{:S(2)}) collective-permute-start(bf16[256,1024]{1,0:T(8,128)(2,1)S(1)} %collective-permute-done.6.d_ref), channel_id=1, source_target_pairs={{16,17},{17,16},{18,19},{19,18},{20,21},{21,20},{22,23},{23,22},{2... | collective-permute-start | bytes 1572872 | tf_op jit(solution)/shard_map/ppermute | solution.py:474
  24.5 0.2 collective-permute-start.8
  24.7 0.0 collective-permute-done.5.other_t_ref
  24.7 1.3 %collective-permute-start.4 = (bf16[512,128]{1,0:T(8,128)(2,1)S(1)}, bf16[512,128]{1,0:T(8,128)(2,1)S(1)}, u32[]{:S(2)}, u32[]{:S(2)}) collective-permute-start(bf16[512,128]{1,0:T(8,128)(2,1)S(1)} %get-tuple-element.52), channel_id=1, source_target_pairs={{16,0},{17,1},{18,2},{19,3},{20,4},{21,5},{22,6},{23,7},{24,8},{25... | collective-permute-start | bytes 393224 | tf_op jit(solution)/shard_map/ppermute | solution.py:411
  26.0 3.9 %shard_map.96 = (f32[512,2048]{1,0:T(8,128)}, f32[1,512,1024]{2,1,0:T(8,128)S(1)}) custom-call(s32[4]{0:T(128)S(1)} %pad_add_fusion.s_ref, bf16[512,512]{1,0:T(8,128)(2,1)S(1)} %get-tuple-element.53.attn_t_ref, bf16[512,4096]{1,0:T(8,128)(2,1)S(1)} %copy-done, bf16[512,512]{1,0:T(8,128)(2,1)S(1)} %collective-permute-done.5.other_t_ref, ...), custom_call_target="tpu_custom_call" | custom-call | flops 1000 | bytes 1000 | tf_op jit(solution)/shard_map/pallas_call | solution.py:265
  30.0 0.0 collective-permute-done.4.suffix_ref
  30.0 0.2 collective-permute-done.7.a1_ref
  30.2 1.0 %collective-permute-start.10 = (bf16[256,1024]{1,0:T(8,128)(2,1)S(1)}, bf16[256,1024]{1,0:T(8,128)(2,1)S(1)}, u32[]{:S(2)}, u32[]{:S(2)}) collective-permute-start(bf16[256,1024]{1,0:T(8,128)(2,1)S(1)} %collective-permute-done.2.m1_ref), channel_id=1, source_target_pairs={{0,16},{16,0},{1,17},{17,1},{2,18},{18,2},{3,19},{19,3},{4,20},{20... | collective-permute-start | bytes 1572872 | tf_op jit(solution)/shard_map/ppermute | solution.py:480
  31.2 1.1 %collective-permute-done.9.z1_ref = bf16[256,1024]{1,0:T(8,128)(2,1)S(1)} collective-permute-done((bf16[256,1024]{1,0:T(8,128)(2,1)S(1)}, bf16[256,1024]{1,0:T(8,128)(2,1)S(1)}, u32[]{:S(2)}, u32[]{:S(2)}) %collective-permute-start.9) | collective-permute-done | bytes 524320 | tf_op jit(solution)/shard_map/ppermute | solution.py:463
  32.3 0.0 collective-permute-start.11
  32.3 1.1 %collective-permute-start.12 = (bf16[512,512]{1,0:T(8,128)(2,1)S(1)}, bf16[512,512]{1,0:T(8,128)(2,1)S(1)}, u32[]{:S(2)}, u32[]{:S(2)}) collective-permute-start(bf16[512,512]{1,0:T(8,128)(2,1)S(1)} %collective-permute-done.7.a1_ref), channel_id=1, source_target_pairs={{0,8},{4,12},{8,0},{12,4},{16,20},{20,16},{24,28},{28,24},{1,9},{5... | collective-permute-start | bytes 1572872 | tf_op jit(solution)/shard_map/ppermute | solution.py:488
  33.4 4.1 %shard_map.97 = (bf16[512,512]{1,0:T(8,128)(2,1)}, bf16[512,512]{1,0:T(8,128)(2,1)}, bf16[512,512]{1,0:T(8,128)(2,1)}, f32[512,2048]{1,0:T(8,128)}) custom-call(bf16[512,512]{1,0:T(8,128)(2,1)S(1)} %get-tuple-element.40.q_ref, bf16[512,512]{1,0:T(8,128)(2,1)S(1)} %get-tuple-element.41.k_ref, ...), custom_call_target="tpu_custom_call", output_to_operand_aliasing={{3}: (8, {})} | custom-call | flops 1000 | bytes 1000 | tf_op jit(solution)/shard_map/pallas_call | solution.py:331
  37.5 0.0 collective-permute-done.14.dz_ref
  37.5 1.3 %collective-permute-start.13 = (bf16[256,1024]{1,0:T(8,128)(2,1)S(1)}, bf16[256,1024]{1,0:T(8,128)(2,1)S(1)}, u32[]{:S(2)}, u32[]{:S(2)}) collective-permute-start(bf16[256,1024]{1,0:T(8,128)(2,1)S(1)} %collective-permute-done.6.d_ref), channel_id=1, source_target_pairs={{16,0},{17,1},{18,2},{19,3},{20,4},{21,5},{22,6},{23,7},{24,8},{25... | collective-permute-start | bytes 1572872 | tf_op jit(solution)/shard_map/ppermute | solution.py:490
  38.8 0.0 collective-permute-done.8.a2_ref
  38.8 1.3 %collective-permute-start.15 = (bf16[256,1024]{1,0:T(8,128)(2,1)S(1)}, bf16[256,1024]{1,0:T(8,128)(2,1)S(1)}, u32[]{:S(2)}, u32[]{:S(2)}) collective-permute-start(bf16[256,1024]{1,0:T(8,128)(2,1)S(1)} %collective-permute-done.14.dz_ref), channel_id=1, source_target_pairs={{16,0},{17,1},{18,2},{19,3},{20,4},{21,5},{22,6},{23,7},{24,8},{25... | collective-permute-start | bytes 1572872 | tf_op jit(solution)/shard_map/ppermute | solution.py:495
  40.1 0.0 collective-permute-done.10.o1_ref
  40.1 0.0 collective-permute-done.11.oz1_ref
  40.1 1.8 %shard_map.98.near_ref = f32[512,1024]{1,0:T(8,128)S(1)} custom-call(s32[4]{0:T(128)S(1)} %pad_add_fusion.s_ref, f32[512,1024]{1,0:T(8,128)S(1)} %get-tuple-element.61.so_far_ref, bf16[512,512]{1,0:T(8,128)(2,1)S(1)} %collective-permute-done.7.a1_ref, bf16[512,512]{1,0:T(8,128)(2,1)S(1)} %collective-permute-done.8.a2_ref, ...), custom_call_target="tpu_custom_call" | custom-call | flops 1000 | bytes 1000 | tf_op jit(solution)/shard_map/pallas_call | solution.py:360
  42.0 0.0 collective-permute-done.12.a_ref
  42.0 0.0 collective-permute-done.13.od_ref
  42.0 1.2 %collective-permute-done.15.odz_ref = bf16[256,1024]{1,0:T(8,128)(2,1)S(1)} collective-permute-done((bf16[256,1024]{1,0:T(8,128)(2,1)S(1)}, bf16[256,1024]{1,0:T(8,128)(2,1)S(1)}, u32[]{:S(2)}, u32[]{:S(2)}) %collective-permute-start.15) | collective-permute-done | bytes 524320 | tf_op jit(solution)/shard_map/ppermute | solution.py:495
  43.1 2.1 %shard_map.99 = bf16[512,1024]{1,0:T(8,128)(2,1)} custom-call(s32[4]{0:T(128)S(1)} %pad_add_fusion.s_ref, f32[512,1024]{1,0:T(8,128)S(1)} %shard_map.98.near_ref, bf16[512,512]{1,0:T(8,128)(2,1)S(1)} %collective-permute-done.12.a_ref, bf16[256,1024]{1,0:T(8,128)(2,1)S(1)} %collective-permute-done.6.d_ref, ...), custom_call_target="tpu_custom_call" | custom-call | flops 1000 | bytes 1000 | tf_op jit(solution)/shard_map/pallas_call | solution.py:387
Async XLA Ops:
  0.6 12.2 %collective-permute-start = (bf16[512,2048]{1,0:T(8,128)(2,1)}, bf16[512,2048]{1,0:T(8,128)(2,1)S(1)}, u32[]{:S(2)}, u32[]{:S(2)}) collective-permute-start(bf16[512,2048]{1,0:T(8,128)(2,1)} %own_ref.3), channel_id=1, source_target_pairs={{0,16},{16,0},{1,17},{17,1},{2,18},{18,2},{3,19},{19,3},{4,20},{20... | collective-permute-start | bytes 6291464 | tf_op jit(solution)/shard_map/ppermute | solution.py:411
  1.2 11.7 %copy-start = (bf16[512,4096]{1,0:T(8,128)(2,1)S(1)}, bf16[512,4096]{1,0:T(8,128)(2,1)}, u32[]{:S(2)}) copy-start(bf16[512,4096]{1,0:T(8,128)(2,1)} %grad_ref.3) | copy-start | bytes 12582916
  1.2 11.7 %copy-start.1 = (bf16[512,2048]{1,0:T(8,128)(2,1)S(1)}, bf16[512,2048]{1,0:T(8,128)(2,1)}, u32[]{:S(2)}) copy-start(bf16[512,2048]{1,0:T(8,128)(2,1)} %own_ref.3) | copy-start | bytes 6291460
  4.7 14.5 %collective-permute-start.3 = (bf16[512,2048]{1,0:T(8,128)(2,1)S(1)}, bf16[512,2048]{1,0:T(8,128)(2,1)S(1)}, u32[]{:S(2)}, u32[]{:S(2)}) collective-permute-start(bf16[512,2048]{1,0:T(8,128)(2,1)S(1)} %get-tuple-element.46), channel_id=1, source_target_pairs={{0,16},{16,0},{1,17},{17,1},{2,18},{18,2},{3,19},{19,3},{4,20},{20... | collective-permute-start | bytes 6291464 | tf_op jit(solution)/shard_map/ppermute | solution.py:443
  4.8 12.7 %collective-permute-start.2 = (bf16[256,1024]{1,0:T(8,128)(2,1)S(1)}, bf16[256,1024]{1,0:T(8,128)(2,1)S(1)}, u32[]{:S(2)}, u32[]{:S(2)}) collective-permute-start(bf16[256,1024]{1,0:T(8,128)(2,1)S(1)} %get-tuple-element.45), channel_id=1, source_target_pairs={{0,4},{4,0},{24,12},{28,8},{16,24},{20,28},{8,16},{12,20},{1,5},{5... | collective-permute-start | bytes 1572872 | tf_op jit(solution)/shard_map/ppermute | solution.py:441
  7.7 16.1 %collective-permute-start.6 = (bf16[256,1024]{1,0:T(8,128)(2,1)S(1)}, bf16[256,1024]{1,0:T(8,128)(2,1)S(1)}, u32[]{:S(2)}, u32[]{:S(2)}) collective-permute-start(bf16[256,1024]{1,0:T(8,128)(2,1)S(1)} %get-tuple-element.54), channel_id=1, source_target_pairs={{16,28},{20,24},{8,20},{12,16},{17,29},{21,25},{9,21},{13,17},{18,... | collective-permute-start | bytes 1572872 | tf_op jit(solution)/shard_map/ppermute | solution.py:442
  8.4 7.4 %collective-permute-start.1 = (bf16[512,128]{1,0:T(8,128)(2,1)S(1)}, bf16[512,128]{1,0:T(8,128)(2,1)S(1)}, u32[]{:S(2)}, u32[]{:S(2)}) collective-permute-start(bf16[512,128]{1,0:T(8,128)(2,1)S(1)} %get-tuple-element.38), channel_id=1, source_target_pairs={{0,16},{1,17},{2,18},{3,19},{4,20},{5,21},{6,22},{7,23},{8,24},{9,... | collective-permute-start | bytes 393224 | tf_op jit(solution)/shard_map/ppermute | solution.py:411
  17.4 7.3 %collective-permute-start.5 = (bf16[512,512]{1,0:T(8,128)(2,1)S(1)}, bf16[512,512]{1,0:T(8,128)(2,1)S(1)}, u32[]{:S(2)}, u32[]{:S(2)}) collective-permute-start(bf16[512,512]{1,0:T(8,128)(2,1)S(1)} %get-tuple-element.53.attn_t_ref), channel_id=1, source_target_pairs={{0,16},{16,0},{1,17},{17,1},{2,18},{18,2},{3,19},{19,3},{4,20},{20... | collective-permute-start | bytes 1572872 | tf_op jit(solution)/shard_map/ppermute | solution.py:411
  17.5 14.8 %collective-permute-start.9 = (bf16[256,1024]{1,0:T(8,128)(2,1)S(1)}, bf16[256,1024]{1,0:T(8,128)(2,1)S(1)}, u32[]{:S(2)}, u32[]{:S(2)}) collective-permute-start(bf16[256,1024]{1,0:T(8,128)(2,1)S(1)} %collective-permute-done.2.m1_ref), channel_id=1, source_target_pairs={{0,1},{1,0},{2,3},{3,2},{4,5},{5,4},{6,7},{7,6},{8,9},{9,8},{10,11... | collective-permute-start | bytes 1572872 | tf_op jit(solution)/shard_map/ppermute | solution.py:463
  19.2 11.0 %collective-permute-start.7 = (bf16[512,512]{1,0:T(8,128)(2,1)S(1)}, bf16[512,512]{1,0:T(8,128)(2,1)S(1)}, u32[]{:S(2)}, u32[]{:S(2)}) collective-permute-start(bf16[512,512]{1,0:T(8,128)(2,1)S(1)} %get-tuple-element.48.attn_ref), channel_id=1, source_target_pairs={{0,4},{4,0},{8,12},{12,8},{16,24},{20,28},{24,16},{28,20},{1,5},{5... | collective-permute-start | bytes 1572872 | tf_op jit(solution)/shard_map/ppermute | solution.py:461
  23.8 13.7 %collective-permute-start.14 = (bf16[256,1024]{1,0:T(8,128)(2,1)S(1)}, bf16[256,1024]{1,0:T(8,128)(2,1)S(1)}, u32[]{:S(2)}, u32[]{:S(2)}) collective-permute-start(bf16[256,1024]{1,0:T(8,128)(2,1)S(1)} %collective-permute-done.6.d_ref), channel_id=1, source_target_pairs={{16,17},{17,16},{18,19},{19,18},{20,21},{21,20},{22,23},{23,22},{2... | collective-permute-start | bytes 1572872 | tf_op jit(solution)/shard_map/ppermute | solution.py:474
  24.5 14.3 %collective-permute-start.8 = (bf16[512,512]{1,0:T(8,128)(2,1)S(1)}, bf16[512,512]{1,0:T(8,128)(2,1)S(1)}, u32[]{:S(2)}, u32[]{:S(2)}) collective-permute-start(bf16[512,512]{1,0:T(8,128)(2,1)S(1)} %get-tuple-element.48.attn_ref), channel_id=1, source_target_pairs={{0,8},{4,12},{8,0},{12,4},{16,20},{20,16},{24,28},{28,24},{1,9},{5... | collective-permute-start | bytes 1572872 | tf_op jit(solution)/shard_map/ppermute | solution.py:462
  24.7 5.2 %collective-permute-start.4 = (bf16[512,128]{1,0:T(8,128)(2,1)S(1)}, bf16[512,128]{1,0:T(8,128)(2,1)S(1)}, u32[]{:S(2)}, u32[]{:S(2)}) collective-permute-start(bf16[512,128]{1,0:T(8,128)(2,1)S(1)} %get-tuple-element.52), channel_id=1, source_target_pairs={{16,0},{17,1},{18,2},{19,3},{20,4},{21,5},{22,6},{23,7},{24,8},{25... | collective-permute-start | bytes 393224 | tf_op jit(solution)/shard_map/ppermute | solution.py:411
  30.2 9.9 %collective-permute-start.10 = (bf16[256,1024]{1,0:T(8,128)(2,1)S(1)}, bf16[256,1024]{1,0:T(8,128)(2,1)S(1)}, u32[]{:S(2)}, u32[]{:S(2)}) collective-permute-start(bf16[256,1024]{1,0:T(8,128)(2,1)S(1)} %collective-permute-done.2.m1_ref), channel_id=1, source_target_pairs={{0,16},{16,0},{1,17},{17,1},{2,18},{18,2},{3,19},{19,3},{4,20},{20... | collective-permute-start | bytes 1572872 | tf_op jit(solution)/shard_map/ppermute | solution.py:480
  32.3 7.8 %collective-permute-start.11 = (bf16[256,1024]{1,0:T(8,128)(2,1)S(1)}, bf16[256,1024]{1,0:T(8,128)(2,1)S(1)}, u32[]{:S(2)}, u32[]{:S(2)}) collective-permute-start(bf16[256,1024]{1,0:T(8,128)(2,1)S(1)} %collective-permute-done.9.z1_ref), channel_id=1, source_target_pairs={{0,16},{16,0},{1,17},{17,1},{2,18},{18,2},{3,19},{19,3},{4,20},{20... | collective-permute-start | bytes 1572872 | tf_op jit(solution)/shard_map/ppermute | solution.py:489
  32.3 9.6 %collective-permute-start.12 = (bf16[512,512]{1,0:T(8,128)(2,1)S(1)}, bf16[512,512]{1,0:T(8,128)(2,1)S(1)}, u32[]{:S(2)}, u32[]{:S(2)}) collective-permute-start(bf16[512,512]{1,0:T(8,128)(2,1)S(1)} %collective-permute-done.7.a1_ref), channel_id=1, source_target_pairs={{0,8},{4,12},{8,0},{12,4},{16,20},{20,16},{24,28},{28,24},{1,9},{5... | collective-permute-start | bytes 1572872 | tf_op jit(solution)/shard_map/ppermute | solution.py:488
  37.5 4.5 %collective-permute-start.13 = (bf16[256,1024]{1,0:T(8,128)(2,1)S(1)}, bf16[256,1024]{1,0:T(8,128)(2,1)S(1)}, u32[]{:S(2)}, u32[]{:S(2)}) collective-permute-start(bf16[256,1024]{1,0:T(8,128)(2,1)S(1)} %collective-permute-done.6.d_ref), channel_id=1, source_target_pairs={{16,0},{17,1},{18,2},{19,3},{20,4},{21,5},{22,6},{23,7},{24,8},{25... | collective-permute-start | bytes 1572872 | tf_op jit(solution)/shard_map/ppermute | solution.py:490
  38.8 4.3 %collective-permute-start.15 = (bf16[256,1024]{1,0:T(8,128)(2,1)S(1)}, bf16[256,1024]{1,0:T(8,128)(2,1)S(1)}, u32[]{:S(2)}, u32[]{:S(2)}) collective-permute-start(bf16[256,1024]{1,0:T(8,128)(2,1)S(1)} %collective-permute-done.14.dz_ref), channel_id=1, source_target_pairs={{16,0},{17,1},{18,2},{19,3},{20,4},{21,5},{22,6},{23,7},{24,8},{25... | collective-permute-start | bytes 1572872 | tf_op jit(solution)/shard_map/ppermute | solution.py:495

commit v9 on v8

--- a/solution.py
+++ b/solution.py
@@ -232,7 +232,14 @@
     )(scal, attn_grad, queries, raw, attn, own, rest)
 
 
-def weight_grad_kernel(s_ref, attn_t_ref, grad_ref, other_t_ref, other_grad_ref, out_hbm, late_ref, out_buf, sems):
+def weight_grad_kernel(pieces, s_ref, attn_t_ref, grad_ref, other_t_ref, other_grad_ref, *refs):
+    piece_refs, share_refs = refs[:pieces], refs[pieces + 2 : -3]
+    out_hbm, late_ref = refs[pieces : pieces + 2]
+    out_buf, sems, piece_sems = refs[-3:]
+    shares = []
+    for n, piece_ref in enumerate(piece_refs):
+        shares.append(pltpu.make_async_copy(piece_ref, share_refs[0].at[n], piece_sems.at[n]))
+        shares[-1].start()
     width, tok = attn_t_ref.shape
     early, _, block = out_buf.shape
     blocks = early + late_ref.shape[0]
@@ -252,31 +259,35 @@
             moves[-1].start()
         else:
             late_ref[j - early] = acc
-    for move in moves:
+    for move in moves + shares:
         move.wait()
 
 
-def own_weight_grad(scal, attn_t, out_grad, other_t, other_grad):
+def own_weight_grad(scal, attn_t, out_grad, other_t, other_grad, pieces):
     width = attn_t.shape[0]
     own_width = other_grad.shape[1]
-    block = min(1024, own_width // 2)
+    block = min(256, own_width // 2)
     blocks = own_width // block
     early = blocks // 2
-    return pl.pallas_call(
-        weight_grad_kernel,
-        out_shape=(
+    vmem = pl.BlockSpec(memory_space=pltpu.VMEM)
+    share = [shape_of((len(pieces), *pieces[0].shape), BF16)] if pieces else []
+    return pl.pallas_call(
+        functools.partial(weight_grad_kernel, len(pieces)),
+        out_shape=[
             shape_of((width, own_width), F32),
             shape_of((blocks - early, width, block), F32),
-        ),
-        in_specs=smem_then_vmem(4),
-        out_specs=(pl.BlockSpec(memory_space=pl.ANY), pl.BlockSpec(memory_space=pltpu.VMEM)),
+            *share,
+        ],
+        in_specs=smem_then_vmem(4 + len(pieces)),
+        out_specs=[pl.BlockSpec(memory_space=pl.ANY), vmem] + [vmem] * len(share),
         scratch_shapes=[
             pltpu.VMEM((early, width, block), F32),
             pltpu.SemaphoreType.DMA((early,)),
+            pltpu.SemaphoreType.DMA((max(1, len(pieces)),)),
         ],
         compiler_params=params(16),
         cost_estimate=cost(1000, 1000),
-    )(scal, attn_t, out_grad, other_t, other_grad)
+    )(scal, attn_t, out_grad, other_t, other_grad, *pieces)
 
 
 def backward_kernel(q_ref, k_ref, v_ref, draw_ref, prefix_ref, suffix_ref, glocal_ref, late_ref, early_hbm,
@@ -337,7 +348,7 @@
         + [pltpu.SemaphoreType.DMA((3, width // DH)), pltpu.SemaphoreType.DMA((late.shape[0],))],
         input_output_aliases={8: 3},
         compiler_params=params(16),
-        cost_estimate=cost(1000, 1000),
+        cost_estimate=cost(256 * queries.size * DH, 64 * queries.size),
     )(queries, keys, values, draw, prefix, suffix, glocal, late, early)
 
 
@@ -351,7 +362,7 @@
     first, second = halves(s_ref, m1_ref.shape[0])
     acc = so_far_ref[...] + dot_nn(a1_ref[:, first], m1_ref[...])
     acc += dot_nn(a1_ref[:, second], z1_ref[...])
-    acc += dot_nn(a2_ref[:, first], o1_ref[...])
+    acc += dot_nn(a2_ref[:, first], o1_ref[0])
     acc += dot_nn(a2_ref[:, second], oz1_ref[...])
     out_ref[...] = acc
 
@@ -372,7 +383,7 @@
     moves = []
     for j in range(blocks):
         here = slice(j * block, (j + 1) * block)
-        acc = near_ref[:, here] + dot_nn(a_ref[:, first], d_ref[:, here] + od_ref[:, here])
+        acc = near_ref[:, here] + dot_nn(a_ref[:, first], d_ref[:, here] + od_ref[1, :, here])
         acc += dot_nn(a_ref[:, second], dz_ref[:, here] + odz_ref[:, here])
         out_buf[j] = acc.astype(BF16)
         moves.append(pltpu.make_async_copy(out_buf.at[j], out_hbm.at[:, here], sems.at[j]))
@@ -474,10 +485,11 @@
         far_z = lax.ppermute(after(far_mine, gsum), ("ctx", "rep"), zfar)
         other_attn = after(other_attn, gsum, far_mine)
 
-    early, late = own_weight_grad(scal, attn_t, out_grad, other_attn, other_grad)
+    pieces = (near_mine, far_mine) if paired else ()
+    early, late, *share = own_weight_grad(scal, attn_t, out_grad, other_attn, other_grad, pieces)
 
     if paired:
-        near_other = lax.ppermute(after(near_mine, late), "ctx", swap)
+        others = lax.ppermute(share[0], "ctx", swap)
         suffix = after(suffix, late, attn_1)
 
     query_grad, key_grad, value_grad, weight_grad = backward(
@@ -487,13 +499,12 @@
     if paired:
         attn_3 = lax.ppermute(after(attn_1, late), group, two)
         near_other_z = lax.ppermute(after(near_z, late), "ctx", swap)
-        far_other = lax.ppermute(after(far_mine, late), "ctx", [(1, 0)])
         near_out = project_near(
             scal, after(own_out, query_grad), (attn_1, attn_2),
-            (near_mine, near_z, near_other, near_other_z),
+            (near_mine, near_z, others, near_other_z),
         )
         far_other_z = lax.ppermute(after(far_z, query_grad), "ctx", [(1, 0)])
-        layer_out = project_far(scal, near_out, attn_3, (far_mine, far_other, far_z, far_other_z))
+        layer_out = project_far(scal, near_out, attn_3, (far_mine, others, far_z, far_other_z))
     else:
         full = lax.all_gather(out_weight, "ctx", axis=1, tiled=True)
         partial_out = jnp.dot(attn, full, preferred_element_type=F32).astype(BF16)

time: 45.5 us -> 44.7 us (0.982)
  starting transfers between devices: 19.6 us -> 17.6 us
  waiting for transfers between devices: 2.53 us -> 4.18 us
    ppermute x1, waiting for transfers between devices: 0.01 us -> 1.74 us  [body(): attn_3 = lax.ppermute(after(attn_1, late), group, two)]
    ppermute x1, waiting for transfers between devices: 1.12 us -> 2.4 us  [body(): near_z = lax.ppermute(near_mine, 'rep', zpair)]
    ppermute x1, waiting for transfers between devices: 1.17 us -> 0.01 us  [body(): far_other_z = lax.ppermute(after(far_z, query_grad), 'ctx', [(1, 0)])]
    ppermute x1, starting transfers between devices: 1.08 us -> 0.16 us  [body(): attn_3 = lax.ppermute(after(attn_1, late), group, two)]
    ppermute x1, starting transfers between devices: 2.34 us -> 1.49 us  [body(): attn_1 = lax.ppermute(attn, group, one)]
    ppermute x4, starting transfers between devices: 6.32 us -> 5.7 us  [shift(): return lax.ppermute(array, axis, pairs)]
    ppermute x2 -> x1, starting transfers between devices: 2.29 us -> 2.63 us  [body(): others = lax.ppermute(share[0], 'ctx', swap)]
  transfers between devices with their start and end apart: 16 -> 15, of which waited for: 3 -> 2; matrix products, arithmetic and copies ran while one was open for 0% -> 0% of each run, Pallas kernels for 44% -> 44%
where the time goes in v9:
time: 44.7 us; the launch traced here: 44.5 us
  Pallas kernels  21.8 us (49%)
  starting transfers between devices  17.6 us (39%)
  waiting for transfers between devices  4.18 us (9%)
  between operations  0.82 us (2%)
    ppermute x4, starting transfers between devices, shift(): return lax.ppermute(array, axis, pairs)  5.7 us
    pallas_call x1, Pallas kernels, backward(): pl.pallas_call(backward_kernel, out_shape=(out, out, out, shape_of(early....  4.12 us
    pallas_call x1, Pallas kernels, own_weight_grad(): pl.pallas_call(functools.partial(weight_grad_kernel, len(pieces)), out_sh...  3.6 us
    pallas_call x1, Pallas kernels, opening(): pl.pallas_call(opening_kernel, out_shape=(shape_of((width, DH), BF16), pi...  3.42 us
    ppermute x1, starting transfers between devices, body(): near_mine = lax.ppermute(near_piece, group, near)  2.94 us
    pallas_call x1, Pallas kernels, attn_gradient(): pl.pallas_call(attn_grad_kernel, out_shape=shape_of((tok, width), BF16),...  2.9 us
    ppermute x1, starting transfers between devices, body(): others = lax.ppermute(share[0], 'ctx', swap)  2.63 us
    ppermute x1, waiting for transfers between devices, body(): near_z = lax.ppermute(near_mine, 'rep', zpair)  2.4 us
  transfers between devices with their start and end apart: 15, of which 2 were waited for; matrix products, arithmetic and copies ran while one was open for 0% of the time, Pallas kernels for 44%

profile of v9, /device:TPU:0, one launch (start us, length us, event | category | flops | bytes accessed | tf_op | source)
XLA Modules:
  0.0 44.5 jit_solution(14802132442946839728)
XLA Ops:
  0.6 0.5 %collective-permute-start = (bf16[512,2048]{1,0:T(8,128)(2,1)}, bf16[512,2048]{1,0:T(8,128)(2,1)S(1)}, u32[]{:S(2)}, u32[]{:S(2)}) collective-permute-start(bf16[512,2048]{1,0:T(8,128)(2,1)} %own_ref.3), channel_id=1, source_target_pairs={{0,16},{16,0},{1,17},{17,1},{2,18},{18,2},{3,19},{19,3},{4,20},{20... | collective-permute-start | bytes 6291464 | tf_op jit(solution)/shard_map/ppermute | solution.py:422
  1.1 0.1 pad_add_fusion.s_ref
  1.2 0.0 copy-start
  1.2 0.0 copy-start.1
  1.2 3.4 %shard_map.92 = (bf16[512,128]{1,0:T(8,128)(2,1)S(1)}, bf16[256,1024]{1,0:T(8,128)(2,1)S(1)}, bf16[256,1024]{1,0:T(8,128)(2,1)S(1)}, bf16[512,2048]{1,0:T(8,128)...) custom-call(s32[4]{0:T(128)S(1)} %pad_add_fusion.s_ref, ...), custom_call_target="tpu_custom_call" | custom-call | flops 67108864 | bytes 1048576 | tf_op jit(solution)/shard_map/pallas_call | solution.py:103
  4.7 0.1 collective-permute-start.3
  4.8 2.9 %collective-permute-start.2 = (bf16[256,1024]{1,0:T(8,128)(2,1)S(1)}, bf16[256,1024]{1,0:T(8,128)(2,1)S(1)}, u32[]{:S(2)}, u32[]{:S(2)}) collective-permute-start(bf16[256,1024]{1,0:T(8,128)(2,1)S(1)} %get-tuple-element.44), channel_id=1, source_target_pairs={{0,4},{4,0},{24,12},{28,8},{16,24},{20,28},{8,16},{12,20},{1,5},{5... | collective-permute-start | bytes 1572872 | tf_op jit(solution)/shard_map/ppermute | solution.py:452
  7.7 1.7 %collective-permute-start.1 = (bf16[512,128]{1,0:T(8,128)(2,1)S(1)}, bf16[512,128]{1,0:T(8,128)(2,1)S(1)}, u32[]{:S(2)}, u32[]{:S(2)}) collective-permute-start(bf16[512,128]{1,0:T(8,128)(2,1)S(1)} %get-tuple-element.37), channel_id=1, source_target_pairs={{0,16},{1,17},{2,18},{3,19},{4,20},{5,21},{6,22},{7,23},{8,24},{9,... | collective-permute-start | bytes 393224 | tf_op jit(solution)/shard_map/ppermute | solution.py:422
  9.4 0.7 %collective-permute-start.6 = (bf16[256,1024]{1,0:T(8,128)(2,1)S(1)}, bf16[256,1024]{1,0:T(8,128)(2,1)S(1)}, u32[]{:S(2)}, u32[]{:S(2)}) collective-permute-start(bf16[256,1024]{1,0:T(8,128)(2,1)S(1)} %get-tuple-element.53), channel_id=1, source_target_pairs={{16,28},{20,24},{8,20},{12,16},{17,29},{21,25},{9,21},{13,17},{18,... | collective-permute-start | bytes 1572872 | tf_op jit(solution)/shard_map/ppermute | solution.py:453
  10.1 0.0 collective-permute-done.rest_ref
  10.2 0.0 copy-done
  10.2 0.0 copy-done.1
  10.2 2.9 %shard_map.93.attn_grad_ref = bf16[512,512]{1,0:T(8,128)(2,1)S(1)} custom-call(s32[4]{0:T(128)S(1)} %pad_add_fusion.s_ref, bf16[512,2048]{1,0:T(8,128)(2,1)S(1)} %copy-done.1, bf16[512,4096]{1,0:T(8,128)(2,1)S(1)} %copy-done, bf16[512,2048]{1,0:T(8,128)(2,1)S(1)} %collective-permute-done.rest_ref), custom_call_target="tpu_custom_call" | custom-call | flops 2147483648 | bytes 8388608 | tf_op jit(solution)/shard_map/pallas_call | solution.py:181
  13.1 0.0 collective-permute-done.1.carried_ref
  13.1 1.6 %shard_map.94 = (bf16[512,512]{1,0:T(8,128)(2,1)S(1)}, bf16[512,512]{1,0:T(8,128)(2,1)S(1)}, f32[512,512]{1,0:T(8,128)S(1)}, bf16[2,512,128]{2,1,0:T(8,128)(2,1)S(1)}) custom-call(bf16[512,512]{1,0:T(8,128)(2,1)S(1)} %get-tuple-element.39.q_ref, bf16[512,512]{1,0:T(8,128)(2,1)S(1)} %get-tuple-element.40.k_ref, bf16[512,512]{1,0:T(8,128)(2,1)S(1)} %get-tuple-element.41.v_ref, ...), custom_call_target="tpu_custom_call" | custom-call | flops 536870912 | bytes 3145728 | tf_op jit(solution)/shard_map/pallas_call | solution.py:148
  14.7 2.2 %collective-permute-start.5 = (bf16[512,512]{1,0:T(8,128)(2,1)S(1)}, bf16[512,512]{1,0:T(8,128)(2,1)S(1)}, u32[]{:S(2)}, u32[]{:S(2)}) collective-permute-start(bf16[512,512]{1,0:T(8,128)(2,1)S(1)} %get-tuple-element.52.attn_t_ref), channel_id=1, source_target_pairs={{0,16},{16,0},{1,17},{17,1},{2,18},{18,2},{3,19},{19,3},{4,20},{20... | collective-permute-start | bytes 1572872 | tf_op jit(solution)/shard_map/ppermute | solution.py:422
  16.9 1.5 %collective-permute-start.7 = (bf16[512,512]{1,0:T(8,128)(2,1)S(1)}, bf16[512,512]{1,0:T(8,128)(2,1)S(1)}, u32[]{:S(2)}, u32[]{:S(2)}) collective-permute-start(bf16[512,512]{1,0:T(8,128)(2,1)S(1)} %get-tuple-element.47.attn_ref), channel_id=1, source_target_pairs={{0,4},{4,0},{8,12},{12,8},{16,24},{20,28},{24,16},{28,20},{1,5},{5... | collective-permute-start | bytes 1572872 | tf_op jit(solution)/shard_map/ppermute | solution.py:472
  18.4 0.0 collective-permute-done.2.refs_0_.m1_ref
  18.4 1.6 %collective-permute-start.9 = (bf16[256,1024]{1,0:T(8,128)(2,1)S(1)}, bf16[256,1024]{1,0:T(8,128)(2,1)S(1)}, u32[]{:S(2)}, u32[]{:S(2)}) collective-permute-start(bf16[256,1024]{1,0:T(8,128)(2,1)S(1)} %collective-permute-done.2.refs_0_.m1_ref), channel_id=1, source_target_pairs={{0,1},{1,0},{2,3},{3,2},{4,5},{5,4},{6,7},{7,6},{8,9},{9,8},{10,11... | collective-permute-start | bytes 1572872 | tf_op jit(solution)/shard_map/ppermute | solution.py:474
  20.0 0.0 collective-permute-done.3.other_grad_ref
  20.0 2.3 %shard_map.95 = (bf16[512,512]{1,0:T(8,128)(2,1)S(1)}, bf16[512,128]{1,0:T(8,128)(2,1)S(1)}, f32[2,512,128]{2,1,0:T(8,128)S(1)}, f32[512,1024]{1,0:T(8,128)S(1)}) custom-call(s32[4]{0:T(128)S(1)} %pad_add_fusion.s_ref, bf16[512,512]{1,0:T(8,128)(2,1)S(1)} %shard_map.93.attn_grad_ref, bf16[512,512]{1,0:T(8,128)(2,1)S(1)} %get-tuple-element.39.q_ref, ...), custom_call_target="tpu_custom_call" | custom-call | flops 536870912 | bytes 4194304 | tf_op jit(solution)/shard_map/pallas_call | solution.py:221
  22.3 1.3 %collective-permute-start.4 = (bf16[512,128]{1,0:T(8,128)(2,1)S(1)}, bf16[512,128]{1,0:T(8,128)(2,1)S(1)}, u32[]{:S(2)}, u32[]{:S(2)}) collective-permute-start(bf16[512,128]{1,0:T(8,128)(2,1)S(1)} %get-tuple-element.51), channel_id=1, source_target_pairs={{16,0},{17,1},{18,2},{19,3},{20,4},{21,5},{22,6},{23,7},{24,8},{25... | collective-permute-start | bytes 393224 | tf_op jit(solution)/shard_map/ppermute | solution.py:422
  23.6 0.0 collective-permute-done.6.refs_1_.d_ref
  23.6 0.3 collective-permute-start.8
  23.8 0.0 collective-permute-done.5.other_t_ref
  23.8 0.7 %collective-permute-start.13 = (bf16[256,1024]{1,0:T(8,128)(2,1)S(1)}, bf16[256,1024]{1,0:T(8,128)(2,1)S(1)}, u32[]{:S(2)}, u32[]{:S(2)}) collective-permute-start(bf16[256,1024]{1,0:T(8,128)(2,1)S(1)} %collective-permute-done.6.refs_1_.d_ref), channel_id=1, source_target_pairs={{16,17},{17,16},{18,19},{19,18},{20,21},{21,20},{22,23},{23,22},{2... | collective-permute-start | bytes 1572872 | tf_op jit(solution)/shard_map/ppermute | solution.py:485
  24.5 3.6 %shard_map.96 = (f32[512,2048]{1,0:T(8,128)}, f32[4,512,256]{2,1,0:T(8,128)S(1)}, bf16[2,256,1024]{2,1,0:T(8,128)(2,1)S(1)}) custom-call(s32[4]{0:T(128)S(1)} %pad_add_fusion.s_ref, bf16[512,512]{1,0:T(8,128)(2,1)S(1)} %get-tuple-element.52.attn_t_ref, bf16[512,4096]{1,0:T(8,128)(2,1)S(1)} %copy-done, ...), custom_call_target="tpu_custom_call" | custom-call | flops 1000 | bytes 1000 | tf_op jit(solution)/shard_map/pallas_call | solution.py:274
  28.1 0.0 collective-permute-done.4.suffix_ref
  28.1 0.0 collective-permute-done.7.a1_ref
  28.2 2.6 %collective-permute-start.10 = (bf16[2,256,1024]{2,1,0:T(8,128)(2,1)S(1)}, bf16[2,256,1024]{2,1,0:T(8,128)(2,1)S(1)}, u32[]{:S(2)}, u32[]{:S(2)}) collective-permute-start(bf16[2,256,1024]{2,1,0:T(8,128)(2,1)S(1)} %get-tuple-element.61), channel_id=1, source_target_pairs={{0,16},{16,0},{1,17},{17,1},{2,18},{18,2},{3,19},{19,3},{4,20},{20... | collective-permute-start | bytes 3145736 | tf_op jit(solution)/shard_map/ppermute | solution.py:492
  30.8 2.4 %collective-permute-done.9.z1_ref = bf16[256,1024]{1,0:T(8,128)(2,1)S(1)} collective-permute-done((bf16[256,1024]{1,0:T(8,128)(2,1)S(1)}, bf16[256,1024]{1,0:T(8,128)(2,1)S(1)}, u32[]{:S(2)}, u32[]{:S(2)}) %collective-permute-start.9) | collective-permute-done | bytes 524320 | tf_op jit(solution)/shard_map/ppermute | solution.py:474
  33.2 0.0 collective-permute-start.11
  33.2 0.2 collective-permute-start.12
  33.3 4.1 %shard_map.97 = (bf16[512,512]{1,0:T(8,128)(2,1)}, bf16[512,512]{1,0:T(8,128)(2,1)}, bf16[512,512]{1,0:T(8,128)(2,1)}, f32[512,2048]{1,0:T(8,128)}) custom-call(bf16[512,512]{1,0:T(8,128)(2,1)S(1)} %get-tuple-element.39.q_ref, bf16[512,512]{1,0:T(8,128)(2,1)S(1)} %get-tuple-element.40.k_ref, ...), custom_call_target="tpu_custom_call", output_to_operand_aliasing={{3}: (8, {})} | custom-call | flops 8589934592 | bytes 16777216 | tf_op jit(solution)/shard_map/pallas_call | solution.py:342
  37.5 0.0 collective-permute-done.13.dz_ref
  37.5 1.3 %collective-permute-start.14 = (bf16[256,1024]{1,0:T(8,128)(2,1)S(1)}, bf16[256,1024]{1,0:T(8,128)(2,1)S(1)}, u32[]{:S(2)}, u32[]{:S(2)}) collective-permute-start(bf16[256,1024]{1,0:T(8,128)(2,1)S(1)} %collective-permute-done.13.dz_ref), channel_id=1, source_target_pairs={{16,0},{17,1},{18,2},{19,3},{20,4},{21,5},{22,6},{23,7},{24,8},{25... | collective-permute-start | bytes 1572872 | tf_op jit(solution)/shard_map/ppermute | solution.py:506
  38.8 0.0 collective-permute-done.8.a2_ref
  38.8 0.0 collective-permute-done.11.oz1_ref
  38.8 0.0 collective-permute-done.10.o1_ref.od_ref
  38.8 1.8 %shard_map.98.near_ref = f32[512,1024]{1,0:T(8,128)S(1)} custom-call(s32[4]{0:T(128)S(1)} %pad_add_fusion.s_ref, f32[512,1024]{1,0:T(8,128)S(1)} %get-tuple-element.60.so_far_ref, bf16[512,512]{1,0:T(8,128)(2,1)S(1)} %collective-permute-done.7.a1_ref, bf16[512,512]{1,0:T(8,128)(2,1)S(1)} %collective-permute-done.8.a2_ref, ...), custom_call_target="tpu_custom_call" | custom-call | flops 1000 | bytes 1000 | tf_op jit(solution)/shard_map/pallas_call | solution.py:371
  40.6 1.7 %collective-permute-done.12.a_ref = bf16[512,512]{1,0:T(8,128)(2,1)S(1)} collective-permute-done((bf16[512,512]{1,0:T(8,128)(2,1)S(1)}, bf16[512,512]{1,0:T(8,128)(2,1)S(1)}, u32[]{:S(2)}, u32[]{:S(2)}) %collective-permute-start.12) | collective-permute-done | bytes 524320 | tf_op jit(solution)/shard_map/ppermute | solution.py:500
  42.4 0.0 collective-permute-done.14.odz_ref
  42.4 2.1 %shard_map.99 = bf16[512,1024]{1,0:T(8,128)(2,1)} custom-call(s32[4]{0:T(128)S(1)} %pad_add_fusion.s_ref, f32[512,1024]{1,0:T(8,128)S(1)} %shard_map.98.near_ref, bf16[512,512]{1,0:T(8,128)(2,1)S(1)} %collective-permute-done.12.a_ref, bf16[256,1024]{1,0:T(8,128)(2,1)S(1)} %collective-permute-done.6.refs_1_.d_ref, ...), custom_call_target="tpu_custom_call" | custom-call | flops 1000 | bytes 1000 | tf_op jit(solution)/shard_map/pallas_call | solution.py:398
Async XLA Ops:
  0.6 9.5 %collective-permute-start = (bf16[512,2048]{1,0:T(8,128)(2,1)}, bf16[512,2048]{1,0:T(8,128)(2,1)S(1)}, u32[]{:S(2)}, u32[]{:S(2)}) collective-permute-start(bf16[512,2048]{1,0:T(8,128)(2,1)} %own_ref.3), channel_id=1, source_target_pairs={{0,16},{16,0},{1,17},{17,1},{2,18},{18,2},{3,19},{19,3},{4,20},{20... | collective-permute-start | bytes 6291464 | tf_op jit(solution)/shard_map/ppermute | solution.py:422
  1.2 8.9 %copy-start = (bf16[512,4096]{1,0:T(8,128)(2,1)S(1)}, bf16[512,4096]{1,0:T(8,128)(2,1)}, u32[]{:S(2)}) copy-start(bf16[512,4096]{1,0:T(8,128)(2,1)} %grad_ref.3) | copy-start | bytes 12582916
  1.2 8.9 %copy-start.1 = (bf16[512,2048]{1,0:T(8,128)(2,1)S(1)}, bf16[512,2048]{1,0:T(8,128)(2,1)}, u32[]{:S(2)}) copy-start(bf16[512,2048]{1,0:T(8,128)(2,1)} %own_ref.3) | copy-start | bytes 6291460
  4.7 15.3 %collective-permute-start.3 = (bf16[512,2048]{1,0:T(8,128)(2,1)S(1)}, bf16[512,2048]{1,0:T(8,128)(2,1)S(1)}, u32[]{:S(2)}, u32[]{:S(2)}) collective-permute-start(bf16[512,2048]{1,0:T(8,128)(2,1)S(1)} %get-tuple-element.45), channel_id=1, source_target_pairs={{0,16},{16,0},{1,17},{17,1},{2,18},{18,2},{3,19},{19,3},{4,20},{20... | collective-permute-start | bytes 6291464 | tf_op jit(solution)/shard_map/ppermute | solution.py:454
  4.8 13.6 %collective-permute-start.2 = (bf16[256,1024]{1,0:T(8,128)(2,1)S(1)}, bf16[256,1024]{1,0:T(8,128)(2,1)S(1)}, u32[]{:S(2)}, u32[]{:S(2)}) collective-permute-start(bf16[256,1024]{1,0:T(8,128)(2,1)S(1)} %get-tuple-element.44), channel_id=1, source_target_pairs={{0,4},{4,0},{24,12},{28,8},{16,24},{20,28},{8,16},{12,20},{1,5},{5... | collective-permute-start | bytes 1572872 | tf_op jit(solution)/shard_map/ppermute | solution.py:452
  7.7 5.4 %collective-permute-start.1 = (bf16[512,128]{1,0:T(8,128)(2,1)S(1)}, bf16[512,128]{1,0:T(8,128)(2,1)S(1)}, u32[]{:S(2)}, u32[]{:S(2)}) collective-permute-start(bf16[512,128]{1,0:T(8,128)(2,1)S(1)} %get-tuple-element.37), channel_id=1, source_target_pairs={{0,16},{1,17},{2,18},{3,19},{4,20},{5,21},{6,22},{7,23},{8,24},{9,... | collective-permute-start | bytes 393224 | tf_op jit(solution)/shard_map/ppermute | solution.py:422
  9.4 14.1 %collective-permute-start.6 = (bf16[256,1024]{1,0:T(8,128)(2,1)S(1)}, bf16[256,1024]{1,0:T(8,128)(2,1)S(1)}, u32[]{:S(2)}, u32[]{:S(2)}) collective-permute-start(bf16[256,1024]{1,0:T(8,128)(2,1)S(1)} %get-tuple-element.53), channel_id=1, source_target_pairs={{16,28},{20,24},{8,20},{12,16},{17,29},{21,25},{9,21},{13,17},{18,... | collective-permute-start | bytes 1572872 | tf_op jit(solution)/shard_map/ppermute | solution.py:453
  14.7 9.1 %collective-permute-start.5 = (bf16[512,512]{1,0:T(8,128)(2,1)S(1)}, bf16[512,512]{1,0:T(8,128)(2,1)S(1)}, u32[]{:S(2)}, u32[]{:S(2)}) collective-permute-start(bf16[512,512]{1,0:T(8,128)(2,1)S(1)} %get-tuple-element.52.attn_t_ref), channel_id=1, source_target_pairs={{0,16},{16,0},{1,17},{17,1},{2,18},{18,2},{3,19},{19,3},{4,20},{20... | collective-permute-start | bytes 1572872 | tf_op jit(solution)/shard_map/ppermute | solution.py:422
  16.9 11.3 %collective-permute-start.7 = (bf16[512,512]{1,0:T(8,128)(2,1)S(1)}, bf16[512,512]{1,0:T(8,128)(2,1)S(1)}, u32[]{:S(2)}, u32[]{:S(2)}) collective-permute-start(bf16[512,512]{1,0:T(8,128)(2,1)S(1)} %get-tuple-element.47.attn_ref), channel_id=1, source_target_pairs={{0,4},{4,0},{8,12},{12,8},{16,24},{20,28},{24,16},{28,20},{1,5},{5... | collective-permute-start | bytes 1572872 | tf_op jit(solution)/shard_map/ppermute | solution.py:472
  18.4 14.8 %collective-permute-start.9 = (bf16[256,1024]{1,0:T(8,128)(2,1)S(1)}, bf16[256,1024]{1,0:T(8,128)(2,1)S(1)}, u32[]{:S(2)}, u32[]{:S(2)}) collective-permute-start(bf16[256,1024]{1,0:T(8,128)(2,1)S(1)} %collective-permute-done.2.refs_0_.m1_ref), channel_id=1, source_target_pairs={{0,1},{1,0},{2,3},{3,2},{4,5},{5,4},{6,7},{7,6},{8,9},{9,8},{10,11... | collective-permute-start | bytes 1572872 | tf_op jit(solution)/shard_map/ppermute | solution.py:474
  22.3 5.9 %collective-permute-start.4 = (bf16[512,128]{1,0:T(8,128)(2,1)S(1)}, bf16[512,128]{1,0:T(8,128)(2,1)S(1)}, u32[]{:S(2)}, u32[]{:S(2)}) collective-permute-start(bf16[512,128]{1,0:T(8,128)(2,1)S(1)} %get-tuple-element.51), channel_id=1, source_target_pairs={{16,0},{17,1},{18,2},{19,3},{20,4},{21,5},{22,6},{23,7},{24,8},{25... | collective-permute-start | bytes 393224 | tf_op jit(solution)/shard_map/ppermute | solution.py:422
  23.6 15.2 %collective-permute-start.8 = (bf16[512,512]{1,0:T(8,128)(2,1)S(1)}, bf16[512,512]{1,0:T(8,128)(2,1)S(1)}, u32[]{:S(2)}, u32[]{:S(2)}) collective-permute-start(bf16[512,512]{1,0:T(8,128)(2,1)S(1)} %get-tuple-element.47.attn_ref), channel_id=1, source_target_pairs={{0,8},{4,12},{8,0},{12,4},{16,20},{20,16},{24,28},{28,24},{1,9},{5... | collective-permute-start | bytes 1572872 | tf_op jit(solution)/shard_map/ppermute | solution.py:473
  23.8 13.6 %collective-permute-start.13 = (bf16[256,1024]{1,0:T(8,128)(2,1)S(1)}, bf16[256,1024]{1,0:T(8,128)(2,1)S(1)}, u32[]{:S(2)}, u32[]{:S(2)}) collective-permute-start(bf16[256,1024]{1,0:T(8,128)(2,1)S(1)} %collective-permute-done.6.refs_1_.d_ref), channel_id=1, source_target_pairs={{16,17},{17,16},{18,19},{19,18},{20,21},{21,20},{22,23},{23,22},{2... | collective-permute-start | bytes 1572872 | tf_op jit(solution)/shard_map/ppermute | solution.py:485
  28.2 10.7 %collective-permute-start.10 = (bf16[2,256,1024]{2,1,0:T(8,128)(2,1)S(1)}, bf16[2,256,1024]{2,1,0:T(8,128)(2,1)S(1)}, u32[]{:S(2)}, u32[]{:S(2)}) collective-permute-start(bf16[2,256,1024]{2,1,0:T(8,128)(2,1)S(1)} %get-tuple-element.61), channel_id=1, source_target_pairs={{0,16},{16,0},{1,17},{17,1},{2,18},{18,2},{3,19},{19,3},{4,20},{20... | collective-permute-start | bytes 3145736 | tf_op jit(solution)/shard_map/ppermute | solution.py:492
  33.2 5.6 %collective-permute-start.11 = (bf16[256,1024]{1,0:T(8,128)(2,1)S(1)}, bf16[256,1024]{1,0:T(8,128)(2,1)S(1)}, u32[]{:S(2)}, u32[]{:S(2)}) collective-permute-start(bf16[256,1024]{1,0:T(8,128)(2,1)S(1)} %collective-permute-done.9.z1_ref), channel_id=1, source_target_pairs={{0,16},{16,0},{1,17},{17,1},{2,18},{18,2},{3,19},{19,3},{4,20},{20... | collective-permute-start | bytes 1572872 | tf_op jit(solution)/shard_map/ppermute | solution.py:501
  33.2 9.2 %collective-permute-start.12 = (bf16[512,512]{1,0:T(8,128)(2,1)S(1)}, bf16[512,512]{1,0:T(8,128)(2,1)S(1)}, u32[]{:S(2)}, u32[]{:S(2)}) collective-permute-start(bf16[512,512]{1,0:T(8,128)(2,1)S(1)} %collective-permute-done.7.a1_ref), channel_id=1, source_target_pairs={{0,8},{4,12},{8,0},{12,4},{16,20},{20,16},{24,28},{28,24},{1,9},{5... | collective-permute-start | bytes 1572872 | tf_op jit(solution)/shard_map/ppermute | solution.py:500
  37.5 4.9 %collective-permute-start.14 = (bf16[256,1024]{1,0:T(8,128)(2,1)S(1)}, bf16[256,1024]{1,0:T(8,128)(2,1)S(1)}, u32[]{:S(2)}, u32[]{:S(2)}) collective-permute-start(bf16[256,1024]{1,0:T(8,128)(2,1)S(1)} %collective-permute-done.13.dz_ref), channel_id=1, source_target_pairs={{16,0},{17,1},{18,2},{19,3},{20,4},{21,5},{22,6},{23,7},{24,8},{25... | collective-permute-start | bytes 1572872 | tf_op jit(solution)/shard_map/ppermute | solution.py:506

commit v10 on v9

--- a/solution.py
+++ b/solution.py
@@ -500,7 +500,7 @@
         attn_3 = lax.ppermute(after(attn_1, late), group, two)
         near_other_z = lax.ppermute(after(near_z, late), "ctx", swap)
         near_out = project_near(
-            scal, after(own_out, query_grad), (attn_1, attn_2),
+            scal, after(own_out, query_grad, attn_3), (attn_1, attn_2),
             (near_mine, near_z, others, near_other_z),
         )
         far_other_z = lax.ppermute(after(far_z, query_grad), "ctx", [(1, 0)])

time: 44.7 us -> 43.5 us (0.973)
  waiting for transfers between devices: 4.18 us -> 1.87 us
  starting transfers between devices: 17.6 us -> 18.6 us
    ppermute x1, waiting for transfers between devices: 1.74 us -> 0.01 us  [body(): attn_3 = lax.ppermute(after(attn_1, late), group, two)]
    ppermute x1, starting transfers between devices: 0.16 us -> 1.9 us  [body(): attn_3 = lax.ppermute(after(attn_1, late), group, two)]
    ppermute x1, waiting for transfers between devices: 2.4 us -> 1.19 us  [body(): near_z = lax.ppermute(near_mine, 'rep', zpair)]
    ppermute x1, starting transfers between devices: 2.63 us -> 1.95 us  [body(): others = lax.ppermute(share[0], 'ctx', swap)]
    ppermute x1, waiting for transfers between devices: 0.01 us -> 0.65 us  [body(): far_other_z = lax.ppermute(after(far_z, query_grad), 'ctx', [(1, 0)])]
  transfers between devices with their start and end apart: 15 -> 15, of which waited for: 2 -> 2; matrix products, arithmetic and copies ran while one was open for 0% -> 0% of each run, Pallas kernels for 44% -> 46%
where the time goes in v10:
time: 43.5 us; the launch traced here: 43.2 us
  Pallas kernels  21.8 us (50%)
  starting transfers between devices  18.6 us (43%)
  waiting for transfers between devices  1.87 us (4%)
  between operations  0.83 us (2%)
    ppermute x4, starting transfers between devices, shift(): return lax.ppermute(array, axis, pairs)  5.7 us
    pallas_call x1, Pallas kernels, backward(): pl.pallas_call(backward_kernel, out_shape=(out, out, out, shape_of(early....  4.12 us
    pallas_call x1, Pallas kernels, own_weight_grad(): pl.pallas_call(functools.partial(weight_grad_kernel, len(pieces)), out_sh...  3.6 us
    pallas_call x1, Pallas kernels, opening(): pl.pallas_call(opening_kernel, out_shape=(shape_of((width, DH), BF16), pi...  3.42 us
    ppermute x1, starting transfers between devices, body(): near_mine = lax.ppermute(near_piece, group, near)  2.94 us
    pallas_call x1, Pallas kernels, attn_gradient(): pl.pallas_call(attn_grad_kernel, out_shape=shape_of((tok, width), BF16),...  2.9 us
    pallas_call x1, Pallas kernels, cotangent(): pl.pallas_call(cotangent_kernel, out_shape=(shape_of((tok, width), BF16),...  2.29 us
    pallas_call x1, Pallas kernels, project_far(): pl.pallas_call(project_far_kernel, out_shape=shape_of((tok, out_width), B...  2.08 us
  transfers between devices with their start and end apart: 15, of which 2 were waited for; matrix products, arithmetic and copies ran while one was open for 0% of the time, Pallas kernels for 46%

profile of v10, /device:TPU:0, one launch (start us, length us, event | category | flops | bytes accessed | tf_op | source)
XLA Modules:
  0.0 43.2 jit_solution(6885872038624375762)
XLA Ops:
  0.6 0.5 %collective-permute-start = (bf16[512,2048]{1,0:T(8,128)(2,1)}, bf16[512,2048]{1,0:T(8,128)(2,1)S(1)}, u32[]{:S(2)}, u32[]{:S(2)}) collective-permute-start(bf16[512,2048]{1,0:T(8,128)(2,1)} %own_ref.3), channel_id=1, source_target_pairs={{0,16},{16,0},{1,17},{17,1},{2,18},{18,2},{3,19},{19,3},{4,20},{20... | collective-permute-start | bytes 6291464 | tf_op jit(solution)/shard_map/ppermute | solution.py:422
  1.1 0.1 pad_add_fusion.s_ref
  1.2 0.0 copy-start
  1.2 0.0 copy-start.1
  1.2 3.4 %shard_map.92 = (bf16[512,128]{1,0:T(8,128)(2,1)S(1)}, bf16[256,1024]{1,0:T(8,128)(2,1)S(1)}, bf16[256,1024]{1,0:T(8,128)(2,1)S(1)}, bf16[512,2048]{1,0:T(8,128)...) custom-call(s32[4]{0:T(128)S(1)} %pad_add_fusion.s_ref, ...), custom_call_target="tpu_custom_call" | custom-call | flops 67108864 | bytes 1048576 | tf_op jit(solution)/shard_map/pallas_call | solution.py:103
  4.7 0.1 collective-permute-start.3
  4.8 2.9 %collective-permute-start.2 = (bf16[256,1024]{1,0:T(8,128)(2,1)S(1)}, bf16[256,1024]{1,0:T(8,128)(2,1)S(1)}, u32[]{:S(2)}, u32[]{:S(2)}) collective-permute-start(bf16[256,1024]{1,0:T(8,128)(2,1)S(1)} %get-tuple-element.44), channel_id=1, source_target_pairs={{0,4},{4,0},{24,12},{28,8},{16,24},{20,28},{8,16},{12,20},{1,5},{5... | collective-permute-start | bytes 1572872 | tf_op jit(solution)/shard_map/ppermute | solution.py:452
  7.7 1.7 %collective-permute-start.1 = (bf16[512,128]{1,0:T(8,128)(2,1)S(1)}, bf16[512,128]{1,0:T(8,128)(2,1)S(1)}, u32[]{:S(2)}, u32[]{:S(2)}) collective-permute-start(bf16[512,128]{1,0:T(8,128)(2,1)S(1)} %get-tuple-element.37), channel_id=1, source_target_pairs={{0,16},{1,17},{2,18},{3,19},{4,20},{5,21},{6,22},{7,23},{8,24},{9,... | collective-permute-start | bytes 393224 | tf_op jit(solution)/shard_map/ppermute | solution.py:422
  9.4 0.7 %collective-permute-start.6 = (bf16[256,1024]{1,0:T(8,128)(2,1)S(1)}, bf16[256,1024]{1,0:T(8,128)(2,1)S(1)}, u32[]{:S(2)}, u32[]{:S(2)}) collective-permute-start(bf16[256,1024]{1,0:T(8,128)(2,1)S(1)} %get-tuple-element.53), channel_id=1, source_target_pairs={{16,28},{20,24},{8,20},{12,16},{17,29},{21,25},{9,21},{13,17},{18,... | collective-permute-start | bytes 1572872 | tf_op jit(solution)/shard_map/ppermute | solution.py:453
  10.1 0.0 collective-permute-done.rest_ref
  10.2 0.0 copy-done
  10.2 0.0 copy-done.1
  10.2 2.9 %shard_map.93.attn_grad_ref = bf16[512,512]{1,0:T(8,128)(2,1)S(1)} custom-call(s32[4]{0:T(128)S(1)} %pad_add_fusion.s_ref, bf16[512,2048]{1,0:T(8,128)(2,1)S(1)} %copy-done.1, bf16[512,4096]{1,0:T(8,128)(2,1)S(1)} %copy-done, bf16[512,2048]{1,0:T(8,128)(2,1)S(1)} %collective-permute-done.rest_ref), custom_call_target="tpu_custom_call" | custom-call | flops 2147483648 | bytes 8388608 | tf_op jit(solution)/shard_map/pallas_call | solution.py:181
  13.1 0.0 collective-permute-done.1.carried_ref
  13.1 1.6 %shard_map.94 = (bf16[512,512]{1,0:T(8,128)(2,1)S(1)}, bf16[512,512]{1,0:T(8,128)(2,1)S(1)}, f32[512,512]{1,0:T(8,128)S(1)}, bf16[2,512,128]{2,1,0:T(8,128)(2,1)S(1)}) custom-call(bf16[512,512]{1,0:T(8,128)(2,1)S(1)} %get-tuple-element.39.q_ref, bf16[512,512]{1,0:T(8,128)(2,1)S(1)} %get-tuple-element.40.k_ref, bf16[512,512]{1,0:T(8,128)(2,1)S(1)} %get-tuple-element.41.v_ref, ...), custom_call_target="tpu_custom_call" | custom-call | flops 536870912 | bytes 3145728 | tf_op jit(solution)/shard_map/pallas_call | solution.py:148
  14.7 2.2 %collective-permute-start.5 = (bf16[512,512]{1,0:T(8,128)(2,1)S(1)}, bf16[512,512]{1,0:T(8,128)(2,1)S(1)}, u32[]{:S(2)}, u32[]{:S(2)}) collective-permute-start(bf16[512,512]{1,0:T(8,128)(2,1)S(1)} %get-tuple-element.52.attn_t_ref), channel_id=1, source_target_pairs={{0,16},{16,0},{1,17},{17,1},{2,18},{18,2},{3,19},{19,3},{4,20},{20... | collective-permute-start | bytes 1572872 | tf_op jit(solution)/shard_map/ppermute | solution.py:422
  16.9 1.5 %collective-permute-start.7 = (bf16[512,512]{1,0:T(8,128)(2,1)S(1)}, bf16[512,512]{1,0:T(8,128)(2,1)S(1)}, u32[]{:S(2)}, u32[]{:S(2)}) collective-permute-start(bf16[512,512]{1,0:T(8,128)(2,1)S(1)} %get-tuple-element.47.attn_ref), channel_id=1, source_target_pairs={{0,4},{4,0},{8,12},{12,8},{16,24},{20,28},{24,16},{28,20},{1,5},{5... | collective-permute-start | bytes 1572872 | tf_op jit(solution)/shard_map/ppermute | solution.py:472
  18.4 0.0 collective-permute-done.2.refs_0_.m1_ref
  18.4 1.6 %collective-permute-start.10 = (bf16[256,1024]{1,0:T(8,128)(2,1)S(1)}, bf16[256,1024]{1,0:T(8,128)(2,1)S(1)}, u32[]{:S(2)}, u32[]{:S(2)}) collective-permute-start(bf16[256,1024]{1,0:T(8,128)(2,1)S(1)} %collective-permute-done.2.refs_0_.m1_ref), channel_id=1, source_target_pairs={{0,1},{1,0},{2,3},{3,2},{4,5},{5,4},{6,7},{7,6},{8,9},{9,8},{10,11... | collective-permute-start | bytes 1572872 | tf_op jit(solution)/shard_map/ppermute | solution.py:474
  20.0 0.0 collective-permute-done.3.other_grad_ref
  20.0 2.3 %shard_map.95 = (bf16[512,512]{1,0:T(8,128)(2,1)S(1)}, bf16[512,128]{1,0:T(8,128)(2,1)S(1)}, f32[2,512,128]{2,1,0:T(8,128)S(1)}, f32[512,1024]{1,0:T(8,128)S(1)}) custom-call(s32[4]{0:T(128)S(1)} %pad_add_fusion.s_ref, bf16[512,512]{1,0:T(8,128)(2,1)S(1)} %shard_map.93.attn_grad_ref, bf16[512,512]{1,0:T(8,128)(2,1)S(1)} %get-tuple-element.39.q_ref, ...), custom_call_target="tpu_custom_call" | custom-call | flops 536870912 | bytes 4194304 | tf_op jit(solution)/shard_map/pallas_call | solution.py:221
  22.3 1.3 %collective-permute-start.4 = (bf16[512,128]{1,0:T(8,128)(2,1)S(1)}, bf16[512,128]{1,0:T(8,128)(2,1)S(1)}, u32[]{:S(2)}, u32[]{:S(2)}) collective-permute-start(bf16[512,128]{1,0:T(8,128)(2,1)S(1)} %get-tuple-element.51), channel_id=1, source_target_pairs={{16,0},{17,1},{18,2},{19,3},{20,4},{21,5},{22,6},{23,7},{24,8},{25... | collective-permute-start | bytes 393224 | tf_op jit(solution)/shard_map/ppermute | solution.py:422
  23.6 0.0 collective-permute-done.6.refs_1_.d_ref
  23.6 0.3 collective-permute-start.9
  23.8 0.0 collective-permute-done.5.other_t_ref
  23.8 0.7 %collective-permute-start.13 = (bf16[256,1024]{1,0:T(8,128)(2,1)S(1)}, bf16[256,1024]{1,0:T(8,128)(2,1)S(1)}, u32[]{:S(2)}, u32[]{:S(2)}) collective-permute-start(bf16[256,1024]{1,0:T(8,128)(2,1)S(1)} %collective-permute-done.6.refs_1_.d_ref), channel_id=1, source_target_pairs={{16,17},{17,16},{18,19},{19,18},{20,21},{21,20},{22,23},{23,22},{2... | collective-permute-start | bytes 1572872 | tf_op jit(solution)/shard_map/ppermute | solution.py:485
  24.5 3.6 %shard_map.96 = (f32[512,2048]{1,0:T(8,128)}, f32[4,512,256]{2,1,0:T(8,128)S(1)}, bf16[2,256,1024]{2,1,0:T(8,128)(2,1)S(1)}) custom-call(s32[4]{0:T(128)S(1)} %pad_add_fusion.s_ref, bf16[512,512]{1,0:T(8,128)(2,1)S(1)} %get-tuple-element.52.attn_t_ref, bf16[512,4096]{1,0:T(8,128)(2,1)S(1)} %copy-done, ...), custom_call_target="tpu_custom_call" | custom-call | flops 1000 | bytes 1000 | tf_op jit(solution)/shard_map/pallas_call | solution.py:274
  28.1 0.0 collective-permute-done.4.suffix_ref
  28.1 0.0 collective-permute-done.7.a1_ref
  28.2 1.9 %collective-permute-start.8 = (bf16[512,512]{1,0:T(8,128)(2,1)S(1)}, bf16[512,512]{1,0:T(8,128)(2,1)S(1)}, u32[]{:S(2)}, u32[]{:S(2)}) collective-permute-start(bf16[512,512]{1,0:T(8,128)(2,1)S(1)} %collective-permute-done.7.a1_ref), channel_id=1, source_target_pairs={{0,8},{4,12},{8,0},{12,4},{16,20},{20,16},{24,28},{28,24},{1,9},{5... | collective-permute-start | bytes 1572872 | tf_op jit(solution)/shard_map/ppermute | solution.py:500
  30.0 2.0 %collective-permute-start.11 = (bf16[2,256,1024]{2,1,0:T(8,128)(2,1)S(1)}, bf16[2,256,1024]{2,1,0:T(8,128)(2,1)S(1)}, u32[]{:S(2)}, u32[]{:S(2)}) collective-permute-start(bf16[2,256,1024]{2,1,0:T(8,128)(2,1)S(1)} %get-tuple-element.62), channel_id=1, source_target_pairs={{0,16},{16,0},{1,17},{17,1},{2,18},{18,2},{3,19},{19,3},{4,20},{20... | collective-permute-start | bytes 3145736 | tf_op jit(solution)/shard_map/ppermute | solution.py:492
  32.0 1.2 %collective-permute-done.10.z1_ref = bf16[256,1024]{1,0:T(8,128)(2,1)S(1)} collective-permute-done((bf16[256,1024]{1,0:T(8,128)(2,1)S(1)}, bf16[256,1024]{1,0:T(8,128)(2,1)S(1)}, u32[]{:S(2)}, u32[]{:S(2)}) %collective-permute-start.10) | collective-permute-done | bytes 524320 | tf_op jit(solution)/shard_map/ppermute | solution.py:474
  33.2 0.0 collective-permute-start.12
  33.2 4.1 %shard_map.97 = (bf16[512,512]{1,0:T(8,128)(2,1)}, bf16[512,512]{1,0:T(8,128)(2,1)}, bf16[512,512]{1,0:T(8,128)(2,1)}, f32[512,2048]{1,0:T(8,128)}) custom-call(bf16[512,512]{1,0:T(8,128)(2,1)S(1)} %get-tuple-element.39.q_ref, bf16[512,512]{1,0:T(8,128)(2,1)S(1)} %get-tuple-element.40.k_ref, ...), custom_call_target="tpu_custom_call", output_to_operand_aliasing={{3}: (8, {})} | custom-call | flops 8589934592 | bytes 16777216 | tf_op jit(solution)/shard_map/pallas_call | solution.py:342
  37.3 0.0 collective-permute-done.13.dz_ref
  37.3 1.3 %collective-permute-start.14 = (bf16[256,1024]{1,0:T(8,128)(2,1)S(1)}, bf16[256,1024]{1,0:T(8,128)(2,1)S(1)}, u32[]{:S(2)}, u32[]{:S(2)}) collective-permute-start(bf16[256,1024]{1,0:T(8,128)(2,1)S(1)} %collective-permute-done.13.dz_ref), channel_id=1, source_target_pairs={{16,0},{17,1},{18,2},{19,3},{20,4},{21,5},{22,6},{23,7},{24,8},{25... | collective-permute-start | bytes 1572872 | tf_op jit(solution)/shard_map/ppermute | solution.py:506
  38.6 0.0 collective-permute-done.8.a_ref
  38.6 0.0 collective-permute-done.9.a2_ref
  38.7 0.0 collective-permute-done.12.oz1_ref
  38.7 0.0 collective-permute-done.11.o1_ref.od_ref
  38.7 1.8 %shard_map.98.near_ref = f32[512,1024]{1,0:T(8,128)S(1)} custom-call(s32[4]{0:T(128)S(1)} %pad_add_fusion.s_ref, f32[512,1024]{1,0:T(8,128)S(1)} %get-tuple-element.61.so_far_ref, bf16[512,512]{1,0:T(8,128)(2,1)S(1)} %collective-permute-done.7.a1_ref, bf16[512,512]{1,0:T(8,128)(2,1)S(1)} %collective-permute-done.9.a2_ref, ...), custom_call_target="tpu_custom_call" | custom-call | flops 1000 | bytes 1000 | tf_op jit(solution)/shard_map/pallas_call | solution.py:371
  40.5 0.6 %collective-permute-done.14.odz_ref = bf16[256,1024]{1,0:T(8,128)(2,1)S(1)} collective-permute-done((bf16[256,1024]{1,0:T(8,128)(2,1)S(1)}, bf16[256,1024]{1,0:T(8,128)(2,1)S(1)}, u32[]{:S(2)}, u32[]{:S(2)}) %collective-permute-start.14) | collective-permute-done | bytes 524320 | tf_op jit(solution)/shard_map/ppermute | solution.py:506
  41.1 2.1 %shard_map.99 = bf16[512,1024]{1,0:T(8,128)(2,1)} custom-call(s32[4]{0:T(128)S(1)} %pad_add_fusion.s_ref, f32[512,1024]{1,0:T(8,128)S(1)} %shard_map.98.near_ref, bf16[512,512]{1,0:T(8,128)(2,1)S(1)} %collective-permute-done.8.a_ref, bf16[256,1024]{1,0:T(8,128)(2,1)S(1)} %collective-permute-done.6.refs_1_.d_ref, ...), custom_call_target="tpu_custom_call" | custom-call | flops 1000 | bytes 1000 | tf_op jit(solution)/shard_map/pallas_call | solution.py:398
Async XLA Ops:
  0.6 9.5 %collective-permute-start = (bf16[512,2048]{1,0:T(8,128)(2,1)}, bf16[512,2048]{1,0:T(8,128)(2,1)S(1)}, u32[]{:S(2)}, u32[]{:S(2)}) collective-permute-start(bf16[512,2048]{1,0:T(8,128)(2,1)} %own_ref.3), channel_id=1, source_target_pairs={{0,16},{16,0},{1,17},{17,1},{2,18},{18,2},{3,19},{19,3},{4,20},{20... | collective-permute-start | bytes 6291464 | tf_op jit(solution)/shard_map/ppermute | solution.py:422
  1.2 8.9 %copy-start = (bf16[512,4096]{1,0:T(8,128)(2,1)S(1)}, bf16[512,4096]{1,0:T(8,128)(2,1)}, u32[]{:S(2)}) copy-start(bf16[512,4096]{1,0:T(8,128)(2,1)} %grad_ref.3) | copy-start | bytes 12582916
  1.2 8.9 %copy-start.1 = (bf16[512,2048]{1,0:T(8,128)(2,1)S(1)}, bf16[512,2048]{1,0:T(8,128)(2,1)}, u32[]{:S(2)}) copy-start(bf16[512,2048]{1,0:T(8,128)(2,1)} %own_ref.3) | copy-start | bytes 6291460
  4.7 15.3 %collective-permute-start.3 = (bf16[512,2048]{1,0:T(8,128)(2,1)S(1)}, bf16[512,2048]{1,0:T(8,128)(2,1)S(1)}, u32[]{:S(2)}, u32[]{:S(2)}) collective-permute-start(bf16[512,2048]{1,0:T(8,128)(2,1)S(1)} %get-tuple-element.45), channel_id=1, source_target_pairs={{0,16},{16,0},{1,17},{17,1},{2,18},{18,2},{3,19},{19,3},{4,20},{20... | collective-permute-start | bytes 6291464 | tf_op jit(solution)/shard_map/ppermute | solution.py:454
  4.8 13.6 %collective-permute-start.2 = (bf16[256,1024]{1,0:T(8,128)(2,1)S(1)}, bf16[256,1024]{1,0:T(8,128)(2,1)S(1)}, u32[]{:S(2)}, u32[]{:S(2)}) collective-permute-start(bf16[256,1024]{1,0:T(8,128)(2,1)S(1)} %get-tuple-element.44), channel_id=1, source_target_pairs={{0,4},{4,0},{24,12},{28,8},{16,24},{20,28},{8,16},{12,20},{1,5},{5... | collective-permute-start | bytes 1572872 | tf_op jit(solution)/shard_map/ppermute | solution.py:452
  7.7 5.4 %collective-permute-start.1 = (bf16[512,128]{1,0:T(8,128)(2,1)S(1)}, bf16[512,128]{1,0:T(8,128)(2,1)S(1)}, u32[]{:S(2)}, u32[]{:S(2)}) collective-permute-start(bf16[512,128]{1,0:T(8,128)(2,1)S(1)} %get-tuple-element.37), channel_id=1, source_target_pairs={{0,16},{1,17},{2,18},{3,19},{4,20},{5,21},{6,22},{7,23},{8,24},{9,... | collective-permute-start | bytes 393224 | tf_op jit(solution)/shard_map/ppermute | solution.py:422
  9.4 14.1 %collective-permute-start.6 = (bf16[256,1024]{1,0:T(8,128)(2,1)S(1)}, bf16[256,1024]{1,0:T(8,128)(2,1)S(1)}, u32[]{:S(2)}, u32[]{:S(2)}) collective-permute-start(bf16[256,1024]{1,0:T(8,128)(2,1)S(1)} %get-tuple-element.53), channel_id=1, source_target_pairs={{16,28},{20,24},{8,20},{12,16},{17,29},{21,25},{9,21},{13,17},{18,... | collective-permute-start | bytes 1572872 | tf_op jit(solution)/shard_map/ppermute | solution.py:453
  14.7 9.1 %collective-permute-start.5 = (bf16[512,512]{1,0:T(8,128)(2,1)S(1)}, bf16[512,512]{1,0:T(8,128)(2,1)S(1)}, u32[]{:S(2)}, u32[]{:S(2)}) collective-permute-start(bf16[512,512]{1,0:T(8,128)(2,1)S(1)} %get-tuple-element.52.attn_t_ref), channel_id=1, source_target_pairs={{0,16},{16,0},{1,17},{17,1},{2,18},{18,2},{3,19},{19,3},{4,20},{20... | collective-permute-start | bytes 1572872 | tf_op jit(solution)/shard_map/ppermute | solution.py:422
  16.9 11.3 %collective-permute-start.7 = (bf16[512,512]{1,0:T(8,128)(2,1)S(1)}, bf16[512,512]{1,0:T(8,128)(2,1)S(1)}, u32[]{:S(2)}, u32[]{:S(2)}) collective-permute-start(bf16[512,512]{1,0:T(8,128)(2,1)S(1)} %get-tuple-element.47.attn_ref), channel_id=1, source_target_pairs={{0,4},{4,0},{8,12},{12,8},{16,24},{20,28},{24,16},{28,20},{1,5},{5... | collective-permute-start | bytes 1572872 | tf_op jit(solution)/shard_map/ppermute | solution.py:472
  18.4 14.8 %collective-permute-start.10 = (bf16[256,1024]{1,0:T(8,128)(2,1)S(1)}, bf16[256,1024]{1,0:T(8,128)(2,1)S(1)}, u32[]{:S(2)}, u32[]{:S(2)}) collective-permute-start(bf16[256,1024]{1,0:T(8,128)(2,1)S(1)} %collective-permute-done.2.refs_0_.m1_ref), channel_id=1, source_target_pairs={{0,1},{1,0},{2,3},{3,2},{4,5},{5,4},{6,7},{7,6},{8,9},{9,8},{10,11... | collective-permute-start | bytes 1572872 | tf_op jit(solution)/shard_map/ppermute | solution.py:474
  22.3 5.9 %collective-permute-start.4 = (bf16[512,128]{1,0:T(8,128)(2,1)S(1)}, bf16[512,128]{1,0:T(8,128)(2,1)S(1)}, u32[]{:S(2)}, u32[]{:S(2)}) collective-permute-start(bf16[512,128]{1,0:T(8,128)(2,1)S(1)} %get-tuple-element.51), channel_id=1, source_target_pairs={{16,0},{17,1},{18,2},{19,3},{20,4},{21,5},{22,6},{23,7},{24,8},{25... | collective-permute-start | bytes 393224 | tf_op jit(solution)/shard_map/ppermute | solution.py:422
  23.6 15.1 %collective-permute-start.9 = (bf16[512,512]{1,0:T(8,128)(2,1)S(1)}, bf16[512,512]{1,0:T(8,128)(2,1)S(1)}, u32[]{:S(2)}, u32[]{:S(2)}) collective-permute-start(bf16[512,512]{1,0:T(8,128)(2,1)S(1)} %get-tuple-element.47.attn_ref), channel_id=1, source_target_pairs={{0,8},{4,12},{8,0},{12,4},{16,20},{20,16},{24,28},{28,24},{1,9},{5... | collective-permute-start | bytes 1572872 | tf_op jit(solution)/shard_map/ppermute | solution.py:473
  23.8 13.5 %collective-permute-start.13 = (bf16[256,1024]{1,0:T(8,128)(2,1)S(1)}, bf16[256,1024]{1,0:T(8,128)(2,1)S(1)}, u32[]{:S(2)}, u32[]{:S(2)}) collective-permute-start(bf16[256,1024]{1,0:T(8,128)(2,1)S(1)} %collective-permute-done.6.refs_1_.d_ref), channel_id=1, source_target_pairs={{16,17},{17,16},{18,19},{19,18},{20,21},{21,20},{22,23},{23,22},{2... | collective-permute-start | bytes 1572872 | tf_op jit(solution)/shard_map/ppermute | solution.py:485
  28.2 10.5 %collective-permute-start.8 = (bf16[512,512]{1,0:T(8,128)(2,1)S(1)}, bf16[512,512]{1,0:T(8,128)(2,1)S(1)}, u32[]{:S(2)}, u32[]{:S(2)}) collective-permute-start(bf16[512,512]{1,0:T(8,128)(2,1)S(1)} %collective-permute-done.7.a1_ref), channel_id=1, source_target_pairs={{0,8},{4,12},{8,0},{12,4},{16,20},{20,16},{24,28},{28,24},{1,9},{5... | collective-permute-start | bytes 1572872 | tf_op jit(solution)/shard_map/ppermute | solution.py:500
  30.0 8.6 %collective-permute-start.11 = (bf16[2,256,1024]{2,1,0:T(8,128)(2,1)S(1)}, bf16[2,256,1024]{2,1,0:T(8,128)(2,1)S(1)}, u32[]{:S(2)}, u32[]{:S(2)}) collective-permute-start(bf16[2,256,1024]{2,1,0:T(8,128)(2,1)S(1)} %get-tuple-element.62), channel_id=1, source_target_pairs={{0,16},{16,0},{1,17},{17,1},{2,18},{18,2},{3,19},{19,3},{4,20},{20... | collective-permute-start | bytes 3145736 | tf_op jit(solution)/shard_map/ppermute | solution.py:492
  33.2 5.5 %collective-permute-start.12 = (bf16[256,1024]{1,0:T(8,128)(2,1)S(1)}, bf16[256,1024]{1,0:T(8,128)(2,1)S(1)}, u32[]{:S(2)}, u32[]{:S(2)}) collective-permute-start(bf16[256,1024]{1,0:T(8,128)(2,1)S(1)} %collective-permute-done.10.z1_ref), channel_id=1, source_target_pairs={{0,16},{16,0},{1,17},{17,1},{2,18},{18,2},{3,19},{19,3},{4,20},{20... | collective-permute-start | bytes 1572872 | tf_op jit(solution)/shard_map/ppermute | solution.py:501
  37.3 3.8 %collective-permute-start.14 = (bf16[256,1024]{1,0:T(8,128)(2,1)S(1)}, bf16[256,1024]{1,0:T(8,128)(2,1)S(1)}, u32[]{:S(2)}, u32[]{:S(2)}) collective-permute-start(bf16[256,1024]{1,0:T(8,128)(2,1)S(1)} %collective-permute-done.13.dz_ref), channel_id=1, source_target_pairs={{16,0},{17,1},{18,2},{19,3},{20,4},{21,5},{22,6},{23,7},{24,8},{25... | collective-permute-start | bytes 1572872 | tf_op jit(solution)/shard_map/ppermute | solution.py:506
